TPU v7x, 32 devices: a whole 2x2x4 slice. The times are simulated.
32 devices in a mesh: fsdp: 4 (over y, x), ctx: 2 (over core), tp: 4 (over z).
Axes of the slice: x: 2, y: 2, z: 4, core: 2. Of those that a mesh axis runs over, the one named last changes fastest.
Arguments:
- hidden_in: bfloat16 [8, 2048, 1536], P('fsdp', 'ctx', 'tp'), may hold values from -6 to 6
- lengths: int32 [8], P('fsdp'), may hold values from 512 to 2048, as said below
- norm_gain: bfloat16 [1536], P('tp'), may hold values from 0.5 to 1.5
- proj_gate_inner: bfloat16 [1536, 2, 3072], P(('fsdp', 'ctx'), None, 'tp'), may hold values from -0.15625 to 0.15625
- proj_write_read: bfloat16 [1536, 256], P(('fsdp', 'ctx')), may hold values from -0.15625 to 0.15625
- proj_step: bfloat16 [1536, 48], P(('fsdp', 'ctx'), 'tp'), may hold values from -0.15625 to 0.15625
- conv_inner: float32 [4, 3072], P(None, 'tp'), may hold values from -3 to 3
- conv_inner_bias: float32 [3072], P('tp'), may hold values from -1.75 to 1.75
- conv_write_read: float32 [4, 256], replicated, may hold values from -3 to 3
- conv_write_read_bias: float32 [256], replicated, may hold values from -1.75 to 1.75
- step_bias: float32 [48], P('tp'), may hold values from -7 to -1
- log_rate: float32 [48], P('tp'), may hold values from -3 to 1
- skip_gain: float32 [48], P('tp'), may hold values from 0.5 to 1.5
- gate_gain: float32 [3072], P('tp'), may hold values from 0.5 to 1.5
- proj_out: bfloat16 [1536, 3072], P(('fsdp', 'ctx'), 'tp'), may hold values from -0.109375 to 0.109375
- out_cotangent: bfloat16 [8, 2048, 1536], P('fsdp', 'ctx', 'tp'), may hold values from -6 to 6
Outputs:
- hidden_out: bfloat16 [8, 2048, 1536], P('fsdp', 'ctx', 'tp')
- grad_hidden_in: float32 [8, 2048, 1536], P('fsdp', 'ctx', 'tp')
- grad_norm_gain: float32 [1536], P('tp')
- grad_proj_gate_inner: float32 [1536, 2, 3072], P(('fsdp', 'ctx'), None, 'tp')
- grad_proj_write_read: float32 [1536, 256], P(('fsdp', 'ctx'))
- grad_proj_step: float32 [1536, 48], P(('fsdp', 'ctx'), 'tp')
- grad_conv_inner: float32 [4, 3072], P(None, 'tp')
- grad_conv_inner_bias: float32 [3072], P('tp')
- grad_conv_write_read: float32 [4, 256], replicated
- grad_conv_write_read_bias: float32 [256], replicated
- grad_step_bias: float32 [48], P('tp')
- grad_log_rate: float32 [48], P('tp')
- grad_skip_gain: float32 [48], P('tp')
- grad_gate_gain: float32 [3072], P('tp')
- grad_proj_out: float32 [1536, 3072], P(('fsdp', 'ctx'), 'tp')
Inputs may be any that keep to these rules, and one draw needn't show every extreme that they name: lengths[s] is the number of valid leading positions of slot s; in every draw some slot is full.
All inputs are finite; a program needn't handle non-finite values.
Results may differ from a plain program's by a relative error of at most 0.017.
Values may be sent and summed in bfloat16 or wider, within the bound.
A program may use at most 192 MiB of HBM per device.

v0:
```python
import jax
import jax.numpy as jnp
from jax import lax
from jax.sharding import PartitionSpec as P

HEADDIM = 64
STATE = 128
CONV = 4
GROUP = 256
INNER = 3072


EPSILON = 1e-05


def passed_along(x, axis, by):
    count = lax.axis_size(axis)
    pairs = [(i, i + by) for i in range(count) if 0 <= i + by < count]
    return lax.ppermute(x, axis, pairs)


def carried_in(x, axis, combine, identity, reverse):
    count, position = (lax.axis_size(axis), lax.axis_index(axis))
    everything = jax.tree.map(
        lambda part, kind: lax.all_gather(part.astype(kind), axis), x, (jnp.bfloat16, jnp.bfloat16)
    )
    start = jax.tree.map(
        lambda part, zero: jnp.broadcast_to(jnp.asarray(zero, part.dtype), part.shape), x, identity
    )

    def lap(k, before):
        at = count - 1 - k if reverse else k
        reached = at > position if reverse else at < position
        new = combine(
            before, jax.tree.map(lambda part, own: part[at].astype(own.dtype), everything, x)
        )
        return jax.tree.map(lambda a, b: jnp.where(reached, a, b), new, before)

    return lax.fori_loop(0, count, lap, start)


def conv_silu(padded, conv_taps, conv_bias):
    tap_count = conv_taps.shape[0]
    length = padded.shape[-2] - tap_count + 1
    summed = conv_bias
    for offset in range(tap_count):
        summed = summed + conv_taps[offset] * padded[..., offset : offset + length, :]
    return jax.nn.silu(summed)


def decay_terms(scores, write_piece, read_piece, step_rows, log_rate):
    length = scores.shape[0]
    cumulative = jnp.cumsum(step_rows * (-jnp.exp(log_rate))[:, None], axis=1)
    lower_mask = jnp.arange(length)[:, None] >= jnp.arange(length)[None, :]
    spread = jnp.where(lower_mask[None], cumulative[:, :, None] - cumulative[:, None, :], 0.0)
    weights = (
        scores[None] * jnp.where(lower_mask[None], jnp.exp(spread), 0.0) * step_rows[:, None, :]
    )
    read_scaled = read_piece[None] * jnp.exp(cumulative)[:, :, None]
    write_scaled = (
        write_piece[None] * (jnp.exp(cumulative[:, -1:] - cumulative) * step_rows)[:, :, None]
    )
    return (weights, read_scaled, write_scaled, jnp.exp(cumulative[:, -1]))


def on_device(
    hidden_in,
    lengths,
    norm_gain,
    proj_gate_inner,
    proj_write_read,
    proj_step,
    conv_inner,
    conv_inner_bias,
    conv_write_read,
    conv_write_read_bias,
    step_bias,
    log_rate,
    skip_gain,
    gate_gain,
    proj_out,
    out_cotangent,
):
    slot_count, seq_here, width_here = hidden_in.shape
    heads_here = step_bias.shape[0]
    inner_here = gate_gain.shape[0]
    groups_here = seq_here // GROUP
    block_count = slot_count * groups_here
    rim_rows = CONV - 1
    full_x, full_gain, full_cot = (
        lax.all_gather(hidden_in, "tp", axis=2, tiled=True),
        lax.all_gather(norm_gain, "tp", axis=0, tiled=True),
        lax.all_gather(out_cotangent, "tp", axis=2, tiled=True),
    )
    full_gate_inner, full_write_read, full_step, full_out = (
        lax.all_gather(proj_gate_inner, ("fsdp", "ctx"), axis=0, tiled=True),
        lax.all_gather(proj_write_read, ("fsdp", "ctx"), axis=0, tiled=True),
        lax.all_gather(proj_step, ("fsdp", "ctx"), axis=0, tiled=True),
        lax.all_gather(proj_out, ("fsdp", "ctx"), axis=0, tiled=True),
    )
    in_float = full_x.astype(jnp.float32)
    in_scale = lax.rsqrt(jnp.mean(in_float * in_float, axis=-1, keepdims=True) + EPSILON)
    in_hat = in_float * in_scale
    gain_float = full_gain.astype(jnp.float32)
    normed = (in_hat * gain_float).astype(jnp.bfloat16)
    gate_inner = jnp.einsum(
        "bsd,dki->bski", normed, full_gate_inner, preferred_element_type=jnp.float32
    )
    gate_pre = gate_inner[:, :, 0]
    inner_pre = gate_inner[:, :, 1].astype(jnp.bfloat16)
    write_read_pre = jnp.einsum(
        "bsd,dn->bsn", normed, full_write_read, preferred_element_type=jnp.float32
    ).astype(jnp.bfloat16)
    step_raw = jnp.einsum("bsd,dh->bsh", normed, full_step, preferred_element_type=jnp.float32)
    inner_rim, write_read_rim = passed_along(
        (inner_pre[:, seq_here - rim_rows :], write_read_pre[:, seq_here - rim_rows :]), "ctx", 1
    )
    inner_pad = jnp.concatenate([inner_rim, inner_pre], axis=1).astype(jnp.float32)
    write_read_pad = jnp.concatenate([write_read_rim, write_read_pre], axis=1).astype(jnp.float32)
    inner_act = conv_silu(inner_pad, conv_inner, conv_inner_bias).astype(jnp.bfloat16)
    write_read_act = conv_silu(write_read_pad, conv_write_read, conv_write_read_bias).astype(
        jnp.bfloat16
    )
    step_size = jax.nn.softplus(step_raw + step_bias)
    inner_blocks = inner_act.reshape(block_count, GROUP, heads_here, HEADDIM)
    write_blocks = write_read_act[:, :, :STATE].reshape(block_count, GROUP, STATE)
    read_blocks = write_read_act[:, :, STATE:].reshape(block_count, GROUP, STATE)
    step_blocks = step_size.reshape(block_count, GROUP, heads_here).transpose(0, 2, 1)

    def forward_block(pieces):
        inner_piece, write_piece, read_piece, step_rows = pieces
        scores = jnp.dot(read_piece, write_piece.T, preferred_element_type=jnp.float32)
        weights, read_scaled, write_scaled, block_decay = decay_terms(
            scores,
            write_piece.astype(jnp.float32),
            read_piece.astype(jnp.float32),
            step_rows,
            log_rate,
        )
        intra_part = jnp.einsum(
            "hts,shp->thp",
            weights.astype(jnp.bfloat16),
            inner_piece,
            preferred_element_type=jnp.float32,
        )
        local_state = jnp.einsum(
            "shp,hsn->hpn",
            inner_piece,
            write_scaled.astype(jnp.bfloat16),
            preferred_element_type=jnp.float32,
        )
        return (intra_part, local_state, block_decay, read_scaled.astype(jnp.bfloat16))

    intra_part, local_state, block_decay, read_decayed = lax.map(
        forward_block, (inner_blocks, write_blocks, read_blocks, step_blocks)
    )
    local_state = local_state.reshape(slot_count, groups_here, heads_here, HEADDIM, STATE)
    block_decay = block_decay.reshape(slot_count, groups_here, heads_here)
    carried = jnp.zeros((slot_count, heads_here, HEADDIM, STATE), jnp.float32)
    device_decay = jnp.ones((slot_count, heads_here), jnp.float32)
    for position in range(groups_here):
        carried = block_decay[:, position, :, None, None] * carried + local_state[:, position]
        device_decay = device_decay * block_decay[:, position]

    def combine_states(earlier, latter):
        return (earlier[0] * latter[0], latter[0][:, :, None, None] * earlier[1] + latter[1])

    identity = (jnp.ones_like(device_decay), jnp.zeros_like(carried))
    prior = carried_in((device_decay, carried), "ctx", combine_states, identity, False)
    current = prior[1]
    state_list = []
    for position in range(groups_here):
        state_list.append(current)
        current = block_decay[:, position, :, None, None] * current + local_state[:, position]
    group_states = jnp.stack(state_list, axis=1)
    states_low = group_states.reshape(block_count, heads_here, HEADDIM, STATE).astype(jnp.bfloat16)
    inter_part = jnp.einsum(
        "bhtn,bhpn->bthp", read_decayed, states_low, preferred_element_type=jnp.float32
    )
    diag_part = intra_part + inter_part
    inner_heads = inner_act.reshape(slot_count, seq_here, heads_here, HEADDIM)
    mixed_out = (
        diag_part.reshape(slot_count, seq_here, heads_here, HEADDIM)
        + skip_gain[:, None] * inner_heads.astype(jnp.float32)
    ).reshape(slot_count, seq_here, inner_here)
    gate_act = jax.nn.silu(gate_pre)
    gated_out = mixed_out * gate_act
    square_sum = lax.psum(jnp.sum(gated_out * gated_out, axis=-1), "tp")
    out_scale = lax.rsqrt(square_sum / INNER + EPSILON)[..., None]
    gate_hat = gated_out * out_scale
    normed_out = (gate_hat * gate_gain).astype(jnp.bfloat16)
    partial_out = jnp.einsum(
        "bsi,di->bsd", normed_out, full_out, preferred_element_type=jnp.float32
    )
    branch = lax.psum_scatter(
        partial_out.astype(jnp.bfloat16), "tp", scatter_dimension=2, tiled=True
    ).astype(jnp.float32)
    position_ids = lax.axis_index("ctx") * seq_here + jnp.arange(seq_here)
    valid_rows = (position_ids[None, :] < lengths[:, None]).astype(jnp.float32)
    hidden_out = (hidden_in.astype(jnp.float32) + valid_rows[..., None] * branch).astype(
        jnp.bfloat16
    )
    masked = (full_cot.astype(jnp.float32) * valid_rows[..., None]).astype(jnp.bfloat16)
    grad_proj_out = jnp.einsum(
        "bsd,bsi->di", masked, normed_out, preferred_element_type=jnp.float32
    )
    grad_normed_out = jnp.einsum(
        "bsd,di->bsi", masked, full_out, preferred_element_type=jnp.float32
    )
    grad_gate_gain = jnp.sum(grad_normed_out * gate_hat, axis=(0, 1))
    grad_hat = grad_normed_out * gate_gain
    cross_term = lax.psum(jnp.sum(grad_hat * gate_hat, axis=-1), "tp")
    grad_gated = out_scale * (grad_hat - gate_hat * (cross_term / INNER)[..., None])
    grad_mixed = grad_gated * gate_act
    gate_sigmoid = jax.nn.sigmoid(gate_pre)
    grad_gate_pre = grad_gated * mixed_out * gate_sigmoid * (1.0 + gate_pre * (1.0 - gate_sigmoid))
    grad_heads = grad_mixed.reshape(slot_count, seq_here, heads_here, HEADDIM)
    grad_skip_gain = jnp.sum(grad_heads * inner_heads.astype(jnp.float32), axis=(0, 1, 3))
    grad_diag = grad_heads.astype(jnp.bfloat16).reshape(block_count, GROUP, heads_here, HEADDIM)
    inter_grad = jnp.einsum(
        "bthp,bhtn->bhpn", grad_diag, read_decayed, preferred_element_type=jnp.float32
    )
    inter_grad = inter_grad.reshape(slot_count, groups_here, heads_here, HEADDIM, STATE)

    def chain_back(final_grad):
        flowing = final_grad
        state_grads = []
        decay_grads = []
        for position in reversed(range(groups_here)):
            state_grads.insert(0, flowing)
            decay_grads.insert(0, jnp.sum(flowing * group_states[:, position], axis=(2, 3)))
            flowing = block_decay[:, position, :, None, None] * flowing + inter_grad[:, position]
        return (flowing, state_grads, decay_grads)

    local_grad = chain_back(jnp.zeros_like(carried))[0]

    def combine_grads(earlier, latter):
        return (earlier[0] * latter[0], latter[1] + latter[0][:, :, None, None] * earlier[1])

    after = carried_in((device_decay, local_grad), "ctx", combine_grads, identity, True)
    unused_grad, state_grads, decay_grads = chain_back(after[1])
    state_grad_blocks = (
        jnp.stack(state_grads, axis=1)
        .reshape(block_count, heads_here, HEADDIM, STATE)
        .astype(jnp.bfloat16)
    )
    decay_grad_blocks = jnp.stack(decay_grads, axis=1).reshape(block_count, heads_here)

    def backward_block(pieces):
        (
            inner_piece,
            write_piece,
            read_piece,
            step_rows,
            grad_piece,
            state_grad,
            decay_grad,
            state_piece,
        ) = pieces
        scores = jnp.dot(read_piece, write_piece.T, preferred_element_type=jnp.float32)
        forward_terms, pull_back = jax.vjp(
            decay_terms,
            scores,
            write_piece.astype(jnp.float32),
            read_piece.astype(jnp.float32),
            step_rows,
            log_rate,
        )
        weights, read_scaled, write_scaled, unused_decay = forward_terms
        grad_inner = jnp.einsum(
            "hts,thp->shp",
            weights.astype(jnp.bfloat16),
            grad_piece,
            preferred_element_type=jnp.float32,
        ) + jnp.einsum(
            "hsn,hpn->shp",
            write_scaled.astype(jnp.bfloat16),
            state_grad,
            preferred_element_type=jnp.float32,
        )
        grad_weights = jnp.einsum(
            "thp,shp->hts", grad_piece, inner_piece, preferred_element_type=jnp.float32
        )
        grad_read_scaled = jnp.einsum(
            "thp,hpn->htn", grad_piece, state_piece, preferred_element_type=jnp.float32
        )
        grad_write_scaled = jnp.einsum(
            "shp,hpn->hsn", inner_piece, state_grad, preferred_element_type=jnp.float32
        )
        grad_scores, grad_write, grad_read, grad_steps, grad_rate = pull_back(
            (grad_weights, grad_read_scaled, grad_write_scaled, decay_grad)
        )
        scores_low = grad_scores.astype(jnp.bfloat16)
        grad_read = grad_read + jnp.dot(scores_low, write_piece, preferred_element_type=jnp.float32)
        grad_write = grad_write + jnp.dot(
            scores_low.T, read_piece, preferred_element_type=jnp.float32
        )
        return (grad_inner, grad_write, grad_read, grad_steps, grad_rate)

    grad_inner_blocks, grad_write_blocks, grad_read_blocks, grad_step_blocks, grad_rate_blocks = (
        lax.map(
            backward_block,
            (
                inner_blocks,
                write_blocks,
                read_blocks,
                step_blocks,
                grad_diag,
                state_grad_blocks,
                decay_grad_blocks,
                states_low,
            ),
        )
    )
    grad_inner_act = grad_inner_blocks.reshape(slot_count, seq_here, inner_here) + (
        skip_gain[:, None] * grad_heads
    ).reshape(slot_count, seq_here, inner_here)
    grad_write_read_act = lax.psum(
        jnp.concatenate(
            [
                grad_write_blocks.reshape(slot_count, seq_here, STATE),
                grad_read_blocks.reshape(slot_count, seq_here, STATE),
            ],
            axis=2,
        ).astype(jnp.bfloat16),
        "tp",
    ).astype(jnp.float32)
    grad_step_size = grad_step_blocks.transpose(0, 2, 1).reshape(slot_count, seq_here, heads_here)
    grad_log_rate = jnp.sum(grad_rate_blocks, axis=0)
    unused_inner, inner_pull = jax.vjp(conv_silu, inner_pad, conv_inner, conv_inner_bias)
    grad_inner_pad, grad_conv_inner, grad_conv_inner_bias = inner_pull(grad_inner_act)
    unused_write_read, write_read_pull = jax.vjp(
        conv_silu, write_read_pad, conv_write_read, conv_write_read_bias
    )
    grad_write_read_pad, grad_conv_write_read, grad_conv_write_read_bias = write_read_pull(
        grad_write_read_act
    )
    inner_back, write_read_back = passed_along(
        (grad_inner_pad[:, :rim_rows], grad_write_read_pad[:, :rim_rows]), "ctx", -1
    )
    grad_inner_pre = (
        grad_inner_pad[:, rim_rows:]
        .at[:, seq_here - rim_rows :]
        .add(inner_back)
        .astype(jnp.bfloat16)
    )
    grad_write_read_pre = (
        grad_write_read_pad[:, rim_rows:]
        .at[:, seq_here - rim_rows :]
        .add(write_read_back)
        .astype(jnp.bfloat16)
    )
    grad_step_raw = grad_step_size * jax.nn.sigmoid(step_raw + step_bias)
    grad_step_bias = jnp.sum(grad_step_raw, axis=(0, 1))
    grad_step_low = grad_step_raw.astype(jnp.bfloat16)
    grad_gate_inner = jnp.stack([grad_gate_pre.astype(jnp.bfloat16), grad_inner_pre], axis=2)
    partial_normed = jnp.einsum(
        "bski,dki->bsd", grad_gate_inner, full_gate_inner, preferred_element_type=jnp.float32
    ) + jnp.einsum("bsh,dh->bsd", grad_step_low, full_step, preferred_element_type=jnp.float32)
    grad_proj_gate_inner = jnp.einsum(
        "bsd,bski->dki", normed, grad_gate_inner, preferred_element_type=jnp.float32
    )
    grad_proj_write_read = jnp.einsum(
        "bsd,bsn->dn", normed, grad_write_read_pre, preferred_element_type=jnp.float32
    )
    grad_proj_step = jnp.einsum(
        "bsd,bsh->dh", normed, grad_step_low, preferred_element_type=jnp.float32
    )
    reduced = (
        lax.psum_scatter(grad_proj_gate_inner, ("fsdp", "ctx"), scatter_dimension=0, tiled=True),
        lax.psum_scatter(grad_proj_write_read, ("fsdp", "ctx"), scatter_dimension=0, tiled=True),
        lax.psum_scatter(grad_proj_step, ("fsdp", "ctx"), scatter_dimension=0, tiled=True),
        lax.psum_scatter(grad_proj_out, ("fsdp", "ctx"), scatter_dimension=0, tiled=True),
    )
    start_col = lax.axis_index("tp") * width_here
    grad_normed = lax.psum(partial_normed.astype(jnp.bfloat16), "tp").astype(
        jnp.float32
    ) + jnp.einsum(
        "bsn,dn->bsd", grad_write_read_pre, full_write_read, preferred_element_type=jnp.float32
    )
    grad_hat_in = grad_normed * gain_float
    cross_in = jnp.mean(grad_hat_in * in_hat, axis=-1, keepdims=True)
    grad_full = in_scale * (grad_hat_in - in_hat * cross_in)
    grad_hidden_in = lax.dynamic_slice_in_dim(
        grad_full, start_col, width_here, 2
    ) + out_cotangent.astype(jnp.float32)
    grad_gain_full = jnp.sum(grad_normed * in_hat, axis=(0, 1))
    grad_norm_gain = lax.dynamic_slice_in_dim(grad_gain_full, start_col, width_here, 0)
    smalls = lax.psum(
        (
            grad_norm_gain,
            grad_conv_inner,
            grad_conv_inner_bias,
            grad_conv_write_read,
            grad_conv_write_read_bias,
            grad_step_bias,
            grad_log_rate,
            grad_skip_gain,
            grad_gate_gain,
        ),
        ("fsdp", "ctx"),
    )
    return (
        hidden_out,
        grad_hidden_in,
        smalls[0],
        reduced[0],
        reduced[1],
        reduced[2],
        smalls[1],
        smalls[2],
        smalls[3],
        smalls[4],
        smalls[5],
        smalls[6],
        smalls[7],
        smalls[8],
        reduced[3],
    )


def solution(mesh):
    placed = (
        P("fsdp", "ctx", "tp"),
        P("fsdp"),
        P("tp"),
        P(("fsdp", "ctx"), None, "tp"),
        P(("fsdp", "ctx"), None),
        P(("fsdp", "ctx"), "tp"),
        P(None, "tp"),
        P("tp"),
        P(),
        P(),
        P("tp"),
        P("tp"),
        P("tp"),
        P("tp"),
        P(("fsdp", "ctx"), "tp"),
        P("fsdp", "ctx", "tp"),
    )
    return jax.shard_map(
        on_device,
        mesh=mesh,
        in_specs=placed,
        out_specs=(
            P("fsdp", "ctx", "tp"),
            P("fsdp", "ctx", "tp"),
            P("tp"),
            P(("fsdp", "ctx"), None, "tp"),
            P(("fsdp", "ctx"), None),
            P(("fsdp", "ctx"), "tp"),
            P(None, "tp"),
            P("tp"),
            P(),
            P(),
            P("tp"),
            P("tp"),
            P("tp"),
            P("tp"),
            P(("fsdp", "ctx"), "tp"),
        ),
        check_vma=False,
    )
```

profile of v0, /device:TPU:0, one launch (start us, length us, event | category | flops | bytes accessed | tf_op | source)
XLA Modules:
  0.0 1388.8 jit_solution(6042050297375189682)
XLA Ops:
  12.1 13.6 all-gather.1
  26.7 12.4 all_gather.38
  49.8 77.9 %all-gather.8.cloned.1.call-done = bf16[2,1024,1536]{2,1,0:T(8,128)(2,1)} async-done(((bf16[2,1024,384]{2,1,0:T(8,128)(2,1)}), bf16[2,1024,1536]{2,1,0:T(8,128)(2,1)}) %all-gather.8.cloned.1.call-update) | async-done | bytes 6291472 | tf_op jit(solution)/shard_map/all_gather | solution.py:91
  131.8 35.4 %all-gather.10.cloned.1.call-done = bf16[1536,2,768]{2,0,1:T(8,128)(2,1)} async-done(((bf16[192,2,768]{2,0,1:T(8,128)(2,1)}), bf16[1536,2,768]{2,0,1:T(8,128)(2,1)}) %all-gather.10.cloned.1.call-update) | async-done | bytes 4718608 | tf_op jit(solution)/shard_map/all_gather | solution.py:96
  167.2 13.5 fusion.89
  225.3 82.2 %while.70 = (s32[]{:T(128)}, f32[8,256,12,64]{1,3,2,0:T(8,128)}, f32[8,12,64,128]{3,2,1,0:T(8,128)}, f32[8,12]{1,0:T(8,128)S(1)}, bf16[8,12,256,128]{3,2,1,0:T(8...) while((s32[]{:T(128)}, f32[8,256,12,64]{1,3,2,0:T(8,128)}, ...), condition=%wide.region_4.5_spmd, body=%wide.region_1.4_spmd.sunk | while | flops 174597152 | bytes 4580029 | solution.py:154
  346.1 10.3 copy.228
  364.0 11.8 psum.91
  375.9 11.6 multiply_reduce_fusion.9
  396.2 12.9 fusion.86
  442.2 289.8 %while.71 = (s32[]{:T(128)}, f32[8,256,12,64]{1,0,3,2:T(8,128)}, bf16[8,256,128]{2,1,0:T(8,128)(2,1)}, bf16[8,256,128]{2,1,0:T(8,128)(2,1)}, f32[8,12,256]{2,1,0...) while((s32[]{:T(128)}, f32[8,256,12,64]{1,0,3,2:T(8,128)}, ...), condition=%wide.region_33.34_spmd, body=%wide.region_18.0_spmd.sunk | while | flops 424201344 | bytes 13303985 | solution.py:301
  458.1 18.5 %dynamic_update_slice.73 = f32[8,256,12,64]{1,0,3,2:T(8,128)} dynamic-update-slice(f32[8,256,12,64]{1,0,3,2:T(8,128)} %get-tuple-element.1362, f32[1,256,12,64]{1,0,3,2:T(1,128)S(1)} %copy.350, s32[]{:T(128)} %get-tuple-element.1361, s32[]{:T(128)} %constant.219.clone.1..sunk.1, s32[]{:T(128)} %constant.219.clone.1..sunk.1, s32[]{:T(128)} %constant.219.clone.1..sunk.1) | dynamic-update-slice | bytes 1572868 | tf_op jit(solution)/shard_map/while/body/jit(dynamic_update_index_in_dim)/dynamic_update_slice | solution.py:154
  494.4 18.5 %dynamic_update_slice.73 = f32[8,256,12,64]{1,0,3,2:T(8,128)} dynamic-update-slice(f32[8,256,12,64]{1,0,3,2:T(8,128)} %get-tuple-element.1362, f32[1,256,12,64]{1,0,3,2:T(1,128)S(1)} %copy.350, s32[]{:T(128)} %get-tuple-element.1361, s32[]{:T(128)} %constant.219.clone.1..sunk.1, s32[]{:T(128)} %constant.219.clone.1..sunk.1, s32[]{:T(128)} %constant.219.clone.1..sunk.1) | dynamic-update-slice | bytes 1572868 | tf_op jit(solution)/shard_map/while/body/jit(dynamic_update_index_in_dim)/dynamic_update_slice | solution.py:154
  530.6 18.5 %dynamic_update_slice.73 = f32[8,256,12,64]{1,0,3,2:T(8,128)} dynamic-update-slice(f32[8,256,12,64]{1,0,3,2:T(8,128)} %get-tuple-element.1362, f32[1,256,12,64]{1,0,3,2:T(1,128)S(1)} %copy.350, s32[]{:T(128)} %get-tuple-element.1361, s32[]{:T(128)} %constant.219.clone.1..sunk.1, s32[]{:T(128)} %constant.219.clone.1..sunk.1, s32[]{:T(128)} %constant.219.clone.1..sunk.1) | dynamic-update-slice | bytes 1572868 | tf_op jit(solution)/shard_map/while/body/jit(dynamic_update_index_in_dim)/dynamic_update_slice | solution.py:154
  566.8 18.5 %dynamic_update_slice.73 = f32[8,256,12,64]{1,0,3,2:T(8,128)} dynamic-update-slice(f32[8,256,12,64]{1,0,3,2:T(8,128)} %get-tuple-element.1362, f32[1,256,12,64]{1,0,3,2:T(1,128)S(1)} %copy.350, s32[]{:T(128)} %get-tuple-element.1361, s32[]{:T(128)} %constant.219.clone.1..sunk.1, s32[]{:T(128)} %constant.219.clone.1..sunk.1, s32[]{:T(128)} %constant.219.clone.1..sunk.1) | dynamic-update-slice | bytes 1572868 | tf_op jit(solution)/shard_map/while/body/jit(dynamic_update_index_in_dim)/dynamic_update_slice | solution.py:154
  603.0 18.5 %dynamic_update_slice.73 = f32[8,256,12,64]{1,0,3,2:T(8,128)} dynamic-update-slice(f32[8,256,12,64]{1,0,3,2:T(8,128)} %get-tuple-element.1362, f32[1,256,12,64]{1,0,3,2:T(1,128)S(1)} %copy.350, s32[]{:T(128)} %get-tuple-element.1361, s32[]{:T(128)} %constant.219.clone.1..sunk.1, s32[]{:T(128)} %constant.219.clone.1..sunk.1, s32[]{:T(128)} %constant.219.clone.1..sunk.1) | dynamic-update-slice | bytes 1572868 | tf_op jit(solution)/shard_map/while/body/jit(dynamic_update_index_in_dim)/dynamic_update_slice | solution.py:154
  639.3 18.5 %dynamic_update_slice.73 = f32[8,256,12,64]{1,0,3,2:T(8,128)} dynamic-update-slice(f32[8,256,12,64]{1,0,3,2:T(8,128)} %get-tuple-element.1362, f32[1,256,12,64]{1,0,3,2:T(1,128)S(1)} %copy.350, s32[]{:T(128)} %get-tuple-element.1361, s32[]{:T(128)} %constant.219.clone.1..sunk.1, s32[]{:T(128)} %constant.219.clone.1..sunk.1, s32[]{:T(128)} %constant.219.clone.1..sunk.1) | dynamic-update-slice | bytes 1572868 | tf_op jit(solution)/shard_map/while/body/jit(dynamic_update_index_in_dim)/dynamic_update_slice | solution.py:154
  675.5 18.5 %dynamic_update_slice.73 = f32[8,256,12,64]{1,0,3,2:T(8,128)} dynamic-update-slice(f32[8,256,12,64]{1,0,3,2:T(8,128)} %get-tuple-element.1362, f32[1,256,12,64]{1,0,3,2:T(1,128)S(1)} %copy.350, s32[]{:T(128)} %get-tuple-element.1361, s32[]{:T(128)} %constant.219.clone.1..sunk.1, s32[]{:T(128)} %constant.219.clone.1..sunk.1, s32[]{:T(128)} %constant.219.clone.1..sunk.1) | dynamic-update-slice | bytes 1572868 | tf_op jit(solution)/shard_map/while/body/jit(dynamic_update_index_in_dim)/dynamic_update_slice | solution.py:154
  711.7 18.5 %dynamic_update_slice.73 = f32[8,256,12,64]{1,0,3,2:T(8,128)} dynamic-update-slice(f32[8,256,12,64]{1,0,3,2:T(8,128)} %get-tuple-element.1362, f32[1,256,12,64]{1,0,3,2:T(1,128)S(1)} %copy.350, s32[]{:T(128)} %get-tuple-element.1361, s32[]{:T(128)} %constant.219.clone.1..sunk.1, s32[]{:T(128)} %constant.219.clone.1..sunk.1, s32[]{:T(128)} %constant.219.clone.1..sunk.1) | dynamic-update-slice | bytes 1572868 | tf_op jit(solution)/shard_map/while/body/jit(dynamic_update_index_in_dim)/dynamic_update_slice | solution.py:154
  750.6 19.8 %multiply_reduce_fusion.13 = (f32[768]{0:T(1024)}, f32[768]{0:T(1024)S(1)}, f32[768]{0:T(1024)S(1)}, f32[768]{0:T(1024)S(1)}, f32[768]{0:T(1024)S(1)}, /*index=5*/f32[2,1024,768]{2,1,0:T(8,128)}) fusion(f32[2,1027,768]{2,1,0:T(8,128)} %copy-done, f32[2,1024,768]{2,1,0:T(8,128)} %get-tuple-element.953, f32[2,1024,768]{2,1,0:T(8,128)} %copy.243, ...), kind=kLoop, calls=%fused_computation.165 | loop fusion | flops 31453440 | bytes 50350080 | tf_op jit(solution)/shard_map/transpose(jvp())/reduce_sum | solution.py:47
  801.9 13.1 fusion.99
  820.2 10.4 convolution_convert_fusion
  830.6 16.6 %copy.258 = bf16[2,1024,1536]{1,0,2:T(2,128)(2,1)} copy(bf16[2,1024,1536]{2,1,0:T(8,128)(2,1)} %convolution_convert_fusion) | data formatting | bytes 12582912
  855.2 15.7 %fusion.96 = f32[1536,2,768]{2,0,1:T(8,128)} fusion(bf16[2,1024,1,768]{3,1,0,2:T(8,128)(2,1)} %bitcast.491, bf16[2,1024,1,768]{3,1,0,2:T(8,128)(2,1)S(1)} %copy-done.22, bf16[2,1024,1536]{2,1,0:T(8,128)(2,1)} %all-gather.8.cloned.1.call-done, f32[1536]{0:T(1024)S(1)} %copy-done.32, f32[2,1024]{1,0:T(2,128)S(1)} %copy-done.30), kind=kOutput, calls=%fused_computation.179 | convolution fusion | flops 9688842240 | bytes 22034432 | tf_op jit(solution)/shard_map/bsd,bski->dki/dot_general | solution.py:360
  871.6 12.5 fusion.103
  886.3 202.8 %all-reduce.22.cloned.1.call-done = (bf16[2,1024,256]{2,1,0:T(8,128)(2,1)}, bf16[2,1024,1536]{2,1,0:T(8,128)(2,1)}) async-done(((bf16[2,1024,256]{2,1,0:T(8,128)(2,1)}, bf16[2,1024,1536]{2,1,0:T(8,128)(2,1)}), (bf16[2,1024,256]{2,1,0:T(8,128)(2,1)}, bf16[2,1024,1536]{2,1,0:T(8,128)(2,1)})) %all-reduce.22.cloned.1.call-update) | async-done | bytes 7340048 | tf_op jit(solution)/shard_map/psum | solution.py:318
  1103.5 13.5 multiply_reduce_fusion.7
  1117.1 25.8 %all-reduce.18 = (f32[384]{0:T(512)}, f32[4,768]{1,0:T(4,128)}, f32[768]{0:T(1024)}, f32[4,256]{1,0:T(4,128)}, f32[256]{0:T(256)}, /*index=5*/f32[12]{0:T(128)}, f32[12]{0:T(128)}, f32[12]{0:T(128)}, f32[768]{0:T(1024)}) all-reduce(f32[384]{0:T(512)S(1)} %dynamic_slice.106, ...), channel_id=1, replica_groups=mesh['fsdp'=4,'ctx'=2,'tp'=4] {'fsdp','ctx'}, use_global_device_ids=true, to_apply=%region_38.39 | all-reduce | flops 6308 | bytes 50464 | tf_op jit(solution)/shard_map/psum | solution.py:389
  1147.4 53.8 %reduce-scatter.16.cloned.1.call-done = bf16[384,2048]{1,0:T(8,128)(2,1)} async-done(((bf16[1536,2048]{1,0:T(8,128)(2,1)}), bf16[384,2048]{1,0:T(8,128)(2,1)}) %reduce-scatter.16.cloned.1.call-update) | async-done | bytes 1572880
  1210.1 71.7 %reduce-scatter.10.cloned.1.call-done = f32[192,2,768]{2,0,1:T(8,128)} async-done(((f32[1536,2,768]{2,0,1:T(8,128)}), f32[192,2,768]{2,0,1:T(8,128)}) %reduce-scatter.10.cloned.1.call-update) | async-done | bytes 1179664 | tf_op jit(solution)/shard_map/reduce_scatter | solution.py:370
  1285.1 54.6 %reduce-scatter.14.cloned.1.call-done = f32[192,768]{1,0:T(8,128)} async-done(((f32[1536,768]{1,0:T(8,128)}), f32[192,768]{1,0:T(8,128)}) %reduce-scatter.14.cloned.1.call-update) | async-done | bytes 589840 | tf_op jit(solution)/shard_map/reduce_scatter | solution.py:373
  1339.7 42.1 %reduce-scatter.12.cloned.1.call-done = f32[192,256]{1,0:T(8,128)} async-done(((f32[1536,256]{1,0:T(8,128)}), f32[192,256]{1,0:T(8,128)}) %reduce-scatter.12.cloned.1.call-update) | async-done | bytes 196624 | tf_op jit(solution)/shard_map/reduce_scatter | solution.py:371
  (888 shorter events, 476.0 us)
Async XLA Ops:
  7.2 41.8 %copy-start.60 = (f32[12]{0:T(128)S(1)}, f32[12]{0:T(128)}, u32[]{:S(2)}) copy-start(f32[12]{0:T(128)} %param.39) | copy-start | bytes 148
  7.2 42.4 %copy-start.58 = (f32[12]{0:T(128)S(1)}, f32[12]{0:T(128)}, u32[]{:S(2)}) copy-start(f32[12]{0:T(128)} %param.40) | copy-start | bytes 148
  7.2 42.5 %copy-start.59 = (s32[2]{0:T(128)S(1)}, s32[2]{0:T(128)}, u32[]{:S(2)}) copy-start(s32[2]{0:T(128)} %param.29) | copy-start | bytes 28
  7.2 120.5 %all-gather.8.cloned.1.call-start = ((), (), s32[]{:S(2)}) async-start(), calls=%async_computation.5 | async-start | bytes 7864320 | tf_op jit(solution)/shard_map/all_gather | solution.py:91
  7.9 159.2 %all-gather.10.cloned.1.call-start = ((), (), s32[]{:S(2)}) async-start(), calls=%async_computation.6 | async-start | bytes 5308416 | tf_op jit(solution)/shard_map/all_gather | solution.py:96
  10.0 365.9 %all-gather.12.cloned.1.call-start = ((), (), s32[]{:S(2)}) async-start(), calls=%async_computation.7 | async-start | bytes 2654208 | tf_op jit(solution)/shard_map/all_gather | solution.py:99
  10.7 365.1 %all-gather.14.cloned.1.call-start = ((), (), s32[]{:S(2)}) async-start(), calls=%async_computation.8 | async-start | bytes 7864320 | tf_op jit(solution)/shard_map/all_gather | solution.py:93
  11.3 873.3 %reduce-scatter.18.cloned.1.call-start = ((), (), s32[]{:S(2)}) async-start(), calls=%async_computation.13 | async-start | bytes 884736
  25.7 168.0 %copy-start.31 = (f32[1536]{0:T(1024)}, f32[1536]{0:T(1024)S(1)}, u32[]{:S(2)}) copy-start(f32[1536]{0:T(1024)S(1)} %reshape.923) | copy-start | bytes 18436
  26.6 176.9 %copy-start.33 = (f32[768]{0:T(1024)}, f32[768]{0:T(1024)S(1)}, u32[]{:S(2)}) copy-start(f32[768]{0:T(1024)S(1)} %get-tuple-element.846) | copy-start | bytes 9220
  26.7 176.9 %copy-start.35 = (f32[768]{0:T(1024)}, f32[768]{0:T(1024)S(1)}, u32[]{:S(2)}) copy-start(f32[768]{0:T(1024)S(1)} %get-tuple-element.847) | copy-start | bytes 9220
  26.7 176.9 %copy-start.37 = (f32[768]{0:T(1024)}, f32[768]{0:T(1024)S(1)}, u32[]{:S(2)}) copy-start(f32[768]{0:T(1024)S(1)} %get-tuple-element.848) | copy-start | bytes 9220
  26.7 176.9 %copy-start.39 = (f32[768]{0:T(1024)}, f32[768]{0:T(1024)S(1)}, u32[]{:S(2)}) copy-start(f32[768]{0:T(1024)S(1)} %get-tuple-element.849) | copy-start | bytes 9220
  40.5 157.7 %copy-start.49 = (f32[1,256]{1,0:T(1,128)}, f32[1,256]{1,0:T(1,128)S(1)}, u32[]{:S(2)}) copy-start(f32[1,256]{1,0:T(1,128)S(1)} %get-tuple-element.985) | copy-start | bytes 3076
  49.0 144.7 %copy-start.26 = (bf16[1536,12,1]{0,1,2:T(8,128)(2,1)}, bf16[1536,12,1]{0,1,2:T(8,128)(2,1)S(1)}, u32[]{:S(2)}) copy-start(bf16[1536,12,1]{0,1,2:T(8,128)(2,1)S(1)} %reshape.931) | copy-start | bytes 110596
  49.8 326.1 %copy-start.41 = (f32[2,1024]{1,0:T(2,128)}, f32[2,1024]{1,0:T(2,128)S(1)}, u32[]{:S(2)}) copy-start(f32[2,1024]{1,0:T(2,128)S(1)} %compare_convert_fusion) | copy-start | bytes 24580
  131.8 61.9 %copy-start.29 = (f32[2,1024]{1,0:T(2,128)}, f32[2,1024]{1,0:T(2,128)S(1)}, u32[]{:S(2)}) copy-start(f32[2,1024]{1,0:T(2,128)S(1)} %add_rsqrt_fusion.1) | copy-start | bytes 24580
  181.7 21.2 %collective-permute-start = (bf16[2,3,768]{2,1,0:T(4,128)(2,1)}, bf16[2,3,768]{2,1,0:T(4,128)(2,1)S(1)}, u32[]{:S(2)}, u32[]{:S(2)}) collective-permute-start(bf16[2,3,768]{2,1,0:T(4,128)(2,1)} %slice.293), channel_id=1, source_target_pairs={{0,4},{1,5},{2,6},{3,7},{8,12},{9,13},{10,14},{11,15},{16,20},{17,... | collective-permute-start | bytes 27656 | tf_op jit(solution)/shard_map/ppermute | solution.py:19
  190.8 5.9 collective-permute-start.1
  375.8 20.4 %copy-start.43 = (f32[2,1024]{1,0:T(2,128)}, f32[2,1024]{1,0:T(2,128)S(1)}, u32[]{:S(2)}) copy-start(f32[2,1024]{1,0:T(2,128)S(1)} %add_rsqrt_fusion) | copy-start | bytes 24580
  750.6 19.8 %copy-start.38 = (f32[768]{0:T(1024)S(1)}, f32[768]{0:T(1024)}, u32[]{:S(2)}) copy-start(f32[768]{0:T(1024)} %copy-done.37) | copy-start | bytes 9220
  750.6 19.8 %copy-start.40 = (f32[768]{0:T(1024)S(1)}, f32[768]{0:T(1024)}, u32[]{:S(2)}) copy-start(f32[768]{0:T(1024)} %copy-done.39) | copy-start | bytes 9220
  786.5 12.6 collective-permute-start.2
  794.3 294.8 %all-reduce.22.cloned.1.call-start = ((), (), s32[]{:S(2)}) async-start(), calls=%async_computation.14 | async-start | bytes 14680064 | tf_op jit(solution)/shard_map/psum | solution.py:318
  819.5 381.6 %reduce-scatter.16.cloned.1.call-start = ((), (), s32[]{:S(2)}) async-start(), calls=%async_computation.12 | async-start | bytes 7864320
  855.2 426.7 %reduce-scatter.10.cloned.1.call-start = ((), (), s32[]{:S(2)}) async-start(), calls=%async_computation.9 | async-start | bytes 10616832 | tf_op jit(solution)/shard_map/reduce_scatter | solution.py:370
  871.0 468.7 %reduce-scatter.14.cloned.1.call-start = ((), (), s32[]{:S(2)}) async-start(), calls=%async_computation.11 | async-start | bytes 5308416 | tf_op jit(solution)/shard_map/reduce_scatter | solution.py:373
  884.1 205.0 %copy-start.2 = (f32[2,1027,256]{2,1,0:T(8,128)S(1)}, f32[2,1027,256]{2,1,0:T(8,128)}, u32[]{:S(2)}) copy-start(f32[2,1027,256]{2,1,0:T(8,128)} %copy-done.1) | copy-start | bytes 6309892
  884.2 497.6 %reduce-scatter.12.cloned.1.call-start = ((), (), s32[]{:S(2)}) async-start(), calls=%async_computation.10 | async-start | bytes 1769472 | tf_op jit(solution)/shard_map/reduce_scatter | solution.py:371
  1093.4 3.1 collective-permute-start.3
  1103.5 39.4 %copy-start.21 = (bf16[2,1024,384]{2,1,0:T(8,128)(2,1)S(1)}, bf16[2,1024,384]{2,1,0:T(8,128)(2,1)}, u32[]{:S(2)}) copy-start(bf16[2,1024,384]{2,1,0:T(8,128)(2,1)} %param.43) | copy-start | bytes 4718596
  1142.9 64.2 %copy-start.20 = (bf16[2,1024,384]{2,1,0:T(8,128)(2,1)S(1)}, bf16[2,1024,384]{2,1,0:T(8,128)(2,1)}, u32[]{:S(2)}) copy-start(bf16[2,1024,384]{2,1,0:T(8,128)(2,1)} %param.28) | copy-start | bytes 4718596
  (47 other events, 317.1 us)
Sparse Core Ops, SparseCore 0:
  9.6 118.0 all-gather.7
  130.1 36.9 all-gather.9
  169.0 28.8 all-gather.11
  199.4 115.3 all-gather.13
  794.4 35.0 reduce-scatter.17
  832.3 256.7 all-reduce.21
  1091.5 109.6 reduce-scatter.15
  1204.6 77.1 reduce-scatter.9
  1285.9 53.7 reduce-scatter.13
  1343.4 38.3 reduce-scatter.11
where the time goes:
time: 1400 us; the launch traced here: 1390 us
  waiting for transfers between devices  541 us (39%)
  local copies, waits for them, and re-layouts  316 us (23%)
  matrix products  260 us (19%)
  other arithmetic  157 us (11%)
  blocking collectives  87.8 us (6%)
  between operations  15.6 us (1%)
    psum x1, waiting for transfers between devices, on_device(): lax.psum(jnp.concatenate([grad_write_blocks.reshape(slot_count, seq_here,...  203 us
    dynamic_update_slice x32, local copies, waits for them, and re-layouts, on_device(): lax.map(forward_block, (inner_blocks, write_blocks, read_blocks, step_blo...  155 us
    all_gather x1, waiting for transfers between devices, on_device(): lax.all_gather(hidden_in, 'tp', axis=2, tiled=True)  77.9 us
    reduce_scatter x1, waiting for transfers between devices, on_device(): lax.psum_scatter(grad_proj_gate_inner, ('fsdp', 'ctx'), scatter_dimension...  71.7 us
    unnamed x140, local copies, waits for them, and re-layouts  56.8 us
    unnamed x12, waiting for transfers between devices  55.8 us
    reduce_scatter x1, waiting for transfers between devices, on_device(): lax.psum_scatter(grad_proj_out, ('fsdp', 'ctx'), scatter_dimension=0, til...  54.6 us
    reduce_scatter x1, waiting for transfers between devices, on_device(): lax.psum_scatter(grad_proj_write_read, ('fsdp', 'ctx'), scatter_dimension...  42.1 us
  transfers between devices with their start and end apart: 14, of which 8 were waited for; matrix products, arithmetic and copies ran while one was open for 24% of the time, Pallas kernels for 0%

commit v1 on v0

v1 whole, which is shorter than its diff:
```python
import functools

import jax
import jax.numpy as jnp
from jax import lax
from jax.experimental import pallas as pl
from jax.experimental.pallas import tpu as pltpu
from jax.sharding import PartitionSpec as P

HEADDIM = 64
STATE = 128
CONV = 4
GROUP = 256
INNER = 3072
EPSILON = 1e-05
PAIR = 2 * HEADDIM
HEADS_STEP = 6
LANES_STEP = HEADS_STEP * HEADDIM
F32 = jnp.float32
BF16 = jnp.bfloat16
HIGHEST = lax.Precision.HIGHEST
OUTER = (("fsdp", "ctx"))


def swap(x, bit):
    count = lax.axis_size("tp")
    return lax.ppermute(x, "tp", [(i, i ^ bit) for i in range(count)])


def passed_along(x, axis, by):
    count = lax.axis_size(axis)
    pairs = [(i, i + by) for i in range(count) if 0 <= i + by < count]
    return lax.ppermute(x, axis, pairs)


def carried_in(decay, final, combine, reverse):
    count, position = (lax.axis_size("ctx"), lax.axis_index("ctx"))
    if count == 2:
        return passed_along(final.astype(BF16), "ctx", -1 if reverse else 1).astype(F32)
    decays = lax.all_gather(decay.astype(BF16), "ctx").astype(F32)
    finals = lax.all_gather(final.astype(BF16), "ctx")
    start = jnp.zeros_like(final)

    def lap(k, before):
        at = count - 1 - k if reverse else k
        reached = at > position if reverse else at < position
        new = decays[at] * before + finals[at].astype(F32)
        return jnp.where(reached, new, before)

    return lax.fori_loop(0, count, lap, start)


def conv_silu(padded, conv_taps, conv_bias):
    tap_count = conv_taps.shape[0]
    length = padded.shape[-2] - tap_count + 1
    summed = conv_bias
    for offset in range(tap_count):
        summed = summed + conv_taps[offset] * padded[..., offset : offset + length, :]
    return jax.nn.silu(summed)


def dot(a, b, da, db):
    return lax.dot_general(a, b, (((da,), (db,)), ((), ())), preferred_element_type=F32)


def low_lanes(rows):
    return lax.broadcasted_iota(jnp.int32, (rows, PAIR), 1) < HEADDIM


def spread_heads(cols, pair, low_half):
    return jnp.where(low_half, cols[:, 2 * pair : 2 * pair + 1], cols[:, 2 * pair + 1 : 2 * pair + 2])


def state_kernel(a_ref, b_ref, scale_ref, out_ref):
    scale = scale_ref[0]
    low_half = low_lanes(GROUP)
    for pair in range(HEADS_STEP // 2):
        lanes = slice(PAIR * pair, PAIR * (pair + 1))
        scaled = (b_ref[:, lanes].astype(F32) * spread_heads(scale, pair, low_half)).astype(BF16)
        out_ref[0, :, lanes] = dot(a_ref[...], scaled, 0, 0)


def block_outer(rows_a, cols_b, scale):
    tokens, width = cols_b.shape
    blocks, steps = tokens // GROUP, width // LANES_STEP
    return pl.pallas_call(
        state_kernel,
        grid=(blocks, steps),
        in_specs=[
            pl.BlockSpec((GROUP, STATE), lambda b, g: (b, 0)),
            pl.BlockSpec((GROUP, LANES_STEP), lambda b, g: (b, g)),
            pl.BlockSpec((1, GROUP, HEADS_STEP), lambda b, g: (g, b, 0)),
        ],
        out_specs=pl.BlockSpec((1, STATE, LANES_STEP), lambda b, g: (b, 0, g)),
        out_shape=jax.ShapeDtypeStruct((blocks, STATE, width), F32),
        cost_estimate=pl.CostEstimate(
            flops=2 * tokens * STATE * width,
            bytes_accessed=tokens * width * 2 + blocks * STATE * width * 4,
            transcendentals=0,
        ),
        name="block_outer",
    )(rows_a, cols_b, scale)


def mix_kernel(
    x_ref, gate_ref, w_ref, r_ref, step_ref, cum_ref, cumt_ref, state_ref, skip_ref,
    mixed_ref, square_ref, scores_ref,
):
    g = pl.program_id(1)

    @pl.when(g == 0)
    def _():
        scores_ref[...] = dot(r_ref[...], w_ref[...], 1, 1)
        square_ref[...] = jnp.zeros_like(square_ref)

    cum, cumt, step = cum_ref[0], cumt_ref[0, 0], step_ref[0]
    grown = jnp.exp(cum)
    low_half = low_lanes(GROUP)
    lower = lax.broadcasted_iota(jnp.int32, (GROUP, GROUP), 0) >= lax.broadcasted_iota(
        jnp.int32, (GROUP, GROUP), 1
    )
    squares = jnp.zeros((GROUP, 1), F32)
    for pair in range(HEADS_STEP // 2):
        lanes = slice(PAIR * pair, PAIR * (pair + 1))
        x = x_ref[:, lanes].astype(F32)
        stepped = x * spread_heads(step, pair, low_half)
        halves = (
            jnp.where(low_half, stepped, 0.0).astype(BF16),
            jnp.where(low_half, 0.0, stepped).astype(BF16),
        )
        total = dot(r_ref[...], state_ref[0, :, lanes], 1, 0) * spread_heads(grown, pair, low_half)
        for side in range(2):
            head = 2 * pair + side
            spread = jnp.where(lower, cum[:, head : head + 1] - cumt[head : head + 1, :], -1e30)
            weights = (scores_ref[...] * jnp.exp(spread)).astype(BF16)
            total = total + dot(weights, halves[side], 1, 0)
        mixed = total + skip_ref[:, lanes] * x
        mixed_ref[:, lanes] = mixed
        gate = gate_ref[:, lanes].astype(F32)
        gated = mixed * (gate * jax.nn.sigmoid(gate))
        squares = squares + jnp.sum(gated * gated, axis=1, keepdims=True)
    square_ref[...] += squares


def mix_blocks(x, gate, write, read, step, cum, cumt, states, skip):
    tokens, width = x.shape
    blocks, steps = tokens // GROUP, width // LANES_STEP
    wide = pl.BlockSpec((GROUP, LANES_STEP), lambda b, g: (b, g))
    narrow = pl.BlockSpec((GROUP, STATE), lambda b, g: (b, 0))
    cols = pl.BlockSpec((1, GROUP, HEADS_STEP), lambda b, g: (g, b, 0))
    return pl.pallas_call(
        mix_kernel,
        grid=(blocks, steps),
        in_specs=[
            wide, wide, narrow, narrow, cols, cols,
            pl.BlockSpec((1, 1, HEADS_STEP, GROUP), lambda b, g: (g, b, 0, 0)),
            pl.BlockSpec((1, STATE, LANES_STEP), lambda b, g: (b, 0, g)),
            pl.BlockSpec((1, LANES_STEP), lambda b, g: (0, g)),
        ],
        out_specs=[wide, pl.BlockSpec((GROUP, 1), lambda b, g: (b, 0))],
        out_shape=[
            jax.ShapeDtypeStruct((tokens, width), F32),
            jax.ShapeDtypeStruct((tokens, 1), F32),
        ],
        scratch_shapes=[pltpu.VMEM((GROUP, GROUP), F32)],
        cost_estimate=pl.CostEstimate(
            flops=2 * tokens * width * (2 * GROUP + 2 * STATE) * 2,
            bytes_accessed=tokens * width * 10,
            transcendentals=tokens * GROUP * width // HEADDIM,
        ),
        name="mix_blocks",
    )(x, gate, write, read, step, cum, cumt, states, skip)


def segment_sums(values):
    rows = lax.broadcasted_iota(jnp.int32, (LANES_STEP, HEADS_STEP), 0) // HEADDIM
    chosen = (rows == lax.broadcasted_iota(jnp.int32, (LANES_STEP, HEADS_STEP), 1)).astype(BF16)
    high = values.astype(BF16)
    rest = (values - high.astype(F32)).astype(BF16)
    return dot(high, chosen, 1, 0) + dot(rest, chosen, 1, 0)


def back_kernel(
    x_ref, mixed_ref, grad_ref, w_ref, r_ref, step_ref, cum_ref, cumt_ref, state_ref, flow_ref, skip_ref,
    gx_ref, gw_ref, gr_ref, u_ref, v_ref, i_ref,
    scores_ref, gscores_ref, prod_ref,
):
    g = pl.program_id(1)

    @pl.when(g == 0)
    def _():
        scores_ref[...] = dot(r_ref[...], w_ref[...], 1, 1)
        gscores_ref[...] = jnp.zeros_like(gscores_ref)
        gw_ref[...] = jnp.zeros_like(gw_ref)
        gr_ref[...] = jnp.zeros_like(gr_ref)

    cum, cumt, step = cum_ref[0], cumt_ref[0, 0], step_ref[0]
    grown = jnp.exp(cum)
    shrunk = jnp.exp(cum[GROUP - 1 : GROUP, :] - cum)
    low_half = low_lanes(GROUP)
    lower = lax.broadcasted_iota(jnp.int32, (GROUP, GROUP), 0) >= lax.broadcasted_iota(
        jnp.int32, (GROUP, GROUP), 1
    )
    grad_write = jnp.zeros((GROUP, STATE), F32)
    grad_read = jnp.zeros((GROUP, STATE), F32)
    for pair in range(HEADS_STEP // 2):
        lanes = slice(PAIR * pair, PAIR * (pair + 1))
        x = x_ref[:, lanes].astype(F32)
        grad = grad_ref[:, lanes]
        grad_f = grad.astype(F32)
        skip = skip_ref[:, lanes]
        steps = spread_heads(step, pair, low_half)
        tail = spread_heads(shrunk, pair, low_half)
        stepped = x * steps
        x_halves = (
            jnp.where(low_half, stepped, 0.0).astype(BF16),
            jnp.where(low_half, 0.0, stepped).astype(BF16),
        )
        g_halves = (
            jnp.where(low_half, grad_f, 0.0).astype(BF16),
            jnp.where(low_half, 0.0, grad_f).astype(BF16),
        )
        flow = flow_ref[0, :, lanes]
        grad_read = grad_read + dot(
            (grad_f * spread_heads(grown, pair, low_half)).astype(BF16), state_ref[0, :, lanes], 1, 1
        )
        grad_write = grad_write + dot((stepped * tail).astype(BF16), flow, 1, 1)
        stepped_low = stepped.astype(BF16).astype(F32)
        inter = dot(w_ref[...], flow, 1, 0) * tail
        total = jnp.zeros_like(inter)
        for side in range(2):
            head = 2 * pair + side
            decay = jnp.exp(jnp.where(lower, cum[:, head : head + 1] - cumt[head : head + 1, :], -1e30))
            weights = (scores_ref[...] * decay).astype(BF16)
            total = total + dot(weights, g_halves[side], 0, 0)
            gscores_ref[...] += dot(grad, x_halves[side], 1, 1) * decay
        both = total + inter
        gx_ref[:, lanes] = steps * both + skip * grad_f
        prod_ref[0, :, lanes] = x * both
        prod_ref[1, :, lanes] = grad_f * (mixed_ref[:, lanes] - skip * x) - stepped_low * total
        prod_ref[2, :, lanes] = stepped_low * inter
    u_ref[0] = segment_sums(prod_ref[0])
    v_ref[0] = segment_sums(prod_ref[1])
    i_ref[0] = segment_sums(prod_ref[2])
    gw_ref[...] += grad_write
    gr_ref[...] += grad_read

    @pl.when(g == pl.num_programs(1) - 1)
    def _():
        low = gscores_ref[...].astype(BF16)
        gr_ref[...] += dot(low, w_ref[...], 1, 0)
        gw_ref[...] += dot(low, r_ref[...], 0, 0)


def back_blocks(x, mixed, grad, write, read, step, cum, cumt, states, flows, skip):
    tokens, width = x.shape
    blocks, steps = tokens // GROUP, width // LANES_STEP
    wide = pl.BlockSpec((GROUP, LANES_STEP), lambda b, g: (b, g))
    narrow = pl.BlockSpec((GROUP, STATE), lambda b, g: (b, 0))
    cols = pl.BlockSpec((1, GROUP, HEADS_STEP), lambda b, g: (g, b, 0))
    state = pl.BlockSpec((1, STATE, LANES_STEP), lambda b, g: (b, 0, g))
    return pl.pallas_call(
        back_kernel,
        grid=(blocks, steps),
        in_specs=[
            wide, wide, wide, narrow, narrow, cols, cols,
            pl.BlockSpec((1, 1, HEADS_STEP, GROUP), lambda b, g: (g, b, 0, 0)),
            state, state,
            pl.BlockSpec((1, LANES_STEP), lambda b, g: (0, g)),
        ],
        out_specs=[wide, narrow, narrow, cols, cols, cols],
        out_shape=[
            jax.ShapeDtypeStruct((tokens, width), F32),
            jax.ShapeDtypeStruct((tokens, STATE), F32),
            jax.ShapeDtypeStruct((tokens, STATE), F32),
            jax.ShapeDtypeStruct((steps, tokens, HEADS_STEP), F32),
            jax.ShapeDtypeStruct((steps, tokens, HEADS_STEP), F32),
            jax.ShapeDtypeStruct((steps, tokens, HEADS_STEP), F32),
        ],
        scratch_shapes=[
            pltpu.VMEM((GROUP, GROUP), F32),
            pltpu.VMEM((GROUP, GROUP), F32),
            pltpu.VMEM((3, GROUP, LANES_STEP), F32),
        ],
        cost_estimate=pl.CostEstimate(
            flops=2 * tokens * width * (4 * GROUP + 4 * STATE) * 2,
            bytes_accessed=tokens * width * 14,
            transcendentals=tokens * GROUP * width // HEADDIM,
        ),
        name="back_blocks",
    )(x, mixed, grad, write, read, step, cum, cumt, states, flows, skip)


def pack(parts):
    return jnp.concatenate([part.reshape(-1) for part in parts])


def unpack(vector, shapes):
    parts, at = [], 0
    for shape in shapes:
        size = 1
        for dim in shape:
            size *= dim
        parts.append(vector[at : at + size].reshape(shape))
        at += size
    return parts


def on_device(
    hidden_in,
    lengths,
    norm_gain,
    proj_gate_inner,
    proj_write_read,
    proj_step,
    conv_inner,
    conv_inner_bias,
    conv_write_read,
    conv_write_read_bias,
    step_bias,
    log_rate,
    skip_gain,
    gate_gain,
    proj_out,
    out_cotangent,
):
    slot_count, seq_here, width_here = hidden_in.shape
    slots = slot_count // 2
    tokens = slots * seq_here
    heads_own = step_bias.shape[0]
    inner_own = gate_gain.shape[0]
    heads = 2 * heads_own
    inner = 2 * inner_own
    tp_count = lax.axis_size("tp")
    width = tp_count * width_here
    groups = seq_here // GROUP
    blocks = slots * groups
    head_steps = heads // HEADS_STEP
    rim_rows = CONV - 1
    place = lax.axis_index("tp")
    far_half, near_side = place // 2, place % 2

    def half_of(whole, which):
        return lax.dynamic_slice_in_dim(whole, which * slots, slots, 0)

    def ordered(own, near, far, both, axis):
        first = lambda a, b: jnp.where(near_side == 0, a, b)
        a0, a1, b0, b1 = first(own, near), first(near, own), first(far, both), first(both, far)
        lower = lambda a, b: jnp.where(far_half == 0, a, b)
        return jnp.concatenate(
            [lower(a0, b0), lower(a1, b1), lower(b0, a0), lower(b1, a1)], axis=axis
        )

    def all_features(local):
        mine, other = half_of(local, far_half), half_of(local, 1 - far_half)
        far = swap(other, 2)
        near = swap(mine, 1)
        both = swap(far, 1)
        return ordered(mine, near, far, both, 2).reshape(tokens, width)

    def own_features(piece):
        relay = swap(piece(place ^ 3).astype(BF16), 1)
        keep = swap(piece(place ^ 1).astype(BF16), 1)
        sent = swap((piece(place ^ 2) + relay.astype(F32)).astype(BF16), 2)
        kept = (piece(place) + keep.astype(F32)).reshape(slots, seq_here, width_here)
        other = sent.astype(F32).reshape(slots, seq_here, width_here)
        return both_halves(kept, other)

    def both_halves(kept, other):
        return jnp.where(
            far_half == 0,
            jnp.concatenate([kept, other], axis=0),
            jnp.concatenate([other, kept], axis=0),
        )

    full_x = all_features(hidden_in)
    full_gain = ordered(norm_gain, swap(norm_gain, 1), swap(norm_gain, 2), swap(norm_gain, 3), 0)

    small_shapes = [(CONV, inner_own), (inner_own,), (inner_own,), (heads_own,), (heads_own,), (heads_own,)]
    own_small = pack([conv_inner, conv_inner_bias, gate_gain, step_bias, log_rate, skip_gain])
    far_small = unpack(swap(own_small, 2), small_shapes)
    taps = jnp.concatenate([conv_inner, far_small[0]], axis=1)
    taps_bias = jnp.concatenate([conv_inner_bias, far_small[1]])
    gain_gate = jnp.concatenate([gate_gain, far_small[2]])
    bias_step = jnp.concatenate([step_bias, far_small[3]])
    rate_log = jnp.concatenate([log_rate, far_small[4]])
    gain_skip = jnp.concatenate([skip_gain, far_small[5]])
    rate = -jnp.exp(rate_log)
    skip_lanes = jnp.repeat(gain_skip, HEADDIM)[None]

    def gathered(x):
        return lax.all_gather(x, ("fsdp", "ctx"), axis=0, tiled=True)

    narrow_cols = 2 * STATE + heads
    narrow_pad = -narrow_cols % 128
    narrow_shard = jnp.concatenate(
        [proj_write_read, proj_step, swap(proj_step, 2)]
        + [jnp.zeros((proj_step.shape[0], narrow_pad), BF16)],
        axis=1,
    )
    full_narrow = gathered(narrow_shard)
    own_gi, far_gi = gathered(proj_gate_inner), gathered(swap(proj_gate_inner, 2))
    own_out, far_out = gathered(proj_out), gathered(swap(proj_out, 2))
    full_gate = jnp.concatenate([own_gi[:, 0], far_gi[:, 0]], axis=1)
    full_inner = jnp.concatenate([own_gi[:, 1], far_gi[:, 1]], axis=1)
    full_out = jnp.concatenate([own_out, far_out], axis=1)
    full_cot = all_features(out_cotangent)

    in_float = full_x.astype(F32)
    in_scale = lax.rsqrt(jnp.mean(in_float * in_float, axis=-1, keepdims=True) + EPSILON)
    normed = (in_float * in_scale * full_gain.astype(F32)).astype(BF16)
    narrow_pre = dot(normed, full_narrow, 1, 0)
    write_read_pre = narrow_pre[:, : 2 * STATE].astype(BF16)
    step_raw = narrow_pre[:, 2 * STATE : narrow_cols]
    gate_pre = dot(normed, full_gate, 1, 0).astype(BF16)
    inner_pre = dot(normed, full_inner, 1, 0).astype(BF16)

    def padded(pre):
        by_slot = pre.reshape(slots, seq_here, pre.shape[-1])
        rim = passed_along(by_slot[:, seq_here - rim_rows :], "ctx", 1)
        return jnp.concatenate([rim, by_slot], axis=1).astype(F32)

    inner_pad, write_read_pad = padded(inner_pre), padded(write_read_pre)
    write_read_act = (
        conv_silu(write_read_pad, conv_write_read, conv_write_read_bias)
        .astype(BF16)
        .reshape(tokens, 2 * STATE)
    )
    inner_act = conv_silu(inner_pad, taps, taps_bias).astype(BF16).reshape(tokens, inner)
    write, read = write_read_act[:, :STATE], write_read_act[:, STATE:]

    step_size = jax.nn.softplus(step_raw + bias_step)
    step_blocks = step_size.reshape(blocks, GROUP, heads)
    lower = (jnp.arange(GROUP)[:, None] >= jnp.arange(GROUP)[None, :]).astype(F32)
    cum = jnp.einsum("ts,bsh->bth", lower, step_blocks * rate, precision=HIGHEST)

    def by_steps(cols):
        return cols.reshape(tokens, head_steps, HEADS_STEP).transpose(1, 0, 2)

    def from_steps(cols):
        return cols.transpose(1, 0, 2).reshape(blocks, GROUP, heads)

    step_cols, cum_cols = by_steps(step_size), by_steps(cum)
    cum_rows = cum.reshape(blocks, GROUP, head_steps, HEADS_STEP).transpose(2, 0, 3, 1)
    last = cum[:, GROUP - 1]
    write_scale = by_steps(jnp.exp(last[:, None] - cum) * step_blocks)
    decay = jnp.exp(last)
    decay_lanes = jnp.repeat(decay, HEADDIM, axis=1).reshape(slots, groups, 1, inner)

    local_state = block_outer(write, inner_act, write_scale).reshape(slots, groups, STATE, inner)
    carried = local_state[:, 0]
    device_decay = decay_lanes[:, 0]
    for position in range(1, groups):
        carried = decay_lanes[:, position] * carried + local_state[:, position]
        device_decay = device_decay * decay_lanes[:, position]
    current = carried_in(device_decay, carried, None, False)
    state_list = []
    for position in range(groups):
        state_list.append(current)
        current = decay_lanes[:, position] * current + local_state[:, position]
    states = jnp.stack(state_list, axis=1)
    states_low = states.astype(BF16).reshape(blocks, STATE, inner)

    mixed_out, squares = mix_blocks(
        inner_act, gate_pre, write, read, step_cols, cum_cols, cum_rows, states_low, skip_lanes
    )
    square_sum = squares + swap(squares, 1)
    out_scale = lax.rsqrt(square_sum / INNER + EPSILON)
    gate_float = gate_pre.astype(F32)
    gate_sigmoid = jax.nn.sigmoid(gate_float)
    gate_act = gate_float * gate_sigmoid
    gated_out = mixed_out * gate_act
    gate_hat = gated_out * out_scale
    normed_out = (gate_hat * gain_gate).astype(BF16)

    def branch_piece(which):
        rows = lax.dynamic_slice_in_dim(full_out, which * width_here, width_here, 0)
        return dot(normed_out, rows, 1, 1)

    branch = own_features(branch_piece)
    position_ids = lax.axis_index("ctx") * seq_here + jnp.arange(seq_here)
    valid_rows = (position_ids[None, :] < lengths[:, None]).astype(F32)
    hidden_out = (hidden_in.astype(F32) + valid_rows[..., None] * branch).astype(BF16)
    valid_here = half_of(valid_rows, far_half).reshape(tokens, 1)
    masked = (full_cot.astype(F32) * valid_here).astype(BF16)

    grad_proj_out = dot(masked, normed_out, 0, 0).astype(BF16)
    grad_normed_out = dot(masked, full_out, 1, 0)
    grad_gate_gain = jnp.sum(grad_normed_out * gate_hat, axis=0)
    grad_hat = grad_normed_out * gain_gate
    cross_part = jnp.sum(grad_hat * gate_hat, axis=-1, keepdims=True)
    cross_term = cross_part + swap(cross_part, 1)
    grad_gated = out_scale * (grad_hat - gate_hat * (cross_term / INNER))
    grad_mixed = grad_gated * gate_act
    grad_gate_pre = (
        grad_gated * mixed_out * gate_sigmoid * (1.0 + gate_float * (1.0 - gate_sigmoid))
    ).astype(BF16)
    grad_skip_lanes = jnp.sum(grad_mixed * inner_act.astype(F32), axis=0)
    grad_diag = grad_mixed.astype(BF16)
    grad_gate_w = dot(normed, grad_gate_pre, 0, 0).astype(BF16)

    read_scale = by_steps(jnp.exp(cum))
    local_grad = block_outer(read, grad_diag, read_scale).reshape(slots, groups, STATE, inner)
    flowing = local_grad[:, groups - 1]
    for position in reversed(range(groups - 1)):
        flowing = decay_lanes[:, position] * flowing + local_grad[:, position]
    flowing = carried_in(device_decay, flowing, None, True)
    flow_list = []
    for position in reversed(range(groups)):
        flow_list.insert(0, flowing)
        flowing = decay_lanes[:, position] * flowing + local_grad[:, position]
    flows = jnp.stack(flow_list, axis=1)
    last_grad = (
        jnp.sum(flows * states, axis=2).reshape(blocks, heads, HEADDIM).sum(axis=2) * decay
    )
    flows_low = flows.astype(BF16).reshape(blocks, STATE, inner)

    grad_inner_act, grad_write, grad_read, u_cols, v_cols, inter_cols = back_blocks(
        inner_act, mixed_out, grad_diag, write, read, step_cols, cum_cols, cum_rows,
        states_low, flows_low, skip_lanes,
    )
    u_blocks, v_blocks, inter_blocks = from_steps(u_cols), from_steps(v_cols), from_steps(inter_cols)
    reverse_sum = (
        jnp.einsum("ts,bth->bsh", lower, v_blocks, precision=HIGHEST)
        + jnp.einsum("st,bth->bsh", lower - jnp.eye(GROUP, dtype=F32), inter_blocks, precision=HIGHEST)
        + last_grad[:, None]
    )
    grad_step_size = u_blocks + rate * reverse_sum
    grad_log_rate = jnp.sum(reverse_sum * step_blocks, axis=(0, 1)) * rate
    grad_step_raw = grad_step_size.reshape(tokens, heads) * jax.nn.sigmoid(step_raw + bias_step)
    grad_step_bias = jnp.sum(grad_step_raw, axis=0)

    unused_inner, inner_pull = jax.vjp(conv_silu, inner_pad, taps, taps_bias)
    grad_inner_pad, grad_taps, grad_taps_bias = inner_pull(
        grad_inner_act.reshape(slots, seq_here, inner)
    )
    unused_write_read, write_read_pull = jax.vjp(
        conv_silu, write_read_pad, conv_write_read, conv_write_read_bias
    )
    grad_write_read_pad, grad_conv_write_read, grad_conv_write_read_bias = write_read_pull(
        jnp.concatenate([grad_write, grad_read], axis=1).reshape(slots, seq_here, 2 * STATE)
    )

    def unpadded(grad):
        back = passed_along(grad[:, :rim_rows], "ctx", -1)
        full = grad[:, rim_rows:].at[:, seq_here - rim_rows :].add(back)
        return full.astype(BF16).reshape(tokens, grad.shape[-1])

    grad_inner_pre, grad_write_read_pre = unpadded(grad_inner_pad), unpadded(grad_write_read_pad)
    grad_narrow = jnp.concatenate(
        [grad_write_read_pre, grad_step_raw.astype(BF16), jnp.zeros((tokens, narrow_pad), BF16)], axis=1
    )
    grad_inner_w = dot(normed, grad_inner_pre, 0, 0).astype(BF16)
    grad_narrow_w = dot(normed, grad_narrow, 0, 0).astype(BF16)

    def normed_piece(which):
        def rows(full):
            return lax.dynamic_slice_in_dim(full, which * width_here, width_here, 0)

        return (
            dot(grad_gate_pre, rows(full_gate), 1, 1)
            + dot(grad_inner_pre, rows(full_inner), 1, 1)
            + dot(grad_narrow, rows(full_narrow), 1, 1)
        )

    grad_normed = own_features(normed_piece)

    def reduced(x):
        return lax.psum_scatter(x, ("fsdp", "ctx"), scatter_dimension=0, tiled=True)

    def home(x, axis):
        own = lax.slice_in_dim(x, 0, x.shape[axis] // 2, axis=axis).astype(F32)
        away = lax.slice_in_dim(x, x.shape[axis] // 2, x.shape[axis], axis=axis)
        return own + swap(away, 2).astype(F32)

    grad_out_home = home(reduced(grad_proj_out), 1)
    grad_gate_home = home(reduced(grad_gate_w), 1)
    grad_inner_home = home(reduced(grad_inner_w), 1)
    narrow_reduced = reduced(grad_narrow_w)
    write_read_home = narrow_reduced[:, : 2 * STATE].astype(F32)
    write_read_home = write_read_home + swap(write_read_home, 1)
    write_read_home = write_read_home + swap(write_read_home, 2)
    step_home = home(narrow_reduced[:, 2 * STATE : narrow_cols], 1)

    own_gain = norm_gain.astype(F32)
    other_scale = swap(in_scale, 2)
    own_scale = both_halves(
        in_scale.reshape(slots, seq_here, 1), other_scale.reshape(slots, seq_here, 1)
    )
    own_hat = hidden_in.astype(F32) * own_scale
    grad_hat_in = grad_normed * own_gain
    cross_in = jnp.sum(grad_hat_in * own_hat, axis=-1, keepdims=True)
    cross_in = lax.psum(cross_in, "tp") / width
    grad_hidden_in = own_scale * (grad_hat_in - own_hat * cross_in) + out_cotangent.astype(F32)
    grad_norm_gain = jnp.sum(grad_normed * own_hat, axis=(0, 1))

    grad_skip_gain = jnp.sum(grad_skip_lanes.reshape(heads, HEADDIM), axis=1)
    shared_shapes = [(CONV, 2 * STATE), (2 * STATE,), (width_here,)]
    head_shapes = [(CONV, inner), (inner,), (inner,), (heads,), (heads,), (heads,)]
    smalls = lax.psum(
        pack(
            [
                grad_taps, grad_taps_bias, grad_gate_gain, grad_step_bias, grad_log_rate, grad_skip_gain,
                grad_conv_write_read, grad_conv_write_read_bias, grad_norm_gain,
            ]
        ),
        ("fsdp", "ctx"),
    )
    parts = unpack(smalls, head_shapes + shared_shapes)
    shared = pack(parts[6:8])
    shared = shared + swap(shared, 1)
    shared = shared + swap(shared, 2)
    wr_taps, wr_bias = unpack(shared, shared_shapes[:2])
    away = swap(pack([lax.slice_in_dim(p, p.shape[-1] // 2, p.shape[-1], axis=p.ndim - 1) for p in parts[:6]]), 2)
    homes = [
        lax.slice_in_dim(p, 0, p.shape[-1] // 2, axis=p.ndim - 1) + a
        for p, a in zip(parts[:6], unpack(away, small_shapes))
    ]
    return (
        hidden_out,
        grad_hidden_in,
        parts[8],
        jnp.stack([grad_gate_home, grad_inner_home], axis=1),
        write_read_home,
        step_home,
        homes[0],
        homes[1],
        wr_taps,
        wr_bias,
        homes[3],
        homes[4],
        homes[5],
        homes[2],
        grad_out_home,
    )


def solution(mesh):
    rows = ("fsdp", "ctx")
    acts = P("fsdp", "ctx", "tp")
    placed = (
        acts,
        P("fsdp"),
        P("tp"),
        P(rows, None, "tp"),
        P(rows, None),
        P(rows, "tp"),
        P(None, "tp"),
        P("tp"),
        P(),
        P(),
        P("tp"),
        P("tp"),
        P("tp"),
        P("tp"),
        P(rows, "tp"),
        acts,
    )
    return jax.shard_map(
        on_device,
        mesh=mesh,
        in_specs=placed,
        out_specs=(
            acts,
            acts,
            P("tp"),
            P(rows, None, "tp"),
            P(rows, None),
            P(rows, "tp"),
            P(None, "tp"),
            P("tp"),
            P(),
            P(),
            P("tp"),
            P("tp"),
            P("tp"),
            P("tp"),
            P(rows, "tp"),
        ),
        check_vma=False,
    )
```

time: 1400 us -> 757 us (0.54)
  waiting for transfers between devices: 541 us -> 254 us
  local copies, waits for them, and re-layouts: 316 us -> 77 us
  matrix products: 260 us -> 109 us
  Pallas kernels: 0 us -> 97.4 us
  blocking collectives: 87.8 us -> 35.4 us
  other arithmetic: 157 us -> 111 us
  starting transfers between devices: 8.4 us -> 49.8 us
    ppermute x0 -> x31, waiting for transfers between devices: none -> 252 us  [swap(): return lax.ppermute(x, 'tp', [(i, i ^ bit) for i in range(count)])]
    psum x1 -> x0, waiting for transfers between devices: 203 us -> none  [on_device(): lax.psum(jnp.concatenate([grad_write_blocks.reshape(slot_count, seq_here,...]
    reduce_scatter x3 -> x4, waiting for transfers between devices: 168 us -> 0.01 us  [reduced(): return lax.psum_scatter(x, ('fsdp', 'ctx'), scatter_dimension=0, tiled=True)]
    dynamic_update_slice x32 -> x0, local copies, waits for them, and re-layouts: 155 us -> none  [on_device(): lax.map(forward_block, (inner_blocks, write_blocks, read_blocks, step_blo...]
    dot_general x102 -> x27, matrix products: 260 us -> 109 us  [the longest x24 107 us: dot(): lax.dot_general(a, b, (((da,), (db,)), ((), ())), preferred_element_type=...]
    all_gather x4 -> x5, waiting for transfers between devices: 113 us -> 0.05 us  [gathered(): return lax.all_gather(x, ('fsdp', 'ctx'), axis=0, tiled=True)]
    pallas_call x0 -> x4, Pallas kernels: none -> 97.4 us  [the longest x1 40.8 us: back_blocks(): pl.pallas_call(back_kernel, grid=(blocks, steps), in_specs=[wide, wide, w...]
    unnamed x12 -> x9, waiting for transfers between devices: 55.8 us -> 0.65 us
  transfers between devices with their start and end apart: 14 -> 46, of which waited for: 8 -> 17; matrix products, arithmetic and copies ran while one was open for 24% -> 31% of each run, Pallas kernels for 0% -> 6%
where the time goes in v1:
time: 757 us; the launch traced here: 750 us
  waiting for transfers between devices  254 us (34%)
  other arithmetic  111 us (15%)
  matrix products  109 us (14%)
  Pallas kernels  97.4 us (13%)
  local copies, waits for them, and re-layouts  77 us (10%)
  starting transfers between devices  49.8 us (7%)
  blocking collectives  35.4 us (5%)
  between operations  15.9 us (2%)
    ppermute x31, waiting for transfers between devices, swap(): return lax.ppermute(x, 'tp', [(i, i ^ bit) for i in range(count)])  252 us
    dot_general x24, matrix products, dot(): lax.dot_general(a, b, (((da,), (db,)), ((), ())), preferred_element_type=...  107 us
    pallas_call x1, Pallas kernels, back_blocks(): pl.pallas_call(back_kernel, grid=(blocks, steps), in_specs=[wide, wide, w...  40.8 us
    ppermute x31, starting transfers between devices, swap(): return lax.ppermute(x, 'tp', [(i, i ^ bit) for i in range(count)])  39.5 us
    pallas_call x2, Pallas kernels, block_outer(): pl.pallas_call(state_kernel, grid=(blocks, steps), in_specs=[pl.BlockSpec...  29.1 us
    pallas_call x1, Pallas kernels, mix_blocks(): pl.pallas_call(mix_kernel, grid=(blocks, steps), in_specs=[wide, wide, na...  27.5 us
    psum x1, blocking collectives, on_device(): lax.psum(pack([grad_taps, grad_taps_bias, grad_gate_gain, grad_step_bias,...  25.3 us
    reduce_sum x2, other arithmetic, conv_silu(): summed = summed + conv_taps[offset] * padded[..., offset:offset + length, :]  22.3 us
  transfers between devices with their start and end apart: 46, of which 17 were waited for; matrix products, arithmetic and copies ran while one was open for 31% of the time, Pallas kernels for 6%

profile of v1, /device:TPU:0, one launch (start us, length us, event | category | flops | bytes accessed | tf_op | source)
XLA Modules:
  0.0 750.4 jit_solution(8383292097807768179)
XLA Ops:
  20.2 25.1 %collective-permute-done.7 = bf16[192,2,768]{2,0,1:T(8,128)(2,1)} collective-permute-done((bf16[192,2,768]{2,0,1:T(8,128)(2,1)}, bf16[192,2,768]{2,0,1:T(8,128)(2,1)}, u32[]{:S(2)}, u32[]{:S(2)}) %collective-permute-start.7) | collective-permute-done | bytes 589856 | tf_op jit(solution)/shard_map/ppermute | solution.py:27
  62.1 56.3 %collective-permute-done = f32[4644]{0:T(1024)S(1)} collective-permute-done((f32[4644]{0:T(1024)S(1)}, f32[4644]{0:T(1024)S(1)}, u32[]{:S(2)}, u32[]{:S(2)}) %collective-permute-start) | collective-permute-done | bytes 18608 | tf_op jit(solution)/shard_map/ppermute | solution.py:27
  124.3 10.0 %collective-permute-done.19 = bf16[1,1024,384]{2,1,0:T(8,128)(2,1)} collective-permute-done((bf16[1,1024,384]{2,1,0:T(8,128)(2,1)S(1)}, bf16[1,1024,384]{2,1,0:T(8,128)(2,1)}, u32[]{:S(2)}, u32[]{:S(2)}) %collective-permute-start.19) | collective-permute-done | bytes 786464 | tf_op jit(solution)/shard_map/ppermute | solution.py:27
  134.3 33.6 %collective-permute-done.3 = bf16[1,1024,384]{2,1,0:T(8,128)(2,1)S(1)} collective-permute-done((bf16[1,1024,384]{2,1,0:T(8,128)(2,1)}, bf16[1,1024,384]{2,1,0:T(8,128)(2,1)S(1)}, u32[]{:S(2)}, u32[]{:S(2)}) %collective-permute-start.3) | collective-permute-done | bytes 786464 | tf_op jit(solution)/shard_map/ppermute | solution.py:27
  171.6 13.0 %collective-permute-done.20 = bf16[1,1024,384]{2,1,0:T(8,128)(2,1)S(1)} collective-permute-done((bf16[1,1024,384]{2,1,0:T(8,128)(2,1)}, bf16[1,1024,384]{2,1,0:T(8,128)(2,1)S(1)}, u32[]{:S(2)}, u32[]{:S(2)}) %collective-permute-start.20) | collective-permute-done | bytes 786464 | tf_op jit(solution)/shard_map/ppermute | solution.py:27
  211.8 5.1 slice_bitcast_fusion
  217.4 5.4 fusion.19
  230.3 6.3 fusion.46
  236.7 14.3 %block_outer.2 = f32[4,128,1536]{2,1,0:T(8,128)} custom-call(bf16[1024,128]{1,0:T(8,128)(2,1)} %get-tuple-element.175.a_ref.w_ref, bf16[1024,1536]{1,0:T(8,128)(2,1)} %get-tuple-element.135.b_ref.x_ref, f32[4,1024,6]{2,1,0:T(8,128)} %bitcast.255), custom_call_target="tpu_custom_call" | custom-call | flops 402653184 | bytes 6291456 | tf_op jit(solution)/shard_map/block_outer/pallas_call | solution.py:86
  254.8 8.7 %fusion.18.gate_ref = bf16[1024,1536]{1,0:T(8,128)(2,1)} fusion(bf16[1024,1536]{1,0:T(8,128)(2,1)} %copy-done.61, bf16[1536,768]{1,0:T(8,128)(2,1)S(1)} %copy-done.10, bf16[1536,768]{1,0:T(8,128)(2,1)S(1)} %get-tuple-element.144), kind=kOutput, calls=%fused_computation.65 | convolution fusion | flops 4842848256 | bytes 11010048 | tf_op jit(solution)/shard_map/dot_general | solution.py:63
  267.2 27.5 %mix_blocks.1 = (f32[1024,1536]{1,0:T(8,128)}, f32[1024,1]{1,0:T(8,128)}) custom-call(bf16[1024,1536]{1,0:T(8,128)(2,1)} %get-tuple-element.135.b_ref.x_ref, bf16[1024,1536]{1,0:T(8,128)(2,1)} %fusion.18.gate_ref, bf16[1024,128]{1,0:T(8,128)(2,1)} %get-tuple-element.175.a_ref.w_ref, bf16[1024,128]{1,0:T(8,128)(2,1)} %get-tuple-element.174.r_ref.a_ref, ...), custom_call_target="tpu_custom_call" | custom-call | flops 4831838208 | bytes 15728640 | tf_op jit(solution)/shard_map/mix_blocks/pallas_call | solution.py:151
  298.3 10.0 %collective-permute-done.12 = f32[1024,1]{1,0:T(8,128)} collective-permute-done((f32[1024,1]{1,0:T(8,128)}, f32[1024,1]{1,0:T(8,128)}, u32[]{:S(2)}, u32[]{:S(2)}) %collective-permute-start.12) | collective-permute-done | bytes 4128 | tf_op jit(solution)/shard_map/ppermute | solution.py:27
  309.8 13.9 %multiply_reduce_fusion.1 = (f32[1536]{0:T(1024)}, f32[1024]{0:T(1024)}, f32[1024,1536]{1,0:T(8,128)}, f32[1024,1536]{1,0:T(8,128)}) fusion(f32[1536]{0:T(1024)S(1)} %copy-done.102, f32[1024]{0:T(1024)S(1)} %rsqrt_reduce_fusion, f32[1024,1536]{1,0:T(8,128)} %get-tuple-element.47.mixed_ref, bf16[1024,1536]{1,0:T(8,128)(2,1)S(1)} %copy-done.35, ...), kind=kOutput, calls=%fused_computation.45 | convolution fusion | flops 4868011520 | bytes 29908992 | tf_op jit(solution)/shard_map/dot_general | solution.py:63
  331.9 6.3 collective-permute-done.21
  339.6 10.1 %multiply_reduce_fusion = (f32[1536]{0:T(1024)}, f32[1024,1536]{1,0:T(8,128)S(1)}, bf16[1024,1536]{1,0:T(8,128)(2,1)}) fusion(bf16[1024,1536]{1,0:T(8,128)(2,1)S(1)} %copy-done.22, bf16[1024,1536]{1,0:T(8,128)(2,1)} %fusion.18.gate_ref, f32[1024,1536]{1,0:T(8,128)} %get-tuple-element.132, f32[1024]{0:T(1024)S(1)} %multiply_reduce_fusion.11, ...), kind=kLoop, calls=%fused_computation.44 | loop fusion | flops 23591424 | bytes 28332032 | tf_op jit(solution)/shard_map/reduce_sum | solution.py:498
  349.7 7.0 fusion.8
  356.7 14.8 %block_outer.3 = f32[4,128,1536]{2,1,0:T(8,128)} custom-call(bf16[1024,128]{1,0:T(8,128)(2,1)} %get-tuple-element.174.r_ref.a_ref, bf16[1024,1536]{1,0:T(8,128)(2,1)} %get-tuple-element.138.b_ref.grad_ref, f32[4,1024,6]{2,1,0:T(8,128)} %bitcast.256), custom_call_target="tpu_custom_call" | custom-call | flops 402653184 | bytes 6291456 | tf_op jit(solution)/shard_map/block_outer/pallas_call | solution.py:86
  381.0 40.8 %back_blocks.1 = (f32[1024,1536]{1,0:T(8,128)}, f32[1024,128]{1,0:T(8,128)}, f32[1024,128]{1,0:T(8,128)}, f32[4,1024,6]{2,1,0:T(8,128)}, f32[4,1024,6]{2,1,0:T(8,128)}, /*index=5*/f32[4,1024,6]{2,1,0:T(8,128)}) custom-call(bf16[1024,1536]{1,0:T(8,128)(2,1)} %get-tuple-element.135.b_ref.x_ref, f32[1024,1536]{1,0:T(8,128)} %get-tuple-element.47.mixed_ref, ...), custom_call_target="tpu_custom_call" | custom-call | flops 9663676416 | bytes 22020096 | tf_op jit(solution)/shard_map/back_blocks/pallas_call | solution.py:262
  453.7 10.3 %convolution_convert_fusion = bf16[1536,1536]{1,0:T(8,128)(2,1)} fusion(bf16[1024,1536]{1,0:T(8,128)(2,1)} %get-tuple-element.139, bf16[1,1024,384]{2,1,0:T(8,128)(2,1)} %get-tuple-element.159, bf16[1,1024,384]{2,1,0:T(8,128)(2,1)} %get-tuple-element.158, bf16[1,1024,384]{2,1,0:T(8,128)(2,1)} %get-tuple-element.157, ...), kind=kOutput, calls=%fused_computation.6 | convolution fusion | flops 4851499008 | bytes 11014144 | tf_op jit(solution)/shard_map/dot_general | solution.py:63
  469.5 5.1 convolution_convert_fusion.4
  483.7 6.9 convolution_convert_fusion.2
  490.6 18.2 %multiply_reduce_fusion.5 = (f32[1536]{0:T(1024)S(1)}, f32[1536]{0:T(1024)S(1)}, f32[1536]{0:T(1024)S(1)}, f32[1536]{0:T(1024)S(1)}, f32[1536]{0:T(1024)S(1)}, /*index=5*/f32[1,1024,1536]{2,1,0:T(8,128)}) fusion(f32[1,1027,1536]{2,1,0:T(8,128)} %copy-done, f32[1,1024,1536]{2,1,0:T(8,128)} %get-tuple-element.136, f32[1024,1536]{1,0:T(8,128)} %get-tuple-element.49), kind=kLoop, calls=%fused_computation.49 | loop fusion | flops 28303872 | bytes 44070912 | tf_op jit(solution)/shard_map/transpose(jvp())/reduce_sum | solution.py:58
  509.0 5.3 broadcast_multiply_fusion
  545.9 7.5 convolution_convert_fusion.1
  575.0 14.0 %collective-permute-done.25 = bf16[1024,384]{1,0:T(8,128)(2,1)S(1)} collective-permute-done((bf16[1024,384]{1,0:T(8,128)(2,1)S(1)}, bf16[1024,384]{1,0:T(8,128)(2,1)S(1)}, u32[]{:S(2)}, u32[]{:S(2)}) %collective-permute-start.25) | collective-permute-done | bytes 786464 | tf_op jit(solution)/shard_map/ppermute | solution.py:27
  590.9 30.2 %collective-permute-done.16 = bf16[1024,384]{1,0:T(8,128)(2,1)S(1)} collective-permute-done((bf16[1024,384]{1,0:T(8,128)(2,1)S(1)}, bf16[1024,384]{1,0:T(8,128)(2,1)S(1)}, u32[]{:S(2)}, u32[]{:S(2)}) %collective-permute-start.16) | collective-permute-done | bytes 786464 | tf_op jit(solution)/shard_map/ppermute | solution.py:27
  622.4 15.5 %collective-permute-done.27 = bf16[1024,384]{1,0:T(8,128)(2,1)S(1)} collective-permute-done((bf16[1024,384]{1,0:T(8,128)(2,1)S(1)}, bf16[1024,384]{1,0:T(8,128)(2,1)S(1)}, u32[]{:S(2)}, u32[]{:S(2)}) %collective-permute-start.27) | collective-permute-done | bytes 786464 | tf_op jit(solution)/shard_map/ppermute | solution.py:27
  639.5 25.3 %psum.15 = f32[10952]{0:T(1024)S(1)} all-reduce(f32[10952]{0:T(1024)S(1)} %concatenate.184), channel_id=1, replica_groups=mesh['fsdp'=4,'ctx'=2,'tp'=4] {'fsdp','ctx'}, use_global_device_ids=true, to_apply=%region_22.23 | all-reduce | flops 10952 | bytes 87616 | tf_op jit(solution)/shard_map/psum | solution.py:600
  667.9 10.1 %psum.14 = f32[2,1024,1]{1,0,2:T(2,128)S(1)} all-reduce(f32[2,1024,1]{1,0,2:T(2,128)S(1)} %bitcast.278), channel_id=1, replica_groups=mesh['fsdp'=4,'ctx'=2,'tp'=4] {'tp'}, use_global_device_ids=true, to_apply=%region_5.6 | all-reduce | flops 2048 | bytes 16384 | tf_op jit(solution)/shard_map/psum | solution.py:593
  678.2 8.7 %fusion.23 = (f32[2,1024,384]{2,1,0:T(8,128)}, bf16[2,1024,384]{2,1,0:T(8,128)(2,1)}) fusion(bf16[2,1024,384]{2,1,0:T(8,128)(2,1)S(1)} %copy-done.32, bf16[2,1024,384]{2,1,0:T(8,128)(2,1)} %param.35, f32[2,1024]{1,0:T(2,128)S(1)} %multiply_bitcast_fusion, f32[384]{0:T(512)S(1)} %copy-done.104, f32[2,1024]{1,0:T(2,128)S(1)} %maximum_select_fusion.2, ...), kind=kLoop, calls=%fused_computation.71 | loop fusion | flops 13369344 | bytes 14181889 | tf_op jit(solution)/shard_map/add | solution.py:594
  705.2 23.3 %collective-permute-done.31 = f32[192,256]{1,0:T(8,128)S(1)} collective-permute-done((f32[192,256]{1,0:T(8,128)S(1)}, f32[192,256]{1,0:T(8,128)S(1)}, u32[]{:S(2)}, u32[]{:S(2)}) %collective-permute-start.31) | collective-permute-done | bytes 196640 | tf_op jit(solution)/shard_map/ppermute | solution.py:27
  731.3 6.7 collective-permute-done.28
  (535 shorter events, 239.1 us)
Async XLA Ops:
  7.2 181.3 %all-gather.10.cloned.1.call-start = ((), (), s32[]{:S(2)}) async-start(), calls=%async_computation.6 | async-start | bytes 1327104 | tf_op jit(solution)/shard_map/all_gather | solution.py:392
  15.2 192.5 %all-gather.6.cloned.1.call-start = ((), (), s32[]{:S(2)}) async-start(), calls=%async_computation.4 | async-start | bytes 5308416 | tf_op jit(solution)/shard_map/all_gather | solution.py:392
  17.2 194.7 %all-gather.8.cloned.1.call-start = ((), (), s32[]{:S(2)}) async-start(), calls=%async_computation.5 | async-start | bytes 5308416 | tf_op jit(solution)/shard_map/all_gather | solution.py:392
  17.2 28.1 %collective-permute-start.7 = (bf16[192,2,768]{2,0,1:T(8,128)(2,1)}, bf16[192,2,768]{2,0,1:T(8,128)(2,1)}, u32[]{:S(2)}, u32[]{:S(2)}) collective-permute-start(bf16[192,2,768]{2,0,1:T(8,128)(2,1)} %copy.71), channel_id=1, source_target_pairs={{0,2},{1,3},{2,0},{3,1},{4,6},{5,7},{6,4},{7,5},{8,10},{9,11},{10,... | collective-permute-start | bytes 1769480 | tf_op jit(solution)/shard_map/ppermute | solution.py:27
  45.4 180.5 %all-gather.12.cloned.1.call-start = ((), (), s32[]{:S(2)}) async-start(), calls=%async_computation.7 | async-start | bytes 2654208 | tf_op jit(solution)/shard_map/all_gather | solution.py:392
  45.9 248.9 %all-gather.14.cloned.1.call-start = ((), (), s32[]{:S(2)}) async-start(), calls=%async_computation.8 | async-start | bytes 2654208 | tf_op jit(solution)/shard_map/all_gather | solution.py:392
  50.4 73.8 %collective-permute-start.13 = (bf16[192,768]{1,0:T(8,128)(2,1)S(1)}, bf16[192,768]{1,0:T(8,128)(2,1)}, u32[]{:S(2)}, u32[]{:S(2)}) collective-permute-start(bf16[192,768]{1,0:T(8,128)(2,1)S(1)} %copy-done.81), channel_id=1, source_target_pairs={{0,2},{1,3},{2,0},{3,1},{4,6},{5,7},{6,4},{7,5},{8,10},{9,11},{10,... | collective-permute-start | bytes 884744 | tf_op jit(solution)/shard_map/ppermute | solution.py:27
  53.1 67.6 %collective-permute-start.2 = (bf16[1,1024,384]{2,1,0:T(8,128)(2,1)}, bf16[1,1024,384]{2,1,0:T(8,128)(2,1)}, u32[]{:S(2)}, u32[]{:S(2)}) collective-permute-start(bf16[1,1024,384]{2,1,0:T(8,128)(2,1)} %get-tuple-element.162), channel_id=1, source_target_pairs={{0,2},{1,3},{2,0},{3,1},{4,6},{5,7},{6,4},{7,5},{8,10},{9,11},{10,... | collective-permute-start | bytes 2359304 | tf_op jit(solution)/shard_map/ppermute | solution.py:27
  57.2 77.0 %collective-permute-start.1 = (bf16[1,1024,384]{2,1,0:T(8,128)(2,1)S(1)}, bf16[1,1024,384]{2,1,0:T(8,128)(2,1)S(1)}, u32[]{:S(2)}, u32[]{:S(2)}) collective-permute-start(bf16[1,1024,384]{2,1,0:T(8,128)(2,1)S(1)} %copy-done.68), channel_id=1, source_target_pairs={{0,1},{1,0},{2,3},{3,2},{4,5},{5,4},{6,7},{7,6},{8,9},{9,8},{10,11... | collective-permute-start | bytes 2359304 | tf_op jit(solution)/shard_map/ppermute | solution.py:27
  58.5 59.9 %collective-permute-start = (f32[4644]{0:T(1024)S(1)}, f32[4644]{0:T(1024)S(1)}, u32[]{:S(2)}, u32[]{:S(2)}) collective-permute-start(f32[4644]{0:T(1024)S(1)} %concatenate.159), channel_id=1, source_target_pairs={{0,2},{1,3},{2,0},{3,1},{4,6},{5,7},{6,4},{7,5},{8,10},{9,11},{10,... | collective-permute-start | bytes 55736 | tf_op jit(solution)/shard_map/ppermute | solution.py:27
  61.4 72.9 %collective-permute-start.19 = (bf16[1,1024,384]{2,1,0:T(8,128)(2,1)S(1)}, bf16[1,1024,384]{2,1,0:T(8,128)(2,1)}, u32[]{:S(2)}, u32[]{:S(2)}) collective-permute-start(bf16[1,1024,384]{2,1,0:T(8,128)(2,1)S(1)} %get-tuple-element.164), channel_id=1, source_target_pairs={{0,2},{1,3},{2,0},{3,1},{4,6},{5,7},{6,4},{7,5},{8,10},{9,11},{10,... | collective-permute-start | bytes 2359304 | tf_op jit(solution)/shard_map/ppermute | solution.py:27
  118.4 53.2 %collective-permute-start.18 = (bf16[1,1024,384]{2,1,0:T(8,128)(2,1)}, bf16[1,1024,384]{2,1,0:T(8,128)(2,1)}, u32[]{:S(2)}, u32[]{:S(2)}) collective-permute-start(bf16[1,1024,384]{2,1,0:T(8,128)(2,1)} %get-tuple-element.165), channel_id=1, source_target_pairs={{0,1},{1,0},{2,3},{3,2},{4,5},{5,4},{6,7},{7,6},{8,9},{9,8},{10,11... | collective-permute-start | bytes 2359304 | tf_op jit(solution)/shard_map/ppermute | solution.py:27
  120.7 47.2 %collective-permute-start.3 = (bf16[1,1024,384]{2,1,0:T(8,128)(2,1)}, bf16[1,1024,384]{2,1,0:T(8,128)(2,1)S(1)}, u32[]{:S(2)}, u32[]{:S(2)}) collective-permute-start(bf16[1,1024,384]{2,1,0:T(8,128)(2,1)} %collective-permute-done.2), channel_id=1, source_target_pairs={{0,1},{1,0},{2,3},{3,2},{4,5},{5,4},{6,7},{7,6},{8,9},{9,8},{10,11... | collective-permute-start | bytes 2359304 | tf_op jit(solution)/shard_map/ppermute | solution.py:27
  124.3 565.6 %reduce-scatter.9.cloned.1.call-start = ((), (), s32[]{:S(2)}) async-start(), calls=%async_computation.11 | async-start | bytes 1327104 | tf_op jit(solution)/shard_map/reduce_scatter | solution.py:569
  134.3 50.4 %collective-permute-start.20 = (bf16[1,1024,384]{2,1,0:T(8,128)(2,1)}, bf16[1,1024,384]{2,1,0:T(8,128)(2,1)S(1)}, u32[]{:S(2)}, u32[]{:S(2)}) collective-permute-start(bf16[1,1024,384]{2,1,0:T(8,128)(2,1)} %collective-permute-done.19), channel_id=1, source_target_pairs={{0,1},{1,0},{2,3},{3,2},{4,5},{5,4},{6,7},{7,6},{8,9},{9,8},{10,11... | collective-permute-start | bytes 2359304 | tf_op jit(solution)/shard_map/ppermute | solution.py:27
  294.7 13.6 %collective-permute-start.12 = (f32[1024,1]{1,0:T(8,128)}, f32[1024,1]{1,0:T(8,128)}, u32[]{:S(2)}, u32[]{:S(2)}) collective-permute-start(f32[1024,1]{1,0:T(8,128)} %get-tuple-element.48), channel_id=1, source_target_pairs={{0,1},{1,0},{2,3},{3,2},{4,5},{5,4},{6,7},{7,6},{8,9},{9,8},{10,11... | collective-permute-start | bytes 12296 | tf_op jit(solution)/shard_map/ppermute | solution.py:27
  427.6 19.7 %collective-permute-start.24 = (f32[1,3,256]{2,1,0:T(4,128)S(1)}, f32[1,3,256]{2,1,0:T(4,128)S(1)}, u32[]{:S(2)}, u32[]{:S(2)}) collective-permute-start(f32[1,3,256]{2,1,0:T(4,128)S(1)} %pad_add_fusion.4), channel_id=1, source_target_pairs={{4,0},{5,1},{6,2},{7,3},{12,8},{13,9},{14,10},{15,11},{20,16},{21,... | collective-permute-start | bytes 9224 | tf_op jit(solution)/shard_map/ppermute | solution.py:33
  453.5 242.1 %reduce-scatter.11.cloned.1.call-start = ((), (), s32[]{:S(2)}) async-start(), calls=%async_computation.12 | async-start | bytes 5308416 | tf_op jit(solution)/shard_map/reduce_scatter | solution.py:569
  464.1 238.4 %reduce-scatter.5.cloned.1.call-start = ((), (), s32[]{:S(2)}) async-start(), calls=%async_computation.9 | async-start | bytes 5308416 | tf_op jit(solution)/shard_map/reduce_scatter | solution.py:569
  474.6 88.1 %collective-permute-start.15 = (bf16[1024,384]{1,0:T(8,128)(2,1)}, bf16[1024,384]{1,0:T(8,128)(2,1)}, u32[]{:S(2)}, u32[]{:S(2)}) collective-permute-start(bf16[1024,384]{1,0:T(8,128)(2,1)} %convolution_convert_fusion.4), channel_id=1, source_target_pairs={{0,1},{1,0},{2,3},{3,2},{4,5},{5,4},{6,7},{7,6},{8,9},{9,8},{10,11... | collective-permute-start | bytes 2359304 | tf_op jit(solution)/shard_map/ppermute | solution.py:27
  479.4 88.1 %collective-permute-start.14 = (bf16[1024,384]{1,0:T(8,128)(2,1)}, bf16[1024,384]{1,0:T(8,128)(2,1)}, u32[]{:S(2)}, u32[]{:S(2)}) collective-permute-start(bf16[1024,384]{1,0:T(8,128)(2,1)} %convolution_convert_fusion.5), channel_id=1, source_target_pairs={{0,1},{1,0},{2,3},{3,2},{4,5},{5,4},{6,7},{7,6},{8,9},{9,8},{10,11... | collective-permute-start | bytes 2359304 | tf_op jit(solution)/shard_map/ppermute | solution.py:27
  490.5 238.7 %reduce-scatter.7.cloned.1.call-start = ((), (), s32[]{:S(2)}) async-start(), calls=%async_computation.10 | async-start | bytes 5308416 | tf_op jit(solution)/shard_map/reduce_scatter | solution.py:569
  514.4 18.1 %collective-permute-start.23 = (f32[1,3,1536]{2,1,0:T(4,128)S(1)}, f32[1,3,1536]{2,1,0:T(4,128)S(1)}, u32[]{:S(2)}, u32[]{:S(2)}) collective-permute-start(f32[1,3,1536]{2,1,0:T(4,128)S(1)} %pad_add_fusion.2), channel_id=1, source_target_pairs={{4,0},{5,1},{6,2},{7,3},{12,8},{13,9},{14,10},{15,11},{20,16},{21,... | collective-permute-start | bytes 55304 | tf_op jit(solution)/shard_map/ppermute | solution.py:33
  542.1 29.6 %collective-permute-start.26 = (bf16[1024,384]{1,0:T(8,128)(2,1)}, bf16[1024,384]{1,0:T(8,128)(2,1)}, u32[]{:S(2)}, u32[]{:S(2)}) collective-permute-start(bf16[1024,384]{1,0:T(8,128)(2,1)} %add_convert_fusion.1), channel_id=1, source_target_pairs={{0,1},{1,0},{2,3},{3,2},{4,5},{5,4},{6,7},{7,6},{8,9},{9,8},{10,11... | collective-permute-start | bytes 2359304 | tf_op jit(solution)/shard_map/ppermute | solution.py:27
  557.6 31.4 %collective-permute-start.25 = (bf16[1024,384]{1,0:T(8,128)(2,1)S(1)}, bf16[1024,384]{1,0:T(8,128)(2,1)S(1)}, u32[]{:S(2)}, u32[]{:S(2)}) collective-permute-start(bf16[1024,384]{1,0:T(8,128)(2,1)S(1)} %add_convert_fusion.2), channel_id=1, source_target_pairs={{0,1},{1,0},{2,3},{3,2},{4,5},{5,4},{6,7},{7,6},{8,9},{9,8},{10,11... | collective-permute-start | bytes 2359304 | tf_op jit(solution)/shard_map/ppermute | solution.py:27
  566.1 55.0 %collective-permute-start.16 = (bf16[1024,384]{1,0:T(8,128)(2,1)S(1)}, bf16[1024,384]{1,0:T(8,128)(2,1)S(1)}, u32[]{:S(2)}, u32[]{:S(2)}) collective-permute-start(bf16[1024,384]{1,0:T(8,128)(2,1)S(1)} %add_convert_fusion.3), channel_id=1, source_target_pairs={{0,2},{1,3},{2,0},{3,1},{4,6},{5,7},{6,4},{7,5},{8,10},{9,11},{10,... | collective-permute-start | bytes 2359304 | tf_op jit(solution)/shard_map/ppermute | solution.py:27
  573.3 64.6 %collective-permute-start.27 = (bf16[1024,384]{1,0:T(8,128)(2,1)S(1)}, bf16[1024,384]{1,0:T(8,128)(2,1)S(1)}, u32[]{:S(2)}, u32[]{:S(2)}) collective-permute-start(bf16[1024,384]{1,0:T(8,128)(2,1)S(1)} %add_convert_fusion), channel_id=1, source_target_pairs={{0,2},{1,3},{2,0},{3,1},{4,6},{5,7},{6,4},{7,5},{8,10},{9,11},{10,... | collective-permute-start | bytes 2359304 | tf_op jit(solution)/shard_map/ppermute | solution.py:27
  665.1 23.5 %collective-permute-start.33 = (f32[4644]{0:T(1024)S(1)}, f32[4644]{0:T(1024)S(1)}, u32[]{:S(2)}, u32[]{:S(2)}) collective-permute-start(f32[4644]{0:T(1024)S(1)} %concatenate.190), channel_id=1, source_target_pairs={{0,2},{1,3},{2,0},{3,1},{4,6},{5,7},{6,4},{7,5},{8,10},{9,11},{10,... | collective-permute-start | bytes 55736 | tf_op jit(solution)/shard_map/ppermute | solution.py:27
  665.2 12.9 %collective-permute-start.34 = (f32[1280]{0:T(1024)S(1)}, f32[1280]{0:T(1024)S(1)}, u32[]{:S(2)}, u32[]{:S(2)}) collective-permute-start(f32[1280]{0:T(1024)S(1)} %concatenate.192), channel_id=1, source_target_pairs={{0,1},{1,0},{2,3},{3,2},{4,5},{5,4},{6,7},{7,6},{8,9},{9,8},{10,11... | collective-permute-start | bytes 15368 | tf_op jit(solution)/shard_map/ppermute | solution.py:27
  696.6 33.7 %collective-permute-start.36 = (bf16[192,768]{1,0:T(8,128)(2,1)S(1)}, bf16[192,768]{1,0:T(8,128)(2,1)S(1)}, u32[]{:S(2)}, u32[]{:S(2)}) collective-permute-start(bf16[192,768]{1,0:T(8,128)(2,1)S(1)} %slice.508), channel_id=1, source_target_pairs={{0,2},{1,3},{2,0},{3,1},{4,6},{5,7},{6,4},{7,5},{8,10},{9,11},{10,... | collective-permute-start | bytes 884744 | tf_op jit(solution)/shard_map/ppermute | solution.py:27
  699.0 29.5 %collective-permute-start.31 = (f32[192,256]{1,0:T(8,128)S(1)}, f32[192,256]{1,0:T(8,128)S(1)}, u32[]{:S(2)}, u32[]{:S(2)}) collective-permute-start(f32[192,256]{1,0:T(8,128)S(1)} %fusion.117), channel_id=1, source_target_pairs={{0,2},{1,3},{2,0},{3,1},{4,6},{5,7},{6,4},{7,5},{8,10},{9,11},{10,... | collective-permute-start | bytes 589832 | tf_op jit(solution)/shard_map/ppermute | solution.py:27
  703.6 34.4 %collective-permute-start.28 = (bf16[192,768]{1,0:T(8,128)(2,1)S(1)}, bf16[192,768]{1,0:T(8,128)(2,1)S(1)}, u32[]{:S(2)}, u32[]{:S(2)}) collective-permute-start(bf16[192,768]{1,0:T(8,128)(2,1)S(1)} %slice.480), channel_id=1, source_target_pairs={{0,2},{1,3},{2,0},{3,1},{4,6},{5,7},{6,4},{7,5},{8,10},{9,11},{10,... | collective-permute-start | bytes 884744 | tf_op jit(solution)/shard_map/ppermute | solution.py:27
  (149 other events, 2508.2 us)
Sparse Core Ops, SparseCore 0:
  15.3 25.4 all-gather.9
  43.3 38.7 all-gather.5
  84.0 38.7 all-gather.7
  124.6 28.8 all-gather.11
  155.2 28.8 all-gather.13
  453.6 36.7 reduce-scatter.8
  493.8 53.7 reduce-scatter.10
  551.1 53.7 reduce-scatter.4
  608.3 54.3 reduce-scatter.6

commit v2 on v1

--- a/solution.py
+++ b/solution.py
@@ -19,7 +19,6 @@
 F32 = jnp.float32
 BF16 = jnp.bfloat16
 HIGHEST = lax.Precision.HIGHEST
-OUTER = (("fsdp", "ctx"))
 
 
 def swap(x, bit):
@@ -71,47 +70,49 @@
     return jnp.where(low_half, cols[:, 2 * pair : 2 * pair + 1], cols[:, 2 * pair + 1 : 2 * pair + 2])
 
 
-def state_kernel(a_ref, b_ref, scale_ref, out_ref):
+def state_kernel(a_ref, b_ref, scale_ref, out_ref, scaled_ref):
     scale = scale_ref[0]
     low_half = low_lanes(GROUP)
     for pair in range(HEADS_STEP // 2):
         lanes = slice(PAIR * pair, PAIR * (pair + 1))
-        scaled = (b_ref[:, lanes].astype(F32) * spread_heads(scale, pair, low_half)).astype(BF16)
-        out_ref[0, :, lanes] = dot(a_ref[...], scaled, 0, 0)
-
-
-def block_outer(rows_a, cols_b, scale):
+        scaled = b_ref[:, lanes].astype(F32) * spread_heads(scale, pair, low_half)
+        scaled_ref[:, lanes] = scaled.astype(BF16)
+    out_ref[0] = dot(a_ref[...], scaled_ref[...], 1, 0)
+
+
+def block_outer(cols_a, cols_b, scale):
     tokens, width = cols_b.shape
     blocks, steps = tokens // GROUP, width // LANES_STEP
     return pl.pallas_call(
         state_kernel,
         grid=(blocks, steps),
         in_specs=[
-            pl.BlockSpec((GROUP, STATE), lambda b, g: (b, 0)),
+            pl.BlockSpec((STATE, GROUP), lambda b, g: (0, b)),
             pl.BlockSpec((GROUP, LANES_STEP), lambda b, g: (b, g)),
             pl.BlockSpec((1, GROUP, HEADS_STEP), lambda b, g: (g, b, 0)),
         ],
         out_specs=pl.BlockSpec((1, STATE, LANES_STEP), lambda b, g: (b, 0, g)),
         out_shape=jax.ShapeDtypeStruct((blocks, STATE, width), F32),
+        scratch_shapes=[pltpu.VMEM((GROUP, LANES_STEP), BF16)],
         cost_estimate=pl.CostEstimate(
             flops=2 * tokens * STATE * width,
             bytes_accessed=tokens * width * 2 + blocks * STATE * width * 4,
             transcendentals=0,
         ),
         name="block_outer",
-    )(rows_a, cols_b, scale)
+    )(cols_a, cols_b, scale)
 
 
 def mix_kernel(
-    x_ref, gate_ref, w_ref, r_ref, step_ref, cum_ref, cumt_ref, state_ref, skip_ref,
-    mixed_ref, square_ref, scores_ref,
+    x_ref, gate_ref, gno_ref, w_ref, r_ref, step_ref, cum_ref, cumt_ref, state_ref, skip_ref, gain_ref,
+    mixed_ref, stats_ref, scores_ref, sums_ref,
 ):
     g = pl.program_id(1)
 
     @pl.when(g == 0)
     def _():
         scores_ref[...] = dot(r_ref[...], w_ref[...], 1, 1)
-        square_ref[...] = jnp.zeros_like(square_ref)
+        sums_ref[...] = jnp.zeros_like(sums_ref)
 
     cum, cumt, step = cum_ref[0], cumt_ref[0, 0], step_ref[0]
     grown = jnp.exp(cum)
@@ -120,6 +121,7 @@
         jnp.int32, (GROUP, GROUP), 1
     )
     squares = jnp.zeros((GROUP, 1), F32)
+    crosses = jnp.zeros((GROUP, 1), F32)
     for pair in range(HEADS_STEP // 2):
         lanes = slice(PAIR * pair, PAIR * (pair + 1))
         x = x_ref[:, lanes].astype(F32)
@@ -139,10 +141,17 @@
         gate = gate_ref[:, lanes].astype(F32)
         gated = mixed * (gate * jax.nn.sigmoid(gate))
         squares = squares + jnp.sum(gated * gated, axis=1, keepdims=True)
-    square_ref[...] += squares
-
-
-def mix_blocks(x, gate, write, read, step, cum, cumt, states, skip):
+        grad_hat = gno_ref[:, lanes].astype(F32) * gain_ref[:, lanes]
+        crosses = crosses + jnp.sum(gated * grad_hat, axis=1, keepdims=True)
+    lane = lax.broadcasted_iota(jnp.int32, (GROUP, 128), 1)
+    sums_ref[...] += jnp.where(lane == 0, squares, jnp.where(lane == 1, crosses, 0.0))
+
+    @pl.when(g == pl.num_programs(1) - 1)
+    def _():
+        stats_ref[0] = sums_ref[...].T[:8]
+
+
+def mix_blocks(x, gate, gno, write, read, step, cum, cumt, states, skip, gain):
     tokens, width = x.shape
     blocks, steps = tokens // GROUP, width // LANES_STEP
     wide = pl.BlockSpec((GROUP, LANES_STEP), lambda b, g: (b, g))
@@ -152,24 +161,97 @@
         mix_kernel,
         grid=(blocks, steps),
         in_specs=[
-            wide, wide, narrow, narrow, cols, cols,
+            wide, wide, wide, narrow, narrow, cols, cols,
             pl.BlockSpec((1, 1, HEADS_STEP, GROUP), lambda b, g: (g, b, 0, 0)),
             pl.BlockSpec((1, STATE, LANES_STEP), lambda b, g: (b, 0, g)),
             pl.BlockSpec((1, LANES_STEP), lambda b, g: (0, g)),
-        ],
-        out_specs=[wide, pl.BlockSpec((GROUP, 1), lambda b, g: (b, 0))],
+            pl.BlockSpec((1, LANES_STEP), lambda b, g: (0, g)),
+        ],
+        out_specs=[wide, pl.BlockSpec((1, 8, GROUP), lambda b, g: (b, 0, 0))],
         out_shape=[
             jax.ShapeDtypeStruct((tokens, width), F32),
-            jax.ShapeDtypeStruct((tokens, 1), F32),
-        ],
-        scratch_shapes=[pltpu.VMEM((GROUP, GROUP), F32)],
+            jax.ShapeDtypeStruct((blocks, 8, GROUP), F32),
+        ],
+        scratch_shapes=[pltpu.VMEM((GROUP, GROUP), F32), pltpu.VMEM((GROUP, 128), F32)],
         cost_estimate=pl.CostEstimate(
             flops=2 * tokens * width * (2 * GROUP + 2 * STATE) * 2,
             bytes_accessed=tokens * width * 10,
             transcendentals=tokens * GROUP * width // HEADDIM,
         ),
         name="mix_blocks",
-    )(x, gate, write, read, step, cum, cumt, states, skip)
+    )(x, gate, gno, write, read, step, cum, cumt, states, skip, gain)
+
+
+def gate_kernel(
+    mixed_ref, gate_ref, gno_ref, x_ref, stats_ref, gain_ref, rt_ref, cum_ref,
+    normed_ref, ggate_ref, gdiag_ref, gain_sum_ref, skip_sum_ref, flow_ref, scaled_ref,
+):
+    @pl.when(pl.program_id(1) == 0)
+    def _():
+        gain_sum_ref[...] = jnp.zeros_like(gain_sum_ref)
+        skip_sum_ref[...] = jnp.zeros_like(skip_sum_ref)
+
+    stats = stats_ref[0].T
+    scale = lax.rsqrt(stats[:, 0:1] / INNER + EPSILON)
+    cross = scale * stats[:, 1:2] / INNER
+    grown = jnp.exp(cum_ref[0])
+    low_half = low_lanes(GROUP)
+    for pair in range(HEADS_STEP // 2):
+        lanes = slice(PAIR * pair, PAIR * (pair + 1))
+        mixed = mixed_ref[:, lanes]
+        gate = gate_ref[:, lanes].astype(F32)
+        gno = gno_ref[:, lanes].astype(F32)
+        gain = gain_ref[:, lanes]
+        sig = jax.nn.sigmoid(gate)
+        act = gate * sig
+        hat = mixed * act * scale
+        normed_ref[:, lanes] = (hat * gain).astype(BF16)
+        gain_sum_ref[:, lanes] += jnp.sum(gno * hat, axis=0, keepdims=True)
+        grad_gated = scale * (gno * gain - hat * cross)
+        grad_mixed = grad_gated * act
+        ggate_ref[:, lanes] = (grad_gated * mixed * sig * (1.0 + gate * (1.0 - sig))).astype(BF16)
+        skip_sum_ref[:, lanes] += jnp.sum(grad_mixed * x_ref[:, lanes].astype(F32), axis=0, keepdims=True)
+        diag = grad_mixed.astype(BF16)
+        gdiag_ref[:, lanes] = diag
+        scaled_ref[:, lanes] = (diag.astype(F32) * spread_heads(grown, pair, low_half)).astype(BF16)
+    flow_ref[0] = dot(rt_ref[...], scaled_ref[...], 1, 0)
+
+
+def gate_blocks(mixed, gate, gno, x, stats, gain, read_t, cum):
+    tokens, width = x.shape
+    blocks, steps = tokens // GROUP, width // LANES_STEP
+    wide = pl.BlockSpec((GROUP, LANES_STEP), lambda g, b: (b, g))
+    line = pl.BlockSpec((1, LANES_STEP), lambda g, b: (0, g))
+    return pl.pallas_call(
+        gate_kernel,
+        grid=(steps, blocks),
+        in_specs=[
+            wide, wide, wide, wide,
+            pl.BlockSpec((1, 8, GROUP), lambda g, b: (b, 0, 0)),
+            line,
+            pl.BlockSpec((STATE, GROUP), lambda g, b: (0, b)),
+            pl.BlockSpec((1, GROUP, HEADS_STEP), lambda g, b: (g, b, 0)),
+        ],
+        out_specs=[
+            wide, wide, wide, line, line,
+            pl.BlockSpec((1, STATE, LANES_STEP), lambda g, b: (b, 0, g)),
+        ],
+        out_shape=[
+            jax.ShapeDtypeStruct((tokens, width), BF16),
+            jax.ShapeDtypeStruct((tokens, width), BF16),
+            jax.ShapeDtypeStruct((tokens, width), BF16),
+            jax.ShapeDtypeStruct((1, width), F32),
+            jax.ShapeDtypeStruct((1, width), F32),
+            jax.ShapeDtypeStruct((blocks, STATE, width), F32),
+        ],
+        scratch_shapes=[pltpu.VMEM((GROUP, LANES_STEP), BF16)],
+        cost_estimate=pl.CostEstimate(
+            flops=2 * tokens * STATE * width,
+            bytes_accessed=tokens * width * 16 + blocks * STATE * width * 4,
+            transcendentals=tokens * width,
+        ),
+        name="gate_blocks",
+    )(mixed, gate, gno, x, stats, gain, read_t, cum)
 
 
 def segment_sums(values):
@@ -291,6 +373,22 @@
     )(x, mixed, grad, write, read, step, cum, cumt, states, flows, skip)
 
 
+def after(x, other):
+    return lax.optimization_barrier((x, other))[0]
+
+
+def everywhere(x):
+    for axis in ("ctx", "fsdp"):
+        count, bit = lax.axis_size(axis), 1
+        if count & (count - 1):
+            x = lax.psum(x, axis)
+            continue
+        while bit < count:
+            x = x + lax.ppermute(x, axis, [(i, i ^ bit) for i in range(count)])
+            bit *= 2
+    return x
+
+
 def pack(parts):
     return jnp.concatenate([part.reshape(-1) for part in parts])
 
@@ -351,13 +449,6 @@
             [lower(a0, b0), lower(a1, b1), lower(b0, a0), lower(b1, a1)], axis=axis
         )
 
-    def all_features(local):
-        mine, other = half_of(local, far_half), half_of(local, 1 - far_half)
-        far = swap(other, 2)
-        near = swap(mine, 1)
-        both = swap(far, 1)
-        return ordered(mine, near, far, both, 2).reshape(tokens, width)
-
     def own_features(piece):
         relay = swap(piece(place ^ 3).astype(BF16), 1)
         keep = swap(piece(place ^ 1).astype(BF16), 1)
@@ -372,9 +463,6 @@
             jnp.concatenate([kept, other], axis=0),
             jnp.concatenate([other, kept], axis=0),
         )
-
-    full_x = all_features(hidden_in)
-    full_gain = ordered(norm_gain, swap(norm_gain, 1), swap(norm_gain, 2), swap(norm_gain, 3), 0)
 
     small_shapes = [(CONV, inner_own), (inner_own,), (inner_own,), (heads_own,), (heads_own,), (heads_own,)]
     own_small = pack([conv_inner, conv_inner_bias, gate_gain, step_bias, log_rate, skip_gain])
@@ -391,6 +479,8 @@
     def gathered(x):
         return lax.all_gather(x, ("fsdp", "ctx"), axis=0, tiled=True)
 
+    x_mine, x_other = half_of(hidden_in, far_half), half_of(hidden_in, 1 - far_half)
+    cot_mine, cot_other = half_of(out_cotangent, far_half), half_of(out_cotangent, 1 - far_half)
     narrow_cols = 2 * STATE + heads
     narrow_pad = -narrow_cols % 128
     narrow_shard = jnp.concatenate(
@@ -398,13 +488,24 @@
         + [jnp.zeros((proj_step.shape[0], narrow_pad), BF16)],
         axis=1,
     )
+    inner_shard, gate_shard = proj_gate_inner[:, 1], proj_gate_inner[:, 0]
+    inner_far = swap(inner_shard, 2)
+    x_near = swap(x_mine, 1)
+    x_far = swap(after(x_other, inner_far), 2)
+    gate_far = swap(after(gate_shard, x_far), 2)
+    x_both = swap(x_far, 1)
+    cot_dep = after(x_both, gate_far)
+    cot_near = swap(after(cot_mine, cot_dep), 1)
+    cot_far = swap(after(cot_other, cot_dep), 2)
+    out_far = swap(after(proj_out, cot_far), 2)
+    cot_both = swap(cot_far, 1)
     full_narrow = gathered(narrow_shard)
-    own_gi, far_gi = gathered(proj_gate_inner), gathered(swap(proj_gate_inner, 2))
-    own_out, far_out = gathered(proj_out), gathered(swap(proj_out, 2))
-    full_gate = jnp.concatenate([own_gi[:, 0], far_gi[:, 0]], axis=1)
-    full_inner = jnp.concatenate([own_gi[:, 1], far_gi[:, 1]], axis=1)
-    full_out = jnp.concatenate([own_out, far_out], axis=1)
-    full_cot = all_features(out_cotangent)
+    full_inner = gathered(jnp.concatenate([inner_shard, inner_far], axis=1))
+    full_gate = gathered(jnp.concatenate([after(gate_shard, full_inner), gate_far], axis=1))
+    full_out = gathered(jnp.concatenate([after(proj_out, full_gate), out_far], axis=1))
+    full_x = ordered(x_mine, x_near, x_far, x_both, 2).reshape(tokens, width)
+    full_gain = ordered(norm_gain, swap(norm_gain, 1), swap(norm_gain, 2), swap(norm_gain, 3), 0)
+    full_cot = ordered(cot_mine, cot_near, cot_far, cot_both, 2).reshape(tokens, width)
 
     in_float = full_x.astype(F32)
     in_scale = lax.rsqrt(jnp.mean(in_float * in_float, axis=-1, keepdims=True) + EPSILON)
@@ -447,7 +548,7 @@
     decay = jnp.exp(last)
     decay_lanes = jnp.repeat(decay, HEADDIM, axis=1).reshape(slots, groups, 1, inner)
 
-    local_state = block_outer(write, inner_act, write_scale).reshape(slots, groups, STATE, inner)
+    local_state = block_outer(write.T, inner_act, write_scale).reshape(slots, groups, STATE, inner)
     carried = local_state[:, 0]
     device_decay = decay_lanes[:, 0]
     for position in range(1, groups):
@@ -461,46 +562,30 @@
     states = jnp.stack(state_list, axis=1)
     states_low = states.astype(BF16).reshape(blocks, STATE, inner)
 
-    mixed_out, squares = mix_blocks(
-        inner_act, gate_pre, write, read, step_cols, cum_cols, cum_rows, states_low, skip_lanes
-    )
-    square_sum = squares + swap(squares, 1)
-    out_scale = lax.rsqrt(square_sum / INNER + EPSILON)
-    gate_float = gate_pre.astype(F32)
-    gate_sigmoid = jax.nn.sigmoid(gate_float)
-    gate_act = gate_float * gate_sigmoid
-    gated_out = mixed_out * gate_act
-    gate_hat = gated_out * out_scale
-    normed_out = (gate_hat * gain_gate).astype(BF16)
+    position_ids = lax.axis_index("ctx") * seq_here + jnp.arange(seq_here)
+    valid_rows = (position_ids[None, :] < lengths[:, None]).astype(F32)
+    valid_here = half_of(valid_rows, far_half).reshape(tokens, 1)
+    masked = (full_cot.astype(F32) * valid_here).astype(BF16)
+    grad_normed_out = dot(masked, full_out, 1, 0).astype(BF16)
+    mixed_out, stats = mix_blocks(
+        inner_act, gate_pre, grad_normed_out, write, read, step_cols, cum_cols, cum_rows, states_low,
+        skip_lanes, gain_gate[None],
+    )
+    stats = stats + swap(stats, 1)
+    normed_out, grad_gate_pre, grad_diag, grad_gate_gain, grad_skip_lanes, local_grad = gate_blocks(
+        mixed_out, gate_pre, grad_normed_out, inner_act, stats, gain_gate[None], read.T, cum_cols
+    )
+    local_grad = local_grad.reshape(slots, groups, STATE, inner)
 
     def branch_piece(which):
         rows = lax.dynamic_slice_in_dim(full_out, which * width_here, width_here, 0)
         return dot(normed_out, rows, 1, 1)
 
     branch = own_features(branch_piece)
-    position_ids = lax.axis_index("ctx") * seq_here + jnp.arange(seq_here)
-    valid_rows = (position_ids[None, :] < lengths[:, None]).astype(F32)
     hidden_out = (hidden_in.astype(F32) + valid_rows[..., None] * branch).astype(BF16)
-    valid_here = half_of(valid_rows, far_half).reshape(tokens, 1)
-    masked = (full_cot.astype(F32) * valid_here).astype(BF16)
-
     grad_proj_out = dot(masked, normed_out, 0, 0).astype(BF16)
-    grad_normed_out = dot(masked, full_out, 1, 0)
-    grad_gate_gain = jnp.sum(grad_normed_out * gate_hat, axis=0)
-    grad_hat = grad_normed_out * gain_gate
-    cross_part = jnp.sum(grad_hat * gate_hat, axis=-1, keepdims=True)
-    cross_term = cross_part + swap(cross_part, 1)
-    grad_gated = out_scale * (grad_hat - gate_hat * (cross_term / INNER))
-    grad_mixed = grad_gated * gate_act
-    grad_gate_pre = (
-        grad_gated * mixed_out * gate_sigmoid * (1.0 + gate_float * (1.0 - gate_sigmoid))
-    ).astype(BF16)
-    grad_skip_lanes = jnp.sum(grad_mixed * inner_act.astype(F32), axis=0)
-    grad_diag = grad_mixed.astype(BF16)
     grad_gate_w = dot(normed, grad_gate_pre, 0, 0).astype(BF16)
 
-    read_scale = by_steps(jnp.exp(cum))
-    local_grad = block_outer(read, grad_diag, read_scale).reshape(slots, groups, STATE, inner)
     flowing = local_grad[:, groups - 1]
     for position in reversed(range(groups - 1)):
         flowing = decay_lanes[:, position] * flowing + local_grad[:, position]
@@ -514,6 +599,7 @@
         jnp.sum(flows * states, axis=2).reshape(blocks, heads, HEADDIM).sum(axis=2) * decay
     )
     flows_low = flows.astype(BF16).reshape(blocks, STATE, inner)
+    flows_low = after(flows_low, (grad_proj_out, grad_gate_w))
 
     grad_inner_act, grad_write, grad_read, u_cols, v_cols, inter_cols = back_blocks(
         inner_act, mixed_out, grad_diag, write, read, step_cols, cum_cols, cum_rows,
@@ -553,17 +639,30 @@
     grad_inner_w = dot(normed, grad_inner_pre, 0, 0).astype(BF16)
     grad_narrow_w = dot(normed, grad_narrow, 0, 0).astype(BF16)
 
+    kept_sums = []
+
     def normed_piece(which):
         def rows(full):
             return lax.dynamic_slice_in_dim(full, which * width_here, width_here, 0)
 
-        return (
+        piece = (
             dot(grad_gate_pre, rows(full_gate), 1, 1)
             + dot(grad_inner_pre, rows(full_inner), 1, 1)
             + dot(grad_narrow, rows(full_narrow), 1, 1)
         )
+        cols = lax.dynamic_slice_in_dim(full_x, which * width_here, width_here, 1).astype(F32)
+        gain = lax.dynamic_slice_in_dim(full_gain, which * width_here, width_here, 0).astype(F32)
+        by_hat = piece * (cols * in_scale)
+        kept_sums.append((which, jnp.sum(by_hat, axis=0), jnp.sum(by_hat * gain, axis=1)))
+        return piece
 
     grad_normed = own_features(normed_piece)
+    grad_gain_full = jnp.zeros((width,), F32)
+    cross_rows = jnp.zeros((tokens,), F32)
+    for which, by_feature, by_row in kept_sums:
+        grad_gain_full = lax.dynamic_update_slice_in_dim(grad_gain_full, by_feature, which * width_here, 0)
+        cross_rows = cross_rows + by_row
+    cross_rows = cross_rows + swap(cross_rows, 1)
 
     def reduced(x):
         return lax.psum_scatter(x, ("fsdp", "ctx"), scatter_dimension=0, tiled=True)
@@ -589,28 +688,28 @@
     )
     own_hat = hidden_in.astype(F32) * own_scale
     grad_hat_in = grad_normed * own_gain
-    cross_in = jnp.sum(grad_hat_in * own_hat, axis=-1, keepdims=True)
-    cross_in = lax.psum(cross_in, "tp") / width
+    cross_in = both_halves(
+        cross_rows.reshape(slots, seq_here, 1), swap(cross_rows, 2).reshape(slots, seq_here, 1)
+    ) / width
     grad_hidden_in = own_scale * (grad_hat_in - own_hat * cross_in) + out_cotangent.astype(F32)
-    grad_norm_gain = jnp.sum(grad_normed * own_hat, axis=(0, 1))
 
     grad_skip_gain = jnp.sum(grad_skip_lanes.reshape(heads, HEADDIM), axis=1)
-    shared_shapes = [(CONV, 2 * STATE), (2 * STATE,), (width_here,)]
+    shared_shapes = [(CONV, 2 * STATE), (2 * STATE,), (width,)]
     head_shapes = [(CONV, inner), (inner,), (inner,), (heads,), (heads,), (heads,)]
-    smalls = lax.psum(
+    smalls = everywhere(
         pack(
             [
                 grad_taps, grad_taps_bias, grad_gate_gain, grad_step_bias, grad_log_rate, grad_skip_gain,
-                grad_conv_write_read, grad_conv_write_read_bias, grad_norm_gain,
+                grad_conv_write_read, grad_conv_write_read_bias, grad_gain_full,
             ]
-        ),
-        ("fsdp", "ctx"),
+        )
     )
     parts = unpack(smalls, head_shapes + shared_shapes)
-    shared = pack(parts[6:8])
+    shared = pack(parts[6:9])
     shared = shared + swap(shared, 1)
     shared = shared + swap(shared, 2)
-    wr_taps, wr_bias = unpack(shared, shared_shapes[:2])
+    wr_taps, wr_bias, gain_all = unpack(shared, shared_shapes)
+    grad_norm_gain = lax.dynamic_slice_in_dim(gain_all, place * width_here, width_here, 0)
     away = swap(pack([lax.slice_in_dim(p, p.shape[-1] // 2, p.shape[-1], axis=p.ndim - 1) for p in parts[:6]]), 2)
     homes = [
         lax.slice_in_dim(p, 0, p.shape[-1] // 2, axis=p.ndim - 1) + a
@@ -619,7 +718,7 @@
     return (
         hidden_out,
         grad_hidden_in,
-        parts[8],
+        grad_norm_gain,
         jnp.stack([grad_gate_home, grad_inner_home], axis=1),
         write_read_home,
         step_home,

time: 757 us -> 676 us (0.89)
  waiting for transfers between devices: 254 us -> 214 us
  blocking collectives: 35.4 us -> 0 us
  local copies, waits for them, and re-layouts: 77 us -> 52.9 us
  other arithmetic: 111 us -> 97 us
  starting transfers between devices: 49.8 us -> 59.7 us
  Pallas kernels: 97.4 us -> 106 us
  matrix products: 109 us -> 117 us
    ppermute x31 -> x33, waiting for transfers between devices: 252 us -> 213 us  [swap(): return lax.ppermute(x, 'tp', [(i, i ^ bit) for i in range(count)])]
    psum x2 -> x0, blocking collectives: 35.4 us -> none  [the longest x1 25.3 us: on_device(): lax.psum(pack([grad_taps, grad_taps_bias, grad_gate_gain, grad_step_bias,...]
    pallas_call x1 -> x2, Pallas kernels: 27.5 us -> 50.7 us  [the longest x1 29.7 us: mix_blocks(): pl.pallas_call(mix_kernel, grid=(blocks, steps), in_specs=[wide, wide, wi...]
    pallas_call x2 -> x1, Pallas kernels: 29.1 us -> 14.5 us  [block_outer(): pl.pallas_call(state_kernel, grid=(blocks, steps), in_specs=[pl.BlockSpec...]
    reduce_sum x2 -> x0, other arithmetic: 11.5 us -> none  [the longest x1 10.1 us: on_device(): grad_skip_lanes = jnp.sum(grad_mixed * inner_act.astype(F32), axis=0)]
    squeeze x2 -> x0, local copies, waits for them, and re-layouts: 9.24 us -> none  [on_device(): full_gate = jnp.concatenate([own_gi[:, 0], far_gi[:, 0]], axis=1)]
    convert_element_type x4 -> x1, other arithmetic: 9.83 us -> 0.67 us  [normed_piece(): lax.dynamic_slice_in_dim(full_gain, which * width_here, width_here, 0)]
    ppermute x0 -> x3, starting transfers between devices: none -> 8.98 us  [everywhere(): x = x + lax.ppermute(x, axis, [(i, i ^ bit) for i in range(count)])]
  transfers between devices with their start and end apart: 46 -> 50, of which waited for: 17 -> 15; matrix products, arithmetic and copies ran while one was open for 31% -> 32% of each run, Pallas kernels for 6% -> 2%
where the time goes in v2:
time: 676 us; the launch traced here: 664 us
  waiting for transfers between devices  214 us (32%)
  matrix products  117 us (17%)
  Pallas kernels  106 us (16%)
  other arithmetic  97 us (14%)
  starting transfers between devices  59.7 us (9%)
  local copies, waits for them, and re-layouts  52.9 us (8%)
  between operations  16.3 us (2%)
    ppermute x33, waiting for transfers between devices, swap(): return lax.ppermute(x, 'tp', [(i, i ^ bit) for i in range(count)])  213 us
    dot_general x24, matrix products, dot(): lax.dot_general(a, b, (((da,), (db,)), ((), ())), preferred_element_type=...  115 us
    ppermute x33, starting transfers between devices, swap(): return lax.ppermute(x, 'tp', [(i, i ^ bit) for i in range(count)])  42 us
    pallas_call x1, Pallas kernels, back_blocks(): pl.pallas_call(back_kernel, grid=(blocks, steps), in_specs=[wide, wide, w...  41.2 us
    pallas_call x1, Pallas kernels, mix_blocks(): pl.pallas_call(mix_kernel, grid=(blocks, steps), in_specs=[wide, wide, wi...  29.7 us
    pallas_call x1, Pallas kernels, gate_blocks(): pl.pallas_call(gate_kernel, grid=(steps, blocks), in_specs=[wide, wide, w...  21 us
    reduce_sum x2, other arithmetic, conv_silu(): summed = summed + conv_taps[offset] * padded[..., offset:offset + length, :]  20.3 us
    pallas_call x1, Pallas kernels, block_outer(): pl.pallas_call(state_kernel, grid=(blocks, steps), in_specs=[pl.BlockSpec...  14.5 us
  transfers between devices with their start and end apart: 50, of which 15 were waited for; matrix products, arithmetic and copies ran while one was open for 32% of the time, Pallas kernels for 2%

profile of v2, /device:TPU:0, one launch (start us, length us, event | category | flops | bytes accessed | tf_op | source)
XLA Modules:
  0.0 663.5 jit_solution(10349046366869553222)
XLA Ops:
  14.6 13.3 %collective-permute-done.2 = bf16[192,768]{1,0:T(8,128)(2,1)S(1)} collective-permute-done((bf16[192,768]{1,0:T(8,128)(2,1)S(1)}, bf16[192,768]{1,0:T(8,128)(2,1)S(1)}, u32[]{:S(2)}, u32[]{:S(2)}) %collective-permute-start.2) | collective-permute-done | bytes 294944 | tf_op jit(solution)/shard_map/ppermute | solution.py:26
  35.8 35.2 %collective-permute-done.3 = bf16[1,1024,384]{2,1,0:T(8,128)(2,1)S(1)} collective-permute-done((bf16[1,1024,384]{2,1,0:T(8,128)(2,1)S(1)}, bf16[1,1024,384]{2,1,0:T(8,128)(2,1)S(1)}, u32[]{:S(2)}, u32[]{:S(2)}) %collective-permute-start.3) | collective-permute-done | bytes 786464 | tf_op jit(solution)/shard_map/ppermute | solution.py:26
  71.9 14.5 %collective-permute-done.9 = bf16[192,768]{1,0:T(8,128)(2,1)S(1)} collective-permute-done((bf16[192,768]{1,0:T(8,128)(2,1)S(1)}, bf16[192,768]{1,0:T(8,128)(2,1)S(1)}, u32[]{:S(2)}, u32[]{:S(2)}) %collective-permute-start.9) | collective-permute-done | bytes 294944 | tf_op jit(solution)/shard_map/ppermute | solution.py:26
  99.1 28.8 %collective-permute-done.4 = bf16[1,1024,384]{2,1,0:T(8,128)(2,1)S(1)} collective-permute-done((bf16[1,1024,384]{2,1,0:T(8,128)(2,1)S(1)}, bf16[1,1024,384]{2,1,0:T(8,128)(2,1)S(1)}, u32[]{:S(2)}, u32[]{:S(2)}) %collective-permute-start.4) | collective-permute-done | bytes 786464 | tf_op jit(solution)/shard_map/ppermute | solution.py:26
  144.3 24.6 %collective-permute-done.11 = bf16[1,1024,384]{2,1,0:T(8,128)(2,1)} collective-permute-done((bf16[1,1024,384]{2,1,0:T(8,128)(2,1)}, bf16[1,1024,384]{2,1,0:T(8,128)(2,1)}, u32[]{:S(2)}, u32[]{:S(2)}) %collective-permute-start.11) | collective-permute-done | bytes 786464 | tf_op jit(solution)/shard_map/ppermute | solution.py:26
  180.4 7.8 %fusion.6 = bf16[1,1024,1536]{2,1,0:T(8,128)(2,1)S(1)} fusion(bf16[1536,1536]{1,0:T(8,128)(2,1)} %all-gather.5.cloned.1.call-done, bf16[1,1024,1536]{2,1,0:T(8,128)(2,1)S(1)} %copy-done.3, f32[1536]{0:T(1024)S(1)} %get-tuple-element.236, f32[1024]{0:T(1024)S(1)} %add_rsqrt_fusion), kind=kOutput, calls=%fused_computation.29 | convolution fusion | flops 4839702528 | bytes 11020288 | tf_op jit(solution)/shard_map/dot_general | solution.py:62
  196.9 6.3 fusion.33
  203.2 14.5 %block_outer.1 = f32[4,128,1536]{2,1,0:T(8,128)} custom-call(bf16[128,1024]{1,0:T(8,128)(2,1)} %copy.83.a_ref, bf16[1024,1536]{1,0:T(8,128)(2,1)} %get-tuple-element.172.b_ref.x_ref, f32[4,1024,6]{2,1,0:T(8,128)} %bitcast.265), custom_call_target="tpu_custom_call" | custom-call | flops 402653184 | bytes 6291456 | tf_op jit(solution)/shard_map/block_outer/pallas_call | solution.py:86
  229.3 6.7 %convolution_convert_fusion.4.gate_ref = bf16[1024,1536]{1,0:T(8,128)(2,1)} fusion(bf16[1536,1536]{1,0:T(8,128)(2,1)S(1)} %bitcast.287, bf16[1,1024,1536]{2,1,0:T(8,128)(2,1)S(1)} %copy-done.4, f32[1536]{0:T(1024)S(1)} %copy-done.69, f32[1024]{0:T(1024)S(1)} %add_rsqrt_fusion), kind=kOutput, calls=%fused_computation.27 | convolution fusion | flops 4839702528 | bytes 11020288 | tf_op jit(solution)/shard_map/dot_general | solution.py:62
  236.0 9.4 %convolution_convert_fusion.3.gno_ref = bf16[1024,1536]{1,0:T(8,128)(2,1)} fusion(bf16[1536,1536]{1,0:T(8,128)(2,1)} %all-gather.9.cloned.1.call-done, bf16[1,1024,384]{2,1,0:T(8,128)(2,1)} %get-tuple-element.187, bf16[1,1024,384]{2,1,0:T(8,128)(2,1)} %get-tuple-element.186, bf16[1,1024,384]{2,1,0:T(8,128)(2,1)} %get-tuple-element.185, ...), kind=kOutput, calls=%fused_computation.26 | convolution fusion | flops 4850712576 | bytes 11014144 | tf_op jit(solution)/shard_map/dot_general | solution.py:62
  245.5 29.7 %mix_blocks.1 = (f32[1024,1536]{1,0:T(8,128)}, f32[4,8,256]{2,1,0:T(8,128)}) custom-call(bf16[1024,1536]{1,0:T(8,128)(2,1)} %get-tuple-element.172.b_ref.x_ref, bf16[1024,1536]{1,0:T(8,128)(2,1)} %convolution_convert_fusion.4.gate_ref, bf16[1024,1536]{1,0:T(8,128)(2,1)} %convolution_convert_fusion.3.gno_ref, bf16[1024,128]{1,0:T(8,128)(2,1)} %get-tuple-element.213.w_ref, ...), custom_call_target="tpu_custom_call" | custom-call | flops 4831838208 | bytes 15728640 | tf_op jit(solution)/shard_map/mix_blocks/pallas_call | solution.py:160
  280.8 21.0 %gate_blocks.1 = (bf16[1024,1536]{1,0:T(8,128)(2,1)}, bf16[1024,1536]{1,0:T(8,128)(2,1)}, bf16[1024,1536]{1,0:T(8,128)(2,1)}, f32[1,1536]{1,0:T(1,128)}, f32[1,1536]{1,0:T(1,128)}, /*index=5*/f32[4,128,1536]{2,1,0:T(8,128)}) custom-call(f32[1024,1536]{1,0:T(8,128)} %get-tuple-element.70.mixed_ref, bf16[1024,1536]{1,0:T(8,128)(2,1)} %convolution_convert_fusion.4.gate_ref, ...), custom_call_target="tpu_custom_call" | custom-call | flops 402653184 | bytes 28311552 | tf_op jit(solution)/shard_map/gate_blocks/pallas_call | solution.py:225
  306.4 9.0 %convolution_convert_fusion.1 = bf16[1536,1536]{1,0:T(8,128)(2,1)} fusion(bf16[1024,1536]{1,0:T(8,128)(2,1)} %get-tuple-element.73, bf16[1,1024,1536]{2,1,0:T(8,128)(2,1)S(1)} %copy-done.5, f32[1536]{0:T(1024)S(1)} %copy-done.70, f32[1024]{0:T(1024)S(1)} %add_rsqrt_fusion), kind=kOutput, calls=%fused_computation.4 | convolution fusion | flops 4840488960 | bytes 11020288 | tf_op jit(solution)/shard_map/dot_general | solution.py:62
  315.3 10.2 %convolution_convert_fusion.2 = bf16[1536,1536]{1,0:T(8,128)(2,1)} fusion(bf16[1024,1536]{1,0:T(8,128)(2,1)} %get-tuple-element.72, bf16[1,1024,384]{2,1,0:T(8,128)(2,1)} %get-tuple-element.187, bf16[1,1024,384]{2,1,0:T(8,128)(2,1)} %get-tuple-element.186, bf16[1,1024,384]{2,1,0:T(8,128)(2,1)} %get-tuple-element.185, ...), kind=kOutput, calls=%fused_computation.5 | convolution fusion | flops 4851499008 | bytes 11014144 | tf_op jit(solution)/shard_map/dot_general | solution.py:62
  334.4 41.2 %back_blocks.1 = (f32[1024,1536]{1,0:T(8,128)}, f32[1024,128]{1,0:T(8,128)}, f32[1024,128]{1,0:T(8,128)}, f32[4,1024,6]{2,1,0:T(8,128)}, f32[4,1024,6]{2,1,0:T(8,128)}, /*index=5*/f32[4,1024,6]{2,1,0:T(8,128)}) custom-call(bf16[1024,1536]{1,0:T(8,128)(2,1)} %get-tuple-element.172.b_ref.x_ref, f32[1024,1536]{1,0:T(8,128)} %get-tuple-element.70.mixed_ref, ...), custom_call_target="tpu_custom_call" | custom-call | flops 9663676416 | bytes 22020096 | tf_op jit(solution)/shard_map/back_blocks/pallas_call | solution.py:344
  392.0 4.9 convolution_convert_fusion.6
  403.1 5.0 convolution_convert_fusion.8
  414.3 17.5 %multiply_reduce_fusion.3 = (f32[1536]{0:T(1024)S(1)}, f32[1536]{0:T(1024)S(1)}, f32[1536]{0:T(1024)S(1)}, f32[1536]{0:T(1024)S(1)}, f32[1536]{0:T(1024)}, /*index=5*/f32[1,1024,1536]{2,1,0:T(8,128)}) fusion(f32[1,1027,1536]{2,1,0:T(8,128)} %copy-done, f32[1,1024,1536]{2,1,0:T(8,128)} %get-tuple-element.173, f32[1024,1536]{1,0:T(8,128)} %get-tuple-element.77), kind=kLoop, calls=%fused_computation.20 | loop fusion | flops 28303872 | bytes 44070912 | tf_op jit(solution)/shard_map/transpose(jvp())/reduce_sum | solution.py:57
  432.5 5.4 broadcast_multiply_fusion
  439.2 4.8 pad_add_fusion
  462.7 4.7 fusion.133
  469.4 7.5 %convolution_convert_fusion = bf16[1536,1536]{1,0:T(8,128)(2,1)} fusion(bf16[1024,384]{1,0:T(8,128)(2,1)S(1)} %bitcast.275, bf16[1024,384]{1,0:T(8,128)(2,1)S(1)} %bitcast.274, bf16[1024,384]{1,0:T(8,128)(2,1)S(1)} %bitcast.273, bf16[1024,384]{1,0:T(8,128)(2,1)S(1)} %bitcast.272, bf16[1,1024,1536]{2,1,0:T(8,128)(2,1)S(1)} %copy-done.18, ...), kind=kOutput, calls=%fused_computation.3 | convolution fusion | flops 4851499008 | bytes 11020288 | tf_op jit(solution)/shard_map/dot_general | solution.py:62
  494.5 5.1 fusion.57
  502.9 4.6 add_convert_fusion.1
  510.8 5.5 collective-permute-start.31
  516.3 4.5 add_bitcast_fusion.1
  526.5 36.4 %collective-permute-done.29 = f32[1024]{0:T(1024)S(1)} collective-permute-done((f32[1024]{0:T(1024)S(1)}, f32[1024]{0:T(1024)S(1)}, u32[]{:S(2)}, u32[]{:S(2)}) %collective-permute-start.29) | collective-permute-done | bytes 4128 | tf_op jit(solution)/shard_map/ppermute | solution.py:26
  568.5 12.1 %collective-permute-done.40 = f32[4644]{0:T(1024)S(1)} collective-permute-done((f32[4644]{0:T(1024)S(1)}, f32[4644]{0:T(1024)S(1)}, u32[]{:S(2)}, u32[]{:S(2)}) %collective-permute-start.40) | collective-permute-done | bytes 18608 | tf_op jit(solution)/shard_map/ppermute | solution.py:26
  592.7 7.7 %fusion.11 = (f32[2,1024,384]{2,1,0:T(8,128)}, bf16[2,1024,384]{2,1,0:T(8,128)(2,1)}) fusion(bf16[2,1024,384]{2,1,0:T(8,128)(2,1)S(1)} %copy-done.10, f32[1,1024,384]{2,1,0:T(8,128)} %bitcast_convert_fusion, f32[1,1024,384]{2,1,0:T(8,128)} %add_bitcast_fusion, bf16[2,1024,384]{2,1,0:T(8,128)(2,1)S(1)} %copy-done.12, f32[2,1024]{1,0:T(2,128)S(1)} %fusion.95, ...), kind=kLoop, calls=%fused_computation.35 | loop fusion | flops 13369344 | bytes 14181889 | tf_op jit(solution)/shard_map/add | solution.py:694
  610.9 24.4 %collective-permute-done.38 = f32[192,256]{1,0:T(8,128)S(1)} collective-permute-done((f32[192,256]{1,0:T(8,128)S(1)}, f32[192,256]{1,0:T(8,128)S(1)}, u32[]{:S(2)}, u32[]{:S(2)}) %collective-permute-start.38) | collective-permute-done | bytes 196640 | tf_op jit(solution)/shard_map/ppermute | solution.py:26
  638.1 9.9 %collective-permute-done.35 = bf16[192,768]{1,0:T(8,128)(2,1)S(1)} collective-permute-done((bf16[192,768]{1,0:T(8,128)(2,1)S(1)}, bf16[192,768]{1,0:T(8,128)(2,1)S(1)}, u32[]{:S(2)}, u32[]{:S(2)}) %collective-permute-start.35) | collective-permute-done | bytes 294944 | tf_op jit(solution)/shard_map/ppermute | solution.py:26
  648.0 6.2 collective-permute-done.36
  (482 shorter events, 208.6 us)
Async XLA Ops:
  7.2 64.7 %all-gather.5.cloned.1.call-start = ((), (), s32[]{:S(2)}) async-start(), calls=%async_computation.4 | async-start | bytes 5308416 | tf_op jit(solution)/shard_map/all_gather | solution.py:480
  10.5 17.5 %collective-permute-start.2 = (bf16[192,768]{1,0:T(8,128)(2,1)S(1)}, bf16[192,768]{1,0:T(8,128)(2,1)S(1)}, u32[]{:S(2)}, u32[]{:S(2)}) collective-permute-start(bf16[192,768]{1,0:T(8,128)(2,1)S(1)} %bitcast.283), channel_id=1, source_target_pairs={{0,2},{1,3},{2,0},{3,1},{4,6},{5,7},{6,4},{7,5},{8,10},{9,11},{10,... | collective-permute-start | bytes 884744 | tf_op jit(solution)/shard_map/ppermute | solution.py:26
  28.8 105.0 %all-gather.11.cloned.1.call-start = ((), (), s32[]{:S(2)}) async-start(), calls=%async_computation.7 | async-start | bytes 1327104 | tf_op jit(solution)/shard_map/all_gather | solution.py:480
  34.6 142.9 %all-gather.7.cloned.1.call-start = ((), (), s32[]{:S(2)}) async-start(), calls=%async_computation.5 | async-start | bytes 5308416 | tf_op jit(solution)/shard_map/all_gather | solution.py:480
  35.7 35.3 %collective-permute-start.3 = (bf16[1,1024,384]{2,1,0:T(8,128)(2,1)S(1)}, bf16[1,1024,384]{2,1,0:T(8,128)(2,1)S(1)}, u32[]{:S(2)}, u32[]{:S(2)}) collective-permute-start(bf16[1,1024,384]{2,1,0:T(8,128)(2,1)S(1)} %get-tuple-element.62), channel_id=1, source_target_pairs={{0,2},{1,3},{2,0},{3,1},{4,6},{5,7},{6,4},{7,5},{8,10},{9,11},{10,... | collective-permute-start | bytes 2359304 | tf_op jit(solution)/shard_map/ppermute | solution.py:26
  71.9 14.5 %collective-permute-start.9 = (bf16[192,768]{1,0:T(8,128)(2,1)S(1)}, bf16[192,768]{1,0:T(8,128)(2,1)S(1)}, u32[]{:S(2)}, u32[]{:S(2)}) collective-permute-start(bf16[192,768]{1,0:T(8,128)(2,1)S(1)} %bitcast.281), channel_id=1, source_target_pairs={{0,2},{1,3},{2,0},{3,1},{4,6},{5,7},{6,4},{7,5},{8,10},{9,11},{10,... | collective-permute-start | bytes 884744 | tf_op jit(solution)/shard_map/ppermute | solution.py:26
  87.2 148.8 %all-gather.9.cloned.1.call-start = ((), (), s32[]{:S(2)}) async-start(), calls=%async_computation.6 | async-start | bytes 5308416 | tf_op jit(solution)/shard_map/all_gather | solution.py:480
  91.9 38.6 %collective-permute-start.1 = (bf16[1,1024,384]{2,1,0:T(8,128)(2,1)}, bf16[1,1024,384]{2,1,0:T(8,128)(2,1)}, u32[]{:S(2)}, u32[]{:S(2)}) collective-permute-start(bf16[1,1024,384]{2,1,0:T(8,128)(2,1)} %get-tuple-element.199), channel_id=1, source_target_pairs={{0,1},{1,0},{2,3},{3,2},{4,5},{5,4},{6,7},{7,6},{8,9},{9,8},{10,11... | collective-permute-start | bytes 2359304 | tf_op jit(solution)/shard_map/ppermute | solution.py:26
  97.0 30.9 %collective-permute-start.4 = (bf16[1,1024,384]{2,1,0:T(8,128)(2,1)S(1)}, bf16[1,1024,384]{2,1,0:T(8,128)(2,1)S(1)}, u32[]{:S(2)}, u32[]{:S(2)}) collective-permute-start(bf16[1,1024,384]{2,1,0:T(8,128)(2,1)S(1)} %copy-done.39), channel_id=1, source_target_pairs={{0,1},{1,0},{2,3},{3,2},{4,5},{5,4},{6,7},{7,6},{8,9},{9,8},{10,11... | collective-permute-start | bytes 2359304 | tf_op jit(solution)/shard_map/ppermute | solution.py:26
  127.9 93.6 %collective-permute-start.10 = (bf16[1,1024,384]{2,1,0:T(8,128)(2,1)}, bf16[1,1024,384]{2,1,0:T(8,128)(2,1)}, u32[]{:S(2)}, u32[]{:S(2)}) collective-permute-start(bf16[1,1024,384]{2,1,0:T(8,128)(2,1)} %get-tuple-element.66), channel_id=1, source_target_pairs={{0,1},{1,0},{2,3},{3,2},{4,5},{5,4},{6,7},{7,6},{8,9},{9,8},{10,11... | collective-permute-start | bytes 2359304 | tf_op jit(solution)/shard_map/ppermute | solution.py:26
  129.3 39.6 %collective-permute-start.11 = (bf16[1,1024,384]{2,1,0:T(8,128)(2,1)}, bf16[1,1024,384]{2,1,0:T(8,128)(2,1)}, u32[]{:S(2)}, u32[]{:S(2)}) collective-permute-start(bf16[1,1024,384]{2,1,0:T(8,128)(2,1)} %get-tuple-element.67), channel_id=1, source_target_pairs={{0,2},{1,3},{2,0},{3,1},{4,6},{5,7},{6,4},{7,5},{8,10},{9,11},{10,... | collective-permute-start | bytes 2359304 | tf_op jit(solution)/shard_map/ppermute | solution.py:26
  178.4 412.6 %reduce-scatter.9.cloned.1.call-start = ((), (), s32[]{:S(2)}) async-start(), calls=%async_computation.10 | async-start | bytes 1327104 | tf_op jit(solution)/shard_map/reduce_scatter | solution.py:668
  194.0 27.5 %collective-permute-start.12 = (bf16[1,1024,384]{2,1,0:T(8,128)(2,1)}, bf16[1,1024,384]{2,1,0:T(8,128)(2,1)S(1)}, u32[]{:S(2)}, u32[]{:S(2)}) collective-permute-start(bf16[1,1024,384]{2,1,0:T(8,128)(2,1)} %collective-permute-done.11), channel_id=1, source_target_pairs={{0,1},{1,0},{2,3},{3,2},{4,5},{5,4},{6,7},{7,6},{8,9},{9,8},{10,11... | collective-permute-start | bytes 2359304 | tf_op jit(solution)/shard_map/ppermute | solution.py:26
  304.8 20.7 %collective-permute-start.22 = (bf16[1,128,1536]{2,1,0:T(8,128)(2,1)}, bf16[1,128,1536]{2,1,0:T(8,128)(2,1)S(1)}, u32[]{:S(2)}, u32[]{:S(2)}) collective-permute-start(bf16[1,128,1536]{2,1,0:T(8,128)(2,1)} %fusion.61), channel_id=1, source_target_pairs={{4,0},{5,1},{6,2},{7,3},{12,8},{13,9},{14,10},{15,11},{20,16},{21,... | collective-permute-start | bytes 1179656 | tf_op jit(solution)/shard_map/ppermute | solution.py:32
  396.9 207.1 %reduce-scatter.11.cloned.1.call-start = ((), (), s32[]{:S(2)}) async-start(), calls=%async_computation.11 | async-start | bytes 5308416 | tf_op jit(solution)/shard_map/reduce_scatter | solution.py:668
  397.5 211.5 %reduce-scatter.5.cloned.1.call-start = ((), (), s32[]{:S(2)}) async-start(), calls=%async_computation.8 | async-start | bytes 5308416 | tf_op jit(solution)/shard_map/reduce_scatter | solution.py:668
  408.1 108.1 %collective-permute-start.18 = (bf16[1024,384]{1,0:T(8,128)(2,1)}, bf16[1024,384]{1,0:T(8,128)(2,1)}, u32[]{:S(2)}, u32[]{:S(2)}) collective-permute-start(bf16[1024,384]{1,0:T(8,128)(2,1)} %convolution_convert_fusion.8), channel_id=1, source_target_pairs={{0,1},{1,0},{2,3},{3,2},{4,5},{5,4},{6,7},{7,6},{8,9},{9,8},{10,11... | collective-permute-start | bytes 2359304 | tf_op jit(solution)/shard_map/ppermute | solution.py:26
  414.2 88.8 %collective-permute-start.19 = (bf16[1024,384]{1,0:T(8,128)(2,1)}, bf16[1024,384]{1,0:T(8,128)(2,1)}, u32[]{:S(2)}, u32[]{:S(2)}) collective-permute-start(bf16[1024,384]{1,0:T(8,128)(2,1)} %convolution_convert_fusion.7), channel_id=1, source_target_pairs={{0,1},{1,0},{2,3},{3,2},{4,5},{5,4},{6,7},{7,6},{8,9},{9,8},{10,11... | collective-permute-start | bytes 2359304 | tf_op jit(solution)/shard_map/ppermute | solution.py:26
  414.2 221.8 %reduce-scatter.7.cloned.1.call-start = ((), (), s32[]{:S(2)}) async-start(), calls=%async_computation.9 | async-start | bytes 5308416 | tf_op jit(solution)/shard_map/reduce_scatter | solution.py:668
  437.9 18.3 %collective-permute-start.23 = (f32[1,3,1536]{2,1,0:T(4,128)S(1)}, f32[1,3,1536]{2,1,0:T(4,128)}, u32[]{:S(2)}, u32[]{:S(2)}) collective-permute-start(f32[1,3,1536]{2,1,0:T(4,128)S(1)} %pad_add_fusion.2), channel_id=1, source_target_pairs={{4,0},{5,1},{6,2},{7,3},{12,8},{13,9},{14,10},{15,11},{20,16},{21,... | collective-permute-start | bytes 55304 | tf_op jit(solution)/shard_map/ppermute | solution.py:32
  467.4 26.0 %collective-permute-start.26 = (bf16[1024,384]{1,0:T(8,128)(2,1)}, bf16[1024,384]{1,0:T(8,128)(2,1)}, u32[]{:S(2)}, u32[]{:S(2)}) collective-permute-start(bf16[1024,384]{1,0:T(8,128)(2,1)} %get-tuple-element.246), channel_id=1, source_target_pairs={{0,1},{1,0},{2,3},{3,2},{4,5},{5,4},{6,7},{7,6},{8,9},{9,8},{10,11... | collective-permute-start | bytes 2359304 | tf_op jit(solution)/shard_map/ppermute | solution.py:26
  507.6 76.7 %collective-permute-start.20 = (bf16[1024,384]{1,0:T(8,128)(2,1)S(1)}, bf16[1024,384]{1,0:T(8,128)(2,1)S(1)}, u32[]{:S(2)}, u32[]{:S(2)}) collective-permute-start(bf16[1024,384]{1,0:T(8,128)(2,1)S(1)} %add_convert_fusion.1), channel_id=1, source_target_pairs={{0,2},{1,3},{2,0},{3,1},{4,6},{5,7},{6,4},{7,5},{8,10},{9,11},{10,... | collective-permute-start | bytes 2359304 | tf_op jit(solution)/shard_map/ppermute | solution.py:26
  510.7 52.3 %collective-permute-start.29 = (f32[1024]{0:T(1024)S(1)}, f32[1024]{0:T(1024)S(1)}, u32[]{:S(2)}, u32[]{:S(2)}) collective-permute-start(f32[1024]{0:T(1024)S(1)} %add.500), channel_id=1, source_target_pairs={{0,2},{1,3},{2,0},{3,1},{4,6},{5,7},{6,4},{7,5},{8,10},{9,11},{10,... | collective-permute-start | bytes 12296 | tf_op jit(solution)/shard_map/ppermute | solution.py:26
  520.8 64.8 %collective-permute-start.27 = (bf16[1024,384]{1,0:T(8,128)(2,1)}, bf16[1024,384]{1,0:T(8,128)(2,1)}, u32[]{:S(2)}, u32[]{:S(2)}) collective-permute-start(bf16[1024,384]{1,0:T(8,128)(2,1)} %get-tuple-element.194), channel_id=1, source_target_pairs={{0,2},{1,3},{2,0},{3,1},{4,6},{5,7},{6,4},{7,5},{8,10},{9,11},{10,... | collective-permute-start | bytes 2359304 | tf_op jit(solution)/shard_map/ppermute | solution.py:26
  523.5 64.7 %collective-permute-start.25 = (bf16[1024,384]{1,0:T(8,128)(2,1)}, bf16[1024,384]{1,0:T(8,128)(2,1)}, u32[]{:S(2)}, u32[]{:S(2)}) collective-permute-start(bf16[1024,384]{1,0:T(8,128)(2,1)} %get-tuple-element.195), channel_id=1, source_target_pairs={{0,1},{1,0},{2,3},{3,2},{4,5},{5,4},{6,7},{7,6},{8,9},{9,8},{10,11... | collective-permute-start | bytes 2359304 | tf_op jit(solution)/shard_map/ppermute | solution.py:26
  524.9 38.1 %collective-permute-start.32 = (f32[12104]{0:T(1024)S(1)}, f32[12104]{0:T(1024)S(1)}, u32[]{:S(2)}, u32[]{:S(2)}) collective-permute-start(f32[12104]{0:T(1024)S(1)} %add.503), channel_id=1, source_target_pairs={{0,16},{8,24},{16,0},{24,8},{1,17},{9,25},{17,1},{25,9},{2,18},{10... | collective-permute-start | bytes 145256 | tf_op jit(solution)/shard_map/ppermute | solution.py:387
  563.5 17.0 %collective-permute-start.40 = (f32[4644]{0:T(1024)S(1)}, f32[4644]{0:T(1024)S(1)}, u32[]{:S(2)}, u32[]{:S(2)}) collective-permute-start(f32[4644]{0:T(1024)S(1)} %concatenate.213), channel_id=1, source_target_pairs={{0,2},{1,3},{2,0},{3,1},{4,6},{5,7},{6,4},{7,5},{8,10},{9,11},{10,... | collective-permute-start | bytes 55736 | tf_op jit(solution)/shard_map/ppermute | solution.py:26
  567.6 14.8 %collective-permute-start.34 = (f32[2816]{0:T(1024)S(1)}, f32[2816]{0:T(1024)S(1)}, u32[]{:S(2)}, u32[]{:S(2)}) collective-permute-start(f32[2816]{0:T(1024)S(1)} %slice_add_fusion.7), channel_id=1, source_target_pairs={{0,2},{1,3},{2,0},{3,1},{4,6},{5,7},{6,4},{7,5},{8,10},{9,11},{10,... | collective-permute-start | bytes 33800 | tf_op jit(solution)/shard_map/ppermute | solution.py:26
  605.0 32.1 %collective-permute-start.41 = (bf16[192,768]{1,0:T(8,128)(2,1)S(1)}, bf16[192,768]{1,0:T(8,128)(2,1)S(1)}, u32[]{:S(2)}, u32[]{:S(2)}) collective-permute-start(bf16[192,768]{1,0:T(8,128)(2,1)S(1)} %slice.501), channel_id=1, source_target_pairs={{0,2},{1,3},{2,0},{3,1},{4,6},{5,7},{6,4},{7,5},{8,10},{9,11},{10,... | collective-permute-start | bytes 884744 | tf_op jit(solution)/shard_map/ppermute | solution.py:26
  606.1 29.2 %collective-permute-start.38 = (f32[192,256]{1,0:T(8,128)S(1)}, f32[192,256]{1,0:T(8,128)S(1)}, u32[]{:S(2)}, u32[]{:S(2)}) collective-permute-start(f32[192,256]{1,0:T(8,128)S(1)} %fusion.94), channel_id=1, source_target_pairs={{0,2},{1,3},{2,0},{3,1},{4,6},{5,7},{6,4},{7,5},{8,10},{9,11},{10,... | collective-permute-start | bytes 589832 | tf_op jit(solution)/shard_map/ppermute | solution.py:26
  610.1 37.9 %collective-permute-start.35 = (bf16[192,768]{1,0:T(8,128)(2,1)S(1)}, bf16[192,768]{1,0:T(8,128)(2,1)S(1)}, u32[]{:S(2)}, u32[]{:S(2)}) collective-permute-start(bf16[192,768]{1,0:T(8,128)(2,1)S(1)} %slice.473), channel_id=1, source_target_pairs={{0,2},{1,3},{2,0},{3,1},{4,6},{5,7},{6,4},{7,5},{8,10},{9,11},{10,... | collective-permute-start | bytes 884744 | tf_op jit(solution)/shard_map/ppermute | solution.py:26
  637.1 17.1 %collective-permute-start.36 = (bf16[192,768]{1,0:T(8,128)(2,1)S(1)}, bf16[192,768]{1,0:T(8,128)(2,1)S(1)}, u32[]{:S(2)}, u32[]{:S(2)}) collective-permute-start(bf16[192,768]{1,0:T(8,128)(2,1)S(1)} %slice.475), channel_id=1, source_target_pairs={{0,2},{1,3},{2,0},{3,1},{4,6},{5,7},{6,4},{7,5},{8,10},{9,11},{10,... | collective-permute-start | bytes 884744 | tf_op jit(solution)/shard_map/ppermute | solution.py:26
  (119 other events, 1891.1 us)
Sparse Core Ops, SparseCore 0:
  29.0 39.9 all-gather.4
  71.4 23.9 all-gather.10
  97.8 38.8 all-gather.6
  178.5 42.5 all-gather.8
  397.0 41.7 reduce-scatter.8
  442.2 53.7 reduce-scatter.10
  499.4 54.2 reduce-scatter.4
  557.2 53.7 reduce-scatter.6

commit v3 on v2

v3 whole, which is shorter than its diff:
```python
import functools

import jax
import jax.numpy as jnp
from jax import lax
from jax.experimental import pallas as pl
from jax.experimental.pallas import tpu as pltpu
from jax.sharding import PartitionSpec as P

HEADDIM = 64
STATE = 128
CONV = 4
GROUP = 256
INNER = 3072
EPSILON = 1e-05
PAIR = 2 * HEADDIM
HEADS_STEP = 6
LANES_STEP = HEADS_STEP * HEADDIM
F32 = jnp.float32
BF16 = jnp.bfloat16
HIGHEST = lax.Precision.HIGHEST


def swap(x, bit):
    count = lax.axis_size("tp")
    return lax.ppermute(x, "tp", [(i, i ^ bit) for i in range(count)])


def passed_along(x, axis, by):
    count = lax.axis_size(axis)
    pairs = [(i, i + by) for i in range(count) if 0 <= i + by < count]
    return lax.ppermute(x, axis, pairs)


def carried_in(decay, final, combine, reverse):
    count, position = (lax.axis_size("ctx"), lax.axis_index("ctx"))
    if count == 2:
        return passed_along(final.astype(BF16), "ctx", -1 if reverse else 1).astype(F32)
    decays = lax.all_gather(decay.astype(BF16), "ctx").astype(F32)
    finals = lax.all_gather(final.astype(BF16), "ctx")
    start = jnp.zeros_like(final)

    def lap(k, before):
        at = count - 1 - k if reverse else k
        reached = at > position if reverse else at < position
        new = decays[at] * before + finals[at].astype(F32)
        return jnp.where(reached, new, before)

    return lax.fori_loop(0, count, lap, start)


def dot(a, b, da, db):
    return lax.dot_general(a, b, (((da,), (db,)), ((), ())), preferred_element_type=F32)


def low_lanes(rows):
    return lax.broadcasted_iota(jnp.int32, (rows, PAIR), 1) < HEADDIM


def spread_heads(cols, first, low_half):
    return jnp.where(low_half, cols[:, first : first + 1], cols[:, first + 1 : first + 2])


def lower_mask():
    return lax.broadcasted_iota(jnp.int32, (GROUP, GROUP), 0) >= lax.broadcasted_iota(
        jnp.int32, (GROUP, GROUP), 1
    )


def split_dot(ones, values, terms, contract):
    total, rest = None, values
    for _ in range(terms):
        part = rest.astype(BF16)
        rest = rest - part.astype(F32)
        piece = dot(ones, part, contract, 0)
        total = piece if total is None else total + piece
    return total


def turned(cols, heads_before):
    return pltpu.roll(cols, lax.rem(128 - heads_before, 128), 1)


def start_kernel(
    groups, heads,
    inner_ref, rim_ref, narrow_ref, nrim_ref, taps_ref, bias_ref, ntaps_ref, nbias_ref, sbias_ref, rate_ref,
    x_ref, slope_ref, wr_ref, nslope_ref, cols_ref, rows_ref, local_ref, decay_ref,
    ext_ref, next_ref, scaled_ref,
):
    first = lax.rem(pl.program_id(0), groups) == 0

    @pl.when(first)
    def _():
        ext_ref[5:8, :] = rim_ref[0].astype(F32)
        next_ref[5:8, :] = nrim_ref[0].astype(F32)

    @pl.when(jnp.logical_not(first))
    def _():
        ext_ref[0:8, :] = ext_ref[GROUP : GROUP + 8, :]
        next_ref[0:8, :] = next_ref[GROUP : GROUP + 8, :]

    def conv(source, taps, bias, lanes):
        total = bias[:, lanes]
        for k in range(CONV):
            total = total + taps[k : k + 1, lanes] * source[5 + k : 5 + k + GROUP, lanes]
        sig = jax.nn.sigmoid(total)
        return total * sig, sig * (1.0 + total * (1.0 - sig))

    for part in range(2 * STATE // 128):
        lanes = slice(128 * part, 128 * (part + 1))
        next_ref[8 : GROUP + 8, lanes] = narrow_ref[:, lanes].astype(BF16).astype(F32)
        act, slope = conv(next_ref, ntaps_ref, nbias_ref, lanes)
        wr_ref[:, lanes] = act.astype(BF16)
        nslope_ref[:, lanes] = slope

    raw = narrow_ref[:, 2 * STATE :] + sbias_ref[...]
    lane = lax.broadcasted_iota(jnp.int32, (GROUP, 128), 1)
    step = jnp.maximum(raw, 0.0) + jnp.log1p(jnp.exp(-jnp.abs(raw)))
    step = jnp.where(lane < heads, step, 0.0)
    sig = jnp.where(lane < heads, jax.nn.sigmoid(raw), 0.0)
    cum = split_dot(lower_mask().astype(BF16), step * rate_ref[...], 3, 1)
    cols = step + pltpu.roll(cum, heads, 1) + pltpu.roll(sig, 2 * heads, 1)
    cols_ref[...] = cols
    rows_ref[0] = cum.T[:heads]
    last = cum[GROUP - 1 : GROUP, :]
    scale = jnp.exp(last - cum) * step
    decay = jnp.exp(last)
    low_half, low_row = low_lanes(GROUP), low_lanes(1)
    for pair in range(heads // 2):
        lanes = slice(PAIR * pair, PAIR * (pair + 1))
        ext_ref[8 : GROUP + 8, lanes] = inner_ref[:, lanes].astype(F32)
        act, slope = conv(ext_ref, taps_ref, bias_ref, lanes)
        x = act.astype(BF16)
        x_ref[:, lanes] = x
        slope_ref[:, lanes] = slope.astype(BF16)
        scaled_ref[:, lanes] = (x.astype(F32) * spread_heads(scale, 2 * pair, low_half)).astype(BF16)
        decay_ref[0, :, lanes] = spread_heads(decay, 2 * pair, low_row)
    local_ref[0] = dot(wr_ref[:, :STATE], scaled_ref[...], 0, 0)


def start_blocks(inner_pre, rim, narrow, nrim, taps, bias, ntaps, nbias, sbias, rate, groups, heads):
    tokens, width = inner_pre.shape
    blocks = tokens // GROUP
    rows = lambda w: pl.BlockSpec((GROUP, w), lambda b: (b, 0))
    whole = lambda x: pl.BlockSpec(x.shape, lambda b: (0,) * x.ndim)
    return pl.pallas_call(
        functools.partial(start_kernel, groups, heads),
        grid=(blocks,),
        in_specs=[
            rows(width),
            pl.BlockSpec((1, CONV - 1, width), lambda b: (b // groups, 0, 0)),
            rows(narrow.shape[1]),
            pl.BlockSpec((1, CONV - 1, 2 * STATE), lambda b: (b // groups, 0, 0)),
            whole(taps), whole(bias), whole(ntaps), whole(nbias), whole(sbias), whole(rate),
        ],
        out_specs=[
            rows(width), rows(width), rows(2 * STATE), rows(2 * STATE), rows(128),
            pl.BlockSpec((1, heads, GROUP), lambda b: (b, 0, 0)),
            pl.BlockSpec((1, STATE, width), lambda b: (b, 0, 0)),
            pl.BlockSpec((1, 1, width), lambda b: (b, 0, 0)),
        ],
        out_shape=[
            jax.ShapeDtypeStruct((tokens, width), BF16),
            jax.ShapeDtypeStruct((tokens, width), BF16),
            jax.ShapeDtypeStruct((tokens, 2 * STATE), BF16),
            jax.ShapeDtypeStruct((tokens, 2 * STATE), F32),
            jax.ShapeDtypeStruct((tokens, 128), F32),
            jax.ShapeDtypeStruct((blocks, heads, GROUP), F32),
            jax.ShapeDtypeStruct((blocks, STATE, width), F32),
            jax.ShapeDtypeStruct((blocks, 1, width), F32),
        ],
        scratch_shapes=[
            pltpu.VMEM((GROUP + 8, width), F32),
            pltpu.VMEM((GROUP + 8, 2 * STATE), F32),
            pltpu.VMEM((GROUP, width), BF16),
        ],
        cost_estimate=pl.CostEstimate(
            flops=2 * tokens * STATE * width + 20 * tokens * width,
            bytes_accessed=tokens * width * 6 + blocks * STATE * width * 4,
            transcendentals=tokens * width,
        ),
        name="start_blocks",
    )(inner_pre, rim, narrow, nrim, taps, bias, ntaps, nbias, sbias, rate)


def mix_kernel(
    heads,
    x_ref, gate_ref, gno_ref, wr_ref, cols_ref, rows_ref, state_ref, skip_ref, gain_ref,
    mixed_ref, stats_ref, scores_ref, sums_ref,
):
    g = pl.program_id(1)

    @pl.when(g == 0)
    def _():
        scores_ref[...] = dot(wr_ref[:, STATE:], wr_ref[:, :STATE], 1, 1)
        sums_ref[...] = jnp.zeros_like(sums_ref)

    cols = turned(cols_ref[...], g * HEADS_STEP)
    grown = jnp.exp(cols)
    low_half = low_lanes(GROUP)
    lower = lower_mask()
    squares = jnp.zeros((GROUP, 1), F32)
    crosses = jnp.zeros((GROUP, 1), F32)
    for pair in range(HEADS_STEP // 2):
        lanes = slice(PAIR * pair, PAIR * (pair + 1))
        x = x_ref[:, lanes].astype(F32)
        stepped = x * spread_heads(cols, 2 * pair, low_half)
        halves = (
            jnp.where(low_half, stepped, 0.0).astype(BF16),
            jnp.where(low_half, 0.0, stepped).astype(BF16),
        )
        total = dot(wr_ref[:, STATE:], state_ref[0, :, lanes], 1, 0)
        total = total * spread_heads(grown, heads + 2 * pair, low_half)
        for side in range(2):
            head = 2 * pair + side
            row = rows_ref[0, pl.ds(g * HEADS_STEP + head, 1), :]
            spread = jnp.where(lower, cols[:, heads + head : heads + head + 1] - row, -1e30)
            weights = (scores_ref[...] * jnp.exp(spread)).astype(BF16)
            total = total + dot(weights, halves[side], 1, 0)
        mixed = total + skip_ref[:, lanes] * x
        mixed_ref[:, lanes] = mixed
        gate = gate_ref[:, lanes].astype(F32)
        gated = mixed * (gate * jax.nn.sigmoid(gate))
        squares = squares + jnp.sum(gated * gated, axis=1, keepdims=True)
        grad_hat = gno_ref[:, lanes].astype(F32) * gain_ref[:, lanes]
        crosses = crosses + jnp.sum(gated * grad_hat, axis=1, keepdims=True)
    lane = lax.broadcasted_iota(jnp.int32, (GROUP, 128), 1)
    sums_ref[...] += jnp.where(lane == 0, squares, jnp.where(lane == 1, crosses, 0.0))

    @pl.when(g == pl.num_programs(1) - 1)
    def _():
        stats_ref[0] = sums_ref[...].T[:8]


def mix_blocks(x, gate, gno, wr, cols, rows, states, skip, gain):
    tokens, width = x.shape
    blocks, steps, heads = tokens // GROUP, width // LANES_STEP, rows.shape[1]
    wide = pl.BlockSpec((GROUP, LANES_STEP), lambda b, g: (b, g))
    line = pl.BlockSpec((1, LANES_STEP), lambda b, g: (0, g))
    return pl.pallas_call(
        functools.partial(mix_kernel, heads),
        grid=(blocks, steps),
        in_specs=[
            wide, wide, wide,
            pl.BlockSpec((GROUP, 2 * STATE), lambda b, g: (b, 0)),
            pl.BlockSpec((GROUP, 128), lambda b, g: (b, 0)),
            pl.BlockSpec((1, heads, GROUP), lambda b, g: (b, 0, 0)),
            pl.BlockSpec((1, STATE, LANES_STEP), lambda b, g: (b, 0, g)),
            line, line,
        ],
        out_specs=[wide, pl.BlockSpec((1, 8, GROUP), lambda b, g: (b, 0, 0))],
        out_shape=[
            jax.ShapeDtypeStruct((tokens, width), F32),
            jax.ShapeDtypeStruct((blocks, 8, GROUP), F32),
        ],
        scratch_shapes=[pltpu.VMEM((GROUP, GROUP), F32), pltpu.VMEM((GROUP, 128), F32)],
        cost_estimate=pl.CostEstimate(
            flops=2 * tokens * width * (2 * GROUP + 2 * STATE) * 2,
            bytes_accessed=tokens * width * 10,
            transcendentals=tokens * GROUP * width // HEADDIM,
        ),
        name="mix_blocks",
    )(x, gate, gno, wr, cols, rows, states, skip, gain)


def gate_kernel(
    heads,
    mixed_ref, gate_ref, gno_ref, x_ref, stats_ref, gain_ref, wr_ref, cols_ref,
    normed_ref, ggate_ref, gdiag_ref, gain_sum_ref, skip_sum_ref, flow_ref, scaled_ref,
):
    @pl.when(pl.program_id(1) == 0)
    def _():
        gain_sum_ref[...] = jnp.zeros_like(gain_sum_ref)
        skip_sum_ref[...] = jnp.zeros_like(skip_sum_ref)

    stats = stats_ref[0].T
    scale = lax.rsqrt(stats[:, 0:1] / INNER + EPSILON)
    cross = scale * stats[:, 1:2] / INNER
    grown = jnp.exp(turned(cols_ref[...], pl.program_id(0) * HEADS_STEP))
    low_half = low_lanes(GROUP)
    for pair in range(HEADS_STEP // 2):
        lanes = slice(PAIR * pair, PAIR * (pair + 1))
        mixed = mixed_ref[:, lanes]
        gate = gate_ref[:, lanes].astype(F32)
        gno = gno_ref[:, lanes].astype(F32)
        gain = gain_ref[:, lanes]
        sig = jax.nn.sigmoid(gate)
        act = gate * sig
        hat = mixed * act * scale
        normed_ref[:, lanes] = (hat * gain).astype(BF16)
        gain_sum_ref[:, lanes] += jnp.sum(gno * hat, axis=0, keepdims=True)
        grad_gated = scale * (gno * gain - hat * cross)
        grad_mixed = grad_gated * act
        ggate_ref[:, lanes] = (grad_gated * mixed * sig * (1.0 + gate * (1.0 - sig))).astype(BF16)
        skip_sum_ref[:, lanes] += jnp.sum(grad_mixed * x_ref[:, lanes].astype(F32), axis=0, keepdims=True)
        diag = grad_mixed.astype(BF16)
        gdiag_ref[:, lanes] = diag
        scaled = diag.astype(F32) * spread_heads(grown, heads + 2 * pair, low_half)
        scaled_ref[:, lanes] = scaled.astype(BF16)
    flow_ref[0] = dot(wr_ref[...], scaled_ref[...], 0, 0)


def gate_blocks(mixed, gate, gno, x, stats, gain, wr, cols, heads):
    tokens, width = x.shape
    blocks, steps = tokens // GROUP, width // LANES_STEP
    wide = pl.BlockSpec((GROUP, LANES_STEP), lambda g, b: (b, g))
    line = pl.BlockSpec((1, LANES_STEP), lambda g, b: (0, g))
    return pl.pallas_call(
        functools.partial(gate_kernel, heads),
        grid=(steps, blocks),
        in_specs=[
            wide, wide, wide, wide,
            pl.BlockSpec((1, 8, GROUP), lambda g, b: (b, 0, 0)),
            line,
            pl.BlockSpec((GROUP, STATE), lambda g, b: (b, 1)),
            pl.BlockSpec((GROUP, 128), lambda g, b: (b, 0)),
        ],
        out_specs=[
            wide, wide, wide, line, line,
            pl.BlockSpec((1, STATE, LANES_STEP), lambda g, b: (b, 0, g)),
        ],
        out_shape=[
            jax.ShapeDtypeStruct((tokens, width), BF16),
            jax.ShapeDtypeStruct((tokens, width), BF16),
            jax.ShapeDtypeStruct((tokens, width), BF16),
            jax.ShapeDtypeStruct((1, width), F32),
            jax.ShapeDtypeStruct((1, width), F32),
            jax.ShapeDtypeStruct((blocks, STATE, width), F32),
        ],
        scratch_shapes=[pltpu.VMEM((GROUP, LANES_STEP), BF16)],
        cost_estimate=pl.CostEstimate(
            flops=2 * tokens * STATE * width,
            bytes_accessed=tokens * width * 16 + blocks * STATE * width * 4,
            transcendentals=tokens * width,
        ),
        name="gate_blocks",
    )(mixed, gate, gno, x, stats, gain, wr, cols)


def back_kernel(
    groups, heads,
    x_ref, mixed_ref, grad_ref, slope_ref, pre_ref, rim_ref, wr_ref, nslope_ref, npre_ref, nrim_ref,
    cols_ref, rows_ref, state_ref, flow_ref, skip_ref, taps_ref, ntaps_ref, rate_ref,
    gpre_ref, gnarrow_ref, sums_ref, nsums_ref, hsums_ref, halo_ref, nhalo_ref,
    scores_ref, gscores_ref, prod_ref, gw_ref, gr_ref, u_ref, v_ref, i_ref, e_ref, ext_ref, next_ref, head_ref,
):
    step_id, g = pl.program_id(0), pl.program_id(1)
    block = pl.num_programs(0) - 1 - step_id
    last_of_slot = lax.rem(block, groups) == groups - 1
    first_of_slot = lax.rem(block, groups) == 0

    @pl.when(g == 0)
    def _():
        scores_ref[...] = dot(wr_ref[:, STATE:], wr_ref[:, :STATE], 1, 1)
        for ref in (gscores_ref, gw_ref, gr_ref, u_ref, v_ref, i_ref, e_ref):
            ref[...] = jnp.zeros_like(ref)

    @pl.when(jnp.logical_and(g == 0, step_id == 0))
    def _():
        sums_ref[...] = jnp.zeros_like(sums_ref)
        nsums_ref[...] = jnp.zeros_like(nsums_ref)
        hsums_ref[...] = jnp.zeros_like(hsums_ref)

    @pl.when(last_of_slot)
    def _():
        ext_ref[g, GROUP : GROUP + 8, :] = jnp.zeros((8, LANES_STEP), F32)
        next_ref[GROUP : GROUP + 8, :] = jnp.zeros((8, 2 * STATE), F32)

    @pl.when(jnp.logical_not(last_of_slot))
    def _():
        ext_ref[g, GROUP : GROUP + 8, :] = ext_ref[g, 0:8, :]

        @pl.when(g == 0)
        def _():
            next_ref[GROUP : GROUP + 8, :] = next_ref[0:8, :]

    cols = turned(cols_ref[...], g * HEADS_STEP)
    grown = jnp.exp(cols)
    shrunk = jnp.exp(cols[GROUP - 1 : GROUP, :] - cols)
    low_half = low_lanes(GROUP)
    lower = lower_mask()
    grad_write = jnp.zeros((GROUP, STATE), F32)
    grad_read = jnp.zeros((GROUP, STATE), F32)
    for pair in range(HEADS_STEP // 2):
        lanes = slice(PAIR * pair, PAIR * (pair + 1))
        x = x_ref[:, lanes].astype(F32)
        grad = grad_ref[:, lanes]
        grad_f = grad.astype(F32)
        skip = skip_ref[:, lanes]
        steps = spread_heads(cols, 2 * pair, low_half)
        tail = spread_heads(shrunk, heads + 2 * pair, low_half)
        stepped = x * steps
        x_halves = (
            jnp.where(low_half, stepped, 0.0).astype(BF16),
            jnp.where(low_half, 0.0, stepped).astype(BF16),
        )
        g_halves = (
            jnp.where(low_half, grad_f, 0.0).astype(BF16),
            jnp.where(low_half, 0.0, grad_f).astype(BF16),
        )
        flow = flow_ref[0, :, lanes]
        state = state_ref[0, :, lanes]
        e_ref[0:1, lanes] = jnp.sum(flow.astype(F32) * state.astype(F32), axis=0, keepdims=True)
        scaled = (grad_f * spread_heads(grown, heads + 2 * pair, low_half)).astype(BF16)
        grad_read = grad_read + dot(scaled, state, 1, 1)
        grad_write = grad_write + dot((stepped * tail).astype(BF16), flow, 1, 1)
        stepped_low = stepped.astype(BF16).astype(F32)
        inter = dot(wr_ref[:, :STATE], flow, 1, 0) * tail
        total = jnp.zeros_like(inter)
        for side in range(2):
            head = 2 * pair + side
            row = rows_ref[0, pl.ds(g * HEADS_STEP + head, 1), :]
            decay = jnp.exp(jnp.where(lower, cols[:, heads + head : heads + head + 1] - row, -1e30))
            weights = (scores_ref[...] * decay).astype(BF16)
            total = total + dot(weights, g_halves[side], 0, 0)
            gscores_ref[...] += dot(grad, x_halves[side], 1, 1) * decay
        both = total + inter
        prod_ref[0, :, lanes] = x * both
        prod_ref[1, :, lanes] = grad_f * (mixed_ref[:, lanes] - skip * x) - stepped_low * total
        prod_ref[2, :, lanes] = stepped_low * inter
        grad_conv = (steps * both + skip * grad_f) * slope_ref[:, lanes].astype(F32)
        ext_ref[g, 0:GROUP, lanes] = grad_conv
        pre = pre_ref[:, lanes].astype(F32)
        total_pre = jnp.zeros_like(grad_conv)
        for j in range(CONV):
            moved = ext_ref[g, j : j + GROUP, lanes]
            total_pre = total_pre + taps_ref[CONV - 1 - j : CONV - j, lanes] * moved
            sums_ref[g, CONV - 1 - j : CONV - j, lanes] += jnp.sum(pre * moved, axis=0, keepdims=True)
        sums_ref[g, CONV : CONV + 1, lanes] += jnp.sum(grad_conv, axis=0, keepdims=True)
        gpre_ref[:, lanes] = total_pre.astype(BF16)

    @pl.when(first_of_slot)
    def _():
        head_ref[0:8, :LANES_STEP] = jnp.zeros((8, LANES_STEP), F32)
        head_ref[8:16, :LANES_STEP] = ext_ref[g, 0:8, :]
        halo = jnp.zeros((8, LANES_STEP), F32)
        for j in range(CONV):
            moved = head_ref[j : j + 8, :LANES_STEP]
            halo = halo + taps_ref[CONV - 1 - j : CONV - j, :] * moved
            sums_ref[g, CONV - 1 - j : CONV - j, :] += jnp.sum(
                rim_ref[0].astype(F32) * moved[5:8], axis=0, keepdims=True
            )
        halo_ref[0] = halo

    chosen_rows = lax.broadcasted_iota(jnp.int32, (LANES_STEP, 128), 0) // HEADDIM + g * HEADS_STEP
    chosen = (chosen_rows == lax.broadcasted_iota(jnp.int32, (LANES_STEP, 128), 1)).astype(BF16)

    def sums_of(values, terms):
        total, rest = None, values
        for _ in range(terms):
            part = rest.astype(BF16)
            rest = rest - part.astype(F32)
            piece = dot(part, chosen, 1, 0)
            total = piece if total is None else total + piece
        return total

    u_ref[...] += sums_of(prod_ref[0], 2)
    v_ref[...] += sums_of(prod_ref[1], 2)
    i_ref[...] += sums_of(prod_ref[2], 2)
    e_ref[8:16, 0:128] += sums_of(e_ref[0:8, :], 2)
    gw_ref[...] += grad_write
    gr_ref[...] += grad_read

    @pl.when(g == pl.num_programs(1) - 1)
    def _():
        low = gscores_ref[...].astype(BF16)
        gradient = (
            gw_ref[...] + dot(low, wr_ref[:, STATE:], 0, 0),
            gr_ref[...] + dot(low, wr_ref[:, :STATE], 1, 0),
        )
        for part in range(2):
            lanes = slice(STATE * part, STATE * (part + 1))
            grad_conv = gradient[part] * nslope_ref[:, lanes]
            next_ref[0:GROUP, lanes] = grad_conv
            pre = npre_ref[:, lanes].astype(BF16).astype(F32)
            total_pre = jnp.zeros_like(grad_conv)
            for j in range(CONV):
                moved = next_ref[j : j + GROUP, lanes]
                total_pre = total_pre + ntaps_ref[CONV - 1 - j : CONV - j, lanes] * moved
                nsums_ref[CONV - 1 - j : CONV - j, lanes] += jnp.sum(pre * moved, axis=0, keepdims=True)
            nsums_ref[CONV : CONV + 1, lanes] += jnp.sum(grad_conv, axis=0, keepdims=True)
            gnarrow_ref[:, lanes] = total_pre.astype(BF16)

        @pl.when(first_of_slot)
        def _():
            head_ref[0:8, : 2 * STATE] = jnp.zeros((8, 2 * STATE), F32)
            head_ref[8:16, : 2 * STATE] = next_ref[0:8, :]
            halo = jnp.zeros((8, 2 * STATE), F32)
            for j in range(CONV):
                moved = head_ref[j : j + 8, : 2 * STATE]
                halo = halo + ntaps_ref[CONV - 1 - j : CONV - j, :] * moved
                nsums_ref[CONV - 1 - j : CONV - j, :] += jnp.sum(
                    nrim_ref[0].astype(F32) * moved[5:8], axis=0, keepdims=True
                )
            nhalo_ref[0] = halo

        own = cols_ref[...]
        lane = lax.broadcasted_iota(jnp.int32, (GROUP, 128), 1)
        step = jnp.where(lane < heads, own, 0.0)
        cum = pltpu.roll(own, 128 - heads, 1)
        sig = jnp.where(lane < heads, pltpu.roll(own, 128 - 2 * heads, 1), 0.0)
        strict = lax.broadcasted_iota(jnp.int32, (GROUP, GROUP), 0) > lax.broadcasted_iota(
            jnp.int32, (GROUP, GROUP), 1
        )
        reverse_sum = (
            split_dot(lower.astype(BF16), v_ref[...], 2, 0)
            + split_dot(strict.astype(BF16), i_ref[...], 2, 1)
            + jnp.exp(cum[GROUP - 1 : GROUP, :]) * e_ref[8:9, 0:128]
        )
        grad_raw = (u_ref[...] + rate_ref[...] * reverse_sum) * sig
        gnarrow_ref[:, 2 * STATE :] = grad_raw.astype(BF16)
        hsums_ref[0:1, :] += jnp.sum(grad_raw, axis=0, keepdims=True)
        hsums_ref[1:2, :] += jnp.sum(reverse_sum * step, axis=0, keepdims=True) * rate_ref[...]


def back_blocks(
    x, mixed, grad, slope, pre, rim, wr, nslope, npre, nrim, cols, rows, states, flows, skip, taps, ntaps, rate, groups
):
    tokens, width = x.shape
    blocks, steps, heads, slots = tokens // GROUP, width // LANES_STEP, rows.shape[1], rim.shape[0]
    at = lambda b: blocks - 1 - b
    wide = pl.BlockSpec((GROUP, LANES_STEP), lambda b, g: (at(b), g))
    narrow = lambda w: pl.BlockSpec((GROUP, w), lambda b, g: (at(b), 0))
    state = pl.BlockSpec((1, STATE, LANES_STEP), lambda b, g: (at(b), 0, g))
    line = lambda n: pl.BlockSpec((n, LANES_STEP), lambda b, g: (0, g))
    whole = lambda shape: pl.BlockSpec(shape, lambda b, g: (0,) * len(shape))
    return pl.pallas_call(
        functools.partial(back_kernel, groups, heads),
        grid=(blocks, steps),
        in_specs=[
            wide, wide, wide, wide, wide,
            pl.BlockSpec((1, CONV - 1, LANES_STEP), lambda b, g: (at(b) // groups, 0, g)),
            narrow(2 * STATE), narrow(2 * STATE), narrow(npre.shape[1]),
            pl.BlockSpec((1, CONV - 1, 2 * STATE), lambda b, g: (at(b) // groups, 0, 0)),
            narrow(128),
            pl.BlockSpec((1, heads, GROUP), lambda b, g: (at(b), 0, 0)),
            state, state, line(1), line(CONV), whole((CONV, 2 * STATE)), whole((1, 128)),
        ],
        out_specs=[
            wide, narrow(2 * STATE + 128),
            whole((steps, 8, LANES_STEP)), whole((8, 2 * STATE)), whole((8, 128)),
            pl.BlockSpec((1, 8, LANES_STEP), lambda b, g: (at(b) // groups, 0, g)),
            pl.BlockSpec((1, 8, 2 * STATE), lambda b, g: (at(b) // groups, 0, 0)),
        ],
        out_shape=[
            jax.ShapeDtypeStruct((tokens, width), BF16),
            jax.ShapeDtypeStruct((tokens, 2 * STATE + 128), BF16),
            jax.ShapeDtypeStruct((steps, 8, LANES_STEP), F32),
            jax.ShapeDtypeStruct((8, 2 * STATE), F32),
            jax.ShapeDtypeStruct((8, 128), F32),
            jax.ShapeDtypeStruct((slots, 8, width), F32),
            jax.ShapeDtypeStruct((slots, 8, 2 * STATE), F32),
        ],
        scratch_shapes=[
            pltpu.VMEM((GROUP, GROUP), F32),
            pltpu.VMEM((GROUP, GROUP), F32),
            pltpu.VMEM((3, GROUP, LANES_STEP), F32),
            pltpu.VMEM((GROUP, STATE), F32),
            pltpu.VMEM((GROUP, STATE), F32),
            pltpu.VMEM((GROUP, 128), F32),
            pltpu.VMEM((GROUP, 128), F32),
            pltpu.VMEM((GROUP, 128), F32),
            pltpu.VMEM((16, LANES_STEP), F32),
            pltpu.VMEM((steps, GROUP + 8, LANES_STEP), F32),
            pltpu.VMEM((GROUP + 8, 2 * STATE), F32),
            pltpu.VMEM((16, max(LANES_STEP, 2 * STATE)), F32),
        ],
        cost_estimate=pl.CostEstimate(
            flops=2 * tokens * width * (4 * GROUP + 4 * STATE) * 2,
            bytes_accessed=tokens * width * 14,
            transcendentals=tokens * GROUP * width // HEADDIM,
        ),
        name="back_blocks",
    )(x, mixed, grad, slope, pre, rim, wr, nslope, npre, nrim, cols, rows, states, flows, skip, taps, ntaps, rate)


MESH = pl.DeviceIdType.MESH
FAR_PARTS = 4


def fetch_kernel(
    x_ref, inner_ref, gate_ref, step_ref, wr_ref, out_ref, small_ref,
    full_x, full_inner, full_gate, full_step, full_wr, out_far, full_small,
    x_own, inner_own, gate_own, step_own, wr_own, small_own, send_sem, recv_sem, local_sem,
):
    f, c, z = lax.axis_index("fsdp"), lax.axis_index("ctx"), lax.axis_index("tp")
    half = z // 2
    slots, seq, cols = full_x.shape[0], full_x.shape[1], x_ref.shape[2]
    depth = inner_ref.shape[0]
    partners = (
        {"fsdp": f ^ 1}, {"fsdp": f ^ 2}, {"fsdp": f ^ 3}, {"ctx": c ^ 1}, {"tp": z ^ 1}, {"tp": z ^ 2},
    )
    barrier = pltpu.get_barrier_semaphore()
    for partner in partners:
        pl.semaphore_signal(barrier, inc=1, device_id=partner, device_id_type=MESH)
    pl.semaphore_wait(barrier, len(partners))

    copies = []

    def send(src, dst, partner):
        at = len(copies)
        copy = pltpu.make_async_remote_copy(
            src_ref=src, dst_ref=dst, send_sem=send_sem.at[at], recv_sem=recv_sem.at[at],
            device_id=partners[partner], device_id_type=MESH,
        )
        copy.start()
        copies.append([copy, False])
        return at

    def arrived(at):
        copies[at][0].wait_recv()
        copies[at][1] = True

    def feature(which):
        return pl.ds(pl.multiple_of(which * cols, 128), cols)

    def shard(full, row_f, far):
        wide = full.shape[1] // 2
        start = pl.multiple_of((row_f * 2 + c) * depth, depth)
        return full.at[pl.ds(start, depth), pl.ds(far * wide, wide)]

    def shard_one(full, row_f, far):
        start = pl.multiple_of((row_f * 2 + c) * depth, depth)
        return full.at[pl.ds(start, depth), :]

    def spread(full, src, far, part=shard):
        dst = part(full, f, far)
        near = [send(src, dst, k) for k in range(3)]
        send(src, dst, 3)
        return near

    def relay(full, near, far, part=shard):
        for k in range(3):
            arrived(near[k])
            row = part(full, f ^ (k + 1), far)
            send(row, row, 3)

    mine = pl.ds(half * slots, slots)
    other = pl.ds((1 - half) * slots, slots)
    send(small_ref, full_small.at[z], 4)
    far_small = send(small_ref, full_small.at[z], 5)
    send(x_ref.at[mine], full_x.at[:, :, feature(z)], 4)
    far_inner = send(inner_ref, shard(full_inner, f, 1), 5)
    far_step = send(step_ref, shard(full_step, f, 1), 5)
    piece = seq // FAR_PARTS
    far_x = [
        send(x_ref.at[other, pl.ds(piece * i, piece)], full_x.at[:, pl.ds(piece * i, piece), feature(z)], 5)
        for i in range(FAR_PARTS)
    ]
    far_gate = send(gate_ref, shard(full_gate, f, 1), 5)
    send(out_ref, out_far, 5)
    own_inner = spread(full_inner, inner_ref, 0)
    own_step = spread(full_step, step_ref, 0)
    own_wr = spread(full_wr, wr_ref, 0, shard_one)

    staged = (
        (x_ref.at[mine], x_own, full_x.at[:, :, feature(z)]),
        (inner_ref, inner_own, shard(full_inner, f, 0)),
        (gate_ref, gate_own, shard(full_gate, f, 0)),
        (step_ref, step_own, shard(full_step, f, 0)),
        (wr_ref, wr_own, shard_one(full_wr, f, 0)),
        (small_ref, small_own, full_small.at[z]),
    )
    loads = [pltpu.make_async_copy(src, buf, local_sem.at[0, i]) for i, (src, buf, _) in enumerate(staged)]
    stores = [pltpu.make_async_copy(buf, dst, local_sem.at[1, i]) for i, (_, buf, dst) in enumerate(staged)]
    for load in loads:
        load.start()
    for load, store in zip(loads, stores):
        load.wait()
        store.start()

    arrived(far_small)
    send(full_small.at[z ^ 2], full_small.at[z ^ 2], 4)
    arrived(far_inner)
    away_inner = spread(full_inner, shard(full_inner, f, 1), 1)
    arrived(far_step)
    away_step = spread(full_step, shard(full_step, f, 1), 1)
    own_gate = spread(full_gate, gate_ref, 0)

    def both(i):
        arrived(far_x[i])
        part = full_x.at[:, pl.ds(piece * i, piece), feature(z ^ 2)]
        send(part, part, 4)

    relay(full_inner, own_inner, 0)
    relay(full_step, own_step, 0)
    relay(full_wr, own_wr, 0, shard_one)
    both(0)
    relay(full_inner, away_inner, 1)
    relay(full_step, away_step, 1)
    both(1)
    both(2)
    relay(full_gate, own_gate, 0)
    both(3)
    arrived(far_gate)
    away_gate = spread(full_gate, shard(full_gate, f, 1), 1)
    relay(full_gate, away_gate, 1)
    for store in stores:
        store.wait()
    for copy, done in copies:
        if not done:
            copy.wait_recv()
        copy.wait_send()


def fetch(hidden, inner, gate, step, wr, out, small):
    slot_count, seq, cols = hidden.shape
    slots, depth = slot_count // 2, inner.shape[0]
    total = 8 * depth
    count = 1 + 2 * FAR_PARTS + 3 + 7 * 7 + 4
    anywhere = pl.BlockSpec(memory_space=pl.ANY)
    full = lambda x: jax.ShapeDtypeStruct((total, 2 * x.shape[1]), BF16)
    return pl.pallas_call(
        fetch_kernel,
        in_specs=[anywhere] * 7,
        out_specs=[anywhere] * 7,
        out_shape=[
            jax.ShapeDtypeStruct((slots, seq, 4 * cols), BF16),
            full(inner), full(gate), full(step),
            jax.ShapeDtypeStruct((total, wr.shape[1]), BF16),
            jax.ShapeDtypeStruct(out.shape, BF16),
            jax.ShapeDtypeStruct((4,) + small.shape, F32),
        ],
        scratch_shapes=[
            pltpu.VMEM((slots, seq, cols), BF16),
            pltpu.VMEM(inner.shape, BF16),
            pltpu.VMEM(gate.shape, BF16),
            pltpu.VMEM(step.shape, BF16),
            pltpu.VMEM(wr.shape, BF16),
            pltpu.VMEM(small.shape, F32),
            pltpu.SemaphoreType.DMA((count,)),
            pltpu.SemaphoreType.DMA((count,)),
            pltpu.SemaphoreType.DMA((2, 6)),
        ],
        compiler_params=pltpu.CompilerParams(collective_id=0, has_side_effects=True),
        name="fetch",
    )(hidden, inner, gate, step, wr, out, small)


def finish_kernel(
    part_ref, grad_ref, small_ref, cross_ref,
    near_out, other_out, home_out, narrow_out, small_out, small_far, cross_out, cross_far,
    relay_buf, part_buf, sum_buf, core_buf, own_buf, plane_buf, got_buf, sent_buf, home_buf, wr_send, wr_got,
    small_got, cross_got, send_sem, recv_sem, load_sem,
):
    f, c, z = lax.axis_index("fsdp"), lax.axis_index("ctx"), lax.axis_index("tp")
    tokens, cols = near_out.shape
    depth, inner = home_out.shape
    partners = (
        {"fsdp": f ^ 1}, {"fsdp": f ^ 2}, {"fsdp": f ^ 3}, {"ctx": c ^ 1}, {"tp": z ^ 1}, {"tp": z ^ 2},
    )
    barrier = pltpu.get_barrier_semaphore()
    for partner in partners:
        pl.semaphore_signal(barrier, inc=1, device_id=partner, device_id_type=MESH)

    def feature(which):
        return pl.ds(pl.multiple_of(which * cols, 128), cols)

    def rows_of(row_f, core):
        return pl.ds(pl.multiple_of((row_f * 2 + core) * depth, depth), depth)

    piece = tokens // FAR_PARTS
    loads = [
        pltpu.make_async_copy(grad_ref.at[rows_of(f ^ k, c)], own_buf.at[k], load_sem.at[k]) for k in range(4)
    ] + [
        pltpu.make_async_copy(
            part_ref.at[pl.ds(piece * i, piece), feature(z ^ 2)], part_buf.at[i], load_sem.at[4 + i]
        )
        for i in range(FAR_PARTS)
    ]
    for load in loads:
        load.start()
    pl.semaphore_wait(barrier, len(partners))

    copies = []

    def send(src, dst, partner):
        at = len(copies)
        copy = pltpu.make_async_remote_copy(
            src_ref=src, dst_ref=dst, send_sem=send_sem.at[at], recv_sem=recv_sem.at[at],
            device_id=partners[partner], device_id_type=MESH,
        )
        copy.start()
        copies.append([copy, False])
        return at

    def arrived(at):
        copies[at][0].wait_recv()
        copies[at][1] = True

    core = [send(grad_ref.at[rows_of(f ^ k, c ^ 1)], core_buf.at[k], 3) for k in (1, 2, 3, 0)]
    core_of = {1: core[0], 2: core[1], 3: core[2], 0: core[3]}
    small = [send(small_ref, small_got.at[0], 3)]
    cross = [send(cross_ref, cross_got, 4)]
    relays = [
        send(part_ref.at[pl.ds(piece * i, piece), feature(z ^ 3)], relay_buf.at[i], 4) for i in range(FAR_PARTS)
    ]
    for load in loads[:4]:
        load.wait()
    plane = []
    for k in (1, 2, 3):
        arrived(core_of[k])
        sent_buf[k - 1] = (own_buf[k].astype(F32) + core_buf[k].astype(F32)).astype(BF16)
        plane.append(send(sent_buf.at[k - 1], plane_buf.at[k - 1], k - 1))
    arrived(cross[0])
    cross_out[...] = cross_ref[...] + cross_got[...]
    arrived(small[0])
    small_out[...] = small_ref[...] + small_got[0]
    small.append(send(small_out, small_got.at[1], 0))
    cross.append(send(cross_out, cross_far, 5))

    def passed_on(i):
        loads[4 + i].wait()
        arrived(relays[i])
        sum_buf[i] = (part_buf[i].astype(F32) + relay_buf[i].astype(F32)).astype(BF16)
        send(sum_buf.at[i], other_out.at[pl.ds(piece * i, piece)], 5)

    passed_on(0)
    arrived(small[1])
    copies[small[1]][0].wait_send()
    small_out[...] = small_out[...] + small_got[1]
    small.append(send(small_out, small_got.at[2], 1))
    passed_on(1)
    arrived(core_of[0])
    passed_on(2)
    arrived(small[2])
    copies[small[2]][0].wait_send()
    small_out[...] = small_out[...] + small_got[2]
    small.append(send(small_out, small_got.at[3], 4))
    passed_on(3)
    total = own_buf[0].astype(F32) + core_buf[0].astype(F32)
    for at in plane:
        arrived(at)
    for k in range(3):
        total = total + plane_buf[k].astype(F32)
    wr_send[...] = total[:, 2 * inner : 2 * inner + 2 * STATE]
    wr = send(wr_send, wr_got, 4)
    send(part_ref.at[:, feature(z ^ 1)], near_out, 4)
    home_out[...] = total[:, :inner]
    home_buf[:, :inner] = total[:, inner : 2 * inner].astype(BF16)
    narrow_out[:, 2 * STATE : 2 * STATE + 128] = total[:, 2 * inner + 2 * STATE :]
    home_buf[:, inner + 2 * STATE :] = total[:, 2 * inner + 2 * STATE :].astype(BF16)
    arrived(small[3])
    copies[small[3]][0].wait_send()
    shared = small_out.shape[0] // 2
    small_out[shared:, :] = small_out[shared:, :] + small_got[3, shared:, :]
    small.append(send(small_out, small_far, 5))
    arrived(wr)
    both = wr_send[...] + wr_got[...]
    narrow_out[:, : 2 * STATE] = both
    home_buf[:, inner : inner + 2 * STATE] = both.astype(BF16)
    last = send(home_buf, got_buf, 5)
    arrived(last)
    home_out[...] += got_buf[:, :inner].astype(F32)
    narrow_out[:, : 2 * STATE] += got_buf[:, inner : inner + 2 * STATE].astype(F32)
    steps = got_buf[:, inner + 2 * STATE :].astype(F32)
    narrow_out[:, 2 * STATE + 128 :] = steps
    for copy, done in copies:
        if not done:
            copy.wait_recv()
    waited = {small[1], small[2], small[3]}
    for at, (copy, done) in enumerate(copies):
        if at not in waited:
            copy.wait_send()


def finish(part, grad, small, cross, depth):
    tokens, width = part.shape
    cols, total = width // 4, grad.shape[1]
    rest = 2 * STATE + 128
    inner = (total - rest) // 2
    anywhere = pl.BlockSpec(memory_space=pl.ANY)
    vmem = pl.BlockSpec(memory_space=pltpu.VMEM)
    count = 4 + 5 + 2 + FAR_PARTS * 2 + 1 + 3 + 2
    return pl.pallas_call(
        finish_kernel,
        in_specs=[anywhere, anywhere, vmem, vmem],
        out_specs=[anywhere, anywhere, vmem, vmem, vmem, vmem, vmem, vmem],
        out_shape=[
            jax.ShapeDtypeStruct((tokens, cols), BF16),
            jax.ShapeDtypeStruct((tokens, cols), BF16),
            jax.ShapeDtypeStruct((depth, inner), F32),
            jax.ShapeDtypeStruct((depth, rest + 128), F32),
            jax.ShapeDtypeStruct(small.shape, F32),
            jax.ShapeDtypeStruct(small.shape, F32),
            jax.ShapeDtypeStruct(cross.shape, F32),
            jax.ShapeDtypeStruct(cross.shape, F32),
        ],
        scratch_shapes=[
            pltpu.VMEM((FAR_PARTS, tokens // FAR_PARTS, cols), BF16),
            pltpu.VMEM((FAR_PARTS, tokens // FAR_PARTS, cols), BF16),
            pltpu.VMEM((FAR_PARTS, tokens // FAR_PARTS, cols), BF16),
            pltpu.VMEM((4, depth, total), BF16),
            pltpu.VMEM((4, depth, total), BF16),
            pltpu.VMEM((3, depth, total), BF16),
            pltpu.VMEM((depth, inner + rest), BF16),
            pltpu.VMEM((3, depth, total), BF16),
            pltpu.VMEM((depth, inner + rest), BF16),
            pltpu.VMEM((depth, 2 * STATE), F32),
            pltpu.VMEM((depth, 2 * STATE), F32),
            pltpu.VMEM((4,) + small.shape, F32),
            pltpu.VMEM(cross.shape, F32),
            pltpu.SemaphoreType.DMA((count,)),
            pltpu.SemaphoreType.DMA((count,)),
            pltpu.SemaphoreType.DMA((4 + FAR_PARTS,)),
        ],
        compiler_params=pltpu.CompilerParams(collective_id=1, has_side_effects=True),
        name="finish",
    )(part, grad, small, cross)


def after(x, other):
    return lax.optimization_barrier((x, other))[0]


def everywhere(x):
    for axis in ("ctx", "fsdp"):
        count, bit = lax.axis_size(axis), 1
        if count & (count - 1):
            x = lax.psum(x, axis)
            continue
        while bit < count:
            x = x + lax.ppermute(x, axis, [(i, i ^ bit) for i in range(count)])
            bit *= 2
    return x


def pack(parts):
    return jnp.concatenate([part.reshape(-1) for part in parts])


def unpack(vector, shapes):
    parts, at = [], 0
    for shape in shapes:
        size = 1
        for dim in shape:
            size *= dim
        parts.append(vector[at : at + size].reshape(shape))
        at += size
    return parts


def on_device(
    hidden_in,
    lengths,
    norm_gain,
    proj_gate_inner,
    proj_write_read,
    proj_step,
    conv_inner,
    conv_inner_bias,
    conv_write_read,
    conv_write_read_bias,
    step_bias,
    log_rate,
    skip_gain,
    gate_gain,
    proj_out,
    out_cotangent,
):
    slot_count, seq_here, width_here = hidden_in.shape
    slots = slot_count // 2
    tokens = slots * seq_here
    heads_own = step_bias.shape[0]
    inner_own = gate_gain.shape[0]
    heads = 2 * heads_own
    inner = 2 * inner_own
    tp_count = lax.axis_size("tp")
    width = tp_count * width_here
    groups = seq_here // GROUP
    blocks = slots * groups
    head_steps = heads // HEADS_STEP
    rim_rows = CONV - 1
    place = lax.axis_index("tp")
    far_half, near_side = place // 2, place % 2

    def half_of(whole, which):
        return lax.dynamic_slice_in_dim(whole, which * slots, slots, 0)

    def ordered(own, near, far, both, axis):
        first = lambda a, b: jnp.where(near_side == 0, a, b)
        a0, a1, b0, b1 = first(own, near), first(near, own), first(far, both), first(both, far)
        lower = lambda a, b: jnp.where(far_half == 0, a, b)
        return jnp.concatenate(
            [lower(a0, b0), lower(a1, b1), lower(b0, a0), lower(b1, a1)], axis=axis
        )

    def own_features(piece):
        relay = swap(piece(place ^ 3).astype(BF16), 1)
        keep = swap(piece(place ^ 1).astype(BF16), 1)
        sent = swap((piece(place ^ 2) + relay.astype(F32)).astype(BF16), 2)
        kept = (piece(place) + keep.astype(F32)).reshape(slots, seq_here, width_here)
        other = sent.astype(F32).reshape(slots, seq_here, width_here)
        return both_halves(kept, other)

    def both_halves(kept, other):
        return jnp.where(
            far_half == 0,
            jnp.concatenate([kept, other], axis=0),
            jnp.concatenate([other, kept], axis=0),
        )

    small_shapes = [(CONV, inner_own), (inner_own,), (inner_own,), (heads_own,), (heads_own,), (heads_own,)]
    def gathered(x):
        return lax.all_gather(x, ("fsdp", "ctx"), axis=0, tiled=True)

    own_small = pack([conv_inner, conv_inner_bias, gate_gain, step_bias, log_rate, skip_gain])
    cot_mine, cot_other = half_of(out_cotangent, far_half), half_of(out_cotangent, 1 - far_half)
    narrow_cols = 2 * STATE + heads
    narrow_pad = -narrow_cols % 128
    zeros = lambda x, extra: jnp.zeros((x.shape[0], extra), BF16)
    inner_shard, gate_shard = proj_gate_inner[:, 1], proj_gate_inner[:, 0]
    if lax.axis_size("fsdp") == 4 and lax.axis_size("ctx") == 2:
        step_shard = jnp.concatenate([proj_step, zeros(proj_step, 128 - heads_own)], axis=1)
        small = pack([norm_gain.astype(F32), own_small])
        small = jnp.pad(small, (0, -small.size % 1024)).reshape(-1, 128)
        full_x, full_inner, full_gate, full_step, full_wr, out_far, full_small = fetch(
            hidden_in, inner_shard, gate_shard, step_shard, proj_write_read, proj_out, small
        )
        full_small = full_small.reshape(tp_count, -1)
        full_gain = full_small[:, :width_here].reshape(width)
        far_row = lax.dynamic_slice_in_dim(full_small, place ^ 2, 1, 0)[0, width_here:]
        far_small = unpack(far_row, small_shapes)
        full_narrow = jnp.concatenate(
            [full_wr, full_step[:, :heads_own], full_step[:, 128 : 128 + heads_own], zeros(full_wr, narrow_pad)],
            axis=1,
        )
        cot_dep = full_x
    else:
        x_mine, x_other = half_of(hidden_in, far_half), half_of(hidden_in, 1 - far_half)
        narrow_shard = jnp.concatenate(
            [proj_write_read, proj_step, swap(proj_step, 2), zeros(proj_step, narrow_pad)], axis=1
        )
        inner_far = swap(inner_shard, 2)
        x_near = swap(x_mine, 1)
        x_far = swap(after(x_other, inner_far), 2)
        gate_far = swap(after(gate_shard, x_far), 2)
        x_both = swap(x_far, 1)
        cot_dep = after(x_both, gate_far)
        full_narrow = gathered(narrow_shard)
        full_inner = gathered(jnp.concatenate([inner_shard, inner_far], axis=1))
        full_gate = gathered(jnp.concatenate([after(gate_shard, full_inner), gate_far], axis=1))
        full_x = ordered(x_mine, x_near, x_far, x_both, 2)
        out_far = swap(after(proj_out, cot_dep), 2)
        gain = norm_gain.astype(F32)
        full_gain = ordered(gain, swap(gain, 1), swap(gain, 2), swap(gain, 3), 0)
        far_small = unpack(swap(own_small, 2), small_shapes)
    full_x = full_x.reshape(tokens, width)
    cot_near = swap(after(cot_mine, cot_dep), 1)
    cot_far = swap(after(cot_other, cot_dep), 2)
    cot_both = swap(cot_far, 1)
    full_out = gathered(jnp.concatenate([after(proj_out, full_gate), out_far], axis=1))
    full_cot = ordered(cot_mine, cot_near, cot_far, cot_both, 2).reshape(tokens, width)

    taps = jnp.concatenate([conv_inner, far_small[0]], axis=1)
    taps_bias = jnp.concatenate([conv_inner_bias, far_small[1]])
    gain_gate = jnp.concatenate([gate_gain, far_small[2]])
    bias_step = jnp.concatenate([step_bias, far_small[3]])
    rate_log = jnp.concatenate([log_rate, far_small[4]])
    gain_skip = jnp.concatenate([skip_gain, far_small[5]])
    rate = -jnp.exp(rate_log)
    skip_lanes = jnp.repeat(gain_skip, HEADDIM)[None]

    in_float = full_x.astype(F32)
    in_scale = lax.rsqrt(jnp.mean(in_float * in_float, axis=-1, keepdims=True) + EPSILON)
    normed = (in_float * in_scale * full_gain.astype(F32)).astype(BF16)
    narrow_pre = dot(normed, full_narrow, 1, 0)
    inner_pre = dot(normed, full_inner, 1, 0).astype(BF16)
    gate_pre = dot(normed, full_gate, 1, 0).astype(BF16)

    def rim_of(pre):
        by_slot = pre.reshape(slots, seq_here, pre.shape[-1])
        return passed_along(by_slot[:, seq_here - rim_rows :].astype(BF16), "ctx", 1)

    inner_rim, narrow_rim = rim_of(inner_pre), rim_of(narrow_pre[:, : 2 * STATE])
    lane_pad = lambda x: jnp.pad(x, (0, 128 - heads))[None]
    rate_row = lane_pad(rate)
    inner_act, slope, write_read, narrow_slope, cols, cum_rows, local_state, decay_lanes = start_blocks(
        inner_pre, inner_rim, narrow_pre, narrow_rim, taps, taps_bias[None], conv_write_read,
        conv_write_read_bias[None], lane_pad(bias_step), rate_row, groups, heads,
    )
    local_state = local_state.reshape(slots, groups, STATE, inner)
    decay_lanes = decay_lanes.reshape(slots, groups, 1, inner)
    carried = local_state[:, 0]
    device_decay = decay_lanes[:, 0]
    for position in range(1, groups):
        carried = decay_lanes[:, position] * carried + local_state[:, position]
        device_decay = device_decay * decay_lanes[:, position]
    current = carried_in(device_decay, carried, None, False)
    state_list = []
    for position in range(groups):
        state_list.append(current)
        current = decay_lanes[:, position] * current + local_state[:, position]
    states = jnp.stack(state_list, axis=1)
    states_low = states.astype(BF16).reshape(blocks, STATE, inner)

    position_ids = lax.axis_index("ctx") * seq_here + jnp.arange(seq_here)
    valid_rows = (position_ids[None, :] < lengths[:, None]).astype(F32)
    valid_here = half_of(valid_rows, far_half).reshape(tokens, 1)
    masked = (full_cot.astype(F32) * valid_here).astype(BF16)
    grad_normed_out = dot(masked, full_out, 1, 0).astype(BF16)
    mixed_out, stats = mix_blocks(
        inner_act, gate_pre, grad_normed_out, write_read, cols, cum_rows, states_low, skip_lanes, gain_gate[None],
    )
    stats = stats + swap(stats, 1)
    normed_out, grad_gate_pre, grad_diag, grad_gate_gain, grad_skip_lanes, local_grad = gate_blocks(
        mixed_out, gate_pre, grad_normed_out, inner_act, stats, gain_gate[None], write_read, cols, heads
    )
    local_grad = local_grad.reshape(slots, groups, STATE, inner)

    def branch_piece(which):
        rows = lax.dynamic_slice_in_dim(full_out, which * width_here, width_here, 0)
        return dot(normed_out, rows, 1, 1)

    branch = own_features(branch_piece)
    hidden_out = (hidden_in.astype(F32) + valid_rows[..., None] * branch).astype(BF16)
    grad_proj_out = dot(masked, normed_out, 0, 0).astype(BF16)
    grad_gate_w = dot(normed, grad_gate_pre, 0, 0).astype(BF16)
    grad_by_gate = dot(grad_gate_pre, full_gate, 1, 1)
    other_scale = swap(in_scale.reshape(-1, 128), 2)

    flowing = local_grad[:, groups - 1]
    for position in reversed(range(groups - 1)):
        flowing = decay_lanes[:, position] * flowing + local_grad[:, position]
    flowing = carried_in(device_decay, flowing, None, True)
    flow_list = []
    for position in reversed(range(groups)):
        flow_list.insert(0, flowing)
        flowing = decay_lanes[:, position] * flowing + local_grad[:, position]
    flows = jnp.stack(flow_list, axis=1)
    flows_low = flows.astype(BF16).reshape(blocks, STATE, inner)
    flows_low = after(flows_low, (grad_proj_out, grad_gate_w))

    grad_inner_pre, grad_narrow, tap_sums, narrow_sums, head_sums, halo, narrow_halo = back_blocks(
        inner_act, mixed_out, grad_diag, slope, inner_pre, inner_rim, write_read, narrow_slope, narrow_pre,
        narrow_rim, cols, cum_rows, states_low, flows_low, skip_lanes, taps, conv_write_read, rate_row, groups,
    )
    tap_sums = tap_sums.transpose(1, 0, 2).reshape(8, inner)
    grad_taps, grad_taps_bias = tap_sums[:CONV], tap_sums[CONV]
    grad_conv_write_read, grad_conv_write_read_bias = narrow_sums[:CONV], narrow_sums[CONV]
    grad_step_bias, grad_log_rate = head_sums[0, :heads], head_sums[1, :heads]

    def completed(grad, halo):
        back = passed_along(halo, "ctx", -1)
        for slot in range(slots):
            ends = (slot + 1) * seq_here
            rows = grad[ends - 8 : ends, : halo.shape[-1]].astype(F32) + back[slot]
            grad = lax.dynamic_update_slice(grad, rows.astype(BF16), (ends - 8, 0))
        return grad

    grad_inner_pre, grad_narrow = completed(grad_inner_pre, halo), completed(grad_narrow, narrow_halo)
    def reduced(x):
        return lax.psum_scatter(x, ("fsdp", "ctx"), scatter_dimension=0, tiled=True)

    early = reduced(jnp.concatenate([grad_proj_out, grad_gate_w], axis=1))
    early_far = swap(jnp.concatenate([early[:, inner_own:inner], early[:, inner + inner_own :]], axis=1), 2)
    grad_out_home = early[:, :inner_own].astype(F32) + early_far[:, :inner_own].astype(F32)
    grad_gate_home = early[:, inner : inner + inner_own].astype(F32) + early_far[:, inner_own:].astype(F32)

    grad_inner_pre, hidden_out = lax.optimization_barrier((grad_inner_pre, hidden_out))
    late = jnp.concatenate([grad_inner_pre, grad_narrow], axis=1)
    grad_late_w = dot(normed, late, 0, 0).astype(BF16)
    partial_normed = (
        grad_by_gate + dot(grad_inner_pre, full_inner, 1, 1) + dot(grad_narrow, full_narrow, 1, 1)
    )
    by_hat = partial_normed * (full_x.astype(F32) * in_scale)
    grad_gain_full = jnp.sum(by_hat, axis=0)
    cross_part = jnp.sum(by_hat * full_gain.astype(F32), axis=1)
    partial_low = partial_normed.astype(BF16)

    grad_skip_gain = jnp.sum(grad_skip_lanes.reshape(heads, HEADDIM), axis=1)
    shared_shapes = [(CONV, 2 * STATE), (2 * STATE,), (width,)]
    head_shapes = [(CONV, inner), (inner,), (inner,), (heads,), (heads,), (heads,)]
    by_head = pack([grad_taps, grad_taps_bias, grad_gate_gain, grad_step_bias, grad_log_rate, grad_skip_gain])
    by_all = pack([grad_conv_write_read, grad_conv_write_read_bias, grad_gain_full])

    if lax.axis_size("fsdp") == 4 and lax.axis_size("ctx") == 2:
        lines = -(-max(by_head.size, by_all.size) // 1024) * 8
        filled = lambda v: jnp.pad(v, (0, lines * 128 - v.size)).reshape(lines, 128)
        near, other, grad_inner_home, narrow_sum, small_own, small_far, cross_rows, cross_far = finish(
            partial_low,
            after(grad_late_w, early_far),
            jnp.concatenate([filled(by_head), filled(by_all)]),
            cross_part.reshape(-1, 128),
            proj_write_read.shape[0],
        )
        kept = lax.dynamic_slice_in_dim(partial_normed, place * width_here, width_here, 1) + near.astype(F32)
        grad_normed = both_halves(
            kept.reshape(slots, seq_here, width_here), other.astype(F32).reshape(slots, seq_here, width_here)
        )
        write_read_home = narrow_sum[:, : 2 * STATE]
        step_home = (
            narrow_sum[:, 2 * STATE : 2 * STATE + heads_own]
            + narrow_sum[:, 2 * STATE + 128 + heads_own : 2 * STATE + 128 + heads]
        )
        cross_rows, cross_far = cross_rows.reshape(-1), cross_far.reshape(-1)
        parts = unpack(small_own[:lines].reshape(-1), head_shapes)
        far_parts = unpack(small_far[:lines].reshape(-1), head_shapes)
        far_parts = [lax.slice_in_dim(p, p.shape[-1] // 2, p.shape[-1], axis=p.ndim - 1) for p in far_parts]
        shared = (small_own[lines:] + small_far[lines:]).reshape(-1)
    else:

        def normed_piece(which):
            return lax.dynamic_slice_in_dim(partial_normed, which * width_here, width_here, 1)

        grad_normed = own_features(normed_piece)
        late_sum = reduced(grad_late_w)
        late_far = swap(late_sum, 2).astype(F32)
        late_sum = late_sum.astype(F32)
        grad_inner_home = late_sum[:, :inner_own] + late_far[:, inner_own:inner]
        write_read_home = late_sum[:, inner : inner + 2 * STATE] + late_far[:, inner : inner + 2 * STATE]
        write_read_home = write_read_home + swap(write_read_home, 1)
        steps_at = inner + 2 * STATE
        step_home = late_sum[:, steps_at : steps_at + heads_own] + late_far[:, steps_at + heads_own : steps_at + heads]
        cross_rows = cross_part + swap(cross_part, 1)
        cross_far = swap(cross_rows, 2)
        smalls = everywhere(pack([by_head, by_all]))
        parts = unpack(smalls[: by_head.size], head_shapes)
        away = [lax.slice_in_dim(p, p.shape[-1] // 2, p.shape[-1], axis=p.ndim - 1) for p in parts]
        far_parts = unpack(swap(pack(away), 2), small_shapes)
        shared = smalls[by_head.size :]
        shared = shared + swap(shared, 1)
        shared = shared + swap(shared, 2)

    homes = [
        lax.slice_in_dim(p, 0, p.shape[-1] // 2, axis=p.ndim - 1) + a for p, a in zip(parts, far_parts)
    ]
    wr_taps, wr_bias, gain_all = unpack(shared, shared_shapes)
    grad_norm_gain = lax.dynamic_slice_in_dim(gain_all, place * width_here, width_here, 0)

    own_gain = norm_gain.astype(F32)
    own_scale = both_halves(
        in_scale.reshape(slots, seq_here, 1), other_scale.reshape(slots, seq_here, 1)
    )
    own_hat = hidden_in.astype(F32) * own_scale
    grad_hat_in = grad_normed * own_gain
    cross_in = both_halves(
        cross_rows.reshape(slots, seq_here, 1), cross_far.reshape(slots, seq_here, 1)
    ) / width
    grad_hidden_in = own_scale * (grad_hat_in - own_hat * cross_in) + out_cotangent.astype(F32)
    return (
        hidden_out,
        grad_hidden_in,
        grad_norm_gain,
        jnp.stack([grad_gate_home, grad_inner_home], axis=1),
        write_read_home,
        step_home,
        homes[0],
        homes[1],
        wr_taps,
        wr_bias,
        homes[3],
        homes[4],
        homes[5],
        homes[2],
        grad_out_home,
    )


def solution(mesh):
    rows = ("fsdp", "ctx")
    acts = P("fsdp", "ctx", "tp")
    placed = (
        acts,
        P("fsdp"),
        P("tp"),
        P(rows, None, "tp"),
        P(rows, None),
        P(rows, "tp"),
        P(None, "tp"),
        P("tp"),
        P(),
        P(),
        P("tp"),
        P("tp"),
        P("tp"),
        P("tp"),
        P(rows, "tp"),
        acts,
    )
    return jax.shard_map(
        on_device,
        mesh=mesh,
        in_specs=placed,
        out_specs=(
            acts,
            acts,
            P("tp"),
            P(rows, None, "tp"),
            P(rows, None),
            P(rows, "tp"),
            P(None, "tp"),
            P("tp"),
            P(),
            P(),
            P("tp"),
            P("tp"),
            P("tp"),
            P("tp"),
            P(rows, "tp"),
        ),
        check_vma=False,
    )
```

time: 676 us -> 586 us (0.87)
  Pallas kernels: 106 us -> 307 us
  waiting for transfers between devices: 214 us -> 74.2 us
  other arithmetic: 97 us -> 40 us
  starting transfers between devices: 59.7 us -> 15.8 us
  matrix products: 117 us -> 91 us
  local copies, waits for them, and re-layouts: 52.9 us -> 34.9 us
    pallas_call x4 -> x6, Pallas kernels: 106 us -> 307 us  [the longest x1 93.1 us: finish(): pl.pallas_call(finish_kernel, in_specs=[anywhere, anywhere, vmem, vmem],...]
    ppermute x33 -> x9, waiting for transfers between devices: 213 us -> 73.6 us  [swap(): return lax.ppermute(x, 'tp', [(i, i ^ bit) for i in range(count)])]
    ppermute x33 -> x9, starting transfers between devices: 42 us -> 6.17 us  [swap(): return lax.ppermute(x, 'tp', [(i, i ^ bit) for i in range(count)])]
    dot_general x24 -> x14, matrix products: 115 us -> 91 us  [dot(): lax.dot_general(a, b, (((da,), (db,)), ((), ())), preferred_element_type=...]
    reduce_sum x5 -> x0, other arithmetic: 22.8 us -> none  [the longest x2 20.3 us: conv_silu(): summed = summed + conv_taps[offset] * padded[..., offset:offset + length, :]]
    transpose x7 -> x0, local copies, waits for them, and re-layouts: 9.31 us -> none  [the longest x3 6.63 us: from_steps(): return cols.transpose(1, 0, 2).reshape(blocks, GROUP, heads)]
    ppermute x3 -> x0, starting transfers between devices: 8.98 us -> none  [everywhere(): x = x + lax.ppermute(x, axis, [(i, i ^ bit) for i in range(count)])]
    reshape x13 -> x3, local copies, waits for them, and re-layouts: 9.46 us -> 0.67 us  [the longest x1 0.61 us: on_device(): small = jnp.pad(small, (0, -small.size % 1024)).reshape(-1, 128)]
  transfers between devices with their start and end apart: 50 -> 17, of which waited for: 15 -> 6; matrix products, arithmetic and copies ran while one was open for 32% -> 17% of each run, Pallas kernels for 2% -> 12%
where the time goes in v3:
time: 586 us; the launch traced here: 579 us
  Pallas kernels  307 us (52%)
  matrix products  91 us (16%)
  waiting for transfers between devices  74.2 us (13%)
  other arithmetic  40 us (7%)
  local copies, waits for them, and re-layouts  34.9 us (6%)
  starting transfers between devices  15.8 us (3%)
  between operations  15.4 us (3%)
    pallas_call x1, Pallas kernels, finish(): pl.pallas_call(finish_kernel, in_specs=[anywhere, anywhere, vmem, vmem],...  93.1 us
    pallas_call x1, Pallas kernels, fetch(): pl.pallas_call(fetch_kernel, in_specs=[anywhere] * 7, out_specs=[anywhere...  93 us
    dot_general x14, matrix products, dot(): lax.dot_general(a, b, (((da,), (db,)), ((), ())), preferred_element_type=...  91 us
    ppermute x9, waiting for transfers between devices, swap(): return lax.ppermute(x, 'tp', [(i, i ^ bit) for i in range(count)])  73.6 us
    pallas_call x1, Pallas kernels, back_blocks(): pl.pallas_call(functools.partial(back_kernel, groups, heads), grid=(block...  52 us
    pallas_call x1, Pallas kernels, mix_blocks(): pl.pallas_call(functools.partial(mix_kernel, heads), grid=(blocks, steps)...  30.3 us
    pallas_call x1, Pallas kernels, gate_blocks(): pl.pallas_call(functools.partial(gate_kernel, heads), grid=(steps, blocks...  20.6 us
    pallas_call x1, Pallas kernels, start_blocks(): pl.pallas_call(functools.partial(start_kernel, groups, heads), grid=(bloc...  18.4 us
  transfers between devices with their start and end apart: 17, of which 6 were waited for; matrix products, arithmetic and copies ran while one was open for 17% of the time, Pallas kernels for 12%

profile of v3, /device:TPU:0, one launch (start us, length us, event | category | flops | bytes accessed | tf_op | source)
XLA Modules:
  0.0 578.7 jit_solution(15453266463384701075)
XLA Ops:
  10.9 2.4 fusion.57
  14.7 93.0 %fetch.1 = (bf16[1,1024,1536]{2,1,0:T(8,128)(2,1)}, bf16[1536,1536]{1,0:T(8,128)(2,1)}, bf16[1536,1536]{1,0:T(8,128)(2,1)}, bf16[1536,256]{1,0:T(8,128)(2,1)}, b...) custom-call(bf16[2,1024,384]{2,1,0:T(8,128)(2,1)} %x_ref.1, ...), custom_call_target="tpu_custom_call" | custom-call | tf_op jit(solution)/shard_map/fetch/pallas_call | solution.py:713
  107.8 2.0 pad_maximum_fusion.4
  109.8 2.7 constant_dynamic-slice_fusion.1
  112.5 2.9 collective-permute-start.3
  120.8 5.5 convolution_convert_fusion.5.inner_ref.pre_ref
  130.8 9.0 %convolution_convert_fusion.4.gate_ref = bf16[1024,1536]{1,0:T(8,128)(2,1)} fusion(bf16[1536,1536]{1,0:T(8,128)(2,1)} %get-tuple-element.66, bf16[1,1024,1536]{2,1,0:T(8,128)(2,1)S(1)} %copy-done.1, f32[1536]{0:T(1024)S(1)} %mul.238, f32[1024]{0:T(1024)S(1)} %get-tuple-element.176), kind=kOutput, calls=%fused_computation.21 | convolution fusion | flops 4839702528 | bytes 11020288 | tf_op jit(solution)/shard_map/dot_general | solution.py:53
  143.0 18.4 %start_blocks.1 = (bf16[1024,1536]{1,0:T(8,128)(2,1)}, bf16[1024,1536]{1,0:T(8,128)(2,1)}, bf16[1024,256]{1,0:T(8,128)(2,1)}, f32[1024,256]{1,0:T(8,128)}, f32[1...) custom-call(bf16[1024,1536]{1,0:T(8,128)(2,1)} %copy-done.6, ...), custom_call_target="tpu_custom_call" | custom-call | flops 434110464 | bytes 12582912 | tf_op jit(solution)/shard_map/start_blocks/pallas_call | solution.py:146
  162.9 2.1 fusion.23
  169.9 16.3 %collective-permute-done.4 = bf16[1,1024,384]{2,1,0:T(8,128)(2,1)S(1)} collective-permute-done((bf16[1,1024,384]{2,1,0:T(8,128)(2,1)}, bf16[1,1024,384]{2,1,0:T(8,128)(2,1)S(1)}, u32[]{:S(2)}, u32[]{:S(2)}) %collective-permute-start.4) | collective-permute-done | bytes 786464 | tf_op jit(solution)/shard_map/ppermute | solution.py:26
  186.2 3.8 broadcast_select_fusion.7
  189.9 9.7 %convolution_convert_fusion.3.gno_ref = bf16[1024,1536]{1,0:T(8,128)(2,1)} fusion(bf16[1536,1536]{1,0:T(8,128)(2,1)} %all-gather.2.cloned.1.call-done, bf16[1,1024,384]{2,1,0:T(8,128)(2,1)} %get-tuple-element.153, bf16[1,1024,384]{2,1,0:T(8,128)(2,1)} %get-tuple-element.152, bf16[1,1024,384]{2,1,0:T(8,128)(2,1)} %get-tuple-element.151, ...), kind=kOutput, calls=%fused_computation.20 | convolution fusion | flops 4850712576 | bytes 11014144 | tf_op jit(solution)/shard_map/dot_general | solution.py:53
  199.6 30.3 %mix_blocks.1 = (f32[1024,1536]{1,0:T(8,128)}, f32[4,8,256]{2,1,0:T(8,128)}) custom-call(bf16[1024,1536]{1,0:T(8,128)(2,1)} %get-tuple-element.65.x_ref, bf16[1024,1536]{1,0:T(8,128)(2,1)} %convolution_convert_fusion.4.gate_ref, bf16[1024,1536]{1,0:T(8,128)(2,1)} %convolution_convert_fusion.3.gno_ref, bf16[1024,256]{1,0:T(8,128)(2,1)} %get-tuple-element.71.wr_ref, ...), custom_call_target="tpu_custom_call" | custom-call | flops 4831838208 | bytes 15728640 | tf_op jit(solution)/shard_map/mix_blocks/pallas_call | solution.py:240
  230.3 3.8 collective-permute-done.6
  235.5 20.6 %gate_blocks.1 = (bf16[1024,1536]{1,0:T(8,128)(2,1)}, bf16[1024,1536]{1,0:T(8,128)(2,1)}, bf16[1024,1536]{1,0:T(8,128)(2,1)}, f32[1,1536]{1,0:T(1,128)}, f32[1,1536]{1,0:T(1,128)}, /*index=5*/f32[4,128,1536]{2,1,0:T(8,128)}) custom-call(f32[1024,1536]{1,0:T(8,128)} %get-tuple-element.76.mixed_ref, bf16[1024,1536]{1,0:T(8,128)(2,1)} %convolution_convert_fusion.4.gate_ref, ...), custom_call_target="tpu_custom_call" | custom-call | flops 402653184 | bytes 28311552 | tf_op jit(solution)/shard_map/gate_blocks/pallas_call | solution.py:308
  256.2 8.2 %convolution_convert_fusion.1 = bf16[1536,1536]{1,0:T(8,128)(2,1)S(1)} fusion(bf16[1024,1536]{1,0:T(8,128)(2,1)} %get-tuple-element.82, bf16[1,1024,384]{2,1,0:T(8,128)(2,1)} %get-tuple-element.153, bf16[1,1024,384]{2,1,0:T(8,128)(2,1)} %get-tuple-element.152, bf16[1,1024,384]{2,1,0:T(8,128)(2,1)} %get-tuple-element.151, ...), kind=kOutput, calls=%fused_computation.4 | convolution fusion | flops 4851499008 | bytes 11014144 | tf_op jit(solution)/shard_map/dot_general | solution.py:53
  264.4 5.7 convolution_convert_fusion
  270.1 5.1 pad_maximum_fusion
  276.5 3.4 collective-permute-done.12
  284.4 5.5 convolution_convert_fusion.7
  290.3 7.0 %fusion.58 = f32[1024,1536]{1,0:T(8,128)} fusion(bf16[1024,1536]{1,0:T(8,128)(2,1)S(1)} %copy-done.54, bf16[1536,1536]{1,0:T(8,128)(2,1)S(1)} %bitcast.218), kind=kOutput, calls=%fused_computation.160 | convolution fusion | flops 4831838208 | bytes 14155776 | tf_op jit(solution)/shard_map/dot_general | solution.py:53
  297.3 4.0 convolution_convert_fusion.6
  306.6 52.0 %back_blocks.1 = (bf16[1024,1536]{1,0:T(8,128)(2,1)}, bf16[1024,384]{1,0:T(8,128)(2,1)}, f32[4,8,384]{2,1,0:T(8,128)}, f32[8,256]{1,0:T(8,128)}, f32[8,128]{1,0:...) custom-call(bf16[1024,1536]{1,0:T(8,128)(2,1)} %get-tuple-element.65.x_ref, ...), custom_call_target="tpu_custom_call" | custom-call | flops 9663676416 | bytes 22020096 | tf_op jit(solution)/shard_map/back_blocks/pallas_call | solution.py:527
  366.4 4.4 add_convert_fusion
  371.0 3.4 add_bitcast_fusion.1
  374.4 34.6 %collective-permute-done.11 = bf16[1024,384]{1,0:T(8,128)(2,1)S(1)} collective-permute-done((bf16[1024,384]{1,0:T(8,128)(2,1)S(1)}, bf16[1024,384]{1,0:T(8,128)(2,1)S(1)}, u32[]{:S(2)}, u32[]{:S(2)}) %collective-permute-start.11) | collective-permute-done | bytes 786464 | tf_op jit(solution)/shard_map/ppermute | solution.py:26
  411.1 7.0 %fusion.59 = f32[1024,1536]{1,0:T(8,128)} fusion(bf16[1024,1536]{1,0:T(8,128)(2,1)S(1)} %fusion.31, bf16[1536,1536]{1,0:T(8,128)(2,1)S(1)} %bitcast.216), kind=kOutput, calls=%fused_computation.161 | convolution fusion | flops 4831838208 | bytes 14155776 | tf_op jit(solution)/shard_map/dot_general | solution.py:53
  418.1 9.0 %convolution_convert_fusion.2.grad_ref = bf16[1536,1920]{1,0:T(8,128)(2,1)} fusion(bf16[1024,384]{1,0:T(8,128)(2,1)S(1)} %copy-done.14, bf16[1024,1536]{1,0:T(8,128)(2,1)S(1)} %fusion.31, bf16[1,1024,1536]{2,1,0:T(8,128)(2,1)S(1)} %copy-done.2, f32[1536]{0:T(1024)S(1)} %copy-done.30, f32[1024]{0:T(1024)S(1)} %copy-done.28), kind=kOutput, calls=%fused_computation.5 | convolution fusion | flops 6056902656 | bytes 12986368 | tf_op jit(solution)/shard_map/dot_general | solution.py:53
  428.3 10.8 %multiply_reduce_fusion = (f32[1024]{0:T(1024)}, f32[1536]{0:T(1024)S(1)}, bf16[1024,1536]{1,0:T(8,128)(2,1)}, f32[1024,1536]{1,0:T(8,128)}) fusion(bf16[1,1024,1536]{2,1,0:T(8,128)(2,1)} %get-tuple-element.60, f32[1536]{0:T(1024)S(1)} %copy-done.30, f32[1024]{0:T(1024)S(1)} %copy-done.28, bf16[1024,384]{1,0:T(8,128)(2,1)S(1)} %copy-done.14, ...), kind=kOutput, calls=%fused_computation.12 | convolution fusion | flops 1226831360 | bytes 26833664 | tf_op jit(solution)/shard_map/dot_general | solution.py:53
  439.8 15.5 %collective-permute-done.14 = bf16[192,1536]{1,0:T(8,128)(2,1)S(1)} collective-permute-done((bf16[192,1536]{1,0:T(8,128)(2,1)S(1)}, bf16[192,1536]{1,0:T(8,128)(2,1)S(1)}, u32[]{:S(2)}, u32[]{:S(2)}) %collective-permute-start.14) | collective-permute-done | bytes 589856 | tf_op jit(solution)/shard_map/ppermute | solution.py:26
  456.1 93.1 %finish.1 = (bf16[1024,384]{1,0:T(8,128)(2,1)}, bf16[1024,384]{1,0:T(8,128)(2,1)}, f32[192,768]{1,0:T(8,128)}, f32[192,512]{1,0:T(8,128)}, f32[160,128]{1,0:T(8,...) custom-call(bf16[1024,1536]{1,0:T(8,128)(2,1)} %get-tuple-element.143.part_ref, ...), custom_call_target="tpu_custom_call" | custom-call | tf_op jit(solution)/shard_map/finish/pallas_call | solution.py:875
  569.2 2.3 fusion.13
  (246 shorter events, 70.0 us)
Async XLA Ops:
  7.2 182.8 %all-gather.2.cloned.1.call-start = ((), (), s32[]{:S(2)}) async-start(), calls=%async_computation.1 | async-start | bytes 5308416 | tf_op jit(solution)/shard_map/all_gather | solution.py:1005
  10.9 96.9 %copy-start.12 = (bf16[192,768]{1,0:T(8,128)(2,1)S(1)}, bf16[192,768]{1,0:T(8,128)(2,1)}, u32[]{:S(2)}) copy-start(bf16[192,768]{1,0:T(8,128)(2,1)} %out_ref.1) | copy-start | bytes 884740
  109.8 317.3 %reduce-scatter.2.cloned.1.call-start = ((), (), s32[]{:S(2)}) async-start(), calls=%async_computation.2 | async-start | bytes 10616832 | tf_op jit(solution)/shard_map/reduce_scatter | solution.py:1153
  112.5 57.4 %collective-permute-start.2 = (bf16[1,1024,384]{2,1,0:T(8,128)(2,1)}, bf16[1,1024,384]{2,1,0:T(8,128)(2,1)}, u32[]{:S(2)}, u32[]{:S(2)}) collective-permute-start(bf16[1,1024,384]{2,1,0:T(8,128)(2,1)} %get-tuple-element.67), channel_id=1, source_target_pairs={{0,1},{1,0},{2,3},{3,2},{4,5},{5,4},{6,7},{7,6},{8,9},{9,8},{10,11... | collective-permute-start | bytes 2359304 | tf_op jit(solution)/shard_map/ppermute | solution.py:26
  112.5 54.6 %collective-permute-start.3 = (bf16[1,1024,384]{2,1,0:T(8,128)(2,1)}, bf16[1,1024,384]{2,1,0:T(8,128)(2,1)}, u32[]{:S(2)}, u32[]{:S(2)}) collective-permute-start(bf16[1,1024,384]{2,1,0:T(8,128)(2,1)} %get-tuple-element.68), channel_id=1, source_target_pairs={{0,2},{1,3},{2,0},{3,1},{4,6},{5,7},{6,4},{7,5},{8,10},{9,11},{10,... | collective-permute-start | bytes 2359304 | tf_op jit(solution)/shard_map/ppermute | solution.py:26
  115.5 149.0 %copy-start.29 = (f32[1536]{0:T(1024)}, f32[1536]{0:T(1024)S(1)}, u32[]{:S(2)}) copy-start(f32[1536]{0:T(1024)S(1)} %mul.238) | copy-start | bytes 18436
  116.3 163.6 %copy-start.27 = (f32[1024]{0:T(1024)}, f32[1024]{0:T(1024)S(1)}, u32[]{:S(2)}) copy-start(f32[1024]{0:T(1024)S(1)} %get-tuple-element.176) | copy-start | bytes 12292
  118.9 23.5 %collective-permute-start.1 = (bf16[1,3,256]{2,1,0:T(4,128)(2,1)S(1)}, bf16[1,3,256]{2,1,0:T(4,128)(2,1)S(1)}, u32[]{:S(2)}, u32[]{:S(2)}) collective-permute-start(bf16[1,3,256]{2,1,0:T(4,128)(2,1)S(1)} %slice.350), channel_id=1, source_target_pairs={{0,4},{1,5},{2,6},{3,7},{8,12},{9,13},{10,14},{11,15},{16,20},{17,... | collective-permute-start | bytes 4616 | tf_op jit(solution)/shard_map/ppermute | solution.py:32
  127.9 14.4 %collective-permute-start = (bf16[1,3,1536]{2,1,0:T(4,128)(2,1)S(1)}, bf16[1,3,1536]{2,1,0:T(4,128)(2,1)S(1)}, u32[]{:S(2)}, u32[]{:S(2)}) collective-permute-start(bf16[1,3,1536]{2,1,0:T(4,128)(2,1)S(1)} %slice.348), channel_id=1, source_target_pairs={{0,4},{1,5},{2,6},{3,7},{8,12},{9,13},{10,14},{11,15},{16,20},{17,... | collective-permute-start | bytes 27656 | tf_op jit(solution)/shard_map/ppermute | solution.py:32
  143.0 24.0 %copy-start.49 = (s32[2]{0:T(128)S(1)}, s32[2]{0:T(128)}, u32[]{:S(2)}) copy-start(s32[2]{0:T(128)} %param.17) | copy-start | bytes 28
  165.1 3.2 collective-permute-start.5
  167.1 19.1 %collective-permute-start.4 = (bf16[1,1024,384]{2,1,0:T(8,128)(2,1)}, bf16[1,1024,384]{2,1,0:T(8,128)(2,1)S(1)}, u32[]{:S(2)}, u32[]{:S(2)}) collective-permute-start(bf16[1,1024,384]{2,1,0:T(8,128)(2,1)} %collective-permute-done.3), channel_id=1, source_target_pairs={{0,1},{1,0},{2,3},{3,2},{4,5},{5,4},{6,7},{7,6},{8,9},{9,8},{10,11... | collective-permute-start | bytes 2359304 | tf_op jit(solution)/shard_map/ppermute | solution.py:26
  230.0 4.2 collective-permute-start.6
  275.3 4.6 collective-permute-start.12
  282.8 21.5 %collective-permute-start.7 = (bf16[1,128,1536]{2,1,0:T(8,128)(2,1)}, bf16[1,128,1536]{2,1,0:T(8,128)(2,1)S(1)}, u32[]{:S(2)}, u32[]{:S(2)}) collective-permute-start(bf16[1,128,1536]{2,1,0:T(8,128)(2,1)} %fusion.21), channel_id=1, source_target_pairs={{4,0},{5,1},{6,2},{7,3},{12,8},{13,9},{14,10},{15,11},{20,16},{21,... | collective-permute-start | bytes 1179656 | tf_op jit(solution)/shard_map/ppermute | solution.py:32
  289.9 81.1 %collective-permute-start.9 = (bf16[1024,384]{1,0:T(8,128)(2,1)}, bf16[1024,384]{1,0:T(8,128)(2,1)}, u32[]{:S(2)}, u32[]{:S(2)}) collective-permute-start(bf16[1024,384]{1,0:T(8,128)(2,1)} %convolution_convert_fusion.7), channel_id=1, source_target_pairs={{0,1},{1,0},{2,3},{3,2},{4,5},{5,4},{6,7},{7,6},{8,9},{9,8},{10,11... | collective-permute-start | bytes 2359304 | tf_op jit(solution)/shard_map/ppermute | solution.py:26
  301.3 65.1 %collective-permute-start.10 = (bf16[1024,384]{1,0:T(8,128)(2,1)}, bf16[1024,384]{1,0:T(8,128)(2,1)}, u32[]{:S(2)}, u32[]{:S(2)}) collective-permute-start(bf16[1024,384]{1,0:T(8,128)(2,1)} %convolution_convert_fusion.6), channel_id=1, source_target_pairs={{0,1},{1,0},{2,3},{3,2},{4,5},{5,4},{6,7},{7,6},{8,9},{9,8},{10,11... | collective-permute-start | bytes 2359304 | tf_op jit(solution)/shard_map/ppermute | solution.py:26
  306.6 55.7 %copy-start.31 = (f32[1536]{0:T(1024)S(1)}, f32[1536]{0:T(1024)}, u32[]{:S(2)}) copy-start(f32[1536]{0:T(1024)} %reduce.8) | copy-start | bytes 18436
  306.6 55.7 %copy-start.45 = (f32[24]{0:T(128)S(1)}, f32[24]{0:T(128)}, u32[]{:S(2)}) copy-start(f32[24]{0:T(128)} %reduce_sum.37) | copy-start | bytes 292
  360.3 4.8 collective-permute-start.13
  363.8 7.1 %collective-permute-start.8 = (f32[1,8,1536]{2,1,0:T(8,128)}, f32[1,8,1536]{2,1,0:T(8,128)S(1)}, u32[]{:S(2)}, u32[]{:S(2)}) collective-permute-start(f32[1,8,1536]{2,1,0:T(8,128)} %get-tuple-element.86), channel_id=1, source_target_pairs={{4,0},{5,1},{6,2},{7,3},{12,8},{13,9},{14,10},{15,11},{20,16},{21,... | collective-permute-start | bytes 147464 | tf_op jit(solution)/shard_map/ppermute | solution.py:32
  366.4 44.6 %slice-start.2 = ((s8[4718592]{0:T(1024)(128)(4,1)}), s8[4194304]{0:T(1024)(128)(4,1)S(1)}, s32[]{:S(2)}) async-start(s8[4718592]{0:T(1024)(128)(4,1)} %bitcast.215), calls=%async_computation.5 | async-start | bytes 8388608
  370.9 38.2 %collective-permute-start.11 = (bf16[1024,384]{1,0:T(8,128)(2,1)S(1)}, bf16[1024,384]{1,0:T(8,128)(2,1)S(1)}, u32[]{:S(2)}, u32[]{:S(2)}) collective-permute-start(bf16[1024,384]{1,0:T(8,128)(2,1)S(1)} %add_convert_fusion), channel_id=1, source_target_pairs={{0,2},{1,3},{2,0},{3,1},{4,6},{5,7},{6,4},{7,5},{8,10},{9,11},{10,... | collective-permute-start | bytes 2359304 | tf_op jit(solution)/shard_map/ppermute | solution.py:26
  371.0 38.2 %copy-start.25 = (f32[2,1024]{1,0:T(2,128)S(1)}, f32[2,1024]{1,0:T(2,128)}, u32[]{:S(2)}) copy-start(f32[2,1024]{1,0:T(2,128)} %copy-done.24) | copy-start | bytes 24580
  371.0 40.1 %slice-start.3 = ((s8[4718592]{0:T(1024)(128)(4,1)}), s8[524288]{0:T(1024)(128)(4,1)S(1)}, s32[]{:S(2)}) async-start(s8[4718592]{0:T(1024)(128)(4,1)} %bitcast.215), calls=%async_computation.6 | async-start | bytes 1048576
  374.4 34.8 %copy-start = (bf16[2,1024,384]{2,1,0:T(8,128)(2,1)S(1)}, bf16[2,1024,384]{2,1,0:T(8,128)(2,1)}, u32[]{:S(2)}) copy-start(bf16[2,1024,384]{2,1,0:T(8,128)(2,1)} %x_ref.1) | copy-start | bytes 4718596
  418.1 10.2 %copy-start.9 = (bf16[1536,12]{1,0:T(8,128)(2,1)S(1)}, bf16[1536,12]{1,0:T(8,128)(2,1)}, u32[]{:S(2)}) copy-start(bf16[1536,12]{1,0:T(8,128)(2,1)} %copy-done.8) | copy-start | bytes 110596
  418.1 10.2 %copy-start.11 = (bf16[1536,12]{1,0:T(8,128)(2,1)S(1)}, bf16[1536,12]{1,0:T(8,128)(2,1)}, u32[]{:S(2)}) copy-start(bf16[1536,12]{1,0:T(8,128)(2,1)} %copy-done.10) | copy-start | bytes 110596
  418.1 10.2 %copy-start.40 = (bf16[384]{0:T(512)(128)(2,1)S(1)}, bf16[384]{0:T(512)(128)(2,1)}, u32[]{:S(2)}) copy-start(bf16[384]{0:T(512)(128)(2,1)} %copy-done.39) | copy-start | bytes 2308
  428.2 27.0 %collective-permute-start.14 = (bf16[192,1536]{1,0:T(8,128)(2,1)S(1)}, bf16[192,1536]{1,0:T(8,128)(2,1)S(1)}, u32[]{:S(2)}, u32[]{:S(2)}) collective-permute-start(bf16[192,1536]{1,0:T(8,128)(2,1)S(1)} %pad_maximum_fusion.5), channel_id=1, source_target_pairs={{0,2},{1,3},{2,0},{3,1},{4,6},{5,7},{6,4},{7,5},{8,10},{9,11},{10,... | collective-permute-start | bytes 1769480 | tf_op jit(solution)/shard_map/ppermute | solution.py:26
  456.1 105.1 %copy-start.13 = (bf16[192,3072]{1,0:T(8,128)(2,1)S(1)}, bf16[192,3072]{1,0:T(8,128)(2,1)}, u32[]{:S(2)}) copy-start(bf16[192,3072]{1,0:T(8,128)(2,1)} %reduce-scatter.2.cloned.1.call-done) | copy-start | bytes 3538948
  456.1 105.1 %copy-start.20 = (bf16[192,1536]{1,0:T(8,128)(2,1)S(1)}, bf16[192,1536]{1,0:T(8,128)(2,1)}, u32[]{:S(2)}) copy-start(bf16[192,1536]{1,0:T(8,128)(2,1)} %copy-done.19) | copy-start | bytes 1769476
  (46 other events, 228.7 us)
Sparse Core Ops, SparseCore 0:
  109.9 36.9 all-gather.1
  275.4 74.0 reduce-scatter.1

commit v4 on v3

--- a/solution.py
+++ b/solution.py
@@ -579,9 +579,9 @@
 
 
 def fetch_kernel(
-    x_ref, inner_ref, gate_ref, step_ref, wr_ref, out_ref, small_ref,
-    full_x, full_inner, full_gate, full_step, full_wr, out_far, full_small,
-    x_own, inner_own, gate_own, step_own, wr_own, small_own, send_sem, recv_sem, local_sem,
+    x_ref, inner_ref, late_ref, step_ref, wr_ref, small_ref,
+    full_x, full_inner, late_far, full_step, full_wr, full_small,
+    x_own, inner_own, step_own, wr_own, small_own, send_sem, recv_sem, local_sem,
 ):
     f, c, z = lax.axis_index("fsdp"), lax.axis_index("ctx"), lax.axis_index("tp")
     half = z // 2
@@ -647,8 +647,7 @@
         send(x_ref.at[other, pl.ds(piece * i, piece)], full_x.at[:, pl.ds(piece * i, piece), feature(z)], 5)
         for i in range(FAR_PARTS)
     ]
-    far_gate = send(gate_ref, shard(full_gate, f, 1), 5)
-    send(out_ref, out_far, 5)
+    send(late_ref, late_far, 5)
     own_inner = spread(full_inner, inner_ref, 0)
     own_step = spread(full_step, step_ref, 0)
     own_wr = spread(full_wr, wr_ref, 0, shard_one)
@@ -656,7 +655,6 @@
     staged = (
         (x_ref.at[mine], x_own, full_x.at[:, :, feature(z)]),
         (inner_ref, inner_own, shard(full_inner, f, 0)),
-        (gate_ref, gate_own, shard(full_gate, f, 0)),
         (step_ref, step_own, shard(full_step, f, 0)),
         (wr_ref, wr_own, shard_one(full_wr, f, 0)),
         (small_ref, small_own, full_small.at[z]),
@@ -675,7 +673,6 @@
     away_inner = spread(full_inner, shard(full_inner, f, 1), 1)
     arrived(far_step)
     away_step = spread(full_step, shard(full_step, f, 1), 1)
-    own_gate = spread(full_gate, gate_ref, 0)
 
     def both(i):
         arrived(far_x[i])
@@ -690,11 +687,7 @@
     relay(full_step, away_step, 1)
     both(1)
     both(2)
-    relay(full_gate, own_gate, 0)
     both(3)
-    arrived(far_gate)
-    away_gate = spread(full_gate, shard(full_gate, f, 1), 1)
-    relay(full_gate, away_gate, 1)
     for store in stores:
         store.wait()
     for copy, done in copies:
@@ -703,38 +696,36 @@
         copy.wait_send()
 
 
-def fetch(hidden, inner, gate, step, wr, out, small):
+def fetch(hidden, inner, late, step, wr, small):
     slot_count, seq, cols = hidden.shape
     slots, depth = slot_count // 2, inner.shape[0]
     total = 8 * depth
-    count = 1 + 2 * FAR_PARTS + 3 + 7 * 7 + 4
+    count = 1 + 2 * FAR_PARTS + 3 + 5 * 7 + 3
     anywhere = pl.BlockSpec(memory_space=pl.ANY)
     full = lambda x: jax.ShapeDtypeStruct((total, 2 * x.shape[1]), BF16)
     return pl.pallas_call(
         fetch_kernel,
-        in_specs=[anywhere] * 7,
-        out_specs=[anywhere] * 7,
+        in_specs=[anywhere] * 6,
+        out_specs=[anywhere] * 6,
         out_shape=[
             jax.ShapeDtypeStruct((slots, seq, 4 * cols), BF16),
-            full(inner), full(gate), full(step),
+            full(inner), jax.ShapeDtypeStruct(late.shape, BF16), full(step),
             jax.ShapeDtypeStruct((total, wr.shape[1]), BF16),
-            jax.ShapeDtypeStruct(out.shape, BF16),
             jax.ShapeDtypeStruct((4,) + small.shape, F32),
         ],
         scratch_shapes=[
             pltpu.VMEM((slots, seq, cols), BF16),
             pltpu.VMEM(inner.shape, BF16),
-            pltpu.VMEM(gate.shape, BF16),
             pltpu.VMEM(step.shape, BF16),
             pltpu.VMEM(wr.shape, BF16),
             pltpu.VMEM(small.shape, F32),
             pltpu.SemaphoreType.DMA((count,)),
             pltpu.SemaphoreType.DMA((count,)),
-            pltpu.SemaphoreType.DMA((2, 6)),
+            pltpu.SemaphoreType.DMA((2, 5)),
         ],
         compiler_params=pltpu.CompilerParams(collective_id=0, has_side_effects=True),
         name="fetch",
-    )(hidden, inner, gate, step, wr, out, small)
+    )(hidden, inner, late, step, wr, small)
 
 
 def finish_kernel(
@@ -795,39 +786,44 @@
     relays = [
         send(part_ref.at[pl.ds(piece * i, piece), feature(z ^ 3)], relay_buf.at[i], 4) for i in range(FAR_PARTS)
     ]
-    for load in loads[:4]:
-        load.wait()
-    plane = []
-    for k in (1, 2, 3):
-        arrived(core_of[k])
-        sent_buf[k - 1] = (own_buf[k].astype(F32) + core_buf[k].astype(F32)).astype(BF16)
-        plane.append(send(sent_buf.at[k - 1], plane_buf.at[k - 1], k - 1))
-    arrived(cross[0])
-    cross_out[...] = cross_ref[...] + cross_got[...]
-    arrived(small[0])
-    small_out[...] = small_ref[...] + small_got[0]
-    small.append(send(small_out, small_got.at[1], 0))
-    cross.append(send(cross_out, cross_far, 5))
-
     def passed_on(i):
         loads[4 + i].wait()
         arrived(relays[i])
         sum_buf[i] = (part_buf[i].astype(F32) + relay_buf[i].astype(F32)).astype(BF16)
         send(sum_buf.at[i], other_out.at[pl.ds(piece * i, piece)], 5)
 
-    passed_on(0)
+    arrived(small[0])
+    small_out[...] = small_ref[...] + small_got[0]
+    small.append(send(small_out, small_got.at[1], 0))
+    arrived(cross[0])
+    cross_out[...] = cross_ref[...] + cross_got[...]
+    cross.append(send(cross_out, cross_far, 5))
+    for load in loads[:4]:
+        load.wait()
+    for k in (1, 2):
+        arrived(core_of[k])
+        sent_buf[k - 1] = (own_buf[k].astype(F32) + core_buf[k].astype(F32)).astype(BF16)
     arrived(small[1])
     copies[small[1]][0].wait_send()
     small_out[...] = small_out[...] + small_got[1]
     small.append(send(small_out, small_got.at[2], 1))
-    passed_on(1)
-    arrived(core_of[0])
-    passed_on(2)
+    plane = [send(sent_buf.at[0], plane_buf.at[0], 0)]
+    arrived(core_of[3])
+    sent_buf[2] = (own_buf[3].astype(F32) + core_buf[3].astype(F32)).astype(BF16)
+    plane.append(send(sent_buf.at[1], plane_buf.at[1], 1))
+    plane.append(send(sent_buf.at[2], plane_buf.at[2], 2))
     arrived(small[2])
     copies[small[2]][0].wait_send()
     small_out[...] = small_out[...] + small_got[2]
     small.append(send(small_out, small_got.at[3], 4))
-    passed_on(3)
+    for i in range(FAR_PARTS):
+        passed_on(i)
+    arrived(core_of[0])
+    arrived(small[3])
+    copies[small[3]][0].wait_send()
+    shared = small_out.shape[0] // 2
+    small_out[shared:, :] = small_out[shared:, :] + small_got[3, shared:, :]
+    small.append(send(small_out, small_far, 5))
     total = own_buf[0].astype(F32) + core_buf[0].astype(F32)
     for at in plane:
         arrived(at)
@@ -835,21 +831,18 @@
         total = total + plane_buf[k].astype(F32)
     wr_send[...] = total[:, 2 * inner : 2 * inner + 2 * STATE]
     wr = send(wr_send, wr_got, 4)
-    send(part_ref.at[:, feature(z ^ 1)], near_out, 4)
+    middle = tokens // 2
+    send(part_ref.at[pl.ds(0, middle), feature(z ^ 1)], near_out.at[pl.ds(0, middle)], 4)
     home_out[...] = total[:, :inner]
     home_buf[:, :inner] = total[:, inner : 2 * inner].astype(BF16)
     narrow_out[:, 2 * STATE : 2 * STATE + 128] = total[:, 2 * inner + 2 * STATE :]
     home_buf[:, inner + 2 * STATE :] = total[:, 2 * inner + 2 * STATE :].astype(BF16)
-    arrived(small[3])
-    copies[small[3]][0].wait_send()
-    shared = small_out.shape[0] // 2
-    small_out[shared:, :] = small_out[shared:, :] + small_got[3, shared:, :]
-    small.append(send(small_out, small_far, 5))
     arrived(wr)
     both = wr_send[...] + wr_got[...]
     narrow_out[:, : 2 * STATE] = both
     home_buf[:, inner : inner + 2 * STATE] = both.astype(BF16)
     last = send(home_buf, got_buf, 5)
+    send(part_ref.at[pl.ds(middle, middle), feature(z ^ 1)], near_out.at[pl.ds(middle, middle)], 4)
     arrived(last)
     home_out[...] += got_buf[:, :inner].astype(F32)
     narrow_out[:, : 2 * STATE] += got_buf[:, inner : inner + 2 * STATE].astype(F32)
@@ -871,7 +864,7 @@
     inner = (total - rest) // 2
     anywhere = pl.BlockSpec(memory_space=pl.ANY)
     vmem = pl.BlockSpec(memory_space=pltpu.VMEM)
-    count = 4 + 5 + 2 + FAR_PARTS * 2 + 1 + 3 + 2
+    count = 4 + 5 + 2 + FAR_PARTS * 2 + 2 + 3 + 2
     return pl.pallas_call(
         finish_kernel,
         in_specs=[anywhere, anywhere, vmem, vmem],
@@ -985,10 +978,15 @@
             [lower(a0, b0), lower(a1, b1), lower(b0, a0), lower(b1, a1)], axis=axis
         )
 
+    ready = []
+
     def own_features(piece):
-        relay = swap(piece(place ^ 3).astype(BF16), 1)
-        keep = swap(piece(place ^ 1).astype(BF16), 1)
-        sent = swap((piece(place ^ 2) + relay.astype(F32)).astype(BF16), 2)
+        first, second = piece(place ^ 3).astype(BF16), piece(place ^ 1).astype(BF16)
+        relay = swap(first, 1)
+        keep = swap(second, 1)
+        summed = (piece(place ^ 2) + relay.astype(F32)).astype(BF16)
+        ready.extend([first, second, summed])
+        sent = swap(summed, 2)
         kept = (piece(place) + keep.astype(F32)).reshape(slots, seq_here, width_here)
         other = sent.astype(F32).reshape(slots, seq_here, width_here)
         return both_halves(kept, other)
@@ -1014,9 +1012,11 @@
         step_shard = jnp.concatenate([proj_step, zeros(proj_step, 128 - heads_own)], axis=1)
         small = pack([norm_gain.astype(F32), own_small])
         small = jnp.pad(small, (0, -small.size % 1024)).reshape(-1, 128)
-        full_x, full_inner, full_gate, full_step, full_wr, out_far, full_small = fetch(
-            hidden_in, inner_shard, gate_shard, step_shard, proj_write_read, proj_out, small
-        )
+        late_shard = jnp.concatenate([gate_shard, proj_out], axis=1)
+        full_x, full_inner, late_far, full_step, full_wr, full_small = fetch(
+            hidden_in, inner_shard, late_shard, step_shard, proj_write_read, small
+        )
+        gate_far, out_far = late_far[:, :inner_own], late_far[:, inner_own:]
         full_small = full_small.reshape(tp_count, -1)
         full_gain = full_small[:, :width_here].reshape(width)
         far_row = lax.dynamic_slice_in_dim(full_small, place ^ 2, 1, 0)[0, width_here:]
@@ -1037,19 +1037,18 @@
         gate_far = swap(after(gate_shard, x_far), 2)
         x_both = swap(x_far, 1)
         cot_dep = after(x_both, gate_far)
+        out_far = swap(after(proj_out, cot_dep), 2)
         full_narrow = gathered(narrow_shard)
         full_inner = gathered(jnp.concatenate([inner_shard, inner_far], axis=1))
-        full_gate = gathered(jnp.concatenate([after(gate_shard, full_inner), gate_far], axis=1))
         full_x = ordered(x_mine, x_near, x_far, x_both, 2)
-        out_far = swap(after(proj_out, cot_dep), 2)
         gain = norm_gain.astype(F32)
         full_gain = ordered(gain, swap(gain, 1), swap(gain, 2), swap(gain, 3), 0)
         far_small = unpack(swap(own_small, 2), small_shapes)
     full_x = full_x.reshape(tokens, width)
-    cot_near = swap(after(cot_mine, cot_dep), 1)
-    cot_far = swap(after(cot_other, cot_dep), 2)
-    cot_both = swap(cot_far, 1)
-    full_out = gathered(jnp.concatenate([after(proj_out, full_gate), out_far], axis=1))
+    full_late = gathered(jnp.concatenate([gate_shard, gate_far, proj_out, out_far], axis=1))
+    full_gate, full_out = full_late[:, :inner], full_late[:, inner:]
+    cot_mine, cot_other, cot_dep = lax.optimization_barrier((cot_mine, cot_other, cot_dep))
+    cot_near, cot_far, cot_both = swap(cot_mine, 1), swap(cot_other, 2), swap(cot_other, 3)
     full_cot = ordered(cot_mine, cot_near, cot_far, cot_both, 2).reshape(tokens, width)
 
     taps = jnp.concatenate([conv_inner, far_small[0]], axis=1)
@@ -1114,6 +1113,7 @@
 
     branch = own_features(branch_piece)
     hidden_out = (hidden_in.astype(F32) + valid_rows[..., None] * branch).astype(BF16)
+    normed_out, grad_gate_pre, *_ = lax.optimization_barrier((normed_out, grad_gate_pre, ready[0], ready[1]))
     grad_proj_out = dot(masked, normed_out, 0, 0).astype(BF16)
     grad_gate_w = dot(normed, grad_gate_pre, 0, 0).astype(BF16)
     grad_by_gate = dot(grad_gate_pre, full_gate, 1, 1)
@@ -1129,7 +1129,7 @@
         flowing = decay_lanes[:, position] * flowing + local_grad[:, position]
     flows = jnp.stack(flow_list, axis=1)
     flows_low = flows.astype(BF16).reshape(blocks, STATE, inner)
-    flows_low = after(flows_low, (grad_proj_out, grad_gate_w))
+    flows_low = after(flows_low, (grad_proj_out, grad_gate_w, ready[2]))
 
     grad_inner_pre, grad_narrow, tap_sums, narrow_sums, head_sums, halo, narrow_halo = back_blocks(
         inner_act, mixed_out, grad_diag, slope, inner_pre, inner_rim, write_read, narrow_slope, narrow_pre,
@@ -1153,11 +1153,11 @@
         return lax.psum_scatter(x, ("fsdp", "ctx"), scatter_dimension=0, tiled=True)
 
     early = reduced(jnp.concatenate([grad_proj_out, grad_gate_w], axis=1))
+    grad_inner_pre, hidden_out, early = lax.optimization_barrier((grad_inner_pre, hidden_out, early))
     early_far = swap(jnp.concatenate([early[:, inner_own:inner], early[:, inner + inner_own :]], axis=1), 2)
     grad_out_home = early[:, :inner_own].astype(F32) + early_far[:, :inner_own].astype(F32)
     grad_gate_home = early[:, inner : inner + inner_own].astype(F32) + early_far[:, inner_own:].astype(F32)
 
-    grad_inner_pre, hidden_out = lax.optimization_barrier((grad_inner_pre, hidden_out))
     late = jnp.concatenate([grad_inner_pre, grad_narrow], axis=1)
     grad_late_w = dot(normed, late, 0, 0).astype(BF16)
     partial_normed = (

time: 586 us -> 532 us (0.908)
  waiting for transfers between devices: 74.2 us -> 25.6 us
  Pallas kernels: 307 us -> 294 us
  local copies, waits for them, and re-layouts: 34.9 us -> 40.8 us
    ppermute x9, waiting for transfers between devices: 73.6 us -> 24.4 us  [swap(): return lax.ppermute(x, 'tp', [(i, i ^ bit) for i in range(count)])]
    pallas_call x1, Pallas kernels: 93 us -> 83 us  [fetch(): pl.pallas_call(fetch_kernel, in_specs=[anywhere] * 6, out_specs=[anywhere...]
    ppermute x9, starting transfers between devices: 6.17 us -> 12.1 us  [swap(): return lax.ppermute(x, 'tp', [(i, i ^ bit) for i in range(count)])]
  transfers between devices with their start and end apart: 17 -> 17, of which waited for: 6 -> 5; matrix products, arithmetic and copies ran while one was open for 17% -> 17% of each run, Pallas kernels for 12% -> 13%
where the time goes in v4:
time: 532 us; the launch traced here: 525 us
  Pallas kernels  294 us (55%)
  matrix products  86.2 us (16%)
  other arithmetic  42.3 us (8%)
  local copies, waits for them, and re-layouts  40.8 us (8%)
  waiting for transfers between devices  25.6 us (5%)
  starting transfers between devices  20.7 us (4%)
  between operations  15.5 us (3%)
    pallas_call x1, Pallas kernels, finish(): pl.pallas_call(finish_kernel, in_specs=[anywhere, anywhere, vmem, vmem],...  89 us
    dot_general x14, matrix products, dot(): lax.dot_general(a, b, (((da,), (db,)), ((), ())), preferred_element_type=...  86.2 us
    pallas_call x1, Pallas kernels, fetch(): pl.pallas_call(fetch_kernel, in_specs=[anywhere] * 6, out_specs=[anywhere...  83 us
    pallas_call x1, Pallas kernels, back_blocks(): pl.pallas_call(functools.partial(back_kernel, groups, heads), grid=(block...  52.2 us
    pallas_call x1, Pallas kernels, mix_blocks(): pl.pallas_call(functools.partial(mix_kernel, heads), grid=(blocks, steps)...  30.3 us
    ppermute x9, waiting for transfers between devices, swap(): return lax.ppermute(x, 'tp', [(i, i ^ bit) for i in range(count)])  24.4 us
    pallas_call x1, Pallas kernels, gate_blocks(): pl.pallas_call(functools.partial(gate_kernel, heads), grid=(steps, blocks...  20.6 us
    pallas_call x1, Pallas kernels, start_blocks(): pl.pallas_call(functools.partial(start_kernel, groups, heads), grid=(bloc...  18.4 us
  transfers between devices with their start and end apart: 17, of which 5 were waited for; matrix products, arithmetic and copies ran while one was open for 17% of the time, Pallas kernels for 13%

profile of v4, /device:TPU:0, one launch (start us, length us, event | category | flops | bytes accessed | tf_op | source)
XLA Modules:
  0.0 524.7 jit_solution(17787246662904200958)
XLA Ops:
  10.9 2.3 fusion.65
  15.5 83.0 %fetch.1 = (bf16[1,1024,1536]{2,1,0:T(8,128)(2,1)}, bf16[1536,1536]{1,0:T(8,128)(2,1)}, bf16[192,1536]{1,0:T(8,128)(2,1)}, bf16[1536,256]{1,0:T(8,128)(2,1)}, bf...) custom-call(bf16[2,1024,384]{2,1,0:T(8,128)(2,1)} %x_ref.1, bf16[192,768]{1,0:T(8,128)(2,1)} %get-tuple-element.185.inner_ref, ...), custom_call_target="tpu_custom_call" | custom-call | tf_op jit(solution)/shard_map/fetch/pallas_call | solution.py:706
  99.6 2.3 pad_maximum_fusion.3
  102.0 2.7 constant_dynamic-slice_fusion.1
  106.1 2.9 collective-permute-start.2
  114.0 5.5 %convolution_convert_fusion.4.inner_ref.pre_ref = bf16[1024,1536]{1,0:T(8,128)(2,1)S(1)} fusion(bf16[1536,1536]{1,0:T(8,128)(2,1)S(1)} %bitcast.213, bf16[1,1024,1536]{2,1,0:T(8,128)(2,1)S(1)} %copy-done.1, f32[1536]{0:T(1024)S(1)} %mul.238, f32[1024]{0:T(1024)S(1)} %get-tuple-element.180), kind=kOutput, calls=%fused_computation.26 | convolution fusion | flops 4839702528 | bytes 11020288 | tf_op jit(solution)/shard_map/dot_general | solution.py:53
  127.1 18.4 %start_blocks.1 = (bf16[1024,1536]{1,0:T(8,128)(2,1)}, bf16[1024,1536]{1,0:T(8,128)(2,1)}, bf16[1024,256]{1,0:T(8,128)(2,1)}, f32[1024,256]{1,0:T(8,128)}, f32[1...) custom-call(bf16[1024,1536]{1,0:T(8,128)(2,1)} %copy-done.6, ...), custom_call_target="tpu_custom_call" | custom-call | flops 434110464 | bytes 12582912 | tf_op jit(solution)/shard_map/start_blocks/pallas_call | solution.py:146
  153.6 2.8 collective-permute-done.2
  156.4 15.9 %collective-permute-done.3 = bf16[1,1024,384]{2,1,0:T(8,128)(2,1)} collective-permute-done((bf16[1,1024,384]{2,1,0:T(8,128)(2,1)}, bf16[1,1024,384]{2,1,0:T(8,128)(2,1)}, u32[]{:S(2)}, u32[]{:S(2)}) %collective-permute-start.3) | collective-permute-done | bytes 786464 | tf_op jit(solution)/shard_map/ppermute | solution.py:26
  172.3 4.0 broadcast_select_fusion.7
  176.2 9.4 %fusion.13.gate_ref = bf16[1024,1536]{1,0:T(8,128)(2,1)} fusion(bf16[1536,3072]{1,0:T(8,128)(2,1)} %all-gather.2.cloned.1.call-done, bf16[1,1024,1536]{2,1,0:T(8,128)(2,1)S(1)} %copy-done.1, f32[1536]{0:T(1024)S(1)} %mul.238, f32[1024]{0:T(1024)S(1)} %get-tuple-element.180), kind=kOutput, calls=%fused_computation.24 | convolution fusion | flops 4839702528 | bytes 11020288 | tf_op jit(solution)/shard_map/dot_general | solution.py:53
  185.7 6.7 %convolution_convert_fusion.3.gno_ref = bf16[1024,1536]{1,0:T(8,128)(2,1)} fusion(bf16[1536,3072]{1,0:T(8,128)(2,1)S(1)} %copy-done.8, bf16[1,1024,384]{2,1,0:T(8,128)(2,1)S(1)} %copy-done.27, bf16[1,1024,384]{2,1,0:T(8,128)(2,1)S(1)} %copy-done.25, bf16[1,1024,384]{2,1,0:T(8,128)(2,1)S(1)} %copy-done.23, bf16[1,1024,384]{2,1,0:T(8,128)(2,1)S(1)} %copy-done.21, ...), kind=kOutput, calls=%fused_computation.25 | convolution fusion | flops 4850712576 | bytes 11014144 | tf_op jit(solution)/shard_map/dot_general | solution.py:53
  192.3 30.3 %mix_blocks.1 = (f32[1024,1536]{1,0:T(8,128)}, f32[4,8,256]{2,1,0:T(8,128)}) custom-call(bf16[1024,1536]{1,0:T(8,128)(2,1)} %get-tuple-element.66.x_ref, bf16[1024,1536]{1,0:T(8,128)(2,1)} %fusion.13.gate_ref, bf16[1024,1536]{1,0:T(8,128)(2,1)} %convolution_convert_fusion.3.gno_ref, bf16[1024,256]{1,0:T(8,128)(2,1)} %get-tuple-element.70.wr_ref, ...), custom_call_target="tpu_custom_call" | custom-call | flops 4831838208 | bytes 15728640 | tf_op jit(solution)/shard_map/mix_blocks/pallas_call | solution.py:240
  222.8 4.8 slice.368
  228.2 20.6 %gate_blocks.1 = (bf16[1024,1536]{1,0:T(8,128)(2,1)}, bf16[1024,1536]{1,0:T(8,128)(2,1)}, bf16[1024,1536]{1,0:T(8,128)(2,1)}, f32[1,1536]{1,0:T(1,128)}, f32[1,1536]{1,0:T(1,128)}, /*index=5*/f32[4,128,1536]{2,1,0:T(8,128)}) custom-call(f32[1024,1536]{1,0:T(8,128)} %get-tuple-element.75.mixed_ref, bf16[1024,1536]{1,0:T(8,128)(2,1)} %fusion.13.gate_ref, ...), custom_call_target="tpu_custom_call" | custom-call | flops 402653184 | bytes 28311552 | tf_op jit(solution)/shard_map/gate_blocks/pallas_call | solution.py:308
  248.8 5.0 convolution_convert_fusion.5
  253.9 4.1 convolution_convert_fusion.6
  258.0 5.8 %convolution_convert_fusion.1 = bf16[1536,1536]{1,0:T(8,128)(2,1)S(1)} fusion(bf16[1024,1536]{1,0:T(8,128)(2,1)S(1)} %copy-done.58, bf16[1,1024,384]{2,1,0:T(8,128)(2,1)S(1)} %copy-done.28, bf16[1,1024,384]{2,1,0:T(8,128)(2,1)S(1)} %copy-done.26, bf16[1,1024,384]{2,1,0:T(8,128)(2,1)S(1)} %copy-done.24, bf16[1,1024,384]{2,1,0:T(8,128)(2,1)S(1)} %copy-done.22, ...), kind=kOutput, calls=%fused_computation.4 | convolution fusion | flops 4851499008 | bytes 11014144 | tf_op jit(solution)/shard_map/dot_general | solution.py:53
  263.8 5.9 %convolution_convert_fusion = bf16[1536,1536]{1,0:T(8,128)(2,1)S(1)} fusion(bf16[1024,1536]{1,0:T(8,128)(2,1)S(1)} %copy-done.60, bf16[1,1024,1536]{2,1,0:T(8,128)(2,1)S(1)} %copy-done.1, f32[1536]{0:T(1024)S(1)} %mul.238, f32[1024]{0:T(1024)S(1)} %get-tuple-element.180), kind=kOutput, calls=%fused_computation.3 | convolution fusion | flops 4840488960 | bytes 11020288 | tf_op jit(solution)/shard_map/dot_general | solution.py:53
  269.7 4.7 pad_maximum_fusion
  274.5 2.8 collective-permute-start.12
  284.0 10.2 %fusion.5 = f32[1024,1536]{1,0:T(8,128)} fusion(bf16[1024,1536]{1,0:T(8,128)(2,1)S(1)} %copy-done.61, bf16[1536,3072]{1,0:T(8,128)(2,1)} %all-gather.2.cloned.1.call-done), kind=kOutput, calls=%fused_computation.14 | convolution fusion | flops 4831838208 | bytes 14155776 | tf_op jit(solution)/shard_map/dot_general | solution.py:53
  302.7 4.2 add_convert_fusion
  306.9 2.6 collective-permute-start.11
  309.5 52.2 %back_blocks.1 = (bf16[1024,1536]{1,0:T(8,128)(2,1)}, bf16[1024,384]{1,0:T(8,128)(2,1)}, f32[4,8,384]{2,1,0:T(8,128)}, f32[8,256]{1,0:T(8,128)}, f32[8,128]{1,0:...) custom-call(bf16[1024,1536]{1,0:T(8,128)(2,1)} %get-tuple-element.66.x_ref, ...), custom_call_target="tpu_custom_call" | custom-call | flops 9663676416 | bytes 22020096 | tf_op jit(solution)/shard_map/back_blocks/pallas_call | solution.py:527
  368.5 4.3 add_bitcast_fusion.1
  377.7 8.2 %fusion.66 = f32[1024,1536]{1,0:T(8,128)S(1)} fusion(bf16[1024,1536]{1,0:T(8,128)(2,1)} %fusion.37, bf16[1536,1536]{1,0:T(8,128)(2,1)} %get-tuple-element.63), kind=kOutput, calls=%fused_computation.166 | convolution fusion | flops 4831838208 | bytes 14155776 | tf_op jit(solution)/shard_map/dot_general | solution.py:53
  385.9 9.1 %convolution_convert_fusion.2.grad_ref = bf16[1536,1920]{1,0:T(8,128)(2,1)} fusion(bf16[1024,384]{1,0:T(8,128)(2,1)S(1)} %fusion.40, bf16[1024,1536]{1,0:T(8,128)(2,1)S(1)} %copy-done.57, bf16[1,1024,1536]{2,1,0:T(8,128)(2,1)S(1)} %copy-done.2, f32[1536]{0:T(1024)S(1)} %copy-done.38, f32[1024]{0:T(1024)S(1)} %copy-done.36), kind=kOutput, calls=%fused_computation.5 | convolution fusion | flops 6056902656 | bytes 12986368 | tf_op jit(solution)/shard_map/dot_general | solution.py:53
  395.1 6.0 %multiply_reduce_fusion = (f32[1024]{0:T(1024)}, f32[1536]{0:T(1024)S(1)}, bf16[1024,1536]{1,0:T(8,128)(2,1)}, f32[1024,1536]{1,0:T(8,128)}) fusion(bf16[1,1024,1536]{2,1,0:T(8,128)(2,1)S(1)} %copy-done.2, f32[1536]{0:T(1024)S(1)} %copy-done.38, f32[1024]{0:T(1024)S(1)} %copy-done.36, bf16[1024,384]{1,0:T(8,128)(2,1)S(1)} %fusion.40, ...), kind=kOutput, calls=%fused_computation.12 | convolution fusion | flops 1226831360 | bytes 26833664 | tf_op jit(solution)/shard_map/dot_general | solution.py:53
  401.7 4.5 collective-permute-done.14
  406.2 89.0 %finish.1 = (bf16[1024,384]{1,0:T(8,128)(2,1)}, bf16[1024,384]{1,0:T(8,128)(2,1)}, f32[192,768]{1,0:T(8,128)}, f32[192,512]{1,0:T(8,128)}, f32[160,128]{1,0:T(8,...) custom-call(bf16[1024,1536]{1,0:T(8,128)(2,1)} %get-tuple-element.145.part_ref, ...), custom_call_target="tpu_custom_call" | custom-call | tf_op jit(solution)/shard_map/finish/pallas_call | solution.py:868
  515.2 2.3 fusion.20
  (258 shorter events, 76.9 us)
Async XLA Ops:
  7.2 169.0 %all-gather.2.cloned.1.call-start = ((), (), s32[]{:S(2)}) async-start(), calls=%async_computation.1 | async-start | bytes 10616832 | tf_op jit(solution)/shard_map/all_gather | solution.py:1003
  99.6 9.5 %copy-start.29 = (f32[4,40,128]{2,1,0:T(8,128)S(1)}, f32[4,40,128]{2,1,0:T(8,128)}, u32[]{:S(2)}) copy-start(f32[4,40,128]{2,1,0:T(8,128)} %get-tuple-element.62) | copy-start | bytes 245764
  99.6 9.6 %copy-start.1 = (bf16[1,1024,1536]{2,1,0:T(8,128)(2,1)S(1)}, bf16[1,1024,1536]{2,1,0:T(8,128)(2,1)}, u32[]{:S(2)}) copy-start(bf16[1,1024,1536]{2,1,0:T(8,128)(2,1)} %get-tuple-element.61) | copy-start | bytes 9437188
  101.9 274.2 %reduce-scatter.2.cloned.1.call-start = ((), (), s32[]{:S(2)}) async-start(), calls=%async_computation.2 | async-start | bytes 10616832 | tf_op jit(solution)/shard_map/reduce_scatter | solution.py:1153
  104.7 51.7 %collective-permute-start.4 = (bf16[1,1024,384]{2,1,0:T(8,128)(2,1)}, bf16[1,1024,384]{2,1,0:T(8,128)(2,1)}, u32[]{:S(2)}, u32[]{:S(2)}) collective-permute-start(bf16[1,1024,384]{2,1,0:T(8,128)(2,1)} %get-tuple-element.69), channel_id=1, source_target_pairs={{0,3},{1,2},{2,1},{3,0},{4,7},{5,6},{6,5},{7,4},{8,11},{9,10},{10,... | collective-permute-start | bytes 2359304 | tf_op jit(solution)/shard_map/ppermute | solution.py:26
  106.1 66.1 %collective-permute-start.3 = (bf16[1,1024,384]{2,1,0:T(8,128)(2,1)}, bf16[1,1024,384]{2,1,0:T(8,128)(2,1)}, u32[]{:S(2)}, u32[]{:S(2)}) collective-permute-start(bf16[1,1024,384]{2,1,0:T(8,128)(2,1)} %get-tuple-element.69), channel_id=1, source_target_pairs={{0,2},{1,3},{2,0},{3,1},{4,6},{5,7},{6,4},{7,5},{8,10},{9,11},{10,... | collective-permute-start | bytes 2359304 | tf_op jit(solution)/shard_map/ppermute | solution.py:26
  106.1 50.3 %collective-permute-start.2 = (bf16[1,1024,384]{2,1,0:T(8,128)(2,1)}, bf16[1,1024,384]{2,1,0:T(8,128)(2,1)}, u32[]{:S(2)}, u32[]{:S(2)}) collective-permute-start(bf16[1,1024,384]{2,1,0:T(8,128)(2,1)} %get-tuple-element.68), channel_id=1, source_target_pairs={{0,1},{1,0},{2,3},{3,2},{4,5},{5,4},{6,7},{7,6},{8,9},{9,8},{10,11... | collective-permute-start | bytes 2359304 | tf_op jit(solution)/shard_map/ppermute | solution.py:26
  109.1 154.7 %copy-start.37 = (f32[1536]{0:T(1024)}, f32[1536]{0:T(1024)S(1)}, u32[]{:S(2)}) copy-start(f32[1536]{0:T(1024)S(1)} %mul.238) | copy-start | bytes 18436
  109.9 169.1 %copy-start.35 = (f32[1024]{0:T(1024)}, f32[1024]{0:T(1024)S(1)}, u32[]{:S(2)}) copy-start(f32[1024]{0:T(1024)S(1)} %get-tuple-element.180) | copy-start | bytes 12292
  112.6 14.0 %collective-permute-start.1 = (bf16[1,3,256]{2,1,0:T(4,128)(2,1)S(1)}, bf16[1,3,256]{2,1,0:T(4,128)(2,1)S(1)}, u32[]{:S(2)}, u32[]{:S(2)}) collective-permute-start(bf16[1,3,256]{2,1,0:T(4,128)(2,1)S(1)} %slice.366), channel_id=1, source_target_pairs={{0,4},{1,5},{2,6},{3,7},{8,12},{9,13},{10,14},{11,15},{16,20},{17,... | collective-permute-start | bytes 4616 | tf_op jit(solution)/shard_map/ppermute | solution.py:32
  113.9 10.0 %copy-start.42 = (f32[768]{0:T(1024)S(1)}, f32[768]{0:T(1024)}, u32[]{:S(2)}) copy-start(f32[768]{0:T(1024)} %param.29) | copy-start | bytes 9220
  113.9 10.0 %copy-start.43 = (f32[768]{0:T(1024)S(1)}, f32[768]{0:T(1024)}, u32[]{:S(2)}) copy-start(f32[768]{0:T(1024)} %param.23) | copy-start | bytes 9220
  114.0 10.0 %copy-start.34 = (f32[4,768]{1,0:T(4,128)S(1)}, f32[4,768]{1,0:T(4,128)}, u32[]{:S(2)}) copy-start(f32[4,768]{1,0:T(4,128)} %param.22) | copy-start | bytes 36868
  114.0 10.0 %copy-start.55 = (f32[12]{0:T(128)S(1)}, f32[12]{0:T(128)}, u32[]{:S(2)}) copy-start(f32[12]{0:T(128)} %param.26) | copy-start | bytes 148
  121.1 5.4 %collective-permute-start = (bf16[1,3,1536]{2,1,0:T(4,128)(2,1)S(1)}, bf16[1,3,1536]{2,1,0:T(4,128)(2,1)S(1)}, u32[]{:S(2)}, u32[]{:S(2)}) collective-permute-start(bf16[1,3,1536]{2,1,0:T(4,128)(2,1)S(1)} %slice.364), channel_id=1, source_target_pairs={{0,4},{1,5},{2,6},{3,7},{8,12},{9,13},{10,14},{11,15},{16,20},{17,... | collective-permute-start | bytes 27656 | tf_op jit(solution)/shard_map/ppermute | solution.py:32
  127.1 23.5 %copy-start.56 = (s32[2]{0:T(128)S(1)}, s32[2]{0:T(128)}, u32[]{:S(2)}) copy-start(s32[2]{0:T(128)} %param.17) | copy-start | bytes 28
  149.3 2.6 collective-permute-start.5
  176.2 9.4 %copy-start.21 = (bf16[1,1024,384]{2,1,0:T(8,128)(2,1)S(1)}, bf16[1,1024,384]{2,1,0:T(8,128)(2,1)}, u32[]{:S(2)}) copy-start(bf16[1,1024,384]{2,1,0:T(8,128)(2,1)} %get-tuple-element.152) | copy-start | bytes 2359300
  222.7 4.9 collective-permute-start.6
  274.5 4.6 collective-permute-start.12
  279.6 22.4 %collective-permute-start.8 = (bf16[1024,384]{1,0:T(8,128)(2,1)}, bf16[1024,384]{1,0:T(8,128)(2,1)}, u32[]{:S(2)}, u32[]{:S(2)}) collective-permute-start(bf16[1024,384]{1,0:T(8,128)(2,1)} %convolution_convert_fusion.6), channel_id=1, source_target_pairs={{0,1},{1,0},{2,3},{3,2},{4,5},{5,4},{6,7},{7,6},{8,9},{9,8},{10,11... | collective-permute-start | bytes 2359304 | tf_op jit(solution)/shard_map/ppermute | solution.py:26
  281.6 86.9 %collective-permute-start.10 = (bf16[1024,384]{1,0:T(8,128)(2,1)}, bf16[1024,384]{1,0:T(8,128)(2,1)}, u32[]{:S(2)}, u32[]{:S(2)}) collective-permute-start(bf16[1024,384]{1,0:T(8,128)(2,1)} %convolution_convert_fusion.5), channel_id=1, source_target_pairs={{0,1},{1,0},{2,3},{3,2},{4,5},{5,4},{6,7},{7,6},{8,9},{9,8},{10,11... | collective-permute-start | bytes 2359304 | tf_op jit(solution)/shard_map/ppermute | solution.py:26
  282.7 16.8 %collective-permute-start.7 = (bf16[1,128,1536]{2,1,0:T(8,128)(2,1)}, bf16[1,128,1536]{2,1,0:T(8,128)(2,1)S(1)}, u32[]{:S(2)}, u32[]{:S(2)}) collective-permute-start(bf16[1,128,1536]{2,1,0:T(8,128)(2,1)} %fusion.28), channel_id=1, source_target_pairs={{4,0},{5,1},{6,2},{7,3},{12,8},{13,9},{14,10},{15,11},{20,16},{21,... | collective-permute-start | bytes 1179656 | tf_op jit(solution)/shard_map/ppermute | solution.py:32
  306.9 67.5 %collective-permute-start.11 = (bf16[1024,384]{1,0:T(8,128)(2,1)}, bf16[1024,384]{1,0:T(8,128)(2,1)S(1)}, u32[]{:S(2)}, u32[]{:S(2)}) collective-permute-start(bf16[1024,384]{1,0:T(8,128)(2,1)} %add_convert_fusion), channel_id=1, source_target_pairs={{0,2},{1,3},{2,0},{3,1},{4,6},{5,7},{6,4},{7,5},{8,10},{9,11},{10,... | collective-permute-start | bytes 2359304 | tf_op jit(solution)/shard_map/ppermute | solution.py:26
  309.5 58.9 %copy-start.40 = (f32[1536]{0:T(1024)S(1)}, f32[1536]{0:T(1024)}, u32[]{:S(2)}) copy-start(f32[1536]{0:T(1024)} %reduce.8) | copy-start | bytes 18436
  309.5 58.9 %copy-start.52 = (f32[24]{0:T(128)S(1)}, f32[24]{0:T(128)}, u32[]{:S(2)}) copy-start(f32[24]{0:T(128)} %reduce_sum.37) | copy-start | bytes 292
  364.8 8.1 %collective-permute-start.13 = (f32[1,8,256]{2,1,0:T(8,128)}, f32[1,8,256]{2,1,0:T(8,128)S(1)}, u32[]{:S(2)}, u32[]{:S(2)}) collective-permute-start(f32[1,8,256]{2,1,0:T(8,128)} %get-tuple-element.91), channel_id=1, source_target_pairs={{4,0},{5,1},{6,2},{7,3},{12,8},{13,9},{14,10},{15,11},{20,16},{21,... | collective-permute-start | bytes 24584 | tf_op jit(solution)/shard_map/ppermute | solution.py:32
  366.1 6.8 %collective-permute-start.9 = (f32[1,8,1536]{2,1,0:T(8,128)}, f32[1,8,1536]{2,1,0:T(8,128)S(1)}, u32[]{:S(2)}, u32[]{:S(2)}) collective-permute-start(f32[1,8,1536]{2,1,0:T(8,128)} %get-tuple-element.87), channel_id=1, source_target_pairs={{4,0},{5,1},{6,2},{7,3},{12,8},{13,9},{14,10},{15,11},{20,16},{21,... | collective-permute-start | bytes 147464 | tf_op jit(solution)/shard_map/ppermute | solution.py:32
  376.1 18.9 %slice-start = ((s8[6291456]{0:T(1024)(128)(4,1)}), s8[4194304]{0:T(1024)(128)(4,1)S(1)}, s32[]{:S(2)}) async-start(s8[6291456]{0:T(1024)(128)(4,1)} %bitcast.190), calls=%async_computation.3 | async-start | bytes 8388608
  377.4 17.6 %slice-start.1 = ((s8[6291456]{0:T(1024)(128)(4,1)}), s8[2097152]{0:T(1024)(128)(4,1)S(1)}, s32[]{:S(2)}) async-start(s8[6291456]{0:T(1024)(128)(4,1)} %bitcast.190), calls=%async_computation.4 | async-start | bytes 4194304
  377.4 28.7 %collective-permute-start.14 = (bf16[192,1536]{1,0:T(8,128)(2,1)S(1)}, bf16[192,1536]{1,0:T(8,128)(2,1)S(1)}, u32[]{:S(2)}, u32[]{:S(2)}) collective-permute-start(bf16[192,1536]{1,0:T(8,128)(2,1)S(1)} %pad_maximum_fusion.6), channel_id=1, source_target_pairs={{0,2},{1,3},{2,0},{3,1},{4,6},{5,7},{6,4},{7,5},{8,10},{9,11},{10,... | collective-permute-start | bytes 1769480 | tf_op jit(solution)/shard_map/ppermute | solution.py:26
  406.2 101.0 %copy-start.14 = (bf16[192,3072]{1,0:T(8,128)(2,1)S(1)}, bf16[192,3072]{1,0:T(8,128)(2,1)}, u32[]{:S(2)}) copy-start(bf16[192,3072]{1,0:T(8,128)(2,1)} %reduce-scatter.2.cloned.1.call-done) | copy-start | bytes 3538948
  (51 other events, 254.1 us)
Sparse Core Ops, SparseCore 0:
  102.0 57.7 all-gather.1
  274.6 76.4 reduce-scatter.1

commit v5 on v4

--- a/solution.py
+++ b/solution.py
@@ -16,6 +16,8 @@
 PAIR = 2 * HEADDIM
 HEADS_STEP = 6
 LANES_STEP = HEADS_STEP * HEADDIM
+GATE_HEADS = 12
+GATE_LANES = GATE_HEADS * HEADDIM
 F32 = jnp.float32
 BF16 = jnp.bfloat16
 HIGHEST = lax.Precision.HIGHEST
@@ -276,9 +278,9 @@
     stats = stats_ref[0].T
     scale = lax.rsqrt(stats[:, 0:1] / INNER + EPSILON)
     cross = scale * stats[:, 1:2] / INNER
-    grown = jnp.exp(turned(cols_ref[...], pl.program_id(0) * HEADS_STEP))
+    grown = jnp.exp(turned(cols_ref[...], pl.program_id(0) * GATE_HEADS))
     low_half = low_lanes(GROUP)
-    for pair in range(HEADS_STEP // 2):
+    for pair in range(GATE_HEADS // 2):
         lanes = slice(PAIR * pair, PAIR * (pair + 1))
         mixed = mixed_ref[:, lanes]
         gate = gate_ref[:, lanes].astype(F32)
@@ -302,9 +304,9 @@
 
 def gate_blocks(mixed, gate, gno, x, stats, gain, wr, cols, heads):
     tokens, width = x.shape
-    blocks, steps = tokens // GROUP, width // LANES_STEP
-    wide = pl.BlockSpec((GROUP, LANES_STEP), lambda g, b: (b, g))
-    line = pl.BlockSpec((1, LANES_STEP), lambda g, b: (0, g))
+    blocks, steps = tokens // GROUP, width // GATE_LANES
+    wide = pl.BlockSpec((GROUP, GATE_LANES), lambda g, b: (b, g))
+    line = pl.BlockSpec((1, GATE_LANES), lambda g, b: (0, g))
     return pl.pallas_call(
         functools.partial(gate_kernel, heads),
         grid=(steps, blocks),
@@ -317,7 +319,7 @@
         ],
         out_specs=[
             wide, wide, wide, line, line,
-            pl.BlockSpec((1, STATE, LANES_STEP), lambda g, b: (b, 0, g)),
+            pl.BlockSpec((1, STATE, GATE_LANES), lambda g, b: (b, 0, g)),
         ],
         out_shape=[
             jax.ShapeDtypeStruct((tokens, width), BF16),
@@ -327,7 +329,7 @@
             jax.ShapeDtypeStruct((1, width), F32),
             jax.ShapeDtypeStruct((blocks, STATE, width), F32),
         ],
-        scratch_shapes=[pltpu.VMEM((GROUP, LANES_STEP), BF16)],
+        scratch_shapes=[pltpu.VMEM((GROUP, GATE_LANES), BF16)],
         cost_estimate=pl.CostEstimate(
             flops=2 * tokens * STATE * width,
             bytes_accessed=tokens * width * 16 + blocks * STATE * width * 4,
@@ -729,7 +731,7 @@
 
 
 def finish_kernel(
-    part_ref, grad_ref, small_ref, cross_ref,
+    part_ref, relay_ref, grad_ref, core_ref, small_ref, cross_ref,
     near_out, other_out, home_out, narrow_out, small_out, small_far, cross_out, cross_far,
     relay_buf, part_buf, sum_buf, core_buf, own_buf, plane_buf, got_buf, sent_buf, home_buf, wr_send, wr_got,
     small_got, cross_got, send_sem, recv_sem, load_sem,
@@ -754,8 +756,13 @@
     loads = [
         pltpu.make_async_copy(grad_ref.at[rows_of(f ^ k, c)], own_buf.at[k], load_sem.at[k]) for k in range(4)
     ] + [
+        pltpu.make_async_copy(core_ref.at[f ^ k], core_buf.at[k], load_sem.at[4 + k]) for k in range(4)
+    ] + [
+        pltpu.make_async_copy(relay_ref.at[pl.ds(piece * i, piece)], relay_buf.at[i], load_sem.at[8 + i])
+        for i in range(FAR_PARTS)
+    ] + [
         pltpu.make_async_copy(
-            part_ref.at[pl.ds(piece * i, piece), feature(z ^ 2)], part_buf.at[i], load_sem.at[4 + i]
+            part_ref.at[pl.ds(piece * i, piece), feature(z ^ 2)], part_buf.at[i], load_sem.at[8 + FAR_PARTS + i]
         )
         for i in range(FAR_PARTS)
     ]
@@ -779,46 +786,38 @@
         copies[at][0].wait_recv()
         copies[at][1] = True
 
-    core = [send(grad_ref.at[rows_of(f ^ k, c ^ 1)], core_buf.at[k], 3) for k in (1, 2, 3, 0)]
-    core_of = {1: core[0], 2: core[1], 3: core[2], 0: core[3]}
     small = [send(small_ref, small_got.at[0], 3)]
     cross = [send(cross_ref, cross_got, 4)]
-    relays = [
-        send(part_ref.at[pl.ds(piece * i, piece), feature(z ^ 3)], relay_buf.at[i], 4) for i in range(FAR_PARTS)
-    ]
     def passed_on(i):
-        loads[4 + i].wait()
-        arrived(relays[i])
+        loads[8 + i].wait()
+        loads[8 + FAR_PARTS + i].wait()
         sum_buf[i] = (part_buf[i].astype(F32) + relay_buf[i].astype(F32)).astype(BF16)
         send(sum_buf.at[i], other_out.at[pl.ds(piece * i, piece)], 5)
 
+    for load in loads[:8]:
+        load.wait()
     arrived(small[0])
     small_out[...] = small_ref[...] + small_got[0]
     small.append(send(small_out, small_got.at[1], 0))
     arrived(cross[0])
     cross_out[...] = cross_ref[...] + cross_got[...]
     cross.append(send(cross_out, cross_far, 5))
-    for load in loads[:4]:
-        load.wait()
-    for k in (1, 2):
-        arrived(core_of[k])
+    for k in (1, 2, 3):
         sent_buf[k - 1] = (own_buf[k].astype(F32) + core_buf[k].astype(F32)).astype(BF16)
+    passed_on(0)
     arrived(small[1])
     copies[small[1]][0].wait_send()
     small_out[...] = small_out[...] + small_got[1]
     small.append(send(small_out, small_got.at[2], 1))
-    plane = [send(sent_buf.at[0], plane_buf.at[0], 0)]
-    arrived(core_of[3])
-    sent_buf[2] = (own_buf[3].astype(F32) + core_buf[3].astype(F32)).astype(BF16)
-    plane.append(send(sent_buf.at[1], plane_buf.at[1], 1))
-    plane.append(send(sent_buf.at[2], plane_buf.at[2], 2))
+    plane = [send(sent_buf.at[k], plane_buf.at[k], k) for k in range(3)]
+    for i in range(1, FAR_PARTS):
+        passed_on(i)
     arrived(small[2])
     copies[small[2]][0].wait_send()
     small_out[...] = small_out[...] + small_got[2]
     small.append(send(small_out, small_got.at[3], 4))
-    for i in range(FAR_PARTS):
-        passed_on(i)
-    arrived(core_of[0])
+    middle = tokens // 2
+    send(part_ref.at[pl.ds(0, middle), feature(z ^ 1)], near_out.at[pl.ds(0, middle)], 4)
     arrived(small[3])
     copies[small[3]][0].wait_send()
     shared = small_out.shape[0] // 2
@@ -831,8 +830,6 @@
         total = total + plane_buf[k].astype(F32)
     wr_send[...] = total[:, 2 * inner : 2 * inner + 2 * STATE]
     wr = send(wr_send, wr_got, 4)
-    middle = tokens // 2
-    send(part_ref.at[pl.ds(0, middle), feature(z ^ 1)], near_out.at[pl.ds(0, middle)], 4)
     home_out[...] = total[:, :inner]
     home_buf[:, :inner] = total[:, inner : 2 * inner].astype(BF16)
     narrow_out[:, 2 * STATE : 2 * STATE + 128] = total[:, 2 * inner + 2 * STATE :]
@@ -857,17 +854,17 @@
             copy.wait_send()
 
 
-def finish(part, grad, small, cross, depth):
+def finish(part, relay, grad, core, small, cross, depth):
     tokens, width = part.shape
     cols, total = width // 4, grad.shape[1]
     rest = 2 * STATE + 128
     inner = (total - rest) // 2
     anywhere = pl.BlockSpec(memory_space=pl.ANY)
     vmem = pl.BlockSpec(memory_space=pltpu.VMEM)
-    count = 4 + 5 + 2 + FAR_PARTS * 2 + 2 + 3 + 2
+    count = 5 + 2 + FAR_PARTS + 2 + 3 + 2
     return pl.pallas_call(
         finish_kernel,
-        in_specs=[anywhere, anywhere, vmem, vmem],
+        in_specs=[anywhere, anywhere, anywhere, anywhere, vmem, vmem],
         out_specs=[anywhere, anywhere, vmem, vmem, vmem, vmem, vmem, vmem],
         out_shape=[
             jax.ShapeDtypeStruct((tokens, cols), BF16),
@@ -895,11 +892,11 @@
             pltpu.VMEM(cross.shape, F32),
             pltpu.SemaphoreType.DMA((count,)),
             pltpu.SemaphoreType.DMA((count,)),
-            pltpu.SemaphoreType.DMA((4 + FAR_PARTS,)),
+            pltpu.SemaphoreType.DMA((8 + 2 * FAR_PARTS,)),
         ],
         compiler_params=pltpu.CompilerParams(collective_id=1, has_side_effects=True),
         name="finish",
-    )(part, grad, small, cross)
+    )(part, relay, grad, core, small, cross)
 
 
 def after(x, other):
@@ -1049,8 +1046,6 @@
     full_gate, full_out = full_late[:, :inner], full_late[:, inner:]
     cot_mine, cot_other, cot_dep = lax.optimization_barrier((cot_mine, cot_other, cot_dep))
     cot_near, cot_far, cot_both = swap(cot_mine, 1), swap(cot_other, 2), swap(cot_other, 3)
-    full_cot = ordered(cot_mine, cot_near, cot_far, cot_both, 2).reshape(tokens, width)
-
     taps = jnp.concatenate([conv_inner, far_small[0]], axis=1)
     taps_bias = jnp.concatenate([conv_inner_bias, far_small[1]])
     gain_gate = jnp.concatenate([gate_gain, far_small[2]])
@@ -1066,6 +1061,8 @@
     narrow_pre = dot(normed, full_narrow, 1, 0)
     inner_pre = dot(normed, full_inner, 1, 0).astype(BF16)
     gate_pre = dot(normed, full_gate, 1, 0).astype(BF16)
+    cot_near, cot_far, cot_both, gate_pre = lax.optimization_barrier((cot_near, cot_far, cot_both, gate_pre))
+    full_cot = ordered(cot_mine, cot_near, cot_far, cot_both, 2).reshape(tokens, width)
 
     def rim_of(pre):
         by_slot = pre.reshape(slots, seq_here, pre.shape[-1])
@@ -1108,7 +1105,7 @@
     local_grad = local_grad.reshape(slots, groups, STATE, inner)
 
     def branch_piece(which):
-        rows = lax.dynamic_slice_in_dim(full_out, which * width_here, width_here, 0)
+        rows = lax.dynamic_slice(full_late, (which * width_here, inner), (width_here, inner))
         return dot(normed_out, rows, 1, 1)
 
     branch = own_features(branch_piece)
@@ -1153,16 +1150,33 @@
         return lax.psum_scatter(x, ("fsdp", "ctx"), scatter_dimension=0, tiled=True)
 
     early = reduced(jnp.concatenate([grad_proj_out, grad_gate_w], axis=1))
-    grad_inner_pre, hidden_out, early = lax.optimization_barrier((grad_inner_pre, hidden_out, early))
-    early_far = swap(jnp.concatenate([early[:, inner_own:inner], early[:, inner + inner_own :]], axis=1), 2)
+    early_away = jnp.concatenate([early[:, inner_own:inner], early[:, inner + inner_own :]], axis=1)
+    grad_inner_pre, hidden_out, early_away = lax.optimization_barrier((grad_inner_pre, hidden_out, early_away))
+    early_far = swap(early_away, 2)
+    by_kernel = lax.axis_size("fsdp") == 4 and lax.axis_size("ctx") == 2
+    late = jnp.concatenate([grad_inner_pre, grad_narrow], axis=1)
+    if by_kernel:
+        which = (place ^ 3) * width_here
+        rows_at = lambda full: lax.dynamic_slice_in_dim(full, which, width_here, 0)
+        relay_piece = (
+            lax.dynamic_slice_in_dim(grad_by_gate, which, width_here, 1)
+            + dot(grad_inner_pre, rows_at(full_inner), 1, 1)
+            + dot(grad_narrow, rows_at(full_narrow), 1, 1)
+        ).astype(BF16)
+        relay = swap(relay_piece, 1)
+        late = after(late, relay_piece)
+    grad_late_w = dot(normed, late, 0, 0).astype(BF16)
+    if by_kernel:
+        by_core = grad_late_w.reshape(4, 2, -1, grad_late_w.shape[1])
+        away = lax.dynamic_index_in_dim(by_core, 1 - lax.axis_index("ctx"), 1, keepdims=False)
+        core = lax.ppermute(away, "ctx", [(0, 1), (1, 0)])
+        grad_inner_pre, grad_narrow, *_ = lax.optimization_barrier(
+            (grad_inner_pre, grad_narrow, away, early_far)
+        )
+    by_inner = dot(grad_inner_pre, full_inner, 1, 1)
+    partial_normed = grad_by_gate + by_inner + dot(grad_narrow, full_narrow, 1, 1)
     grad_out_home = early[:, :inner_own].astype(F32) + early_far[:, :inner_own].astype(F32)
     grad_gate_home = early[:, inner : inner + inner_own].astype(F32) + early_far[:, inner_own:].astype(F32)
-
-    late = jnp.concatenate([grad_inner_pre, grad_narrow], axis=1)
-    grad_late_w = dot(normed, late, 0, 0).astype(BF16)
-    partial_normed = (
-        grad_by_gate + dot(grad_inner_pre, full_inner, 1, 1) + dot(grad_narrow, full_narrow, 1, 1)
-    )
     by_hat = partial_normed * (full_x.astype(F32) * in_scale)
     grad_gain_full = jnp.sum(by_hat, axis=0)
     cross_part = jnp.sum(by_hat * full_gain.astype(F32), axis=1)
@@ -1174,13 +1188,26 @@
     by_head = pack([grad_taps, grad_taps_bias, grad_gate_gain, grad_step_bias, grad_log_rate, grad_skip_gain])
     by_all = pack([grad_conv_write_read, grad_conv_write_read_bias, grad_gain_full])
 
-    if lax.axis_size("fsdp") == 4 and lax.axis_size("ctx") == 2:
-        lines = -(-max(by_head.size, by_all.size) // 1024) * 8
-        filled = lambda v: jnp.pad(v, (0, lines * 128 - v.size)).reshape(lines, 128)
+    if by_kernel:
+        span = max(inner, width, (CONV + 1) * 2 * STATE)
+        line = lambda v: jnp.pad(v.reshape(-1, v.shape[-1]), ((0, 0), (0, span - v.shape[-1])))
+        by_lines = jnp.concatenate(
+            [
+                line(tap_sums[: CONV + 1]),
+                line(grad_gate_gain),
+                line(jnp.concatenate([grad_step_bias, grad_log_rate, grad_skip_gain])),
+                jnp.zeros((1, span), F32),
+                line(grad_gain_full),
+                line(narrow_sums[: CONV + 1].reshape(-1)),
+                jnp.zeros((6, span), F32),
+            ]
+        )
         near, other, grad_inner_home, narrow_sum, small_own, small_far, cross_rows, cross_far = finish(
             partial_low,
-            after(grad_late_w, early_far),
-            jnp.concatenate([filled(by_head), filled(by_all)]),
+            relay,
+            grad_late_w,
+            core,
+            by_lines,
             cross_part.reshape(-1, 128),
             proj_write_read.shape[0],
         )
@@ -1194,10 +1221,17 @@
             + narrow_sum[:, 2 * STATE + 128 + heads_own : 2 * STATE + 128 + heads]
         )
         cross_rows, cross_far = cross_rows.reshape(-1), cross_far.reshape(-1)
-        parts = unpack(small_own[:lines].reshape(-1), head_shapes)
-        far_parts = unpack(small_far[:lines].reshape(-1), head_shapes)
-        far_parts = [lax.slice_in_dim(p, p.shape[-1] // 2, p.shape[-1], axis=p.ndim - 1) for p in far_parts]
-        shared = (small_own[lines:] + small_far[lines:]).reshape(-1)
+        homes = [
+            small_own[at, :inner_own] + small_far[at, inner_own:inner] for at in (slice(0, CONV), CONV, CONV + 1)
+        ] + [
+            small_own[CONV + 2, k * heads : k * heads + heads_own]
+            + small_far[CONV + 2, k * heads + heads_own : (k + 1) * heads]
+            for k in range(3)
+        ]
+        shared = small_own[8:] + small_far[8:]
+        grad_norm_gain = lax.dynamic_slice_in_dim(shared[0], place * width_here, width_here, 0)
+        wr_sums = shared[1, : (CONV + 1) * 2 * STATE].reshape(CONV + 1, 2 * STATE)
+        wr_taps, wr_bias = wr_sums[:CONV], wr_sums[CONV]
     else:
 
         def normed_piece(which):
@@ -1221,12 +1255,11 @@
         shared = smalls[by_head.size :]
         shared = shared + swap(shared, 1)
         shared = shared + swap(shared, 2)
-
-    homes = [
-        lax.slice_in_dim(p, 0, p.shape[-1] // 2, axis=p.ndim - 1) + a for p, a in zip(parts, far_parts)
-    ]
-    wr_taps, wr_bias, gain_all = unpack(shared, shared_shapes)
-    grad_norm_gain = lax.dynamic_slice_in_dim(gain_all, place * width_here, width_here, 0)
+        homes = [
+            lax.slice_in_dim(p, 0, p.shape[-1] // 2, axis=p.ndim - 1) + a for p, a in zip(parts, far_parts)
+        ]
+        wr_taps, wr_bias, gain_all = unpack(shared, shared_shapes)
+        grad_norm_gain = lax.dynamic_slice_in_dim(gain_all, place * width_here, width_here, 0)
 
     own_gain = norm_gain.astype(F32)
     own_scale = both_halves(

time: 532 us -> 507 us (0.953)
  Pallas kernels: 294 us -> 272 us
  matrix products: 86.2 us -> 92.2 us
    pallas_call x1, Pallas kernels: 89 us -> 72.7 us  [finish(): pl.pallas_call(finish_kernel, in_specs=[anywhere, anywhere, anywhere, any...]
    ppermute x9 -> x10, waiting for transfers between devices: 24.4 us -> 12.9 us  [swap(): return lax.ppermute(x, 'tp', [(i, i ^ bit) for i in range(count)])]
    all_gather x1, waiting for transfers between devices: 0.01 us -> 6.32 us  [gathered(): return lax.all_gather(x, ('fsdp', 'ctx'), axis=0, tiled=True)]
    dot_general x14 -> x16, matrix products: 86.2 us -> 92.2 us  [dot(): lax.dot_general(a, b, (((da,), (db,)), ((), ())), preferred_element_type=...]
    slice x5 -> x4, local copies, waits for them, and re-layouts: 7.1 us -> 1.19 us  [the longest x3 1.18 us: on_device(): wr_taps, wr_bias = (wr_sums[:CONV], wr_sums[CONV])]
    ppermute x9 -> x10, starting transfers between devices: 12.1 us -> 12 us  [swap(): return lax.ppermute(x, 'tp', [(i, i ^ bit) for i in range(count)])]
  transfers between devices with their start and end apart: 17 -> 19, of which waited for: 5 -> 5; matrix products, arithmetic and copies ran while one was open for 17% -> 20% of each run, Pallas kernels for 13% -> 14%
where the time goes in v5:
time: 507 us; the launch traced here: 500 us
  Pallas kernels  272 us (54%)
  matrix products  92.2 us (18%)
  other arithmetic  41.6 us (8%)
  local copies, waits for them, and re-layouts  36.3 us (7%)
  starting transfers between devices  21.9 us (4%)
  waiting for transfers between devices  20.5 us (4%)
  between operations  15.2 us (3%)
    dot_general x16, matrix products, dot(): lax.dot_general(a, b, (((da,), (db,)), ((), ())), preferred_element_type=...  92.2 us
    pallas_call x1, Pallas kernels, fetch(): pl.pallas_call(fetch_kernel, in_specs=[anywhere] * 6, out_specs=[anywhere...  83 us
    pallas_call x1, Pallas kernels, finish(): pl.pallas_call(finish_kernel, in_specs=[anywhere, anywhere, anywhere, any...  72.7 us
    pallas_call x1, Pallas kernels, back_blocks(): pl.pallas_call(functools.partial(back_kernel, groups, heads), grid=(block...  52 us
    pallas_call x1, Pallas kernels, mix_blocks(): pl.pallas_call(functools.partial(mix_kernel, heads), grid=(blocks, steps)...  30.3 us
    pallas_call x1, Pallas kernels, start_blocks(): pl.pallas_call(functools.partial(start_kernel, groups, heads), grid=(bloc...  18.4 us
    pallas_call x1, Pallas kernels, gate_blocks(): pl.pallas_call(functools.partial(gate_kernel, heads), grid=(steps, blocks...  15.5 us
    ppermute x10, waiting for transfers between devices, swap(): return lax.ppermute(x, 'tp', [(i, i ^ bit) for i in range(count)])  12.9 us
  transfers between devices with their start and end apart: 19, of which 5 were waited for; matrix products, arithmetic and copies ran while one was open for 20% of the time, Pallas kernels for 14%

profile of v5, /device:TPU:0, one launch (start us, length us, event | category | flops | bytes accessed | tf_op | source)
XLA Modules:
  0.0 499.6 jit_solution(5583955239206111036)
XLA Ops:
  10.9 2.3 fusion.68
  15.5 83.0 %fetch.1 = (bf16[1,1024,1536]{2,1,0:T(8,128)(2,1)}, bf16[1536,1536]{1,0:T(8,128)(2,1)}, bf16[192,1536]{1,0:T(8,128)(2,1)}, bf16[1536,256]{1,0:T(8,128)(2,1)}, bf...) custom-call(bf16[2,1024,384]{2,1,0:T(8,128)(2,1)} %x_ref.1, bf16[192,768]{1,0:T(8,128)(2,1)} %get-tuple-element.179.inner_ref, ...), custom_call_target="tpu_custom_call" | custom-call | tf_op jit(solution)/shard_map/fetch/pallas_call | solution.py:708
  102.0 2.7 constant_dynamic-slice_fusion.2
  106.1 2.9 collective-permute-start.2
  114.4 5.5 %convolution_convert_fusion.3.inner_ref.pre_ref = bf16[1024,1536]{1,0:T(8,128)(2,1)S(1)} fusion(bf16[1536,1536]{1,0:T(8,128)(2,1)S(1)} %bitcast.215, bf16[1,1024,1536]{2,1,0:T(8,128)(2,1)S(1)} %copy-done.2, f32[1536]{0:T(1024)S(1)} %mul.239, f32[1024]{0:T(1024)S(1)} %get-tuple-element.174), kind=kOutput, calls=%fused_computation.26 | convolution fusion | flops 4839702528 | bytes 11020288 | tf_op jit(solution)/shard_map/dot_general | solution.py:55
  127.6 18.4 %start_blocks.1 = (bf16[1024,1536]{1,0:T(8,128)(2,1)}, bf16[1024,1536]{1,0:T(8,128)(2,1)}, bf16[1024,256]{1,0:T(8,128)(2,1)}, f32[1024,256]{1,0:T(8,128)}, f32[1...) custom-call(bf16[1024,1536]{1,0:T(8,128)(2,1)} %copy-done.12, ...), custom_call_target="tpu_custom_call" | custom-call | flops 434110464 | bytes 12582912 | tf_op jit(solution)/shard_map/start_blocks/pallas_call | solution.py:148
  153.5 6.3 %all-gather.2.cloned.1.call-done = bf16[1536,3072]{1,0:T(8,128)(2,1)} async-done(((bf16[192,3072]{1,0:T(8,128)(2,1)}), bf16[1536,3072]{1,0:T(8,128)(2,1)}) %all-gather.2.cloned.1.call-update) | async-done | bytes 9437200 | tf_op jit(solution)/shard_map/all_gather | solution.py:1000
  159.9 9.4 %fusion.12.gate_ref = bf16[1024,1536]{1,0:T(8,128)(2,1)} fusion(bf16[1536,3072]{1,0:T(8,128)(2,1)} %all-gather.2.cloned.1.call-done, bf16[1,1024,1536]{2,1,0:T(8,128)(2,1)S(1)} %copy-done.2, f32[1536]{0:T(1024)S(1)} %mul.239, f32[1024]{0:T(1024)S(1)} %get-tuple-element.174), kind=kOutput, calls=%fused_computation.24 | convolution fusion | flops 4839702528 | bytes 11020288 | tf_op jit(solution)/shard_map/dot_general | solution.py:55
  169.2 3.0 collective-permute-done.3
  172.2 2.3 broadcast_select_fusion.7
  174.6 6.7 %fusion.15.gno_ref = bf16[1024,1536]{1,0:T(8,128)(2,1)} fusion(bf16[1536,3072]{1,0:T(8,128)(2,1)S(1)} %copy-done.46, bf16[1,1024,384]{2,1,0:T(8,128)(2,1)S(1)} %get-tuple-element.154, bf16[1,1024,384]{2,1,0:T(8,128)(2,1)S(1)} %get-tuple-element.153, bf16[1,1024,384]{2,1,0:T(8,128)(2,1)S(1)} %get-tuple-element.152, ...), kind=kOutput, calls=%fused_computation.25 | convolution fusion | flops 4850712576 | bytes 11014144 | tf_op jit(solution)/shard_map/dot_general | solution.py:55
  181.3 30.3 %mix_blocks.1 = (f32[1024,1536]{1,0:T(8,128)}, f32[4,8,256]{2,1,0:T(8,128)}) custom-call(bf16[1024,1536]{1,0:T(8,128)(2,1)} %get-tuple-element.72.x_ref, bf16[1024,1536]{1,0:T(8,128)(2,1)} %fusion.12.gate_ref, bf16[1024,1536]{1,0:T(8,128)(2,1)} %fusion.15.gno_ref, bf16[1024,256]{1,0:T(8,128)(2,1)} %get-tuple-element.80.wr_ref, ...), custom_call_target="tpu_custom_call" | custom-call | flops 4831838208 | bytes 15728640 | tf_op jit(solution)/shard_map/mix_blocks/pallas_call | solution.py:242
  211.7 4.1 collective-permute-done.6
  217.2 15.5 %gate_blocks.1 = (bf16[1024,1536]{1,0:T(8,128)(2,1)}, bf16[1024,1536]{1,0:T(8,128)(2,1)}, bf16[1024,1536]{1,0:T(8,128)(2,1)}, f32[1,1536]{1,0:T(1,128)}, f32[1,1536]{1,0:T(1,128)}, /*index=5*/f32[4,128,1536]{2,1,0:T(8,128)}) custom-call(f32[1024,1536]{1,0:T(8,128)} %get-tuple-element.85.mixed_ref, bf16[1024,1536]{1,0:T(8,128)(2,1)} %fusion.12.gate_ref, ...), custom_call_target="tpu_custom_call" | custom-call | flops 402653184 | bytes 28311552 | tf_op jit(solution)/shard_map/gate_blocks/pallas_call | solution.py:310
  232.7 5.1 %convolution_convert_fusion.4 = bf16[1024,384]{1,0:T(8,128)(2,1)} fusion(bf16[1024,1536]{1,0:T(8,128)(2,1)} %get-tuple-element.93, bf16[1536,3072]{1,0:T(8,128)(2,1)} %all-gather.2.cloned.1.call-done, s32[]{:T(128)S(6)} %select_n.130), kind=kOutput, calls=%fused_computation.44 | convolution fusion | flops 1208352768 | bytes 5111812 | tf_op jit(solution)/shard_map/dot_general | solution.py:55
  237.7 4.1 convolution_convert_fusion.5
  241.9 5.8 %convolution_convert_fusion.1 = bf16[1536,1536]{1,0:T(8,128)(2,1)S(1)} fusion(bf16[1024,1536]{1,0:T(8,128)(2,1)S(1)} %copy-done.47, bf16[1,1024,384]{2,1,0:T(8,128)(2,1)S(1)} %copy-done.26, bf16[1,1024,384]{2,1,0:T(8,128)(2,1)S(1)} %copy-done.24, bf16[1,1024,384]{2,1,0:T(8,128)(2,1)S(1)} %copy-done.22, bf16[1,1024,384]{2,1,0:T(8,128)(2,1)S(1)} %copy-done.20, ...), kind=kOutput, calls=%fused_computation.4 | convolution fusion | flops 4851499008 | bytes 11014144 | tf_op jit(solution)/shard_map/dot_general | solution.py:55
  247.7 5.9 %convolution_convert_fusion = bf16[1536,1536]{1,0:T(8,128)(2,1)S(1)} fusion(bf16[1024,1536]{1,0:T(8,128)(2,1)S(1)} %copy-done.49, bf16[1,1024,1536]{2,1,0:T(8,128)(2,1)S(1)} %copy-done.2, f32[1536]{0:T(1024)S(1)} %mul.239, f32[1024]{0:T(1024)S(1)} %get-tuple-element.174), kind=kOutput, calls=%fused_computation.3 | convolution fusion | flops 4840488960 | bytes 11020288 | tf_op jit(solution)/shard_map/dot_general | solution.py:55
  253.5 4.8 pad_maximum_fusion
  263.4 9.5 %fusion.7 = f32[1024,1536]{1,0:T(8,128)} fusion(bf16[1024,1536]{1,0:T(8,128)(2,1)S(1)} %copy-done.50, bf16[1536,3072]{1,0:T(8,128)(2,1)} %all-gather.2.cloned.1.call-done), kind=kOutput, calls=%fused_computation.16 | convolution fusion | flops 4831838208 | bytes 14155776 | tf_op jit(solution)/shard_map/dot_general | solution.py:55
  274.6 5.8 %collective-permute-done.8 = bf16[1024,384]{1,0:T(8,128)(2,1)S(1)} collective-permute-done((bf16[1024,384]{1,0:T(8,128)(2,1)}, bf16[1024,384]{1,0:T(8,128)(2,1)S(1)}, u32[]{:S(2)}, u32[]{:S(2)}) %collective-permute-start.8) | collective-permute-done | bytes 786464 | tf_op jit(solution)/shard_map/ppermute | solution.py:28
  280.4 4.0 add_convert_fusion.1
  286.5 52.0 %back_blocks.1 = (bf16[1024,1536]{1,0:T(8,128)(2,1)}, bf16[1024,384]{1,0:T(8,128)(2,1)}, f32[4,8,384]{2,1,0:T(8,128)}, f32[8,256]{1,0:T(8,128)}, f32[8,128]{1,0:...) custom-call(bf16[1024,1536]{1,0:T(8,128)(2,1)} %get-tuple-element.72.x_ref, ...), custom_call_target="tpu_custom_call" | custom-call | flops 9663676416 | bytes 22020096 | tf_op jit(solution)/shard_map/back_blocks/pallas_call | solution.py:529
  341.7 4.3 add_bitcast_fusion.1
  351.9 4.2 fusion.25
  357.4 3.1 add_convert_fusion
  360.5 7.4 %convolution_convert_fusion.2.grad_ref = bf16[1536,1920]{1,0:T(8,128)(2,1)S(1)} fusion(bf16[1024,1920]{1,0:T(8,128)(2,1)S(1)} %pad_maximum_fusion.1, bf16[1,1024,1536]{2,1,0:T(8,128)(2,1)S(1)} %copy-done.3, f32[1536]{0:T(1024)S(1)} %mul.239, f32[1024]{0:T(1024)S(1)} %get-tuple-element.174), kind=kOutput, calls=%fused_computation.5 | convolution fusion | flops 6049038336 | bytes 12986368 | tf_op jit(solution)/shard_map/dot_general | solution.py:55
  368.0 2.5 copy-done.1
  381.8 7.9 %fusion.69 = f32[1024,1536]{1,0:T(8,128)S(1)} fusion(bf16[1024,1536]{1,0:T(8,128)(2,1)} %fusion.40, bf16[1536,1536]{1,0:T(8,128)(2,1)} %get-tuple-element.69), kind=kOutput, calls=%fused_computation.162 | convolution fusion | flops 4831838208 | bytes 14155776 | tf_op jit(solution)/shard_map/dot_general | solution.py:55
  389.7 7.6 %multiply_reduce_fusion = (f32[1024]{0:T(1024)}, f32[1536]{0:T(1024)S(1)}, bf16[1024,1536]{1,0:T(8,128)(2,1)}, f32[1024,1536]{1,0:T(8,128)}) fusion(bf16[1,1024,1536]{2,1,0:T(8,128)(2,1)S(1)} %copy-done.4, f32[1536]{0:T(1024)S(1)} %copy-done.31, f32[1024]{0:T(1024)S(1)} %get-tuple-element.174, bf16[1024,384]{1,0:T(8,128)(2,1)S(1)} %fusion.43, ...), kind=kOutput, calls=%fused_computation.12 | convolution fusion | flops 1222112768 | bytes 27152384 | tf_op jit(solution)/shard_map/dot_general | solution.py:55
  397.4 2.8 concatenate.130.small_ref
  402.4 72.7 %finish.1 = (bf16[1024,384]{1,0:T(8,128)(2,1)}, bf16[1024,384]{1,0:T(8,128)(2,1)}, f32[192,768]{1,0:T(8,128)}, f32[192,512]{1,0:T(8,128)}, f32[16,1536]{1,0:T(8,...) custom-call(bf16[1024,1536]{1,0:T(8,128)(2,1)} %get-tuple-element.144.part_ref, ...), custom_call_target="tpu_custom_call" | custom-call | tf_op jit(solution)/shard_map/finish/pallas_call | solution.py:865
  (231 shorter events, 82.6 us)
Async XLA Ops:
  7.2 152.7 %all-gather.2.cloned.1.call-start = ((), (), s32[]{:S(2)}) async-start(), calls=%async_computation.1 | async-start | bytes 10616832 | tf_op jit(solution)/shard_map/all_gather | solution.py:1000
  99.6 9.4 %copy-start.27 = (f32[4,40,128]{2,1,0:T(8,128)S(1)}, f32[4,40,128]{2,1,0:T(8,128)}, u32[]{:S(2)}) copy-start(f32[4,40,128]{2,1,0:T(8,128)} %get-tuple-element.68) | copy-start | bytes 245764
  99.6 9.6 %copy-start.2 = (bf16[1,1024,1536]{2,1,0:T(8,128)(2,1)S(1)}, bf16[1,1024,1536]{2,1,0:T(8,128)(2,1)}, u32[]{:S(2)}) copy-start(bf16[1,1024,1536]{2,1,0:T(8,128)(2,1)} %get-tuple-element.67) | copy-start | bytes 9437188
  101.9 247.3 %reduce-scatter.2.cloned.1.call-start = ((), (), s32[]{:S(2)}) async-start(), calls=%async_computation.2 | async-start | bytes 10616832 | tf_op jit(solution)/shard_map/reduce_scatter | solution.py:1150
  104.7 64.6 %collective-permute-start.4 = (bf16[1,1024,384]{2,1,0:T(8,128)(2,1)}, bf16[1,1024,384]{2,1,0:T(8,128)(2,1)}, u32[]{:S(2)}, u32[]{:S(2)}) collective-permute-start(bf16[1,1024,384]{2,1,0:T(8,128)(2,1)} %get-tuple-element.74), channel_id=1, source_target_pairs={{0,3},{1,2},{2,1},{3,0},{4,7},{5,6},{6,5},{7,4},{8,11},{9,10},{10,... | collective-permute-start | bytes 2359304 | tf_op jit(solution)/shard_map/ppermute | solution.py:28
  106.1 66.1 %collective-permute-start.3 = (bf16[1,1024,384]{2,1,0:T(8,128)(2,1)}, bf16[1,1024,384]{2,1,0:T(8,128)(2,1)}, u32[]{:S(2)}, u32[]{:S(2)}) collective-permute-start(bf16[1,1024,384]{2,1,0:T(8,128)(2,1)} %get-tuple-element.74), channel_id=1, source_target_pairs={{0,2},{1,3},{2,0},{3,1},{4,6},{5,7},{6,4},{7,5},{8,10},{9,11},{10,... | collective-permute-start | bytes 2359304 | tf_op jit(solution)/shard_map/ppermute | solution.py:28
  106.1 63.1 %collective-permute-start.2 = (bf16[1,1024,384]{2,1,0:T(8,128)(2,1)}, bf16[1,1024,384]{2,1,0:T(8,128)(2,1)}, u32[]{:S(2)}, u32[]{:S(2)}) collective-permute-start(bf16[1,1024,384]{2,1,0:T(8,128)(2,1)} %get-tuple-element.73), channel_id=1, source_target_pairs={{0,1},{1,0},{2,3},{3,2},{4,5},{5,4},{6,7},{7,6},{8,9},{9,8},{10,11... | collective-permute-start | bytes 2359304 | tf_op jit(solution)/shard_map/ppermute | solution.py:28
  109.1 251.5 %copy-start.30 = (f32[1536]{0:T(1024)}, f32[1536]{0:T(1024)S(1)}, u32[]{:S(2)}) copy-start(f32[1536]{0:T(1024)S(1)} %mul.239) | copy-start | bytes 18436
  113.0 14.0 %collective-permute-start.1 = (bf16[1,3,256]{2,1,0:T(4,128)(2,1)S(1)}, bf16[1,3,256]{2,1,0:T(4,128)(2,1)S(1)}, u32[]{:S(2)}, u32[]{:S(2)}) collective-permute-start(bf16[1,3,256]{2,1,0:T(4,128)(2,1)S(1)} %slice.307), channel_id=1, source_target_pairs={{0,4},{1,5},{2,6},{3,7},{8,12},{9,13},{10,14},{11,15},{16,20},{17,... | collective-permute-start | bytes 4616 | tf_op jit(solution)/shard_map/ppermute | solution.py:34
  114.3 9.5 %copy-start.43 = (f32[12]{0:T(128)S(1)}, f32[12]{0:T(128)}, u32[]{:S(2)}) copy-start(f32[12]{0:T(128)} %param.27) | copy-start | bytes 148
  114.3 10.1 %copy-start.33 = (f32[768]{0:T(1024)S(1)}, f32[768]{0:T(1024)}, u32[]{:S(2)}) copy-start(f32[768]{0:T(1024)} %param.29) | copy-start | bytes 9220
  114.4 10.1 %copy-start.34 = (f32[768]{0:T(1024)S(1)}, f32[768]{0:T(1024)}, u32[]{:S(2)}) copy-start(f32[768]{0:T(1024)} %param.23) | copy-start | bytes 9220
  114.4 10.1 %copy-start.29 = (f32[4,768]{1,0:T(4,128)S(1)}, f32[4,768]{1,0:T(4,128)}, u32[]{:S(2)}) copy-start(f32[4,768]{1,0:T(4,128)} %param.22) | copy-start | bytes 36868
  114.4 10.1 %copy-start.44 = (f32[12]{0:T(128)S(1)}, f32[12]{0:T(128)}, u32[]{:S(2)}) copy-start(f32[12]{0:T(128)} %param.26) | copy-start | bytes 148
  121.6 5.5 %collective-permute-start = (bf16[1,3,1536]{2,1,0:T(4,128)(2,1)S(1)}, bf16[1,3,1536]{2,1,0:T(4,128)(2,1)S(1)}, u32[]{:S(2)}, u32[]{:S(2)}) collective-permute-start(bf16[1,3,1536]{2,1,0:T(4,128)(2,1)S(1)} %slice.305), channel_id=1, source_target_pairs={{0,4},{1,5},{2,6},{3,7},{8,12},{9,13},{10,14},{11,15},{16,20},{17,... | collective-permute-start | bytes 27656 | tf_op jit(solution)/shard_map/ppermute | solution.py:34
  127.6 22.9 %copy-start.45 = (s32[2]{0:T(128)S(1)}, s32[2]{0:T(128)}, u32[]{:S(2)}) copy-start(s32[2]{0:T(128)} %param.17) | copy-start | bytes 28
  149.2 2.6 collective-permute-start.5
  159.9 14.7 %copy-start.46 = (bf16[1536,3072]{1,0:T(8,128)(2,1)S(1)}, bf16[1536,3072]{1,0:T(8,128)(2,1)}, u32[]{:S(2)}) copy-start(bf16[1536,3072]{1,0:T(8,128)(2,1)} %all-gather.2.cloned.1.call-done) | copy-start | bytes 28311556
  211.6 4.2 collective-permute-start.6
  258.3 114.9 %collective-permute-start.12 = (f32[8,128]{1,0:T(8,128)}, f32[8,128]{1,0:T(8,128)}, u32[]{:S(2)}, u32[]{:S(2)}) collective-permute-start(f32[8,128]{1,0:T(8,128)} %get-tuple-element.173), channel_id=1, source_target_pairs={{0,2},{1,3},{2,0},{3,1},{4,6},{5,7},{6,4},{7,5},{8,10},{9,11},{10,... | collective-permute-start | bytes 12296 | tf_op jit(solution)/shard_map/ppermute | solution.py:28
  259.8 20.6 %collective-permute-start.8 = (bf16[1024,384]{1,0:T(8,128)(2,1)}, bf16[1024,384]{1,0:T(8,128)(2,1)S(1)}, u32[]{:S(2)}, u32[]{:S(2)}) collective-permute-start(bf16[1024,384]{1,0:T(8,128)(2,1)} %convolution_convert_fusion.5), channel_id=1, source_target_pairs={{0,1},{1,0},{2,3},{3,2},{4,5},{5,4},{6,7},{7,6},{8,9},{9,8},{10,11... | collective-permute-start | bytes 2359304 | tf_op jit(solution)/shard_map/ppermute | solution.py:28
  261.8 79.9 %collective-permute-start.10 = (bf16[1024,384]{1,0:T(8,128)(2,1)}, bf16[1024,384]{1,0:T(8,128)(2,1)}, u32[]{:S(2)}, u32[]{:S(2)}) collective-permute-start(bf16[1024,384]{1,0:T(8,128)(2,1)} %convolution_convert_fusion.4), channel_id=1, source_target_pairs={{0,1},{1,0},{2,3},{3,2},{4,5},{5,4},{6,7},{7,6},{8,9},{9,8},{10,11... | collective-permute-start | bytes 2359304 | tf_op jit(solution)/shard_map/ppermute | solution.py:28
  262.1 10.8 %collective-permute-start.7 = (bf16[1,128,1536]{2,1,0:T(8,128)(2,1)S(1)}, bf16[1,128,1536]{2,1,0:T(8,128)(2,1)S(1)}, u32[]{:S(2)}, u32[]{:S(2)}) collective-permute-start(bf16[1,128,1536]{2,1,0:T(8,128)(2,1)S(1)} %fusion.32), channel_id=1, source_target_pairs={{4,0},{5,1},{6,2},{7,3},{12,8},{13,9},{14,10},{15,11},{20,16},{21,... | collective-permute-start | bytes 1179656 | tf_op jit(solution)/shard_map/ppermute | solution.py:34
  284.4 63.1 %collective-permute-start.11 = (bf16[1024,384]{1,0:T(8,128)(2,1)}, bf16[1024,384]{1,0:T(8,128)(2,1)S(1)}, u32[]{:S(2)}, u32[]{:S(2)}) collective-permute-start(bf16[1024,384]{1,0:T(8,128)(2,1)} %add_convert_fusion.1), channel_id=1, source_target_pairs={{0,2},{1,3},{2,0},{3,1},{4,6},{5,7},{6,4},{7,5},{8,10},{9,11},{10,... | collective-permute-start | bytes 2359304 | tf_op jit(solution)/shard_map/ppermute | solution.py:28
  338.5 7.4 %collective-permute-start.13 = (f32[1,8,256]{2,1,0:T(8,128)}, f32[1,8,256]{2,1,0:T(8,128)S(1)}, u32[]{:S(2)}, u32[]{:S(2)}) collective-permute-start(f32[1,8,256]{2,1,0:T(8,128)} %get-tuple-element.101), channel_id=1, source_target_pairs={{4,0},{5,1},{6,2},{7,3},{12,8},{13,9},{14,10},{15,11},{20,16},{21,... | collective-permute-start | bytes 24584 | tf_op jit(solution)/shard_map/ppermute | solution.py:34
  339.8 6.2 %collective-permute-start.9 = (f32[1,8,1536]{2,1,0:T(8,128)}, f32[1,8,1536]{2,1,0:T(8,128)S(1)}, u32[]{:S(2)}, u32[]{:S(2)}) collective-permute-start(f32[1,8,1536]{2,1,0:T(8,128)} %get-tuple-element.97), channel_id=1, source_target_pairs={{4,0},{5,1},{6,2},{7,3},{12,8},{13,9},{14,10},{15,11},{20,16},{21,... | collective-permute-start | bytes 147464 | tf_op jit(solution)/shard_map/ppermute | solution.py:34
  351.1 30.7 %collective-permute-start.14 = (bf16[192,1536]{1,0:T(8,128)(2,1)}, bf16[192,1536]{1,0:T(8,128)(2,1)}, u32[]{:S(2)}, u32[]{:S(2)}) collective-permute-start(bf16[192,1536]{1,0:T(8,128)(2,1)} %pad_maximum_fusion.7), channel_id=1, source_target_pairs={{0,2},{1,3},{2,0},{3,1},{4,6},{5,7},{6,4},{7,5},{8,10},{9,11},{10,... | collective-permute-start | bytes 1769480 | tf_op jit(solution)/shard_map/ppermute | solution.py:28
  372.3 30.0 %collective-permute-start.16 = (bf16[4,192,1920]{2,1,0:T(8,128)(2,1)}, bf16[4,192,1920]{2,1,0:T(8,128)(2,1)}, u32[]{:S(2)}, u32[]{:S(2)}) collective-permute-start(bf16[4,192,1920]{2,1,0:T(8,128)(2,1)} %dynamic-slice_bitcast_fusion), channel_id=1, source_target_pairs={{0,4},{4,0},{1,5},{5,1},{2,6},{6,2},{3,7},{7,3},{8,12},{12,8},{9,1... | collective-permute-start | bytes 8847368 | tf_op jit(solution)/shard_map/ppermute | solution.py:1172
  380.0 9.7 %copy-start.4 = (bf16[1,1024,1536]{2,1,0:T(8,128)(2,1)S(1)}, bf16[1,1024,1536]{2,1,0:T(8,128)(2,1)}, u32[]{:S(2)}) copy-start(bf16[1,1024,1536]{2,1,0:T(8,128)(2,1)} %get-tuple-element.67) | copy-start | bytes 9437188
  380.0 9.7 %copy-start.31 = (f32[1536]{0:T(1024)S(1)}, f32[1536]{0:T(1024)}, u32[]{:S(2)}) copy-start(f32[1536]{0:T(1024)} %copy-done.30) | copy-start | bytes 18436
  380.0 22.3 %collective-permute-start.15 = (bf16[1024,384]{1,0:T(8,128)(2,1)}, bf16[1024,384]{1,0:T(8,128)(2,1)}, u32[]{:S(2)}, u32[]{:S(2)}) collective-permute-start(bf16[1024,384]{1,0:T(8,128)(2,1)} %add_convert_fusion), channel_id=1, source_target_pairs={{0,1},{1,0},{2,3},{3,2},{4,5},{5,4},{6,7},{7,6},{8,9},{9,8},{10,11... | collective-permute-start | bytes 2359304 | tf_op jit(solution)/shard_map/ppermute | solution.py:28
  475.1 13.3 %copy-start.18 = (bf16[1024,384]{1,0:T(8,128)(2,1)S(1)}, bf16[1024,384]{1,0:T(8,128)(2,1)}, u32[]{:S(2)}) copy-start(bf16[1024,384]{1,0:T(8,128)(2,1)} %get-tuple-element.112) | copy-start | bytes 2359300
  (40 other events, 150.1 us)
Sparse Core Ops, SparseCore 0:
  102.0 57.7 all-gather.1
  258.5 75.9 reduce-scatter.1

commit v6 on v5

--- a/solution.py
+++ b/solution.py
@@ -14,6 +14,7 @@
 INNER = 3072
 EPSILON = 1e-05
 PAIR = 2 * HEADDIM
+HALF = GROUP // 2
 HEADS_STEP = 6
 LANES_STEP = HEADS_STEP * HEADDIM
 GATE_HEADS = 12
@@ -67,6 +68,17 @@
     return lax.broadcasted_iota(jnp.int32, (GROUP, GROUP), 0) >= lax.broadcasted_iota(
         jnp.int32, (GROUP, GROUP), 1
     )
+
+
+def quarter_mask():
+    return lax.broadcasted_iota(jnp.int32, (HALF, HALF), 0) >= lax.broadcasted_iota(jnp.int32, (HALF, HALF), 1)
+
+
+def decays(col, row, mask):
+    early = jnp.exp(jnp.where(mask, col[:HALF] - row[:, :HALF], -1e30))
+    cross = jnp.exp(col[HALF:] - row[:, :HALF])
+    late = jnp.exp(jnp.where(mask, col[HALF:] - row[:, HALF:], -1e30))
+    return early, cross, late
 
 
 def split_dot(ones, values, terms, contract):
@@ -197,13 +209,13 @@
         scores_ref[...] = dot(wr_ref[:, STATE:], wr_ref[:, :STATE], 1, 1)
         sums_ref[...] = jnp.zeros_like(sums_ref)
 
-    cols = turned(cols_ref[...], g * HEADS_STEP)
+    cols = turned(cols_ref[...], g * GATE_HEADS)
     grown = jnp.exp(cols)
     low_half = low_lanes(GROUP)
-    lower = lower_mask()
+    mask = quarter_mask()
     squares = jnp.zeros((GROUP, 1), F32)
     crosses = jnp.zeros((GROUP, 1), F32)
-    for pair in range(HEADS_STEP // 2):
+    for pair in range(GATE_HEADS // 2):
         lanes = slice(PAIR * pair, PAIR * (pair + 1))
         x = x_ref[:, lanes].astype(F32)
         stepped = x * spread_heads(cols, 2 * pair, low_half)
@@ -213,12 +225,23 @@
         )
         total = dot(wr_ref[:, STATE:], state_ref[0, :, lanes], 1, 0)
         total = total * spread_heads(grown, heads + 2 * pair, low_half)
+        top = jnp.zeros((HALF, PAIR), F32)
+        bottom = jnp.zeros((HALF, PAIR), F32)
         for side in range(2):
             head = 2 * pair + side
-            row = rows_ref[0, pl.ds(g * HEADS_STEP + head, 1), :]
-            spread = jnp.where(lower, cols[:, heads + head : heads + head + 1] - row, -1e30)
-            weights = (scores_ref[...] * jnp.exp(spread)).astype(BF16)
-            total = total + dot(weights, halves[side], 1, 0)
+            row = rows_ref[0, pl.ds(g * GATE_HEADS + head, 1), :]
+            early, cross, late = decays(cols[:, heads + head : heads + head + 1], row, mask)
+            upper = (scores_ref[:HALF, :HALF] * early).astype(BF16)
+            under = jnp.concatenate(
+                [
+                    (scores_ref[HALF:, :HALF] * cross).astype(BF16),
+                    (scores_ref[HALF:, HALF:] * late).astype(BF16),
+                ],
+                axis=1,
+            )
+            top = top + dot(upper, halves[side][:HALF], 1, 0)
+            bottom = bottom + dot(under, halves[side], 1, 0)
+        total = total + jnp.concatenate([top, bottom], axis=0)
         mixed = total + skip_ref[:, lanes] * x
         mixed_ref[:, lanes] = mixed
         gate = gate_ref[:, lanes].astype(F32)
@@ -236,9 +259,9 @@
 
 def mix_blocks(x, gate, gno, wr, cols, rows, states, skip, gain):
     tokens, width = x.shape
-    blocks, steps, heads = tokens // GROUP, width // LANES_STEP, rows.shape[1]
-    wide = pl.BlockSpec((GROUP, LANES_STEP), lambda b, g: (b, g))
-    line = pl.BlockSpec((1, LANES_STEP), lambda b, g: (0, g))
+    blocks, steps, heads = tokens // GROUP, width // GATE_LANES, rows.shape[1]
+    wide = pl.BlockSpec((GROUP, GATE_LANES), lambda b, g: (b, g))
+    line = pl.BlockSpec((1, GATE_LANES), lambda b, g: (0, g))
     return pl.pallas_call(
         functools.partial(mix_kernel, heads),
         grid=(blocks, steps),
@@ -247,7 +270,7 @@
             pl.BlockSpec((GROUP, 2 * STATE), lambda b, g: (b, 0)),
             pl.BlockSpec((GROUP, 128), lambda b, g: (b, 0)),
             pl.BlockSpec((1, heads, GROUP), lambda b, g: (b, 0, 0)),
-            pl.BlockSpec((1, STATE, LANES_STEP), lambda b, g: (b, 0, g)),
+            pl.BlockSpec((1, STATE, GATE_LANES), lambda b, g: (b, 0, g)),
             line, line,
         ],
         out_specs=[wide, pl.BlockSpec((1, 8, GROUP), lambda b, g: (b, 0, 0))],
@@ -380,7 +403,7 @@
     grown = jnp.exp(cols)
     shrunk = jnp.exp(cols[GROUP - 1 : GROUP, :] - cols)
     low_half = low_lanes(GROUP)
-    lower = lower_mask()
+    mask = quarter_mask()
     grad_write = jnp.zeros((GROUP, STATE), F32)
     grad_read = jnp.zeros((GROUP, STATE), F32)
     for pair in range(HEADS_STEP // 2):
@@ -408,14 +431,31 @@
         grad_write = grad_write + dot((stepped * tail).astype(BF16), flow, 1, 1)
         stepped_low = stepped.astype(BF16).astype(F32)
         inter = dot(wr_ref[:, :STATE], flow, 1, 0) * tail
-        total = jnp.zeros_like(inter)
+        top = jnp.zeros((HALF, PAIR), F32)
+        bottom = jnp.zeros((HALF, PAIR), F32)
         for side in range(2):
             head = 2 * pair + side
             row = rows_ref[0, pl.ds(g * HEADS_STEP + head, 1), :]
-            decay = jnp.exp(jnp.where(lower, cols[:, heads + head : heads + head + 1] - row, -1e30))
-            weights = (scores_ref[...] * decay).astype(BF16)
-            total = total + dot(weights, g_halves[side], 0, 0)
-            gscores_ref[...] += dot(grad, x_halves[side], 1, 1) * decay
+            early, cross, late = decays(cols[:, heads + head : heads + head + 1], row, mask)
+            left = jnp.concatenate(
+                [
+                    (scores_ref[:HALF, :HALF] * early).astype(BF16),
+                    (scores_ref[HALF:, :HALF] * cross).astype(BF16),
+                ],
+                axis=0,
+            )
+            right = (scores_ref[HALF:, HALF:] * late).astype(BF16)
+            top = top + dot(left, g_halves[side], 0, 0)
+            bottom = bottom + dot(right, g_halves[side][HALF:], 0, 0)
+            under = dot(grad[HALF:], x_halves[side], 1, 1)
+            terms = (
+                dot(grad[:HALF], x_halves[side][:HALF], 1, 1) * early, under[:, :HALF] * cross, under[:, HALF:] * late,
+            )
+            quarters = terms if side == 0 else tuple(a + b for a, b in zip(quarters, terms))
+        gscores_ref[:HALF, :HALF] += quarters[0]
+        gscores_ref[HALF:, :HALF] += quarters[1]
+        gscores_ref[HALF:, HALF:] += quarters[2]
+        total = jnp.concatenate([top, bottom], axis=0)
         both = total + inter
         prod_ref[0, :, lanes] = x * both
         prod_ref[1, :, lanes] = grad_f * (mixed_ref[:, lanes] - skip * x) - stepped_low * total
@@ -505,7 +545,7 @@
             jnp.int32, (GROUP, GROUP), 1
         )
         reverse_sum = (
-            split_dot(lower.astype(BF16), v_ref[...], 2, 0)
+            split_dot(lower_mask().astype(BF16), v_ref[...], 2, 0)
             + split_dot(strict.astype(BF16), i_ref[...], 2, 1)
             + jnp.exp(cum[GROUP - 1 : GROUP, :]) * e_ref[8:9, 0:128]
         )
@@ -1113,7 +1153,7 @@
     normed_out, grad_gate_pre, *_ = lax.optimization_barrier((normed_out, grad_gate_pre, ready[0], ready[1]))
     grad_proj_out = dot(masked, normed_out, 0, 0).astype(BF16)
     grad_gate_w = dot(normed, grad_gate_pre, 0, 0).astype(BF16)
-    grad_by_gate = dot(grad_gate_pre, full_gate, 1, 1)
+    grad_by_gate = dot(grad_gate_pre, full_gate, 1, 1).astype(BF16)
     other_scale = swap(in_scale.reshape(-1, 128), 2)
 
     flowing = local_grad[:, groups - 1]

time: 507 us -> 500 us (0.986)
  waiting for transfers between devices: 20.5 us -> 11.3 us
  starting transfers between devices: 21.9 us -> 30.8 us
  Pallas kernels: 272 us -> 266 us
    ppermute x6, starting transfers between devices: 8.83 us -> 19 us  [passed_along(): return lax.ppermute(x, axis, pairs)]
    all_gather x1, waiting for transfers between devices: 6.32 us -> 0.01 us  [gathered(): return lax.all_gather(x, ('fsdp', 'ctx'), axis=0, tiled=True)]
    unnamed x113 -> x125, local copies, waits for them, and re-layouts: 10.1 us -> 11.9 us
  transfers between devices with their start and end apart: 19 -> 19, of which waited for: 5 -> 3; matrix products, arithmetic and copies ran while one was open for 20% -> 19% of each run, Pallas kernels for 14% -> 14%
where the time goes in v6:
time: 500 us; the launch traced here: 493 us
  Pallas kernels  266 us (53%)
  matrix products  88 us (18%)
  other arithmetic  44.4 us (9%)
  local copies, waits for them, and re-layouts  36.6 us (7%)
  starting transfers between devices  30.8 us (6%)
  between operations  15.3 us (3%)
  waiting for transfers between devices  11.3 us (2%)
    dot_general x16, matrix products, dot(): lax.dot_general(a, b, (((da,), (db,)), ((), ())), preferred_element_type=...  88 us
    pallas_call x1, Pallas kernels, fetch(): pl.pallas_call(fetch_kernel, in_specs=[anywhere] * 6, out_specs=[anywhere...  83 us
    pallas_call x1, Pallas kernels, finish(): pl.pallas_call(finish_kernel, in_specs=[anywhere, anywhere, anywhere, any...  70.2 us
    pallas_call x1, Pallas kernels, back_blocks(): pl.pallas_call(functools.partial(back_kernel, groups, heads), grid=(block...  49.6 us
    pallas_call x1, Pallas kernels, mix_blocks(): pl.pallas_call(functools.partial(mix_kernel, heads), grid=(blocks, steps)...  29.5 us
    ppermute x6, starting transfers between devices, passed_along(): return lax.ppermute(x, axis, pairs)  19 us
    pallas_call x1, Pallas kernels, start_blocks(): pl.pallas_call(functools.partial(start_kernel, groups, heads), grid=(bloc...  18.4 us
    pallas_call x1, Pallas kernels, gate_blocks(): pl.pallas_call(functools.partial(gate_kernel, heads), grid=(steps, blocks...  15.5 us
  transfers between devices with their start and end apart: 19, of which 3 were waited for; matrix products, arithmetic and copies ran while one was open for 19% of the time, Pallas kernels for 14%

profile of v6, /device:TPU:0, one launch (start us, length us, event | category | flops | bytes accessed | tf_op | source)
XLA Modules:
  0.0 492.7 jit_solution(14413248468499701478)
XLA Ops:
  10.9 2.3 fusion.71
  15.5 83.0 %fetch.1 = (bf16[1,1024,1536]{2,1,0:T(8,128)(2,1)}, bf16[1536,1536]{1,0:T(8,128)(2,1)}, bf16[192,1536]{1,0:T(8,128)(2,1)}, bf16[1536,256]{1,0:T(8,128)(2,1)}, bf...) custom-call(bf16[2,1024,384]{2,1,0:T(8,128)(2,1)} %x_ref.1, bf16[192,768]{1,0:T(8,128)(2,1)} %get-tuple-element.178.inner_ref, ...), custom_call_target="tpu_custom_call" | custom-call | tf_op jit(solution)/shard_map/fetch/pallas_call | solution.py:748
  102.0 2.6 constant_dynamic-slice_fusion.2
  106.1 2.9 collective-permute-start.2
  114.4 5.5 %convolution_convert_fusion.3.inner_ref.pre_ref = bf16[1024,1536]{1,0:T(8,128)(2,1)S(1)} fusion(bf16[1536,1536]{1,0:T(8,128)(2,1)S(1)} %bitcast.215, bf16[1,1024,1536]{2,1,0:T(8,128)(2,1)S(1)} %copy-done.3, f32[1536]{0:T(1024)S(1)} %mul.239, f32[1024]{0:T(1024)S(1)} %get-tuple-element.174), kind=kOutput, calls=%fused_computation.27 | convolution fusion | flops 4839702528 | bytes 11020288 | tf_op jit(solution)/shard_map/dot_general | solution.py:56
  121.6 12.4 %collective-permute-start = (bf16[1,3,1536]{2,1,0:T(4,128)(2,1)S(1)}, bf16[1,3,1536]{2,1,0:T(4,128)(2,1)S(1)}, u32[]{:S(2)}, u32[]{:S(2)}) collective-permute-start(bf16[1,3,1536]{2,1,0:T(4,128)(2,1)S(1)} %slice.305), channel_id=1, source_target_pairs={{0,4},{1,5},{2,6},{3,7},{8,12},{9,13},{10,14},{11,15},{16,20},{17,... | collective-permute-start | bytes 27656 | tf_op jit(solution)/shard_map/ppermute | solution.py:35
  138.3 18.4 %start_blocks.1 = (bf16[1024,1536]{1,0:T(8,128)(2,1)}, bf16[1024,1536]{1,0:T(8,128)(2,1)}, bf16[1024,256]{1,0:T(8,128)(2,1)}, f32[1024,256]{1,0:T(8,128)}, f32[1...) custom-call(bf16[1024,1536]{1,0:T(8,128)(2,1)} %copy-done.14, ...), custom_call_target="tpu_custom_call" | custom-call | flops 434110464 | bytes 12582912 | tf_op jit(solution)/shard_map/start_blocks/pallas_call | solution.py:160
  157.6 2.3 fusion.37
  164.3 9.1 %fusion.12.gate_ref = bf16[1024,1536]{1,0:T(8,128)(2,1)} fusion(bf16[1536,3072]{1,0:T(8,128)(2,1)} %all-gather.2.cloned.1.call-done, bf16[1,1024,1536]{2,1,0:T(8,128)(2,1)S(1)} %copy-done.3, f32[1536]{0:T(1024)S(1)} %mul.239, f32[1024]{0:T(1024)S(1)} %get-tuple-element.174), kind=kOutput, calls=%fused_computation.24 | convolution fusion | flops 4839702528 | bytes 11020288 | tf_op jit(solution)/shard_map/dot_general | solution.py:56
  173.4 2.3 broadcast_select_fusion.7
  175.8 6.7 %fusion.18.gno_ref = bf16[1024,1536]{1,0:T(8,128)(2,1)} fusion(bf16[1536,3072]{1,0:T(8,128)(2,1)S(1)} %copy-done.52, bf16[1,1024,384]{2,1,0:T(8,128)(2,1)S(1)} %get-tuple-element.154, bf16[1,1024,384]{2,1,0:T(8,128)(2,1)S(1)} %get-tuple-element.153, bf16[1,1024,384]{2,1,0:T(8,128)(2,1)S(1)} %get-tuple-element.152, ...), kind=kOutput, calls=%fused_computation.26 | convolution fusion | flops 4850712576 | bytes 11014144 | tf_op jit(solution)/shard_map/dot_general | solution.py:56
  182.5 29.5 %mix_blocks.1 = (f32[1024,1536]{1,0:T(8,128)}, f32[4,8,256]{2,1,0:T(8,128)}) custom-call(bf16[1024,1536]{1,0:T(8,128)(2,1)} %get-tuple-element.72.x_ref, bf16[1024,1536]{1,0:T(8,128)(2,1)} %fusion.12.gate_ref, bf16[1024,1536]{1,0:T(8,128)(2,1)} %fusion.18.gno_ref, bf16[1024,256]{1,0:T(8,128)(2,1)} %get-tuple-element.80.wr_ref, ...), custom_call_target="tpu_custom_call" | custom-call | flops 4831838208 | bytes 15728640 | tf_op jit(solution)/shard_map/mix_blocks/pallas_call | solution.py:265
  212.1 4.1 collective-permute-done.6
  217.6 15.5 %gate_blocks.1 = (bf16[1024,1536]{1,0:T(8,128)(2,1)}, bf16[1024,1536]{1,0:T(8,128)(2,1)}, bf16[1024,1536]{1,0:T(8,128)(2,1)}, f32[1,1536]{1,0:T(1,128)}, f32[1,1536]{1,0:T(1,128)}, /*index=5*/f32[4,128,1536]{2,1,0:T(8,128)}) custom-call(f32[1024,1536]{1,0:T(8,128)} %get-tuple-element.85.mixed_ref, bf16[1024,1536]{1,0:T(8,128)(2,1)} %fusion.12.gate_ref, ...), custom_call_target="tpu_custom_call" | custom-call | flops 402653184 | bytes 28311552 | tf_op jit(solution)/shard_map/gate_blocks/pallas_call | solution.py:333
  233.0 5.1 %convolution_convert_fusion.4 = bf16[1024,384]{1,0:T(8,128)(2,1)} fusion(bf16[1024,1536]{1,0:T(8,128)(2,1)} %get-tuple-element.93, bf16[1536,3072]{1,0:T(8,128)(2,1)} %all-gather.2.cloned.1.call-done, s32[]{:T(128)S(6)} %select_n.130), kind=kOutput, calls=%fused_computation.45 | convolution fusion | flops 1208352768 | bytes 5111812 | tf_op jit(solution)/shard_map/dot_general | solution.py:56
  238.2 4.1 convolution_convert_fusion.5
  242.3 6.0 %convolution_convert_fusion.1 = bf16[1536,1536]{1,0:T(8,128)(2,1)S(1)} fusion(bf16[1024,1536]{1,0:T(8,128)(2,1)S(1)} %copy-done.53, bf16[1,1024,384]{2,1,0:T(8,128)(2,1)S(1)} %copy-done.28, bf16[1,1024,384]{2,1,0:T(8,128)(2,1)S(1)} %copy-done.26, bf16[1,1024,384]{2,1,0:T(8,128)(2,1)S(1)} %copy-done.24, bf16[1,1024,384]{2,1,0:T(8,128)(2,1)S(1)} %copy-done.22, ...), kind=kOutput, calls=%fused_computation.4 | convolution fusion | flops 4851499008 | bytes 11014144 | tf_op jit(solution)/shard_map/dot_general | solution.py:56
  248.3 5.7 %convolution_convert_fusion = bf16[1536,1536]{1,0:T(8,128)(2,1)S(1)} fusion(bf16[1024,1536]{1,0:T(8,128)(2,1)S(1)} %copy-done.55, bf16[1,1024,1536]{2,1,0:T(8,128)(2,1)S(1)} %copy-done.3, f32[1536]{0:T(1024)S(1)} %mul.239, f32[1024]{0:T(1024)S(1)} %get-tuple-element.174), kind=kOutput, calls=%fused_computation.3 | convolution fusion | flops 4840488960 | bytes 11020288 | tf_op jit(solution)/shard_map/dot_general | solution.py:56
  254.0 4.8 pad_maximum_fusion
  263.6 9.4 %fusion.15 = bf16[1024,1536]{1,0:T(8,128)(2,1)} fusion(bf16[1024,1536]{1,0:T(8,128)(2,1)S(1)} %copy-done.56, bf16[1536,3072]{1,0:T(8,128)(2,1)} %all-gather.2.cloned.1.call-done), kind=kOutput, calls=%fused_computation.25 | convolution fusion | flops 4833411072 | bytes 11010048 | tf_op jit(solution)/shard_map/dot_general | solution.py:56
  274.7 6.0 %collective-permute-done.8 = bf16[1024,384]{1,0:T(8,128)(2,1)S(1)} collective-permute-done((bf16[1024,384]{1,0:T(8,128)(2,1)}, bf16[1024,384]{1,0:T(8,128)(2,1)S(1)}, u32[]{:S(2)}, u32[]{:S(2)}) %collective-permute-start.8) | collective-permute-done | bytes 786464 | tf_op jit(solution)/shard_map/ppermute | solution.py:29
  280.7 4.0 add_convert_fusion.1
  284.6 2.3 collective-permute-start.11
  287.0 49.6 %back_blocks.1 = (bf16[1024,1536]{1,0:T(8,128)(2,1)}, bf16[1024,384]{1,0:T(8,128)(2,1)}, f32[4,8,384]{2,1,0:T(8,128)}, f32[8,256]{1,0:T(8,128)}, f32[8,128]{1,0:...) custom-call(bf16[1024,1536]{1,0:T(8,128)(2,1)} %get-tuple-element.72.x_ref, ...), custom_call_target="tpu_custom_call" | custom-call | flops 9663676416 | bytes 22020096 | tf_op jit(solution)/shard_map/back_blocks/pallas_call | solution.py:569
  339.3 4.3 add_bitcast_fusion.1
  349.6 4.3 fusion.28
  355.2 2.8 add_convert_fusion
  358.0 7.3 %convolution_convert_fusion.2.grad_ref = bf16[1536,1920]{1,0:T(8,128)(2,1)S(1)} fusion(bf16[1024,1920]{1,0:T(8,128)(2,1)S(1)} %pad_maximum_fusion.1, bf16[1,1024,1536]{2,1,0:T(8,128)(2,1)S(1)} %copy-done.4, f32[1536]{0:T(1024)S(1)} %mul.239, f32[1024]{0:T(1024)S(1)} %get-tuple-element.174), kind=kOutput, calls=%fused_computation.5 | convolution fusion | flops 6049038336 | bytes 12986368 | tf_op jit(solution)/shard_map/dot_general | solution.py:56
  365.3 2.5 copy-done.2
  378.5 8.6 %fusion.72 = f32[1024,1536]{1,0:T(8,128)S(1)} fusion(bf16[1024,1536]{1,0:T(8,128)(2,1)} %fusion.43, bf16[1536,1536]{1,0:T(8,128)(2,1)} %get-tuple-element.69), kind=kOutput, calls=%fused_computation.163 | convolution fusion | flops 4831838208 | bytes 14155776 | tf_op jit(solution)/shard_map/dot_general | solution.py:56
  387.1 3.3 multiply_reduce_fusion
  397.6 70.2 %finish.1 = (bf16[1024,384]{1,0:T(8,128)(2,1)}, bf16[1024,384]{1,0:T(8,128)(2,1)}, f32[192,768]{1,0:T(8,128)}, f32[192,512]{1,0:T(8,128)}, f32[16,1536]{1,0:T(8,...) custom-call(bf16[1024,1536]{1,0:T(8,128)(2,1)} %convert_element_type.196.part_ref, ...), custom_call_target="tpu_custom_call" | custom-call | tf_op jit(solution)/shard_map/finish/pallas_call | solution.py:905
  (244 shorter events, 80.5 us)
Async XLA Ops:
  7.2 157.1 %all-gather.2.cloned.1.call-start = ((), (), s32[]{:S(2)}) async-start(), calls=%async_computation.1 | async-start | bytes 10616832 | tf_op jit(solution)/shard_map/all_gather | solution.py:1040
  99.6 9.6 %copy-start.3 = (bf16[1,1024,1536]{2,1,0:T(8,128)(2,1)S(1)}, bf16[1,1024,1536]{2,1,0:T(8,128)(2,1)}, u32[]{:S(2)}) copy-start(bf16[1,1024,1536]{2,1,0:T(8,128)(2,1)} %get-tuple-element.67) | copy-start | bytes 9437188
  101.9 245.1 %reduce-scatter.2.cloned.1.call-start = ((), (), s32[]{:S(2)}) async-start(), calls=%async_computation.2 | async-start | bytes 10616832 | tf_op jit(solution)/shard_map/reduce_scatter | solution.py:1190
  104.7 68.8 %collective-permute-start.4 = (bf16[1,1024,384]{2,1,0:T(8,128)(2,1)}, bf16[1,1024,384]{2,1,0:T(8,128)(2,1)}, u32[]{:S(2)}, u32[]{:S(2)}) collective-permute-start(bf16[1,1024,384]{2,1,0:T(8,128)(2,1)} %get-tuple-element.74), channel_id=1, source_target_pairs={{0,3},{1,2},{2,1},{3,0},{4,7},{5,6},{6,5},{7,4},{8,11},{9,10},{10,... | collective-permute-start | bytes 2359304 | tf_op jit(solution)/shard_map/ppermute | solution.py:29
  106.1 67.3 %collective-permute-start.3 = (bf16[1,1024,384]{2,1,0:T(8,128)(2,1)}, bf16[1,1024,384]{2,1,0:T(8,128)(2,1)}, u32[]{:S(2)}, u32[]{:S(2)}) collective-permute-start(bf16[1,1024,384]{2,1,0:T(8,128)(2,1)} %get-tuple-element.74), channel_id=1, source_target_pairs={{0,2},{1,3},{2,0},{3,1},{4,6},{5,7},{6,4},{7,5},{8,10},{9,11},{10,... | collective-permute-start | bytes 2359304 | tf_op jit(solution)/shard_map/ppermute | solution.py:29
  106.1 67.3 %collective-permute-start.2 = (bf16[1,1024,384]{2,1,0:T(8,128)(2,1)}, bf16[1,1024,384]{2,1,0:T(8,128)(2,1)}, u32[]{:S(2)}, u32[]{:S(2)}) collective-permute-start(bf16[1,1024,384]{2,1,0:T(8,128)(2,1)} %get-tuple-element.73), channel_id=1, source_target_pairs={{0,1},{1,0},{2,3},{3,2},{4,5},{5,4},{6,7},{7,6},{8,9},{9,8},{10,11... | collective-permute-start | bytes 2359304 | tf_op jit(solution)/shard_map/ppermute | solution.py:29
  109.1 248.9 %copy-start.33 = (f32[1536]{0:T(1024)}, f32[1536]{0:T(1024)S(1)}, u32[]{:S(2)}) copy-start(f32[1536]{0:T(1024)S(1)} %mul.239) | copy-start | bytes 18436
  113.0 24.6 %collective-permute-start.1 = (bf16[1,3,256]{2,1,0:T(4,128)(2,1)S(1)}, bf16[1,3,256]{2,1,0:T(4,128)(2,1)S(1)}, u32[]{:S(2)}, u32[]{:S(2)}) collective-permute-start(bf16[1,3,256]{2,1,0:T(4,128)(2,1)S(1)} %slice.307), channel_id=1, source_target_pairs={{0,4},{1,5},{2,6},{3,7},{8,12},{9,13},{10,14},{11,15},{16,20},{17,... | collective-permute-start | bytes 4616 | tf_op jit(solution)/shard_map/ppermute | solution.py:35
  114.3 20.0 %copy-start.48 = (f32[12]{0:T(128)S(1)}, f32[12]{0:T(128)}, u32[]{:S(2)}) copy-start(f32[12]{0:T(128)} %param.28) | copy-start | bytes 148
  114.3 20.1 %copy-start.49 = (f32[12]{0:T(128)S(1)}, f32[12]{0:T(128)}, u32[]{:S(2)}) copy-start(f32[12]{0:T(128)} %param.27) | copy-start | bytes 148
  114.4 20.7 %copy-start.38 = (f32[768]{0:T(1024)S(1)}, f32[768]{0:T(1024)}, u32[]{:S(2)}) copy-start(f32[768]{0:T(1024)} %param.29) | copy-start | bytes 9220
  114.4 20.7 %copy-start.39 = (f32[768]{0:T(1024)S(1)}, f32[768]{0:T(1024)}, u32[]{:S(2)}) copy-start(f32[768]{0:T(1024)} %param.23) | copy-start | bytes 9220
  114.4 20.7 %copy-start.32 = (f32[4,768]{1,0:T(4,128)S(1)}, f32[4,768]{1,0:T(4,128)}, u32[]{:S(2)}) copy-start(f32[4,768]{1,0:T(4,128)} %param.22) | copy-start | bytes 36868
  114.4 20.7 %copy-start.50 = (f32[12]{0:T(128)S(1)}, f32[12]{0:T(128)}, u32[]{:S(2)}) copy-start(f32[12]{0:T(128)} %param.26) | copy-start | bytes 148
  121.6 16.1 %collective-permute-start = (bf16[1,3,1536]{2,1,0:T(4,128)(2,1)S(1)}, bf16[1,3,1536]{2,1,0:T(4,128)(2,1)S(1)}, u32[]{:S(2)}, u32[]{:S(2)}) collective-permute-start(bf16[1,3,1536]{2,1,0:T(4,128)(2,1)S(1)} %slice.305), channel_id=1, source_target_pairs={{0,4},{1,5},{2,6},{3,7},{8,12},{9,13},{10,14},{11,15},{16,20},{17,... | collective-permute-start | bytes 27656 | tf_op jit(solution)/shard_map/ppermute | solution.py:35
  138.3 23.0 %copy-start.51 = (s32[2]{0:T(128)S(1)}, s32[2]{0:T(128)}, u32[]{:S(2)}) copy-start(s32[2]{0:T(128)} %param.17) | copy-start | bytes 28
  160.0 2.6 collective-permute-start.5
  164.3 11.4 %copy-start.52 = (bf16[1536,3072]{1,0:T(8,128)(2,1)S(1)}, bf16[1536,3072]{1,0:T(8,128)(2,1)}, u32[]{:S(2)}) copy-start(bf16[1536,3072]{1,0:T(8,128)(2,1)} %all-gather.2.cloned.1.call-done) | copy-start | bytes 28311556
  212.0 4.2 collective-permute-start.6
  258.8 111.5 %collective-permute-start.12 = (f32[8,128]{1,0:T(8,128)}, f32[8,128]{1,0:T(8,128)}, u32[]{:S(2)}, u32[]{:S(2)}) collective-permute-start(f32[8,128]{1,0:T(8,128)} %get-tuple-element.173), channel_id=1, source_target_pairs={{0,2},{1,3},{2,0},{3,1},{4,6},{5,7},{6,4},{7,5},{8,10},{9,11},{10,... | collective-permute-start | bytes 12296 | tf_op jit(solution)/shard_map/ppermute | solution.py:29
  260.0 20.6 %collective-permute-start.8 = (bf16[1024,384]{1,0:T(8,128)(2,1)}, bf16[1024,384]{1,0:T(8,128)(2,1)S(1)}, u32[]{:S(2)}, u32[]{:S(2)}) collective-permute-start(bf16[1024,384]{1,0:T(8,128)(2,1)} %convolution_convert_fusion.5), channel_id=1, source_target_pairs={{0,1},{1,0},{2,3},{3,2},{4,5},{5,4},{6,7},{7,6},{8,9},{9,8},{10,11... | collective-permute-start | bytes 2359304 | tf_op jit(solution)/shard_map/ppermute | solution.py:29
  261.6 77.7 %collective-permute-start.10 = (bf16[1024,384]{1,0:T(8,128)(2,1)}, bf16[1024,384]{1,0:T(8,128)(2,1)}, u32[]{:S(2)}, u32[]{:S(2)}) collective-permute-start(bf16[1024,384]{1,0:T(8,128)(2,1)} %convolution_convert_fusion.4), channel_id=1, source_target_pairs={{0,1},{1,0},{2,3},{3,2},{4,5},{5,4},{6,7},{7,6},{8,9},{9,8},{10,11... | collective-permute-start | bytes 2359304 | tf_op jit(solution)/shard_map/ppermute | solution.py:29
  262.3 10.7 %collective-permute-start.7 = (bf16[1,128,1536]{2,1,0:T(8,128)(2,1)S(1)}, bf16[1,128,1536]{2,1,0:T(8,128)(2,1)S(1)}, u32[]{:S(2)}, u32[]{:S(2)}) collective-permute-start(bf16[1,128,1536]{2,1,0:T(8,128)(2,1)S(1)} %fusion.35), channel_id=1, source_target_pairs={{4,0},{5,1},{6,2},{7,3},{12,8},{13,9},{14,10},{15,11},{20,16},{21,... | collective-permute-start | bytes 1179656 | tf_op jit(solution)/shard_map/ppermute | solution.py:35
  284.6 60.5 %collective-permute-start.11 = (bf16[1024,384]{1,0:T(8,128)(2,1)}, bf16[1024,384]{1,0:T(8,128)(2,1)S(1)}, u32[]{:S(2)}, u32[]{:S(2)}) collective-permute-start(bf16[1024,384]{1,0:T(8,128)(2,1)} %add_convert_fusion.1), channel_id=1, source_target_pairs={{0,2},{1,3},{2,0},{3,1},{4,6},{5,7},{6,4},{7,5},{8,10},{9,11},{10,... | collective-permute-start | bytes 2359304 | tf_op jit(solution)/shard_map/ppermute | solution.py:29
  336.6 7.0 %collective-permute-start.13 = (f32[1,8,256]{2,1,0:T(8,128)}, f32[1,8,256]{2,1,0:T(8,128)S(1)}, u32[]{:S(2)}, u32[]{:S(2)}) collective-permute-start(f32[1,8,256]{2,1,0:T(8,128)} %get-tuple-element.101), channel_id=1, source_target_pairs={{4,0},{5,1},{6,2},{7,3},{12,8},{13,9},{14,10},{15,11},{20,16},{21,... | collective-permute-start | bytes 24584 | tf_op jit(solution)/shard_map/ppermute | solution.py:35
  337.9 5.8 %collective-permute-start.9 = (f32[1,8,1536]{2,1,0:T(8,128)}, f32[1,8,1536]{2,1,0:T(8,128)S(1)}, u32[]{:S(2)}, u32[]{:S(2)}) collective-permute-start(f32[1,8,1536]{2,1,0:T(8,128)} %get-tuple-element.97), channel_id=1, source_target_pairs={{4,0},{5,1},{6,2},{7,3},{12,8},{13,9},{14,10},{15,11},{20,16},{21,... | collective-permute-start | bytes 147464 | tf_op jit(solution)/shard_map/ppermute | solution.py:35
  349.0 29.6 %collective-permute-start.14 = (bf16[192,1536]{1,0:T(8,128)(2,1)}, bf16[192,1536]{1,0:T(8,128)(2,1)}, u32[]{:S(2)}, u32[]{:S(2)}) collective-permute-start(bf16[192,1536]{1,0:T(8,128)(2,1)} %pad_maximum_fusion.7), channel_id=1, source_target_pairs={{0,2},{1,3},{2,0},{3,1},{4,6},{5,7},{6,4},{7,5},{8,10},{9,11},{10,... | collective-permute-start | bytes 1769480 | tf_op jit(solution)/shard_map/ppermute | solution.py:29
  369.6 27.9 %collective-permute-start.16 = (bf16[4,192,1920]{2,1,0:T(8,128)(2,1)}, bf16[4,192,1920]{2,1,0:T(8,128)(2,1)}, u32[]{:S(2)}, u32[]{:S(2)}) collective-permute-start(bf16[4,192,1920]{2,1,0:T(8,128)(2,1)} %dynamic-slice_bitcast_fusion), channel_id=1, source_target_pairs={{0,4},{4,0},{1,5},{5,1},{2,6},{6,2},{3,7},{7,3},{8,12},{12,8},{9,1... | collective-permute-start | bytes 8847368 | tf_op jit(solution)/shard_map/ppermute | solution.py:1212
  377.1 10.0 %copy-start.5 = (bf16[1,1024,1536]{2,1,0:T(8,128)(2,1)S(1)}, bf16[1,1024,1536]{2,1,0:T(8,128)(2,1)}, u32[]{:S(2)}) copy-start(bf16[1,1024,1536]{2,1,0:T(8,128)(2,1)} %get-tuple-element.67) | copy-start | bytes 9437188
  377.1 10.0 %copy-start.12 = (bf16[1024,1536]{1,0:T(8,128)(2,1)S(1)}, bf16[1024,1536]{1,0:T(8,128)(2,1)}, u32[]{:S(2)}) copy-start(bf16[1024,1536]{1,0:T(8,128)(2,1)} %fusion.15) | copy-start | bytes 9437188
  377.1 10.0 %copy-start.34 = (f32[1536]{0:T(1024)S(1)}, f32[1536]{0:T(1024)}, u32[]{:S(2)}) copy-start(f32[1536]{0:T(1024)} %copy-done.33) | copy-start | bytes 18436
  377.1 20.4 %collective-permute-start.15 = (bf16[1024,384]{1,0:T(8,128)(2,1)}, bf16[1024,384]{1,0:T(8,128)(2,1)}, u32[]{:S(2)}, u32[]{:S(2)}) collective-permute-start(bf16[1024,384]{1,0:T(8,128)(2,1)} %add_convert_fusion), channel_id=1, source_target_pairs={{0,1},{1,0},{2,3},{3,2},{4,5},{5,4},{6,7},{7,6},{8,9},{9,8},{10,11... | collective-permute-start | bytes 2359304 | tf_op jit(solution)/shard_map/ppermute | solution.py:29
  (46 other events, 180.5 us)
Sparse Core Ops, SparseCore 0:
  102.1 57.7 all-gather.1
  258.9 75.9 reduce-scatter.1

commit v7 on v6

--- a/solution.py
+++ b/solution.py
@@ -1166,7 +1166,7 @@
         flowing = decay_lanes[:, position] * flowing + local_grad[:, position]
     flows = jnp.stack(flow_list, axis=1)
     flows_low = flows.astype(BF16).reshape(blocks, STATE, inner)
-    flows_low = after(flows_low, (grad_proj_out, grad_gate_w, ready[2]))
+    flows_low = after(flows_low, (grad_proj_out, grad_gate_w, ready[2], other_scale))
 
     grad_inner_pre, grad_narrow, tap_sums, narrow_sums, head_sums, halo, narrow_halo = back_blocks(
         inner_act, mixed_out, grad_diag, slope, inner_pre, inner_rim, write_read, narrow_slope, narrow_pre,

time: 500 us -> 503 us (level)
  the two profiles are of different devices: /device:TPU:0 before, /device:TPU:18 now
where the time goes in v7:
time: 503 us; the launch traced here: 498 us
  Pallas kernels  271 us (54%)
  matrix products  87.9 us (17%)
  other arithmetic  43 us (9%)
  local copies, waits for them, and re-layouts  36.9 us (7%)
  starting transfers between devices  35.5 us (7%)
  between operations  15.3 us (3%)
  waiting for transfers between devices  9.1 us (2%)
    dot_general x16, matrix products, dot(): lax.dot_general(a, b, (((da,), (db,)), ((), ())), preferred_element_type=...  87.9 us
    pallas_call x1, Pallas kernels, finish(): pl.pallas_call(finish_kernel, in_specs=[anywhere, anywhere, anywhere, any...  79.8 us
    pallas_call x1, Pallas kernels, fetch(): pl.pallas_call(fetch_kernel, in_specs=[anywhere] * 6, out_specs=[anywhere...  77.6 us
    pallas_call x1, Pallas kernels, back_blocks(): pl.pallas_call(functools.partial(back_kernel, groups, heads), grid=(block...  49.7 us
    pallas_call x1, Pallas kernels, mix_blocks(): pl.pallas_call(functools.partial(mix_kernel, heads), grid=(blocks, steps)...  29.4 us
    ppermute x6, starting transfers between devices, passed_along(): return lax.ppermute(x, axis, pairs)  19 us
    pallas_call x1, Pallas kernels, start_blocks(): pl.pallas_call(functools.partial(start_kernel, groups, heads), grid=(bloc...  18.4 us
    ppermute x10, starting transfers between devices, swap(): return lax.ppermute(x, 'tp', [(i, i ^ bit) for i in range(count)])  15.6 us
  transfers between devices with their start and end apart: 19, of which 3 were waited for; matrix products, arithmetic and copies ran while one was open for 19% of the time, Pallas kernels for 14%

profile of v7, /device:TPU:18, one launch (start us, length us, event | category | flops | bytes accessed | tf_op | source)
XLA Modules:
  0.0 498.3 jit_solution(395729837332421356)
XLA Ops:
  10.9 2.3 fusion.71
  15.5 77.6 %fetch.1 = (bf16[1,1024,1536]{2,1,0:T(8,128)(2,1)}, bf16[1536,1536]{1,0:T(8,128)(2,1)}, bf16[192,1536]{1,0:T(8,128)(2,1)}, bf16[1536,256]{1,0:T(8,128)(2,1)}, bf...) custom-call(bf16[2,1024,384]{2,1,0:T(8,128)(2,1)} %x_ref.1, bf16[192,768]{1,0:T(8,128)(2,1)} %get-tuple-element.178.inner_ref, ...), custom_call_target="tpu_custom_call" | custom-call | tf_op jit(solution)/shard_map/fetch/pallas_call | solution.py:748
  94.3 2.3 pad_maximum_fusion.4
  96.6 2.7 constant_dynamic-slice_fusion.2
  100.7 4.3 collective-permute-start.3
  110.4 5.5 %convolution_convert_fusion.3.inner_ref.pre_ref = bf16[1024,1536]{1,0:T(8,128)(2,1)S(1)} fusion(bf16[1536,1536]{1,0:T(8,128)(2,1)S(1)} %bitcast.216, bf16[1,1024,1536]{2,1,0:T(8,128)(2,1)S(1)} %copy-done.3, f32[1536]{0:T(1024)S(1)} %mul.239, f32[1024]{0:T(1024)S(1)} %get-tuple-element.176), kind=kOutput, calls=%fused_computation.27 | convolution fusion | flops 4839702528 | bytes 11020288 | tf_op jit(solution)/shard_map/dot_general | solution.py:56
  117.5 12.4 %collective-permute-start = (bf16[1,3,1536]{2,1,0:T(4,128)(2,1)S(1)}, bf16[1,3,1536]{2,1,0:T(4,128)(2,1)S(1)}, u32[]{:S(2)}, u32[]{:S(2)}) collective-permute-start(bf16[1,3,1536]{2,1,0:T(4,128)(2,1)S(1)} %slice.305), channel_id=1, source_target_pairs={{0,4},{1,5},{2,6},{3,7},{8,12},{9,13},{10,14},{11,15},{16,20},{17,... | collective-permute-start | bytes 27656 | tf_op jit(solution)/shard_map/ppermute | solution.py:35
  134.2 18.4 %start_blocks.1 = (bf16[1024,1536]{1,0:T(8,128)(2,1)}, bf16[1024,1536]{1,0:T(8,128)(2,1)}, bf16[1024,256]{1,0:T(8,128)(2,1)}, f32[1024,256]{1,0:T(8,128)}, f32[1...) custom-call(bf16[1024,1536]{1,0:T(8,128)(2,1)} %copy-done.14, ...), custom_call_target="tpu_custom_call" | custom-call | flops 434110464 | bytes 12582912 | tf_op jit(solution)/shard_map/start_blocks/pallas_call | solution.py:160
  160.3 9.1 %fusion.12.gate_ref = bf16[1024,1536]{1,0:T(8,128)(2,1)} fusion(bf16[1536,3072]{1,0:T(8,128)(2,1)} %all-gather.2.cloned.1.call-done, bf16[1,1024,1536]{2,1,0:T(8,128)(2,1)S(1)} %copy-done.3, f32[1536]{0:T(1024)S(1)} %mul.239, f32[1024]{0:T(1024)S(1)} %get-tuple-element.176), kind=kOutput, calls=%fused_computation.24 | convolution fusion | flops 4839702528 | bytes 11020288 | tf_op jit(solution)/shard_map/dot_general | solution.py:56
  169.4 2.3 broadcast_select_fusion.7
  171.7 6.7 %fusion.18.gno_ref = bf16[1024,1536]{1,0:T(8,128)(2,1)} fusion(bf16[1536,3072]{1,0:T(8,128)(2,1)S(1)} %copy-done.54, bf16[1,1024,384]{2,1,0:T(8,128)(2,1)S(1)} %get-tuple-element.154, bf16[1,1024,384]{2,1,0:T(8,128)(2,1)S(1)} %get-tuple-element.153, bf16[1,1024,384]{2,1,0:T(8,128)(2,1)S(1)} %get-tuple-element.152, ...), kind=kOutput, calls=%fused_computation.26 | convolution fusion | flops 4850712576 | bytes 11014144 | tf_op jit(solution)/shard_map/dot_general | solution.py:56
  178.5 29.4 %mix_blocks.1 = (f32[1024,1536]{1,0:T(8,128)}, f32[4,8,256]{2,1,0:T(8,128)}) custom-call(bf16[1024,1536]{1,0:T(8,128)(2,1)} %get-tuple-element.72.x_ref, bf16[1024,1536]{1,0:T(8,128)(2,1)} %fusion.12.gate_ref, bf16[1024,1536]{1,0:T(8,128)(2,1)} %fusion.18.gno_ref, bf16[1024,256]{1,0:T(8,128)(2,1)} %get-tuple-element.80.wr_ref, ...), custom_call_target="tpu_custom_call" | custom-call | flops 4831838208 | bytes 15728640 | tf_op jit(solution)/shard_map/mix_blocks/pallas_call | solution.py:265
  207.9 2.2 collective-permute-start.6
  213.6 15.6 %gate_blocks.1 = (bf16[1024,1536]{1,0:T(8,128)(2,1)}, bf16[1024,1536]{1,0:T(8,128)(2,1)}, bf16[1024,1536]{1,0:T(8,128)(2,1)}, f32[1,1536]{1,0:T(1,128)}, f32[1,1536]{1,0:T(1,128)}, /*index=5*/f32[4,128,1536]{2,1,0:T(8,128)}) custom-call(f32[1024,1536]{1,0:T(8,128)} %get-tuple-element.85.mixed_ref, bf16[1024,1536]{1,0:T(8,128)(2,1)} %fusion.12.gate_ref, ...), custom_call_target="tpu_custom_call" | custom-call | flops 402653184 | bytes 28311552 | tf_op jit(solution)/shard_map/gate_blocks/pallas_call | solution.py:333
  229.2 5.1 %convolution_convert_fusion.4 = bf16[1024,384]{1,0:T(8,128)(2,1)} fusion(bf16[1024,1536]{1,0:T(8,128)(2,1)} %get-tuple-element.93, bf16[1536,3072]{1,0:T(8,128)(2,1)} %all-gather.2.cloned.1.call-done, s32[]{:T(128)S(6)} %select_n.130), kind=kOutput, calls=%fused_computation.45 | convolution fusion | flops 1208352768 | bytes 5111812 | tf_op jit(solution)/shard_map/dot_general | solution.py:56
  234.3 4.1 convolution_convert_fusion.5
  238.5 6.0 %convolution_convert_fusion.1 = bf16[1536,1536]{1,0:T(8,128)(2,1)S(1)} fusion(bf16[1024,1536]{1,0:T(8,128)(2,1)S(1)} %copy-done.55, bf16[1,1024,384]{2,1,0:T(8,128)(2,1)S(1)} %copy-done.28, bf16[1,1024,384]{2,1,0:T(8,128)(2,1)S(1)} %copy-done.26, bf16[1,1024,384]{2,1,0:T(8,128)(2,1)S(1)} %copy-done.24, bf16[1,1024,384]{2,1,0:T(8,128)(2,1)S(1)} %copy-done.22, ...), kind=kOutput, calls=%fused_computation.4 | convolution fusion | flops 4851499008 | bytes 11014144 | tf_op jit(solution)/shard_map/dot_general | solution.py:56
  244.5 5.7 %convolution_convert_fusion = bf16[1536,1536]{1,0:T(8,128)(2,1)S(1)} fusion(bf16[1024,1536]{1,0:T(8,128)(2,1)S(1)} %copy-done.57, bf16[1,1024,1536]{2,1,0:T(8,128)(2,1)S(1)} %copy-done.3, f32[1536]{0:T(1024)S(1)} %mul.239, f32[1024]{0:T(1024)S(1)} %get-tuple-element.176), kind=kOutput, calls=%fused_computation.3 | convolution fusion | flops 4840488960 | bytes 11020288 | tf_op jit(solution)/shard_map/dot_general | solution.py:56
  250.1 4.8 pad_maximum_fusion
  261.2 9.7 %fusion.15 = bf16[1024,1536]{1,0:T(8,128)(2,1)} fusion(bf16[1024,1536]{1,0:T(8,128)(2,1)S(1)} %copy-done.58, bf16[1536,3072]{1,0:T(8,128)(2,1)} %all-gather.2.cloned.1.call-done), kind=kOutput, calls=%fused_computation.25 | convolution fusion | flops 4833411072 | bytes 11010048 | tf_op jit(solution)/shard_map/dot_general | solution.py:56
  272.6 5.6 %collective-permute-done.8 = bf16[1024,384]{1,0:T(8,128)(2,1)S(1)} collective-permute-done((bf16[1024,384]{1,0:T(8,128)(2,1)}, bf16[1024,384]{1,0:T(8,128)(2,1)S(1)}, u32[]{:S(2)}, u32[]{:S(2)}) %collective-permute-start.8) | collective-permute-done | bytes 786464 | tf_op jit(solution)/shard_map/ppermute | solution.py:29
  278.2 4.0 add_convert_fusion.1
  283.2 49.7 %back_blocks.1 = (bf16[1024,1536]{1,0:T(8,128)(2,1)}, bf16[1024,384]{1,0:T(8,128)(2,1)}, f32[4,8,384]{2,1,0:T(8,128)}, f32[8,256]{1,0:T(8,128)}, f32[8,128]{1,0:...) custom-call(bf16[1024,1536]{1,0:T(8,128)(2,1)} %get-tuple-element.72.x_ref, ...), custom_call_target="tpu_custom_call" | custom-call | flops 9663676416 | bytes 22020096 | tf_op jit(solution)/shard_map/back_blocks/pallas_call | solution.py:569
  335.7 4.3 add_bitcast_fusion.1
  347.1 4.0 fusion.28
  352.4 2.8 add_convert_fusion
  355.2 7.3 %convolution_convert_fusion.2.grad_ref = bf16[1536,1920]{1,0:T(8,128)(2,1)S(1)} fusion(bf16[1024,1920]{1,0:T(8,128)(2,1)S(1)} %pad_maximum_fusion.1, bf16[1,1024,1536]{2,1,0:T(8,128)(2,1)S(1)} %copy-done.4, f32[1536]{0:T(1024)S(1)} %mul.239, f32[1024]{0:T(1024)S(1)} %get-tuple-element.176), kind=kOutput, calls=%fused_computation.5 | convolution fusion | flops 6049038336 | bytes 12986368 | tf_op jit(solution)/shard_map/dot_general | solution.py:56
  362.6 2.5 copy-done.2
  374.6 8.5 %fusion.72 = f32[1024,1536]{1,0:T(8,128)S(1)} fusion(bf16[1024,1536]{1,0:T(8,128)(2,1)} %fusion.43, bf16[1536,1536]{1,0:T(8,128)(2,1)} %get-tuple-element.69), kind=kOutput, calls=%fused_computation.163 | convolution fusion | flops 4831838208 | bytes 14155776 | tf_op jit(solution)/shard_map/dot_general | solution.py:56
  383.1 3.3 multiply_reduce_fusion
  393.6 79.8 %finish.1 = (bf16[1024,384]{1,0:T(8,128)(2,1)}, bf16[1024,384]{1,0:T(8,128)(2,1)}, f32[192,768]{1,0:T(8,128)}, f32[192,512]{1,0:T(8,128)}, f32[16,1536]{1,0:T(8,...) custom-call(bf16[1024,1536]{1,0:T(8,128)(2,1)} %convert_element_type.196.part_ref, ...), custom_call_target="tpu_custom_call" | custom-call | tf_op jit(solution)/shard_map/finish/pallas_call | solution.py:905
  488.9 2.3 fusion.25
  (248 shorter events, 82.7 us)
Async XLA Ops:
  7.2 153.1 %all-gather.2.cloned.1.call-start = ((), (), s32[]{:S(2)}) async-start(), calls=%async_computation.1 | async-start | bytes 10616832 | tf_op jit(solution)/shard_map/all_gather | solution.py:1040
  94.2 10.8 %copy-start.29 = (f32[4,40,128]{2,1,0:T(8,128)S(1)}, f32[4,40,128]{2,1,0:T(8,128)}, u32[]{:S(2)}) copy-start(f32[4,40,128]{2,1,0:T(8,128)} %get-tuple-element.68) | copy-start | bytes 245764
  94.3 10.9 %copy-start.3 = (bf16[1,1024,1536]{2,1,0:T(8,128)(2,1)S(1)}, bf16[1,1024,1536]{2,1,0:T(8,128)(2,1)}, u32[]{:S(2)}) copy-start(bf16[1,1024,1536]{2,1,0:T(8,128)(2,1)} %get-tuple-element.67) | copy-start | bytes 9437188
  96.6 246.8 %reduce-scatter.2.cloned.1.call-start = ((), (), s32[]{:S(2)}) async-start(), calls=%async_computation.2 | async-start | bytes 10616832 | tf_op jit(solution)/shard_map/reduce_scatter | solution.py:1190
  99.3 70.1 %collective-permute-start.4 = (bf16[1,1024,384]{2,1,0:T(8,128)(2,1)}, bf16[1,1024,384]{2,1,0:T(8,128)(2,1)}, u32[]{:S(2)}, u32[]{:S(2)}) collective-permute-start(bf16[1,1024,384]{2,1,0:T(8,128)(2,1)} %get-tuple-element.74), channel_id=1, source_target_pairs={{0,3},{1,2},{2,1},{3,0},{4,7},{5,6},{6,5},{7,4},{8,11},{9,10},{10,... | collective-permute-start | bytes 2359304 | tf_op jit(solution)/shard_map/ppermute | solution.py:29
  100.7 68.7 %collective-permute-start.3 = (bf16[1,1024,384]{2,1,0:T(8,128)(2,1)}, bf16[1,1024,384]{2,1,0:T(8,128)(2,1)}, u32[]{:S(2)}, u32[]{:S(2)}) collective-permute-start(bf16[1,1024,384]{2,1,0:T(8,128)(2,1)} %get-tuple-element.74), channel_id=1, source_target_pairs={{0,2},{1,3},{2,0},{3,1},{4,6},{5,7},{6,4},{7,5},{8,10},{9,11},{10,... | collective-permute-start | bytes 2359304 | tf_op jit(solution)/shard_map/ppermute | solution.py:29
  105.0 64.4 %collective-permute-start.2 = (bf16[1,1024,384]{2,1,0:T(8,128)(2,1)}, bf16[1,1024,384]{2,1,0:T(8,128)(2,1)}, u32[]{:S(2)}, u32[]{:S(2)}) collective-permute-start(bf16[1,1024,384]{2,1,0:T(8,128)(2,1)} %get-tuple-element.73), channel_id=1, source_target_pairs={{0,1},{1,0},{2,3},{3,2},{4,5},{5,4},{6,7},{7,6},{8,9},{9,8},{10,11... | collective-permute-start | bytes 2359304 | tf_op jit(solution)/shard_map/ppermute | solution.py:29
  105.1 250.2 %copy-start.33 = (f32[1536]{0:T(1024)}, f32[1536]{0:T(1024)S(1)}, u32[]{:S(2)}) copy-start(f32[1536]{0:T(1024)S(1)} %mul.239) | copy-start | bytes 18436
  108.9 24.7 %collective-permute-start.1 = (bf16[1,3,256]{2,1,0:T(4,128)(2,1)S(1)}, bf16[1,3,256]{2,1,0:T(4,128)(2,1)S(1)}, u32[]{:S(2)}, u32[]{:S(2)}) collective-permute-start(bf16[1,3,256]{2,1,0:T(4,128)(2,1)S(1)} %slice.307), channel_id=1, source_target_pairs={{0,4},{1,5},{2,6},{3,7},{8,12},{9,13},{10,14},{11,15},{16,20},{17,... | collective-permute-start | bytes 4616 | tf_op jit(solution)/shard_map/ppermute | solution.py:35
  110.3 20.0 %copy-start.50 = (f32[12]{0:T(128)S(1)}, f32[12]{0:T(128)}, u32[]{:S(2)}) copy-start(f32[12]{0:T(128)} %param.28) | copy-start | bytes 148
  110.3 20.1 %copy-start.51 = (f32[12]{0:T(128)S(1)}, f32[12]{0:T(128)}, u32[]{:S(2)}) copy-start(f32[12]{0:T(128)} %param.27) | copy-start | bytes 148
  110.3 20.7 %copy-start.38 = (f32[768]{0:T(1024)S(1)}, f32[768]{0:T(1024)}, u32[]{:S(2)}) copy-start(f32[768]{0:T(1024)} %param.29) | copy-start | bytes 9220
  110.3 20.7 %copy-start.39 = (f32[768]{0:T(1024)S(1)}, f32[768]{0:T(1024)}, u32[]{:S(2)}) copy-start(f32[768]{0:T(1024)} %param.23) | copy-start | bytes 9220
  110.3 20.7 %copy-start.32 = (f32[4,768]{1,0:T(4,128)S(1)}, f32[4,768]{1,0:T(4,128)}, u32[]{:S(2)}) copy-start(f32[4,768]{1,0:T(4,128)} %param.22) | copy-start | bytes 36868
  110.3 20.7 %copy-start.52 = (f32[12]{0:T(128)S(1)}, f32[12]{0:T(128)}, u32[]{:S(2)}) copy-start(f32[12]{0:T(128)} %param.26) | copy-start | bytes 148
  117.5 16.1 %collective-permute-start = (bf16[1,3,1536]{2,1,0:T(4,128)(2,1)S(1)}, bf16[1,3,1536]{2,1,0:T(4,128)(2,1)S(1)}, u32[]{:S(2)}, u32[]{:S(2)}) collective-permute-start(bf16[1,3,1536]{2,1,0:T(4,128)(2,1)S(1)} %slice.305), channel_id=1, source_target_pairs={{0,4},{1,5},{2,6},{3,7},{8,12},{9,13},{10,14},{11,15},{16,20},{17,... | collective-permute-start | bytes 27656 | tf_op jit(solution)/shard_map/ppermute | solution.py:35
  134.2 23.0 %copy-start.53 = (s32[2]{0:T(128)S(1)}, s32[2]{0:T(128)}, u32[]{:S(2)}) copy-start(s32[2]{0:T(128)} %param.17) | copy-start | bytes 28
  155.8 2.7 collective-permute-start.5
  160.3 11.4 %copy-start.54 = (bf16[1536,3072]{1,0:T(8,128)(2,1)S(1)}, bf16[1536,3072]{1,0:T(8,128)(2,1)}, u32[]{:S(2)}) copy-start(bf16[1536,3072]{1,0:T(8,128)(2,1)} %all-gather.2.cloned.1.call-done) | copy-start | bytes 28311556
  207.9 4.4 collective-permute-start.6
  255.0 28.2 %collective-permute-start.9 = (f32[8,128]{1,0:T(8,128)S(1)}, f32[8,128]{1,0:T(8,128)S(1)}, u32[]{:S(2)}, u32[]{:S(2)}) collective-permute-start(f32[8,128]{1,0:T(8,128)S(1)} %get-tuple-element.175), channel_id=1, source_target_pairs={{0,2},{1,3},{2,0},{3,1},{4,6},{5,7},{6,4},{7,5},{8,10},{9,11},{10,... | collective-permute-start | bytes 12296 | tf_op jit(solution)/shard_map/ppermute | solution.py:29
  257.6 20.6 %collective-permute-start.8 = (bf16[1024,384]{1,0:T(8,128)(2,1)}, bf16[1024,384]{1,0:T(8,128)(2,1)S(1)}, u32[]{:S(2)}, u32[]{:S(2)}) collective-permute-start(bf16[1024,384]{1,0:T(8,128)(2,1)} %convolution_convert_fusion.5), channel_id=1, source_target_pairs={{0,1},{1,0},{2,3},{3,2},{4,5},{5,4},{6,7},{7,6},{8,9},{9,8},{10,11... | collective-permute-start | bytes 2359304 | tf_op jit(solution)/shard_map/ppermute | solution.py:29
  258.2 77.4 %collective-permute-start.11 = (bf16[1024,384]{1,0:T(8,128)(2,1)}, bf16[1024,384]{1,0:T(8,128)(2,1)}, u32[]{:S(2)}, u32[]{:S(2)}) collective-permute-start(bf16[1024,384]{1,0:T(8,128)(2,1)} %convolution_convert_fusion.4), channel_id=1, source_target_pairs={{0,1},{1,0},{2,3},{3,2},{4,5},{5,4},{6,7},{7,6},{8,9},{9,8},{10,11... | collective-permute-start | bytes 2359304 | tf_op jit(solution)/shard_map/ppermute | solution.py:29
  259.9 11.0 %collective-permute-start.7 = (bf16[1,128,1536]{2,1,0:T(8,128)(2,1)S(1)}, bf16[1,128,1536]{2,1,0:T(8,128)(2,1)S(1)}, u32[]{:S(2)}, u32[]{:S(2)}) collective-permute-start(bf16[1,128,1536]{2,1,0:T(8,128)(2,1)S(1)} %fusion.35), channel_id=1, source_target_pairs={{4,0},{5,1},{6,2},{7,3},{12,8},{13,9},{14,10},{15,11},{20,16},{21,... | collective-permute-start | bytes 1179656 | tf_op jit(solution)/shard_map/ppermute | solution.py:35
  282.2 59.3 %collective-permute-start.12 = (bf16[1024,384]{1,0:T(8,128)(2,1)}, bf16[1024,384]{1,0:T(8,128)(2,1)S(1)}, u32[]{:S(2)}, u32[]{:S(2)}) collective-permute-start(bf16[1024,384]{1,0:T(8,128)(2,1)} %add_convert_fusion.1), channel_id=1, source_target_pairs={{0,2},{1,3},{2,0},{3,1},{4,6},{5,7},{6,4},{7,5},{8,10},{9,11},{10,... | collective-permute-start | bytes 2359304 | tf_op jit(solution)/shard_map/ppermute | solution.py:29
  283.2 49.7 %copy-start.45 = (f32[8,128]{1,0:T(8,128)}, f32[8,128]{1,0:T(8,128)S(1)}, u32[]{:S(2)}) copy-start(f32[8,128]{1,0:T(8,128)S(1)} %collective-permute-done.9) | copy-start | bytes 12292
  332.9 7.0 %collective-permute-start.13 = (f32[1,8,256]{2,1,0:T(8,128)}, f32[1,8,256]{2,1,0:T(8,128)S(1)}, u32[]{:S(2)}, u32[]{:S(2)}) collective-permute-start(f32[1,8,256]{2,1,0:T(8,128)} %get-tuple-element.101), channel_id=1, source_target_pairs={{4,0},{5,1},{6,2},{7,3},{12,8},{13,9},{14,10},{15,11},{20,16},{21,... | collective-permute-start | bytes 24584 | tf_op jit(solution)/shard_map/ppermute | solution.py:35
  334.2 5.8 %collective-permute-start.10 = (f32[1,8,1536]{2,1,0:T(8,128)}, f32[1,8,1536]{2,1,0:T(8,128)S(1)}, u32[]{:S(2)}, u32[]{:S(2)}) collective-permute-start(f32[1,8,1536]{2,1,0:T(8,128)} %get-tuple-element.97), channel_id=1, source_target_pairs={{4,0},{5,1},{6,2},{7,3},{12,8},{13,9},{14,10},{15,11},{20,16},{21,... | collective-permute-start | bytes 147464 | tf_op jit(solution)/shard_map/ppermute | solution.py:35
  345.3 29.3 %collective-permute-start.14 = (bf16[192,1536]{1,0:T(8,128)(2,1)}, bf16[192,1536]{1,0:T(8,128)(2,1)}, u32[]{:S(2)}, u32[]{:S(2)}) collective-permute-start(bf16[192,1536]{1,0:T(8,128)(2,1)} %pad_maximum_fusion.7), channel_id=1, source_target_pairs={{0,2},{1,3},{2,0},{3,1},{4,6},{5,7},{6,4},{7,5},{8,10},{9,11},{10,... | collective-permute-start | bytes 1769480 | tf_op jit(solution)/shard_map/ppermute | solution.py:29
  366.9 26.7 %collective-permute-start.16 = (bf16[4,192,1920]{2,1,0:T(8,128)(2,1)}, bf16[4,192,1920]{2,1,0:T(8,128)(2,1)}, u32[]{:S(2)}, u32[]{:S(2)}) collective-permute-start(bf16[4,192,1920]{2,1,0:T(8,128)(2,1)} %dynamic-slice_bitcast_fusion), channel_id=1, source_target_pairs={{0,4},{4,0},{1,5},{5,1},{2,6},{6,2},{3,7},{7,3},{8,12},{12,8},{9,1... | collective-permute-start | bytes 8847368 | tf_op jit(solution)/shard_map/ppermute | solution.py:1212
  373.8 9.3 %copy-start.34 = (f32[1536]{0:T(1024)S(1)}, f32[1536]{0:T(1024)}, u32[]{:S(2)}) copy-start(f32[1536]{0:T(1024)} %copy-done.33) | copy-start | bytes 18436
  373.8 19.8 %collective-permute-start.15 = (bf16[1024,384]{1,0:T(8,128)(2,1)}, bf16[1024,384]{1,0:T(8,128)(2,1)}, u32[]{:S(2)}, u32[]{:S(2)}) collective-permute-start(bf16[1024,384]{1,0:T(8,128)(2,1)} %add_convert_fusion), channel_id=1, source_target_pairs={{0,1},{1,0},{2,3},{3,2},{4,5},{5,4},{6,7},{7,6},{8,9},{9,8},{10,11... | collective-permute-start | bytes 2359304 | tf_op jit(solution)/shard_map/ppermute | solution.py:29
  (48 other events, 197.5 us)
Sparse Core Ops, SparseCore 0:
  96.7 61.5 all-gather.1
  255.1 78.2 reduce-scatter.1

commit v8 on v6

--- a/solution.py
+++ b/solution.py
@@ -19,6 +19,8 @@
 LANES_STEP = HEADS_STEP * HEADDIM
 GATE_HEADS = 12
 GATE_LANES = GATE_HEADS * HEADDIM
+WIDE_HEADS = 24
+WIDE_LANES = WIDE_HEADS * HEADDIM
 F32 = jnp.float32
 BF16 = jnp.bfloat16
 HIGHEST = lax.Precision.HIGHEST
@@ -301,9 +303,9 @@
     stats = stats_ref[0].T
     scale = lax.rsqrt(stats[:, 0:1] / INNER + EPSILON)
     cross = scale * stats[:, 1:2] / INNER
-    grown = jnp.exp(turned(cols_ref[...], pl.program_id(0) * GATE_HEADS))
+    grown = jnp.exp(turned(cols_ref[...], pl.program_id(0) * WIDE_HEADS))
     low_half = low_lanes(GROUP)
-    for pair in range(GATE_HEADS // 2):
+    for pair in range(WIDE_HEADS // 2):
         lanes = slice(PAIR * pair, PAIR * (pair + 1))
         mixed = mixed_ref[:, lanes]
         gate = gate_ref[:, lanes].astype(F32)
@@ -327,9 +329,9 @@
 
 def gate_blocks(mixed, gate, gno, x, stats, gain, wr, cols, heads):
     tokens, width = x.shape
-    blocks, steps = tokens // GROUP, width // GATE_LANES
-    wide = pl.BlockSpec((GROUP, GATE_LANES), lambda g, b: (b, g))
-    line = pl.BlockSpec((1, GATE_LANES), lambda g, b: (0, g))
+    blocks, steps = tokens // GROUP, width // WIDE_LANES
+    wide = pl.BlockSpec((GROUP, WIDE_LANES), lambda g, b: (b, g))
+    line = pl.BlockSpec((1, WIDE_LANES), lambda g, b: (0, g))
     return pl.pallas_call(
         functools.partial(gate_kernel, heads),
         grid=(steps, blocks),
@@ -342,7 +344,7 @@
         ],
         out_specs=[
             wide, wide, wide, line, line,
-            pl.BlockSpec((1, STATE, GATE_LANES), lambda g, b: (b, 0, g)),
+            pl.BlockSpec((1, STATE, WIDE_LANES), lambda g, b: (b, 0, g)),
         ],
         out_shape=[
             jax.ShapeDtypeStruct((tokens, width), BF16),
@@ -352,7 +354,7 @@
             jax.ShapeDtypeStruct((1, width), F32),
             jax.ShapeDtypeStruct((blocks, STATE, width), F32),
         ],
-        scratch_shapes=[pltpu.VMEM((GROUP, GATE_LANES), BF16)],
+        scratch_shapes=[pltpu.VMEM((GROUP, WIDE_LANES), BF16)],
         cost_estimate=pl.CostEstimate(
             flops=2 * tokens * STATE * width,
             bytes_accessed=tokens * width * 16 + blocks * STATE * width * 4,

time: 500 us -> 510 us (1.020)
  waiting for transfers between devices: 11.3 us -> 21.6 us
  matrix products: 88 us -> 97.7 us
  starting transfers between devices: 30.8 us -> 21.2 us
    ppermute x6, starting transfers between devices: 19 us -> 8.16 us  [passed_along(): return lax.ppermute(x, axis, pairs)]
    dot_general x16, matrix products: 88 us -> 97.7 us  [dot(): lax.dot_general(a, b, (((da,), (db,)), ((), ())), preferred_element_type=...]
    all_gather x1, waiting for transfers between devices: 0.01 us -> 6.46 us  [gathered(): return lax.all_gather(x, ('fsdp', 'ctx'), axis=0, tiled=True)]
  transfers between devices with their start and end apart: 19 -> 19, of which waited for: 3 -> 5; matrix products, arithmetic and copies ran while one was open for 19% -> 19% of each run, Pallas kernels for 14% -> 14%
where the time goes in v8:
time: 510 us; the launch traced here: 502 us
  Pallas kernels  265 us (52%)
  matrix products  97.7 us (19%)
  other arithmetic  44.4 us (9%)
  local copies, waits for them, and re-layouts  36.3 us (7%)
  waiting for transfers between devices  21.6 us (4%)
  starting transfers between devices  21.2 us (4%)
  between operations  15.5 us (3%)
    dot_general x16, matrix products, dot(): lax.dot_general(a, b, (((da,), (db,)), ((), ())), preferred_element_type=...  97.7 us
    pallas_call x1, Pallas kernels, fetch(): pl.pallas_call(fetch_kernel, in_specs=[anywhere] * 6, out_specs=[anywhere...  83 us
    pallas_call x1, Pallas kernels, finish(): pl.pallas_call(finish_kernel, in_specs=[anywhere, anywhere, anywhere, any...  69.9 us
    pallas_call x1, Pallas kernels, back_blocks(): pl.pallas_call(functools.partial(back_kernel, groups, heads), grid=(block...  49.6 us
    pallas_call x1, Pallas kernels, mix_blocks(): pl.pallas_call(functools.partial(mix_kernel, heads), grid=(blocks, steps)...  29.5 us
    pallas_call x1, Pallas kernels, start_blocks(): pl.pallas_call(functools.partial(start_kernel, groups, heads), grid=(bloc...  18.4 us
    pallas_call x1, Pallas kernels, gate_blocks(): pl.pallas_call(functools.partial(gate_kernel, heads), grid=(steps, blocks...  14.5 us
    ppermute x10, waiting for transfers between devices, swap(): return lax.ppermute(x, 'tp', [(i, i ^ bit) for i in range(count)])  13.9 us
  transfers between devices with their start and end apart: 19, of which 5 were waited for; matrix products, arithmetic and copies ran while one was open for 19% of the time, Pallas kernels for 14%

profile of v8, /device:TPU:0, one launch (start us, length us, event | category | flops | bytes accessed | tf_op | source)
XLA Modules:
  0.0 501.6 jit_solution(15965956395047800075)
XLA Ops:
  10.9 2.3 fusion.71
  15.5 83.0 %fetch.1 = (bf16[1,1024,1536]{2,1,0:T(8,128)(2,1)}, bf16[1536,1536]{1,0:T(8,128)(2,1)}, bf16[192,1536]{1,0:T(8,128)(2,1)}, bf16[1536,256]{1,0:T(8,128)(2,1)}, bf...) custom-call(bf16[2,1024,384]{2,1,0:T(8,128)(2,1)} %x_ref.1, bf16[192,768]{1,0:T(8,128)(2,1)} %get-tuple-element.178.inner_ref, ...), custom_call_target="tpu_custom_call" | custom-call | tf_op jit(solution)/shard_map/fetch/pallas_call | solution.py:750
  102.0 2.6 constant_dynamic-slice_fusion.2
  106.1 2.9 collective-permute-start.2
  114.4 5.5 %convolution_convert_fusion.3.inner_ref.pre_ref = bf16[1024,1536]{1,0:T(8,128)(2,1)S(1)} fusion(bf16[1536,1536]{1,0:T(8,128)(2,1)S(1)} %bitcast.215, bf16[1,1024,1536]{2,1,0:T(8,128)(2,1)S(1)} %copy-done.3, f32[1536]{0:T(1024)S(1)} %mul.239, f32[1024]{0:T(1024)S(1)} %get-tuple-element.174), kind=kOutput, calls=%fused_computation.27 | convolution fusion | flops 4839702528 | bytes 11020288 | tf_op jit(solution)/shard_map/dot_general | solution.py:58
  127.4 18.4 %start_blocks.1 = (bf16[1024,1536]{1,0:T(8,128)(2,1)}, bf16[1024,1536]{1,0:T(8,128)(2,1)}, bf16[1024,256]{1,0:T(8,128)(2,1)}, f32[1024,256]{1,0:T(8,128)}, f32[1...) custom-call(bf16[1024,1536]{1,0:T(8,128)(2,1)} %copy-done.14, ...), custom_call_target="tpu_custom_call" | custom-call | flops 434110464 | bytes 12582912 | tf_op jit(solution)/shard_map/start_blocks/pallas_call | solution.py:162
  153.4 6.5 %all-gather.2.cloned.1.call-done = bf16[1536,3072]{1,0:T(8,128)(2,1)} async-done(((bf16[192,3072]{1,0:T(8,128)(2,1)}), bf16[1536,3072]{1,0:T(8,128)(2,1)}) %all-gather.2.cloned.1.call-update) | async-done | bytes 9437200 | tf_op jit(solution)/shard_map/all_gather | solution.py:1042
  159.9 9.1 %fusion.12.gate_ref = bf16[1024,1536]{1,0:T(8,128)(2,1)} fusion(bf16[1536,3072]{1,0:T(8,128)(2,1)} %all-gather.2.cloned.1.call-done, bf16[1,1024,1536]{2,1,0:T(8,128)(2,1)S(1)} %copy-done.3, f32[1536]{0:T(1024)S(1)} %mul.239, f32[1024]{0:T(1024)S(1)} %get-tuple-element.174), kind=kOutput, calls=%fused_computation.24 | convolution fusion | flops 4839702528 | bytes 11020288 | tf_op jit(solution)/shard_map/dot_general | solution.py:58
  169.0 3.3 collective-permute-done.3
  172.3 2.3 broadcast_select_fusion.7
  174.6 6.7 %fusion.18.gno_ref = bf16[1024,1536]{1,0:T(8,128)(2,1)} fusion(bf16[1536,3072]{1,0:T(8,128)(2,1)S(1)} %copy-done.52, bf16[1,1024,384]{2,1,0:T(8,128)(2,1)S(1)} %get-tuple-element.154, bf16[1,1024,384]{2,1,0:T(8,128)(2,1)S(1)} %get-tuple-element.153, bf16[1,1024,384]{2,1,0:T(8,128)(2,1)S(1)} %get-tuple-element.152, ...), kind=kOutput, calls=%fused_computation.26 | convolution fusion | flops 4850712576 | bytes 11014144 | tf_op jit(solution)/shard_map/dot_general | solution.py:58
  181.3 29.5 %mix_blocks.1 = (f32[1024,1536]{1,0:T(8,128)}, f32[4,8,256]{2,1,0:T(8,128)}) custom-call(bf16[1024,1536]{1,0:T(8,128)(2,1)} %get-tuple-element.72.x_ref, bf16[1024,1536]{1,0:T(8,128)(2,1)} %fusion.12.gate_ref, bf16[1024,1536]{1,0:T(8,128)(2,1)} %fusion.18.gno_ref, bf16[1024,256]{1,0:T(8,128)(2,1)} %get-tuple-element.80.wr_ref, ...), custom_call_target="tpu_custom_call" | custom-call | flops 4831838208 | bytes 15728640 | tf_op jit(solution)/shard_map/mix_blocks/pallas_call | solution.py:267
  210.9 4.1 collective-permute-done.6
  216.4 14.5 %gate_blocks.1 = (bf16[1024,1536]{1,0:T(8,128)(2,1)}, bf16[1024,1536]{1,0:T(8,128)(2,1)}, bf16[1024,1536]{1,0:T(8,128)(2,1)}, f32[1,1536]{1,0:T(1,128)}, f32[1,1536]{1,0:T(1,128)}, /*index=5*/f32[4,128,1536]{2,1,0:T(8,128)}) custom-call(f32[1024,1536]{1,0:T(8,128)} %get-tuple-element.85.mixed_ref, bf16[1024,1536]{1,0:T(8,128)(2,1)} %fusion.12.gate_ref, ...), custom_call_target="tpu_custom_call" | custom-call | flops 402653184 | bytes 28311552 | tf_op jit(solution)/shard_map/gate_blocks/pallas_call | solution.py:335
  230.9 5.1 %convolution_convert_fusion.4 = bf16[1024,384]{1,0:T(8,128)(2,1)} fusion(bf16[1024,1536]{1,0:T(8,128)(2,1)} %get-tuple-element.93, bf16[1536,3072]{1,0:T(8,128)(2,1)} %all-gather.2.cloned.1.call-done, s32[]{:T(128)S(6)} %select_n.130), kind=kOutput, calls=%fused_computation.45 | convolution fusion | flops 1208352768 | bytes 5111812 | tf_op jit(solution)/shard_map/dot_general | solution.py:58
  236.0 4.1 convolution_convert_fusion.5
  240.1 16.7 %convolution_convert_fusion.1 = bf16[1536,1536]{1,0:T(8,128)(2,1)S(1)} fusion(bf16[1024,1536]{1,0:T(8,128)(2,1)S(1)} %copy-done.53, bf16[1,1024,384]{2,1,0:T(8,128)(2,1)S(1)} %copy-done.28, bf16[1,1024,384]{2,1,0:T(8,128)(2,1)S(1)} %copy-done.26, bf16[1,1024,384]{2,1,0:T(8,128)(2,1)S(1)} %copy-done.24, bf16[1,1024,384]{2,1,0:T(8,128)(2,1)S(1)} %copy-done.22, ...), kind=kOutput, calls=%fused_computation.4 | convolution fusion | flops 4851499008 | bytes 11014144 | tf_op jit(solution)/shard_map/dot_general | solution.py:58
  256.9 5.7 %convolution_convert_fusion = bf16[1536,1536]{1,0:T(8,128)(2,1)S(1)} fusion(bf16[1024,1536]{1,0:T(8,128)(2,1)S(1)} %copy-done.55, bf16[1,1024,1536]{2,1,0:T(8,128)(2,1)S(1)} %copy-done.3, f32[1536]{0:T(1024)S(1)} %mul.239, f32[1024]{0:T(1024)S(1)} %get-tuple-element.174), kind=kOutput, calls=%fused_computation.3 | convolution fusion | flops 4840488960 | bytes 11020288 | tf_op jit(solution)/shard_map/dot_general | solution.py:58
  262.6 4.8 pad_maximum_fusion
  272.5 8.9 %fusion.15 = bf16[1024,1536]{1,0:T(8,128)(2,1)} fusion(bf16[1024,1536]{1,0:T(8,128)(2,1)S(1)} %copy-done.56, bf16[1536,3072]{1,0:T(8,128)(2,1)} %all-gather.2.cloned.1.call-done), kind=kOutput, calls=%fused_computation.25 | convolution fusion | flops 4833411072 | bytes 11010048 | tf_op jit(solution)/shard_map/dot_general | solution.py:58
  282.9 6.5 %collective-permute-done.8 = bf16[1024,384]{1,0:T(8,128)(2,1)S(1)} collective-permute-done((bf16[1024,384]{1,0:T(8,128)(2,1)}, bf16[1024,384]{1,0:T(8,128)(2,1)S(1)}, u32[]{:S(2)}, u32[]{:S(2)}) %collective-permute-start.8) | collective-permute-done | bytes 786464 | tf_op jit(solution)/shard_map/ppermute | solution.py:31
  289.4 4.0 add_convert_fusion.1
  295.6 49.6 %back_blocks.1 = (bf16[1024,1536]{1,0:T(8,128)(2,1)}, bf16[1024,384]{1,0:T(8,128)(2,1)}, f32[4,8,384]{2,1,0:T(8,128)}, f32[8,256]{1,0:T(8,128)}, f32[8,128]{1,0:...) custom-call(bf16[1024,1536]{1,0:T(8,128)(2,1)} %get-tuple-element.72.x_ref, ...), custom_call_target="tpu_custom_call" | custom-call | flops 9663676416 | bytes 22020096 | tf_op jit(solution)/shard_map/back_blocks/pallas_call | solution.py:571
  347.9 4.3 add_bitcast_fusion.1
  358.4 4.2 fusion.28
  363.8 2.8 add_convert_fusion
  366.7 7.3 %convolution_convert_fusion.2.grad_ref = bf16[1536,1920]{1,0:T(8,128)(2,1)S(1)} fusion(bf16[1024,1920]{1,0:T(8,128)(2,1)S(1)} %pad_maximum_fusion.1, bf16[1,1024,1536]{2,1,0:T(8,128)(2,1)S(1)} %copy-done.4, f32[1536]{0:T(1024)S(1)} %mul.239, f32[1024]{0:T(1024)S(1)} %get-tuple-element.174), kind=kOutput, calls=%fused_computation.5 | convolution fusion | flops 6049038336 | bytes 12986368 | tf_op jit(solution)/shard_map/dot_general | solution.py:58
  374.0 2.5 copy-done.2
  387.8 8.2 %fusion.72 = f32[1024,1536]{1,0:T(8,128)S(1)} fusion(bf16[1024,1536]{1,0:T(8,128)(2,1)} %fusion.43, bf16[1536,1536]{1,0:T(8,128)(2,1)} %get-tuple-element.69), kind=kOutput, calls=%fused_computation.163 | convolution fusion | flops 4831838208 | bytes 14155776 | tf_op jit(solution)/shard_map/dot_general | solution.py:58
  396.1 3.3 multiply_reduce_fusion
  406.5 69.9 %finish.1 = (bf16[1024,384]{1,0:T(8,128)(2,1)}, bf16[1024,384]{1,0:T(8,128)(2,1)}, f32[192,768]{1,0:T(8,128)}, f32[192,512]{1,0:T(8,128)}, f32[16,1536]{1,0:T(8,...) custom-call(bf16[1024,1536]{1,0:T(8,128)(2,1)} %convert_element_type.196.part_ref, ...), custom_call_target="tpu_custom_call" | custom-call | tf_op jit(solution)/shard_map/finish/pallas_call | solution.py:907
  492.0 2.3 fusion.25
  (244 shorter events, 85.2 us)
Async XLA Ops:
  7.2 152.7 %all-gather.2.cloned.1.call-start = ((), (), s32[]{:S(2)}) async-start(), calls=%async_computation.1 | async-start | bytes 10616832 | tf_op jit(solution)/shard_map/all_gather | solution.py:1042
  99.6 9.4 %copy-start.29 = (f32[4,40,128]{2,1,0:T(8,128)S(1)}, f32[4,40,128]{2,1,0:T(8,128)}, u32[]{:S(2)}) copy-start(f32[4,40,128]{2,1,0:T(8,128)} %get-tuple-element.68) | copy-start | bytes 245764
  99.6 9.6 %copy-start.3 = (bf16[1,1024,1536]{2,1,0:T(8,128)(2,1)S(1)}, bf16[1,1024,1536]{2,1,0:T(8,128)(2,1)}, u32[]{:S(2)}) copy-start(bf16[1,1024,1536]{2,1,0:T(8,128)(2,1)} %get-tuple-element.67) | copy-start | bytes 9437188
  101.9 253.7 %reduce-scatter.2.cloned.1.call-start = ((), (), s32[]{:S(2)}) async-start(), calls=%async_computation.2 | async-start | bytes 10616832 | tf_op jit(solution)/shard_map/reduce_scatter | solution.py:1192
  104.7 64.3 %collective-permute-start.4 = (bf16[1,1024,384]{2,1,0:T(8,128)(2,1)}, bf16[1,1024,384]{2,1,0:T(8,128)(2,1)}, u32[]{:S(2)}, u32[]{:S(2)}) collective-permute-start(bf16[1,1024,384]{2,1,0:T(8,128)(2,1)} %get-tuple-element.74), channel_id=1, source_target_pairs={{0,3},{1,2},{2,1},{3,0},{4,7},{5,6},{6,5},{7,4},{8,11},{9,10},{10,... | collective-permute-start | bytes 2359304 | tf_op jit(solution)/shard_map/ppermute | solution.py:31
  106.1 66.1 %collective-permute-start.3 = (bf16[1,1024,384]{2,1,0:T(8,128)(2,1)}, bf16[1,1024,384]{2,1,0:T(8,128)(2,1)}, u32[]{:S(2)}, u32[]{:S(2)}) collective-permute-start(bf16[1,1024,384]{2,1,0:T(8,128)(2,1)} %get-tuple-element.74), channel_id=1, source_target_pairs={{0,2},{1,3},{2,0},{3,1},{4,6},{5,7},{6,4},{7,5},{8,10},{9,11},{10,... | collective-permute-start | bytes 2359304 | tf_op jit(solution)/shard_map/ppermute | solution.py:31
  106.1 62.9 %collective-permute-start.2 = (bf16[1,1024,384]{2,1,0:T(8,128)(2,1)}, bf16[1,1024,384]{2,1,0:T(8,128)(2,1)}, u32[]{:S(2)}, u32[]{:S(2)}) collective-permute-start(bf16[1,1024,384]{2,1,0:T(8,128)(2,1)} %get-tuple-element.73), channel_id=1, source_target_pairs={{0,1},{1,0},{2,3},{3,2},{4,5},{5,4},{6,7},{7,6},{8,9},{9,8},{10,11... | collective-permute-start | bytes 2359304 | tf_op jit(solution)/shard_map/ppermute | solution.py:31
  109.1 257.6 %copy-start.33 = (f32[1536]{0:T(1024)}, f32[1536]{0:T(1024)S(1)}, u32[]{:S(2)}) copy-start(f32[1536]{0:T(1024)S(1)} %mul.239) | copy-start | bytes 18436
  113.0 13.8 %collective-permute-start.1 = (bf16[1,3,256]{2,1,0:T(4,128)(2,1)S(1)}, bf16[1,3,256]{2,1,0:T(4,128)(2,1)S(1)}, u32[]{:S(2)}, u32[]{:S(2)}) collective-permute-start(bf16[1,3,256]{2,1,0:T(4,128)(2,1)S(1)} %slice.307), channel_id=1, source_target_pairs={{0,4},{1,5},{2,6},{3,7},{8,12},{9,13},{10,14},{11,15},{16,20},{17,... | collective-permute-start | bytes 4616 | tf_op jit(solution)/shard_map/ppermute | solution.py:37
  114.4 9.8 %copy-start.38 = (f32[768]{0:T(1024)S(1)}, f32[768]{0:T(1024)}, u32[]{:S(2)}) copy-start(f32[768]{0:T(1024)} %param.29) | copy-start | bytes 9220
  114.4 9.8 %copy-start.39 = (f32[768]{0:T(1024)S(1)}, f32[768]{0:T(1024)}, u32[]{:S(2)}) copy-start(f32[768]{0:T(1024)} %param.23) | copy-start | bytes 9220
  114.4 9.8 %copy-start.32 = (f32[4,768]{1,0:T(4,128)S(1)}, f32[4,768]{1,0:T(4,128)}, u32[]{:S(2)}) copy-start(f32[4,768]{1,0:T(4,128)} %param.22) | copy-start | bytes 36868
  114.4 9.8 %copy-start.50 = (f32[12]{0:T(128)S(1)}, f32[12]{0:T(128)}, u32[]{:S(2)}) copy-start(f32[12]{0:T(128)} %param.26) | copy-start | bytes 148
  121.6 5.2 %collective-permute-start = (bf16[1,3,1536]{2,1,0:T(4,128)(2,1)S(1)}, bf16[1,3,1536]{2,1,0:T(4,128)(2,1)S(1)}, u32[]{:S(2)}, u32[]{:S(2)}) collective-permute-start(bf16[1,3,1536]{2,1,0:T(4,128)(2,1)S(1)} %slice.305), channel_id=1, source_target_pairs={{0,4},{1,5},{2,6},{3,7},{8,12},{9,13},{10,14},{11,15},{16,20},{17,... | collective-permute-start | bytes 27656 | tf_op jit(solution)/shard_map/ppermute | solution.py:37
  127.4 23.0 %copy-start.51 = (s32[2]{0:T(128)S(1)}, s32[2]{0:T(128)}, u32[]{:S(2)}) copy-start(s32[2]{0:T(128)} %param.17) | copy-start | bytes 28
  149.1 2.6 collective-permute-start.5
  159.9 14.7 %copy-start.52 = (bf16[1536,3072]{1,0:T(8,128)(2,1)S(1)}, bf16[1536,3072]{1,0:T(8,128)(2,1)}, u32[]{:S(2)}) copy-start(bf16[1536,3072]{1,0:T(8,128)(2,1)} %all-gather.2.cloned.1.call-done) | copy-start | bytes 28311556
  210.8 4.2 collective-permute-start.6
  240.1 16.8 %copy-start.55 = (bf16[1024,1536]{1,0:T(8,128)(2,1)S(1)}, bf16[1024,1536]{1,0:T(8,128)(2,1)}, u32[]{:S(2)}) copy-start(bf16[1024,1536]{1,0:T(8,128)(2,1)} %get-tuple-element.94) | copy-start | bytes 9437188
  267.4 111.8 %collective-permute-start.12 = (f32[8,128]{1,0:T(8,128)}, f32[8,128]{1,0:T(8,128)}, u32[]{:S(2)}, u32[]{:S(2)}) collective-permute-start(f32[8,128]{1,0:T(8,128)} %get-tuple-element.173), channel_id=1, source_target_pairs={{0,2},{1,3},{2,0},{3,1},{4,6},{5,7},{6,4},{7,5},{8,10},{9,11},{10,... | collective-permute-start | bytes 12296 | tf_op jit(solution)/shard_map/ppermute | solution.py:31
  268.8 20.6 %collective-permute-start.8 = (bf16[1024,384]{1,0:T(8,128)(2,1)}, bf16[1024,384]{1,0:T(8,128)(2,1)S(1)}, u32[]{:S(2)}, u32[]{:S(2)}) collective-permute-start(bf16[1024,384]{1,0:T(8,128)(2,1)} %convolution_convert_fusion.5), channel_id=1, source_target_pairs={{0,1},{1,0},{2,3},{3,2},{4,5},{5,4},{6,7},{7,6},{8,9},{9,8},{10,11... | collective-permute-start | bytes 2359304 | tf_op jit(solution)/shard_map/ppermute | solution.py:31
  270.8 77.1 %collective-permute-start.10 = (bf16[1024,384]{1,0:T(8,128)(2,1)}, bf16[1024,384]{1,0:T(8,128)(2,1)}, u32[]{:S(2)}, u32[]{:S(2)}) collective-permute-start(bf16[1024,384]{1,0:T(8,128)(2,1)} %convolution_convert_fusion.4), channel_id=1, source_target_pairs={{0,1},{1,0},{2,3},{3,2},{4,5},{5,4},{6,7},{7,6},{8,9},{9,8},{10,11... | collective-permute-start | bytes 2359304 | tf_op jit(solution)/shard_map/ppermute | solution.py:31
  271.1 10.2 %collective-permute-start.7 = (bf16[1,128,1536]{2,1,0:T(8,128)(2,1)S(1)}, bf16[1,128,1536]{2,1,0:T(8,128)(2,1)S(1)}, u32[]{:S(2)}, u32[]{:S(2)}) collective-permute-start(bf16[1,128,1536]{2,1,0:T(8,128)(2,1)S(1)} %fusion.35), channel_id=1, source_target_pairs={{4,0},{5,1},{6,2},{7,3},{12,8},{13,9},{14,10},{15,11},{20,16},{21,... | collective-permute-start | bytes 1179656 | tf_op jit(solution)/shard_map/ppermute | solution.py:37
  293.4 60.3 %collective-permute-start.11 = (bf16[1024,384]{1,0:T(8,128)(2,1)}, bf16[1024,384]{1,0:T(8,128)(2,1)S(1)}, u32[]{:S(2)}, u32[]{:S(2)}) collective-permute-start(bf16[1024,384]{1,0:T(8,128)(2,1)} %add_convert_fusion.1), channel_id=1, source_target_pairs={{0,2},{1,3},{2,0},{3,1},{4,6},{5,7},{6,4},{7,5},{8,10},{9,11},{10,... | collective-permute-start | bytes 2359304 | tf_op jit(solution)/shard_map/ppermute | solution.py:31
  345.2 7.0 %collective-permute-start.13 = (f32[1,8,256]{2,1,0:T(8,128)}, f32[1,8,256]{2,1,0:T(8,128)S(1)}, u32[]{:S(2)}, u32[]{:S(2)}) collective-permute-start(f32[1,8,256]{2,1,0:T(8,128)} %get-tuple-element.101), channel_id=1, source_target_pairs={{4,0},{5,1},{6,2},{7,3},{12,8},{13,9},{14,10},{15,11},{20,16},{21,... | collective-permute-start | bytes 24584 | tf_op jit(solution)/shard_map/ppermute | solution.py:37
  346.5 5.8 %collective-permute-start.9 = (f32[1,8,1536]{2,1,0:T(8,128)}, f32[1,8,1536]{2,1,0:T(8,128)S(1)}, u32[]{:S(2)}, u32[]{:S(2)}) collective-permute-start(f32[1,8,1536]{2,1,0:T(8,128)} %get-tuple-element.97), channel_id=1, source_target_pairs={{4,0},{5,1},{6,2},{7,3},{12,8},{13,9},{14,10},{15,11},{20,16},{21,... | collective-permute-start | bytes 147464 | tf_op jit(solution)/shard_map/ppermute | solution.py:37
  357.6 30.2 %collective-permute-start.14 = (bf16[192,1536]{1,0:T(8,128)(2,1)}, bf16[192,1536]{1,0:T(8,128)(2,1)}, u32[]{:S(2)}, u32[]{:S(2)}) collective-permute-start(bf16[192,1536]{1,0:T(8,128)(2,1)} %pad_maximum_fusion.7), channel_id=1, source_target_pairs={{0,2},{1,3},{2,0},{3,1},{4,6},{5,7},{6,4},{7,5},{8,10},{9,11},{10,... | collective-permute-start | bytes 1769480 | tf_op jit(solution)/shard_map/ppermute | solution.py:31
  378.3 28.2 %collective-permute-start.16 = (bf16[4,192,1920]{2,1,0:T(8,128)(2,1)}, bf16[4,192,1920]{2,1,0:T(8,128)(2,1)}, u32[]{:S(2)}, u32[]{:S(2)}) collective-permute-start(bf16[4,192,1920]{2,1,0:T(8,128)(2,1)} %dynamic-slice_bitcast_fusion), channel_id=1, source_target_pairs={{0,4},{4,0},{1,5},{5,1},{2,6},{6,2},{3,7},{7,3},{8,12},{12,8},{9,1... | collective-permute-start | bytes 8847368 | tf_op jit(solution)/shard_map/ppermute | solution.py:1214
  386.0 10.0 %copy-start.5 = (bf16[1,1024,1536]{2,1,0:T(8,128)(2,1)S(1)}, bf16[1,1024,1536]{2,1,0:T(8,128)(2,1)}, u32[]{:S(2)}) copy-start(bf16[1,1024,1536]{2,1,0:T(8,128)(2,1)} %get-tuple-element.67) | copy-start | bytes 9437188
  386.0 10.0 %copy-start.12 = (bf16[1024,1536]{1,0:T(8,128)(2,1)S(1)}, bf16[1024,1536]{1,0:T(8,128)(2,1)}, u32[]{:S(2)}) copy-start(bf16[1024,1536]{1,0:T(8,128)(2,1)} %fusion.15) | copy-start | bytes 9437188
  386.0 10.0 %copy-start.34 = (f32[1536]{0:T(1024)S(1)}, f32[1536]{0:T(1024)}, u32[]{:S(2)}) copy-start(f32[1536]{0:T(1024)} %copy-done.33) | copy-start | bytes 18436
  386.0 20.5 %collective-permute-start.15 = (bf16[1024,384]{1,0:T(8,128)(2,1)}, bf16[1024,384]{1,0:T(8,128)(2,1)}, u32[]{:S(2)}, u32[]{:S(2)}) collective-permute-start(bf16[1024,384]{1,0:T(8,128)(2,1)} %add_convert_fusion), channel_id=1, source_target_pairs={{0,1},{1,0},{2,3},{3,2},{4,5},{5,4},{6,7},{7,6},{8,9},{9,8},{10,11... | collective-permute-start | bytes 2359304 | tf_op jit(solution)/shard_map/ppermute | solution.py:31
  (46 other events, 184.5 us)
Sparse Core Ops, SparseCore 0:
  102.1 57.7 all-gather.1
  267.5 75.9 reduce-scatter.1
